TPU v7x, 512 devices: a whole 4x8x8 slice. The times are simulated.
512 devices in a mesh: tile: 64 (over z, y), scan: 8 (over x, core).
Axes of the slice: x: 4, y: 8, z: 8, core: 2. Of those that a mesh axis runs over, the one named last changes fastest.
Arguments:
- object_real: float32 [3, 64, 128, 128], P(None, 'tile'), may hold values from 0.5 to 1.5
- object_imag: float32 [3, 64, 128, 128], P(None, 'tile'), may hold values from -1 to 1
- probe_modes: float32 [2, 2, 128, 128], replicated, may hold values from -6 to 6
- measured: float32 [64, 8, 1, 128, 128], P('tile', 'scan'), may hold values from 1 to 6
- offsets: int32 [64, 8, 1, 2], P('tile', 'scan'), may hold values from 0 to 127
- live: int32 [64, 8, 1], P('tile', 'scan'), may hold values 0 or 1
Outputs:
- object_real_out: float32 [3, 64, 128, 128], P(None, 'tile')
- object_imag_out: float32 [3, 64, 128, 128], P(None, 'tile')
- probe_out: float32 [2, 2, 128, 128], replicated
All inputs are finite; a program needn't handle non-finite values. No bound on the sum of `live` on one device may be relied on, other than what follows from the above.
Results may differ from a plain program's by a relative error of at most 0.0003.
Values sent between devices are 32-bit elements; how exact they have to be, the bound alone decides.
No kernel may reach another device: no remote copies, remote signals or barrier semaphores. Data moves between devices by JAX's collectives and lax.ppermute only.
A program may use at most 64 MiB of HBM per device.

v0:
```python
import math

import jax
import jax.numpy as jnp
from jax import lax
from jax.sharding import PartitionSpec as P

GRID = 8
ITERS = 2


object_rate = 0.008
probe_rate = 0.03


def shifted(shard, axis, by):
    size = lax.axis_size(axis)
    return lax.ppermute(shard, axis, [(i, (i + by) % size) for i in range(size)])


def make_tables(pattern_side):
    positions = lax.iota(jnp.int32, pattern_side)
    product = positions[:, None] * positions[None, :] % pattern_side
    angles = 2.0 * math.pi / pattern_side * product.astype(jnp.float32)
    scaling = 1.0 / math.sqrt(pattern_side)
    frequency = jnp.where(
        positions < pattern_side // 2, positions, positions - pattern_side
    ).astype(jnp.float32)
    phases = (
        -4.0
        * math.pi
        * (frequency[:, None] ** 2 + frequency[None, :] ** 2)
        / (pattern_side * pattern_side)
    )
    return (jnp.cos(angles) * scaling, jnp.sin(angles) * scaling, jnp.cos(phases), jnp.sin(phases))


def from_left(matrix, values):
    return jnp.einsum("jk,mkl->mjl", matrix, values, precision=lax.Precision.HIGHEST)


def from_right(values, matrix):
    return jnp.einsum("mjk,kl->mjl", values, matrix, precision=lax.Precision.HIGHEST)


def transform(part_real, part_imag, tables, sign):
    cosine, sine_table = (tables[0], tables[1])
    left_real = from_left(cosine, part_real) + sign * from_left(sine_table, part_imag)
    left_imag = from_left(cosine, part_imag) - sign * from_left(sine_table, part_real)
    out_real = from_right(left_real, cosine) + sign * from_right(left_imag, sine_table)
    out_imag = from_right(left_imag, cosine) - sign * from_right(left_real, sine_table)
    return (out_real, out_imag)


def slot_loss(patch_cells, mode_values, target, weight, tables):
    depth_count = patch_cells.shape[1]
    wave_real, wave_imag = (mode_values[:, 0], mode_values[:, 1])
    for depth_index in range(depth_count):
        cell_real = patch_cells[0, depth_index]
        cell_imag = patch_cells[1, depth_index]
        wave_real, wave_imag = (
            wave_real * cell_real - wave_imag * cell_imag,
            wave_real * cell_imag + wave_imag * cell_real,
        )
        if depth_index < depth_count - 1:
            freq_real, freq_imag = transform(wave_real, wave_imag, tables, 1.0)
            kern_real, kern_imag = (tables[2], tables[3])
            freq_real, freq_imag = (
                freq_real * kern_real - freq_imag * kern_imag,
                freq_real * kern_imag + freq_imag * kern_real,
            )
            wave_real, wave_imag = transform(freq_real, freq_imag, tables, -1.0)
    far_real, far_imag = transform(wave_real, wave_imag, tables, 1.0)
    intensity = jnp.sum(far_real**2 + far_imag**2, axis=0)
    return 0.5 * weight * jnp.sum((intensity - target) ** 2)


def local(object_real, object_imag, probe_modes, measured, offsets, live):
    slices = object_real.shape[0]
    block_side = object_real.shape[2]
    pattern_side = probe_modes.shape[2]
    slot_count = measured.shape[2]
    tile_count = lax.axis_size("tile")
    group_count = lax.axis_size("scan")
    tables = make_tables(pattern_side)
    anchor = jnp.zeros((), jnp.int32)
    obj_state = jnp.stack([object_real[:, 0], object_imag[:, 0]])
    for iteration in range(ITERS):
        right_part = shifted(obj_state, "tile", -1)
        below_part = shifted(obj_state, "tile", -GRID)
        corner_part = shifted(obj_state, "tile", -GRID - 1)
        upper_half = jnp.concatenate([obj_state, right_part], axis=-1)
        lower_half = jnp.concatenate([below_part, corner_part], axis=-1)
        canvas = jnp.concatenate([upper_half, lower_half], axis=-2)
        current_probe = probe_modes

        def visit_slot(slot_index, running):
            grad_canvas, grad_probe = running
            row_start = offsets[0, 0, slot_index, 0]
            col_start = offsets[0, 0, slot_index, 1]
            starts = (anchor, anchor, row_start, col_start)
            patch_cells = lax.dynamic_slice(canvas, starts, (2, slices, pattern_side, pattern_side))
            target = measured[0, 0, slot_index]
            weight = live[0, 0, slot_index].astype(jnp.float32)
            _, pullback = jax.vjp(
                lambda cell_values, mode_values: slot_loss(
                    cell_values, mode_values, target, weight, tables
                ),
                patch_cells,
                current_probe,
            )
            grad_patch, grad_modes = pullback(jnp.ones((), jnp.float32))
            current = lax.dynamic_slice(
                grad_canvas, starts, (2, slices, pattern_side, pattern_side)
            )
            grad_canvas = lax.dynamic_update_slice(grad_canvas, current + grad_patch, starts)
            return (grad_canvas, grad_probe + grad_modes)

        initial = (jnp.zeros_like(canvas), jnp.zeros_like(probe_modes))
        grad_canvas, grad_probe = lax.fori_loop(0, slot_count, visit_slot, initial)
        own_grad = grad_canvas[:, :, :block_side, :block_side]
        side_grad = grad_canvas[:, :, :block_side, block_side:]
        lower_grads = grad_canvas[:, :, block_side:, :]
        left_grad = shifted(side_grad, "tile", 1)
        above_grad = shifted(lower_grads[..., :block_side], "tile", GRID)
        diagonal_grad = shifted(lower_grads[..., block_side:], "tile", GRID + 1)
        grad_total = own_grad + above_grad + left_grad + diagonal_grad
        grad_total = lax.psum(grad_total, "scan")
        grad_probe = lax.psum(grad_probe, ("tile", "scan"))
        obj_state = obj_state - object_rate / (slot_count * group_count) * grad_total
        probe_modes = (
            probe_modes - probe_rate / (slot_count * tile_count * group_count) * grad_probe
        )
    return (obj_state[0][:, None], obj_state[1][:, None], probe_modes)


def solution(mesh):
    placed = (
        P(None, "tile", None, None),
        P(None, "tile", None, None),
        P(),
        P("tile", "scan", None, None, None),
        P("tile", "scan", None, None),
        P("tile", "scan", None),
    )
    return jax.shard_map(
        local,
        mesh=mesh,
        in_specs=placed,
        out_specs=(P(None, "tile", None, None), P(None, "tile", None, None), P()),
        check_vma=False,
    )
```

profile of v0, /device:TPU:1, one launch (start us, length us, event | category | flops | bytes accessed | tf_op | source)
XLA Modules:
  0.0 896.4 jit_solution(5106531731478892876)
XLA Ops:
  8.1 1.1 pad_maximum_fusion
  9.2 11.5 %collective-permute-start.1 = (f32[2,3,128,128]{3,2,1,0:T(8,128)S(1)}, f32[2,3,128,128]{3,2,1,0:T(8,128)S(1)}, u32[]{:S(2)}, u32[]{:S(2)}) collective-permute-start(f32[2,3,128,128]{3,2,1,0:T(8,128)S(1)} %pad_maximum_fusion), channel_id=1, source_target_pairs={{0,448},{8,456},{16,464},{24,472},{32,480},{40,488},{48,496},{56,5... | collective-permute-start | bytes 1179656 | tf_op jit(solution)/shard_map/ppermute | solution.py:18
  20.7 5.1 collective-permute-start.2
  25.8 3.0 collective-permute-start
  28.8 1.3 fusion.1195
  33.3 1.1 copy.315
  36.0 0.8 collective-permute-done.1
  36.9 13.2 %collective-permute-done = f32[2,3,128,128]{3,2,1,0:T(8,128)S(1)} collective-permute-done((f32[2,3,128,128]{3,2,1,0:T(8,128)S(1)}, f32[2,3,128,128]{3,2,1,0:T(8,128)S(1)}, u32[]{:S(2)}, u32[]{:S(2)}) %collective-permute-start) | collective-permute-done | bytes 393248 | tf_op jit(solution)/shard_map/ppermute | solution.py:18
  55.2 0.6 convolution_multiply_fusion.14
  55.8 0.6 convolution_multiply_fusion.15
  57.5 0.6 fusion.57
  60.9 0.6 fusion.54
  62.0 0.6 fusion.55
  62.6 0.9 fusion.330
  64.6 0.6 convolution_multiply_fusion.10
  65.2 0.6 convolution_multiply_fusion.11
  70.3 0.6 fusion.50
  71.4 0.6 fusion.51
  75.8 0.7 fusion.311
  89.7 0.7 fusion.36
  95.4 0.6 add_bitcast_fusion.3
  96.6 4.3 dynamic_update_slice.8
  101.1 2.9 collective-permute-start.3
  104.0 1.9 collective-permute-start.5
  105.9 1.9 collective-permute-start.4
  107.9 4.9 collective-permute-done.3
  112.8 17.8 %collective-permute-done.5 = f32[2,3,128,128]{3,2,1,0:T(8,128)S(1)} collective-permute-done((f32[2,3,128,128]{3,2,1,0:T(8,128)S(1)}, f32[2,3,128,128]{3,2,1,0:T(8,128)S(1)}, u32[]{:S(2)}, u32[]{:S(2)}) %collective-permute-start.5) | collective-permute-done | bytes 393248 | tf_op jit(solution)/shard_map/ppermute | solution.py:18
  130.6 9.1 %collective-permute-done.4 = f32[2,3,128,128]{3,2,1,0:T(8,128)S(1)} collective-permute-done((f32[2,3,128,128]{3,2,1,0:T(8,128)S(1)}, f32[2,3,128,128]{3,2,1,0:T(8,128)S(1)}, u32[]{:S(2)}, u32[]{:S(2)}) %collective-permute-start.4) | collective-permute-done | bytes 393248 | tf_op jit(solution)/shard_map/ppermute | solution.py:18
  139.6 0.8 fusion.70
  140.5 63.2 %all-reduce.21.cloned.1.call-done = f32[2,3,128,128]{3,2,1,0:T(8,128)} async-done(((f32[2,3,128,128]{3,2,1,0:T(8,128)}), f32[2,3,128,128]{3,2,1,0:T(8,128)}) %all-reduce.21.cloned.1.call-update) | async-done | bytes 393232 | tf_op jit(solution)/shard_map/psum | solution.py:128
  203.7 1.0 multiply_subtract_fusion.1
  204.7 8.0 collective-permute-start.8
  212.7 2.9 collective-permute-start.7
  215.6 3.1 collective-permute-start.6
  218.7 0.7 pad_add_fusion.3
  219.9 265.3 %all-reduce.23.cloned.1.call-done = f32[2,2,128,128]{2,3,0,1:T(8,128)} async-done(((f32[2,2,128,128]{2,3,0,1:T(8,128)}), f32[2,2,128,128]{2,3,0,1:T(8,128)}) %all-reduce.23.cloned.1.call-update) | async-done | bytes 262160 | tf_op jit(solution)/shard_map/psum | solution.py:129
  485.2 1.0 multiply_subtract_fusion.3
  491.3 0.6 convolution_multiply_fusion.6
  491.8 0.6 convolution_multiply_fusion.7
  496.9 0.6 fusion.24
  498.1 0.6 fusion.25
  499.2 0.7 convolution_subtract_fusion.4
  500.5 0.6 convolution_multiply_fusion.2
  501.1 0.6 convolution_multiply_fusion.3
  502.8 0.6 fusion.23
  506.2 0.6 fusion.20
  507.3 0.6 fusion.21
  512.3 0.7 fusion.18
  526.2 0.8 fusion.4
  531.4 0.6 add_bitcast_fusion.1
  532.6 4.3 dynamic_update_slice.9
  537.0 1.0 fusion.1193
  538.0 3.1 collective-permute-start.9
  541.1 2.3 collective-permute-start.11
  543.4 2.2 collective-permute-start.10
  545.6 0.7 pad_add_fusion.2
  546.4 31.3 %collective-permute-done.9 = f32[2,3,128,128]{3,2,1,0:T(8,128)} collective-permute-done((f32[2,3,128,128]{3,2,1,0:T(8,128)}, f32[2,3,128,128]{3,2,1,0:T(8,128)}, u32[]{:S(2)}, u32[]{:S(2)}) %collective-permute-start.9) | collective-permute-done | bytes 393248 | tf_op jit(solution)/shard_map/ppermute | solution.py:18
  577.7 2.0 fusion.68
  579.8 238.7 %all-reduce.27.cloned.1.call-done = f32[2,2,128,128]{2,3,0,1:T(8,128)} async-done(((f32[2,2,128,128]{2,3,0,1:T(8,128)}), f32[2,2,128,128]{2,3,0,1:T(8,128)}) %all-reduce.27.cloned.1.call-update) | async-done | bytes 262160 | tf_op jit(solution)/shard_map/psum | solution.py:129
  818.5 1.0 multiply_subtract_fusion.2
  819.5 0.8 copy.474
  820.3 66.2 %all-reduce.25.cloned.1.call-done = f32[2,3,128,128]{3,2,1,0:T(8,128)} async-done(((f32[2,3,128,128]{3,2,1,0:T(8,128)}), f32[2,3,128,128]{3,2,1,0:T(8,128)}) %all-reduce.25.cloned.1.call-update) | async-done | bytes 393232 | tf_op jit(solution)/shard_map/psum | solution.py:128
  886.5 1.1 multiply_subtract_fusion
  887.6 0.8 slice_bitcast_fusion
  (190 shorter events, 76.6 us)
Async XLA Ops:
  8.0 42.1 %copy-start.1 = (f32[3,1,128,128]{3,2,1,0:T(8,128)S(1)}, f32[3,1,128,128]{3,2,1,0:T(8,128)}, u32[]{:S(2)}) copy-start(f32[3,1,128,128]{3,2,1,0:T(8,128)} %param.7) | copy-start | bytes 589828
  8.0 42.1 %copy-start = (f32[3,1,128,128]{3,2,1,0:T(8,128)S(1)}, f32[3,1,128,128]{3,2,1,0:T(8,128)}, u32[]{:S(2)}) copy-start(f32[3,1,128,128]{3,2,1,0:T(8,128)} %param.6) | copy-start | bytes 589828
  8.0 195.7 %all-reduce.21.cloned.1.call-start = ((), (), s32[]{:S(2)}) async-start(), calls=%async_computation | async-start | bytes 786432 | tf_op jit(solution)/shard_map/psum | solution.py:128
  9.2 27.7 %collective-permute-start.1 = (f32[2,3,128,128]{3,2,1,0:T(8,128)S(1)}, f32[2,3,128,128]{3,2,1,0:T(8,128)S(1)}, u32[]{:S(2)}, u32[]{:S(2)}) collective-permute-start(f32[2,3,128,128]{3,2,1,0:T(8,128)S(1)} %pad_maximum_fusion), channel_id=1, source_target_pairs={{0,448},{8,456},{16,464},{24,472},{32,480},{40,488},{48,496},{56,5... | collective-permute-start | bytes 1179656 | tf_op jit(solution)/shard_map/ppermute | solution.py:18
  20.7 16.2 %collective-permute-start.2 = (f32[2,3,128,128]{3,2,1,0:T(8,128)S(1)}, f32[2,3,128,128]{3,2,1,0:T(8,128)S(1)}, u32[]{:S(2)}, u32[]{:S(2)}) collective-permute-start(f32[2,3,128,128]{3,2,1,0:T(8,128)S(1)} %pad_maximum_fusion), channel_id=1, source_target_pairs={{0,440},{8,448},{16,456},{24,464},{32,472},{40,480},{48,488},{56,4... | collective-permute-start | bytes 1179656 | tf_op jit(solution)/shard_map/ppermute | solution.py:18
  25.8 24.3 %collective-permute-start = (f32[2,3,128,128]{3,2,1,0:T(8,128)S(1)}, f32[2,3,128,128]{3,2,1,0:T(8,128)S(1)}, u32[]{:S(2)}, u32[]{:S(2)}) collective-permute-start(f32[2,3,128,128]{3,2,1,0:T(8,128)S(1)} %pad_maximum_fusion), channel_id=1, source_target_pairs={{0,504},{8,0},{16,8},{24,16},{32,24},{40,32},{48,40},{56,48},{64,5... | collective-permute-start | bytes 1179656 | tf_op jit(solution)/shard_map/ppermute | solution.py:18
  69.7 4.0 copy-start.3
  101.1 11.7 %collective-permute-start.3 = (f32[2,3,128,128]{3,2,1,0:T(8,128)S(1)}, f32[2,3,128,128]{3,2,1,0:T(8,128)S(1)}, u32[]{:S(2)}, u32[]{:S(2)}) collective-permute-start(f32[2,3,128,128]{3,2,1,0:T(8,128)S(1)} %get-tuple-element.121), channel_id=1, source_target_pairs={{0,64},{8,72},{16,80},{24,88},{32,96},{40,104},{48,112},{56,120},{... | collective-permute-start | bytes 1179656 | tf_op jit(solution)/shard_map/ppermute | solution.py:18
  104.0 26.6 %collective-permute-start.5 = (f32[2,3,128,128]{3,2,1,0:T(8,128)S(1)}, f32[2,3,128,128]{3,2,1,0:T(8,128)S(1)}, u32[]{:S(2)}, u32[]{:S(2)}) collective-permute-start(f32[2,3,128,128]{3,2,1,0:T(8,128)S(1)} %get-tuple-element.122), channel_id=1, source_target_pairs={{0,72},{8,80},{16,88},{24,96},{32,104},{40,112},{48,120},{56,128},... | collective-permute-start | bytes 1179656 | tf_op jit(solution)/shard_map/ppermute | solution.py:18
  105.9 33.7 %collective-permute-start.4 = (f32[2,3,128,128]{3,2,1,0:T(8,128)S(1)}, f32[2,3,128,128]{3,2,1,0:T(8,128)S(1)}, u32[]{:S(2)}, u32[]{:S(2)}) collective-permute-start(f32[2,3,128,128]{3,2,1,0:T(8,128)S(1)} %get-tuple-element.123), channel_id=1, source_target_pairs={{0,8},{8,16},{16,24},{24,32},{32,40},{40,48},{48,56},{56,64},{64,7... | collective-permute-start | bytes 1179656 | tf_op jit(solution)/shard_map/ppermute | solution.py:18
  140.5 344.7 %all-reduce.23.cloned.1.call-start = ((), (), s32[]{:S(2)}) async-start(), calls=%async_computation.1 | async-start | bytes 524288 | tf_op jit(solution)/shard_map/psum | solution.py:129
  204.7 281.4 %collective-permute-start.8 = (f32[2,3,128,128]{3,2,1,0:T(8,128)S(1)}, f32[2,3,128,128]{3,2,1,0:T(8,128)S(1)}, u32[]{:S(2)}, u32[]{:S(2)}) collective-permute-start(f32[2,3,128,128]{3,2,1,0:T(8,128)S(1)} %multiply_subtract_fusion.1), channel_id=1, source_target_pairs={{0,440},{8,448},{16,456},{24,464},{32,472},{40,480},{48,488},{56,4... | collective-permute-start | bytes 1179656 | tf_op jit(solution)/shard_map/ppermute | solution.py:18
  212.7 273.5 %collective-permute-start.7 = (f32[2,3,128,128]{3,2,1,0:T(8,128)S(1)}, f32[2,3,128,128]{3,2,1,0:T(8,128)S(1)}, u32[]{:S(2)}, u32[]{:S(2)}) collective-permute-start(f32[2,3,128,128]{3,2,1,0:T(8,128)S(1)} %multiply_subtract_fusion.1), channel_id=1, source_target_pairs={{0,448},{8,456},{16,464},{24,472},{32,480},{40,488},{48,496},{56,5... | collective-permute-start | bytes 1179656 | tf_op jit(solution)/shard_map/ppermute | solution.py:18
  215.6 270.6 %collective-permute-start.6 = (f32[2,3,128,128]{3,2,1,0:T(8,128)S(1)}, f32[2,3,128,128]{3,2,1,0:T(8,128)S(1)}, u32[]{:S(2)}, u32[]{:S(2)}) collective-permute-start(f32[2,3,128,128]{3,2,1,0:T(8,128)S(1)} %multiply_subtract_fusion.1), channel_id=1, source_target_pairs={{0,504},{8,0},{16,8},{24,16},{32,24},{40,32},{48,40},{56,48},{64,5... | collective-permute-start | bytes 1179656 | tf_op jit(solution)/shard_map/ppermute | solution.py:18
  219.4 599.1 %all-reduce.27.cloned.1.call-start = ((), (), s32[]{:S(2)}) async-start(), calls=%async_computation.3 | async-start | bytes 524288 | tf_op jit(solution)/shard_map/psum | solution.py:129
  538.0 39.8 %collective-permute-start.9 = (f32[2,3,128,128]{3,2,1,0:T(8,128)}, f32[2,3,128,128]{3,2,1,0:T(8,128)}, u32[]{:S(2)}, u32[]{:S(2)}) collective-permute-start(f32[2,3,128,128]{3,2,1,0:T(8,128)} %get-tuple-element.118), channel_id=1, source_target_pairs={{0,64},{8,72},{16,80},{24,88},{32,96},{40,104},{48,112},{56,120},{... | collective-permute-start | bytes 1179656 | tf_op jit(solution)/shard_map/ppermute | solution.py:18
  541.1 36.7 %collective-permute-start.11 = (f32[2,3,128,128]{3,2,1,0:T(8,128)}, f32[2,3,128,128]{3,2,1,0:T(8,128)}, u32[]{:S(2)}, u32[]{:S(2)}) collective-permute-start(f32[2,3,128,128]{3,2,1,0:T(8,128)} %get-tuple-element.119), channel_id=1, source_target_pairs={{0,72},{8,80},{16,88},{24,96},{32,104},{40,112},{48,120},{56,128},... | collective-permute-start | bytes 1179656 | tf_op jit(solution)/shard_map/ppermute | solution.py:18
  543.4 34.4 %collective-permute-start.10 = (f32[2,3,128,128]{3,2,1,0:T(8,128)S(1)}, f32[2,3,128,128]{3,2,1,0:T(8,128)}, u32[]{:S(2)}, u32[]{:S(2)}) collective-permute-start(f32[2,3,128,128]{3,2,1,0:T(8,128)S(1)} %get-tuple-element.120), channel_id=1, source_target_pairs={{0,8},{8,16},{16,24},{24,32},{32,40},{40,48},{48,56},{56,64},{64,7... | collective-permute-start | bytes 1179656 | tf_op jit(solution)/shard_map/ppermute | solution.py:18
  546.3 340.2 %copy-start.2 = (f32[2,3,128,128]{3,2,1,0:T(8,128)S(1)}, f32[2,3,128,128]{3,2,1,0:T(8,128)}, u32[]{:S(2)}) copy-start(f32[2,3,128,128]{3,2,1,0:T(8,128)} %all-reduce.21.cloned.1.call-done) | copy-start | bytes 1179652
  546.3 340.2 %all-reduce.25.cloned.1.call-start = ((), (), s32[]{:S(2)}) async-start(), calls=%async_computation.2 | async-start | bytes 786432 | tf_op jit(solution)/shard_map/psum | solution.py:128
Sparse Core Ops, SparseCore 0:
  140.6 63.0 all-reduce.20
Sparse Core Ops, SparseCore 1:
  219.5 265.6 all-reduce.22
  546.4 272.1 all-reduce.26
  820.8 65.7 all-reduce.24
where the time goes:
time: 906 us; the launch traced here: 896 us
  waiting for transfers between devices  711 us (78%)
  matrix products  88.9 us (10%)
  starting transfers between devices  48.4 us (5%)
  between operations  22.3 us (2%)
  local copies, waits for them, and re-layouts  15.2 us (2%)
  other arithmetic  11 us (1%)
    psum x2, waiting for transfers between devices, local(): grad_probe = lax.psum(grad_probe, ('tile', 'scan'))  504 us
    psum x2, waiting for transfers between devices, local(): grad_total = lax.psum(grad_total, 'scan')  129 us
    ppermute x12, waiting for transfers between devices, shifted(): lax.ppermute(shard, axis, [(i, (i + by) % size) for i in range(size)])  77.2 us
    ppermute x12, starting transfers between devices, shifted(): lax.ppermute(shard, axis, [(i, (i + by) % size) for i in range(size)])  47.8 us
    dot_general x80, matrix products, from_left(): jnp.einsum('jk,mkl->mjl', matrix, values, precision=lax.Precision.HIGHEST)  44.9 us
    dot_general x80, matrix products, from_right(): jnp.einsum('mjk,kl->mjl', values, matrix, precision=lax.Precision.HIGHEST)  44 us
  transfers between devices with their start and end apart: 16, of which 10 were waited for; matrix products, arithmetic and copies ran while one was open for 1% of the time, Pallas kernels for 0%

commit v1 on v0

--- a/solution.py
+++ b/solution.py
@@ -75,6 +75,15 @@
     return 0.5 * weight * jnp.sum((intensity - target) ** 2)
 
 
+def xor_sum(values, axis):
+    size = lax.axis_size(axis)
+    step = 1
+    while step < size:
+        values = values + lax.ppermute(values, axis, [(i, i ^ step) for i in range(size)])
+        step *= 2
+    return values
+
+
 def local(object_real, object_imag, probe_modes, measured, offsets, live):
     slices = object_real.shape[0]
     block_side = object_real.shape[2]
@@ -85,17 +94,28 @@
     tables = make_tables(pattern_side)
     anchor = jnp.zeros((), jnp.int32)
     obj_state = jnp.stack([object_real[:, 0], object_imag[:, 0]])
-    for iteration in range(ITERS):
+    parts = 2 * slices
+    modes = probe_modes.shape[0]
+    pending = None
+    for iteration in range(ITERS + 1):
+        if pending is not None:
+            probe_sum = pending
+            for step in (2, 4, 2 * GRID, 4 * GRID):
+                probe_sum = probe_sum + shifted(probe_sum, "tile", step)
+            probe_modes = (
+                probe_modes - probe_rate / (slot_count * tile_count * group_count) * probe_sum
+            )
+        if iteration == ITERS:
+            break
         right_part = shifted(obj_state, "tile", -1)
-        below_part = shifted(obj_state, "tile", -GRID)
-        corner_part = shifted(obj_state, "tile", -GRID - 1)
         upper_half = jnp.concatenate([obj_state, right_part], axis=-1)
-        lower_half = jnp.concatenate([below_part, corner_part], axis=-1)
+        lower_half = shifted(upper_half, "tile", -GRID)
         canvas = jnp.concatenate([upper_half, lower_half], axis=-2)
         current_probe = probe_modes
 
-        def visit_slot(slot_index, running):
-            grad_canvas, grad_probe = running
+        grad_canvas = jnp.zeros_like(canvas)
+        grad_probe = jnp.zeros_like(probe_modes)
+        for slot_index in range(slot_count):
             row_start = offsets[0, 0, slot_index, 0]
             col_start = offsets[0, 0, slot_index, 1]
             starts = (anchor, anchor, row_start, col_start)
@@ -114,23 +134,28 @@
                 grad_canvas, starts, (2, slices, pattern_side, pattern_side)
             )
             grad_canvas = lax.dynamic_update_slice(grad_canvas, current + grad_patch, starts)
-            return (grad_canvas, grad_probe + grad_modes)
-
-        initial = (jnp.zeros_like(canvas), jnp.zeros_like(probe_modes))
-        grad_canvas, grad_probe = lax.fori_loop(0, slot_count, visit_slot, initial)
-        own_grad = grad_canvas[:, :, :block_side, :block_side]
-        side_grad = grad_canvas[:, :, :block_side, block_side:]
-        lower_grads = grad_canvas[:, :, block_side:, :]
-        left_grad = shifted(side_grad, "tile", 1)
-        above_grad = shifted(lower_grads[..., :block_side], "tile", GRID)
-        diagonal_grad = shifted(lower_grads[..., block_side:], "tile", GRID + 1)
-        grad_total = own_grad + above_grad + left_grad + diagonal_grad
-        grad_total = lax.psum(grad_total, "scan")
-        grad_probe = lax.psum(grad_probe, ("tile", "scan"))
+            grad_probe = grad_probe + grad_modes
+        planes = lambda a: a.reshape(-1, block_side, block_side)
+        probe_planes = planes(grad_probe)
+        sent_down = jnp.concatenate(
+            [
+                planes(grad_canvas[:, :, block_side:, :block_side]),
+                planes(grad_canvas[:, :, block_side:, block_side:]),
+                probe_planes,
+            ]
+        )
+        came_down = shifted(sent_down, "tile", GRID)
+        own_part = planes(grad_canvas[:, :, :block_side, :block_side]) + came_down[:parts]
+        right_side = planes(grad_canvas[:, :, :block_side, block_side:]) + came_down[parts : 2 * parts]
+        probe_partial = probe_planes + came_down[2 * parts :]
+        sent_left = jnp.concatenate([right_side, probe_partial])
+        came_left = shifted(sent_left, "tile", 1)
+        own_part = own_part + came_left[:parts]
+        probe_partial = probe_partial + came_left[parts:]
+        reduced = xor_sum(jnp.concatenate([own_part, probe_partial]), "scan")
+        grad_total = reduced[:parts].reshape(obj_state.shape)
+        pending = reduced[parts:].reshape(probe_modes.shape)
         obj_state = obj_state - object_rate / (slot_count * group_count) * grad_total
-        probe_modes = (
-            probe_modes - probe_rate / (slot_count * tile_count * group_count) * grad_probe
-        )
     return (obj_state[0][:, None], obj_state[1][:, None], probe_modes)
 
 

time: 906 us -> 483 us (0.53)
  the two profiles are of different devices: /device:TPU:1 before, /device:TPU:80 now
where the time goes in v1:
time: 483 us; the launch traced here: 474 us
  waiting for transfers between devices  257 us (53%)
  starting transfers between devices  102 us (21%)
  matrix products  88.9 us (18%)
  local copies, waits for them, and re-layouts  13.5 us (3%)
  between operations  7.59 us (2%)
  other arithmetic  5.26 us (1%)
    ppermute x16, waiting for transfers between devices, shifted(): lax.ppermute(shard, axis, [(i, (i + by) % size) for i in range(size)])  193 us
    ppermute x16, starting transfers between devices, shifted(): lax.ppermute(shard, axis, [(i, (i + by) % size) for i in range(size)])  77.9 us
    ppermute x6, waiting for transfers between devices, xor_sum(): lax.ppermute(values, axis, [(i, i ^ step) for i in range(size)])  63.6 us
    dot_general x80, matrix products, from_left(): jnp.einsum('jk,mkl->mjl', matrix, values, precision=lax.Precision.HIGHEST)  45 us
    dot_general x80, matrix products, from_right(): jnp.einsum('mjk,kl->mjl', values, matrix, precision=lax.Precision.HIGHEST)  43.8 us
    ppermute x6, starting transfers between devices, xor_sum(): lax.ppermute(values, axis, [(i, i ^ step) for i in range(size)])  23.8 us
  transfers between devices with their start and end apart: 22, of which 20 were waited for; matrix products, arithmetic and copies ran while one was open for 0% of the time, Pallas kernels for 0%

profile of v1, /device:TPU:80, one launch (start us, length us, event | category | flops | bytes accessed | tf_op | source)
XLA Modules:
  0.0 473.8 jit_solution(14718901503430890776)
XLA Ops:
  0.7 1.1 pad_maximum_fusion.8
  1.8 2.4 collective-permute-start
  4.2 10.4 %collective-permute-done = f32[2,3,128,128]{3,2,1,0:T(8,128)S(1)} collective-permute-done((f32[2,3,128,128]{3,2,1,0:T(8,128)S(1)}, f32[2,3,128,128]{3,2,1,0:T(8,128)S(1)}, u32[]{:S(2)}, u32[]{:S(2)}) %collective-permute-start) | collective-permute-done | bytes 393248 | tf_op jit(solution)/shard_map/ppermute | solution.py:18
  14.5 1.1 pad_maximum_fusion.2
  15.6 1.9 collective-permute-start.1
  17.6 0.6 fusion.1192
  23.2 13.4 %collective-permute-done.1 = f32[2,3,128,256]{3,2,1,0:T(8,128)S(1)} collective-permute-done((f32[2,3,128,256]{3,2,1,0:T(8,128)S(1)}, f32[2,3,128,256]{3,2,1,0:T(8,128)S(1)}, u32[]{:S(2)}, u32[]{:S(2)}) %collective-permute-start.1) | collective-permute-done | bytes 786464 | tf_op jit(solution)/shard_map/ppermute | solution.py:18
  41.5 0.6 convolution_multiply_fusion.14
  47.2 0.6 fusion.54
  48.9 0.9 fusion.324
  51.0 0.6 convolution_multiply_fusion.10
  56.6 0.6 fusion.50
  57.8 0.6 fusion.51
  62.2 0.7 fusion.305
  76.6 0.8 fusion.34
  83.1 4.4 dynamic_update_slice.6
  87.8 4.3 collective-permute-start.2
  92.1 24.3 %collective-permute-done.2 = f32[16,128,128]{2,1,0:T(8,128)S(1)} collective-permute-done((f32[16,128,128]{2,1,0:T(8,128)S(1)}, f32[16,128,128]{2,1,0:T(8,128)S(1)}, u32[]{:S(2)}, u32[]{:S(2)}) %collective-permute-start.2) | collective-permute-done | bytes 1048608 | tf_op jit(solution)/shard_map/ppermute | solution.py:18
  116.6 4.6 collective-permute-start.3
  121.2 11.5 %collective-permute-done.3 = f32[10,128,128]{2,1,0:T(8,128)S(1)} collective-permute-done((f32[10,128,128]{2,1,0:T(8,128)S(1)}, f32[10,128,128]{2,1,0:T(8,128)S(1)}, u32[]{:S(2)}, u32[]{:S(2)}) %collective-permute-start.3) | collective-permute-done | bytes 655392 | tf_op jit(solution)/shard_map/ppermute | solution.py:18
  132.8 1.9 collective-permute-start.4
  134.8 2.1 collective-permute-done.4
  136.9 3.9 collective-permute-start.5
  140.8 15.0 %collective-permute-done.5 = f32[10,128,128]{2,1,0:T(8,128)S(1)} collective-permute-done((f32[10,128,128]{2,1,0:T(8,128)S(1)}, f32[10,128,128]{2,1,0:T(8,128)S(1)}, u32[]{:S(2)}, u32[]{:S(2)}) %collective-permute-start.5) | collective-permute-done | bytes 655392 | tf_op jit(solution)/shard_map/ppermute | solution.py:82
  155.9 5.2 %collective-permute-start.6 = (f32[10,128,128]{2,1,0:T(8,128)S(1)}, f32[10,128,128]{2,1,0:T(8,128)S(1)}, u32[]{:S(2)}, u32[]{:S(2)}) collective-permute-start(f32[10,128,128]{2,1,0:T(8,128)S(1)} %add.814), channel_id=1, source_target_pairs={{0,4},{1,5},{2,6},{3,7},{4,0},{5,1},{6,2},{7,3},{8,12},{9,13},{10,... | collective-permute-start | bytes 1966088 | tf_op jit(solution)/shard_map/ppermute | solution.py:82
  161.1 14.3 %collective-permute-done.6 = f32[10,128,128]{2,1,0:T(8,128)S(1)} collective-permute-done((f32[10,128,128]{2,1,0:T(8,128)S(1)}, f32[10,128,128]{2,1,0:T(8,128)S(1)}, u32[]{:S(2)}, u32[]{:S(2)}) %collective-permute-start.6) | collective-permute-done | bytes 655392 | tf_op jit(solution)/shard_map/ppermute | solution.py:82
  175.6 3.5 collective-permute-start.11
  179.3 5.5 %collective-permute-start.7 = (f32[2,2,128,128]{2,3,0,1:T(8,128)S(1)}, f32[2,2,128,128]{2,3,0,1:T(8,128)S(1)}, u32[]{:S(2)}, u32[]{:S(2)}) collective-permute-start(f32[2,2,128,128]{2,3,0,1:T(8,128)S(1)} %copy.561), channel_id=1, source_target_pairs={{0,16},{8,24},{16,32},{24,40},{32,48},{40,56},{48,64},{56,72},{64,... | collective-permute-start | bytes 786440 | tf_op jit(solution)/shard_map/ppermute | solution.py:18
  184.8 14.8 %collective-permute-done.7 = f32[2,2,128,128]{2,3,0,1:T(8,128)S(1)} collective-permute-done((f32[2,2,128,128]{2,3,0,1:T(8,128)S(1)}, f32[2,2,128,128]{2,3,0,1:T(8,128)S(1)}, u32[]{:S(2)}, u32[]{:S(2)}) %collective-permute-start.7) | collective-permute-done | bytes 262176 | tf_op jit(solution)/shard_map/ppermute | solution.py:18
  199.6 3.0 collective-permute-start.8
  202.7 5.0 %collective-permute-start.12 = (f32[2,3,128,256]{3,2,1,0:T(8,128)S(1)}, f32[2,3,128,256]{3,2,1,0:T(8,128)S(1)}, u32[]{:S(2)}, u32[]{:S(2)}) collective-permute-start(f32[2,3,128,256]{3,2,1,0:T(8,128)S(1)} %pad_maximum_fusion.3), channel_id=1, source_target_pairs={{0,448},{8,456},{16,464},{24,472},{32,480},{40,488},{48,496},{56,5... | collective-permute-start | bytes 2359304 | tf_op jit(solution)/shard_map/ppermute | solution.py:18
  207.7 7.1 %collective-permute-done.8 = f32[2,2,128,128]{2,3,0,1:T(8,128)S(1)} collective-permute-done((f32[2,2,128,128]{2,3,0,1:T(8,128)S(1)}, f32[2,2,128,128]{2,3,0,1:T(8,128)S(1)}, u32[]{:S(2)}, u32[]{:S(2)}) %collective-permute-start.8) | collective-permute-done | bytes 262176 | tf_op jit(solution)/shard_map/ppermute | solution.py:18
  214.8 1.9 collective-permute-start.9
  216.8 8.5 %collective-permute-done.9 = f32[2,2,128,128]{2,3,0,1:T(8,128)S(1)} collective-permute-done((f32[2,2,128,128]{2,3,0,1:T(8,128)S(1)}, f32[2,2,128,128]{2,3,0,1:T(8,128)S(1)}, u32[]{:S(2)}, u32[]{:S(2)}) %collective-permute-start.9) | collective-permute-done | bytes 262176 | tf_op jit(solution)/shard_map/ppermute | solution.py:18
  225.4 2.3 collective-permute-start.10
  227.7 13.6 %collective-permute-done.10 = f32[2,2,128,128]{2,3,0,1:T(8,128)S(1)} collective-permute-done((f32[2,2,128,128]{2,3,0,1:T(8,128)S(1)}, f32[2,2,128,128]{2,3,0,1:T(8,128)S(1)}, u32[]{:S(2)}, u32[]{:S(2)}) %collective-permute-start.10) | collective-permute-done | bytes 262176 | tf_op jit(solution)/shard_map/ppermute | solution.py:18
  246.4 0.6 convolution_multiply_fusion.6
  252.0 0.6 fusion.24
  254.3 0.7 convolution_subtract_fusion.4
  255.6 0.6 convolution_multiply_fusion.2
  261.3 0.6 fusion.20
  267.4 0.7 fusion.18
  281.9 0.8 fusion.5
  287.9 4.4 dynamic_update_slice.7
  292.6 5.7 %collective-permute-start.13 = (f32[16,128,128]{2,1,0:T(8,128)S(1)}, f32[16,128,128]{2,1,0:T(8,128)S(1)}, u32[]{:S(2)}, u32[]{:S(2)}) collective-permute-start(f32[16,128,128]{2,1,0:T(8,128)S(1)} %pad_maximum_fusion.1), channel_id=1, source_target_pairs={{0,64},{8,72},{16,80},{24,88},{32,96},{40,104},{48,112},{56,120},{... | collective-permute-start | bytes 3145736 | tf_op jit(solution)/shard_map/ppermute | solution.py:18
  298.3 16.3 %collective-permute-done.13 = f32[16,128,128]{2,1,0:T(8,128)S(1)} collective-permute-done((f32[16,128,128]{2,1,0:T(8,128)S(1)}, f32[16,128,128]{2,1,0:T(8,128)S(1)}, u32[]{:S(2)}, u32[]{:S(2)}) %collective-permute-start.13) | collective-permute-done | bytes 1048608 | tf_op jit(solution)/shard_map/ppermute | solution.py:18
  314.8 8.1 %collective-permute-start.14 = (f32[10,128,128]{2,1,0:T(8,128)S(1)}, f32[10,128,128]{2,1,0:T(8,128)S(1)}, u32[]{:S(2)}, u32[]{:S(2)}) collective-permute-start(f32[10,128,128]{2,1,0:T(8,128)S(1)} %pad_maximum_fusion.6), channel_id=1, source_target_pairs={{0,8},{8,16},{16,24},{24,32},{32,40},{40,48},{48,56},{56,64},{64,7... | collective-permute-start | bytes 1966088 | tf_op jit(solution)/shard_map/ppermute | solution.py:18
  322.9 20.9 %collective-permute-done.14 = f32[10,128,128]{2,1,0:T(8,128)S(1)} collective-permute-done((f32[10,128,128]{2,1,0:T(8,128)S(1)}, f32[10,128,128]{2,1,0:T(8,128)S(1)}, u32[]{:S(2)}, u32[]{:S(2)}) %collective-permute-start.14) | collective-permute-done | bytes 655392 | tf_op jit(solution)/shard_map/ppermute | solution.py:18
  344.0 1.9 collective-permute-start.15
  345.9 2.1 collective-permute-done.15
  348.0 6.3 %collective-permute-start.16 = (f32[10,128,128]{2,1,0:T(8,128)S(1)}, f32[10,128,128]{2,1,0:T(8,128)S(1)}, u32[]{:S(2)}, u32[]{:S(2)}) collective-permute-start(f32[10,128,128]{2,1,0:T(8,128)S(1)} %fusion.1188), channel_id=1, source_target_pairs={{0,2},{1,3},{2,0},{3,1},{4,6},{5,7},{6,4},{7,5},{8,10},{9,11},{10,... | collective-permute-start | bytes 1966088 | tf_op jit(solution)/shard_map/ppermute | solution.py:82
  354.3 15.0 %collective-permute-done.16 = f32[10,128,128]{2,1,0:T(8,128)S(1)} collective-permute-done((f32[10,128,128]{2,1,0:T(8,128)S(1)}, f32[10,128,128]{2,1,0:T(8,128)S(1)}, u32[]{:S(2)}, u32[]{:S(2)}) %collective-permute-start.16) | collective-permute-done | bytes 655392 | tf_op jit(solution)/shard_map/ppermute | solution.py:82
  369.4 4.6 collective-permute-start.17
  374.0 15.1 %collective-permute-done.17 = f32[10,128,128]{2,1,0:T(8,128)S(1)} collective-permute-done((f32[10,128,128]{2,1,0:T(8,128)S(1)}, f32[10,128,128]{2,1,0:T(8,128)S(1)}, u32[]{:S(2)}, u32[]{:S(2)}) %collective-permute-start.17) | collective-permute-done | bytes 655392 | tf_op jit(solution)/shard_map/ppermute | solution.py:82
  389.3 9.3 %collective-permute-start.18 = (f32[2,2,128,128]{2,3,0,1:T(8,128)S(1)}, f32[2,2,128,128]{2,3,0,1:T(8,128)S(1)}, u32[]{:S(2)}, u32[]{:S(2)}) collective-permute-start(f32[2,2,128,128]{2,3,0,1:T(8,128)S(1)} %copy.643), channel_id=1, source_target_pairs={{0,16},{8,24},{16,32},{24,40},{32,48},{40,56},{48,64},{56,72},{64,... | collective-permute-start | bytes 786440 | tf_op jit(solution)/shard_map/ppermute | solution.py:18
  398.6 15.3 %collective-permute-done.18 = f32[2,2,128,128]{2,3,0,1:T(8,128)S(1)} collective-permute-done((f32[2,2,128,128]{2,3,0,1:T(8,128)S(1)}, f32[2,2,128,128]{2,3,0,1:T(8,128)S(1)}, u32[]{:S(2)}, u32[]{:S(2)}) %collective-permute-start.18) | collective-permute-done | bytes 262176 | tf_op jit(solution)/shard_map/ppermute | solution.py:18
  413.9 3.0 collective-permute-start.19
  417.0 17.5 %collective-permute-done.19 = f32[2,2,128,128]{2,3,0,1:T(8,128)S(1)} collective-permute-done((f32[2,2,128,128]{2,3,0,1:T(8,128)S(1)}, f32[2,2,128,128]{2,3,0,1:T(8,128)S(1)}, u32[]{:S(2)}, u32[]{:S(2)}) %collective-permute-start.19) | collective-permute-done | bytes 262176 | tf_op jit(solution)/shard_map/ppermute | solution.py:18
  434.5 1.9 collective-permute-start.20
  436.5 9.4 %collective-permute-done.20 = f32[2,2,128,128]{2,3,0,1:T(8,128)S(1)} collective-permute-done((f32[2,2,128,128]{2,3,0,1:T(8,128)S(1)}, f32[2,2,128,128]{2,3,0,1:T(8,128)S(1)}, u32[]{:S(2)}, u32[]{:S(2)}) %collective-permute-start.20) | collective-permute-done | bytes 262176 | tf_op jit(solution)/shard_map/ppermute | solution.py:18
  445.9 15.4 %collective-permute-start.21 = (f32[2,2,128,128]{2,3,0,1:T(8,128)S(1)}, f32[2,2,128,128]{2,3,0,1:T(8,128)S(1)}, u32[]{:S(2)}, u32[]{:S(2)}) collective-permute-start(f32[2,2,128,128]{2,3,0,1:T(8,128)S(1)} %add.851), channel_id=1, source_target_pairs={{0,256},{8,264},{16,272},{24,280},{32,288},{40,296},{48,304},{56,3... | collective-permute-start | bytes 786440 | tf_op jit(solution)/shard_map/ppermute | solution.py:18
  461.4 0.8 slice_bitcast_fusion
  462.2 10.3 %collective-permute-done.21 = f32[2,2,128,128]{2,3,0,1:T(8,128)S(1)} collective-permute-done((f32[2,2,128,128]{2,3,0,1:T(8,128)S(1)}, f32[2,2,128,128]{2,3,0,1:T(8,128)S(1)}, u32[]{:S(2)}, u32[]{:S(2)}) %collective-permute-start.21) | collective-permute-done | bytes 262176 | tf_op jit(solution)/shard_map/ppermute | solution.py:18
  472.6 0.8 copy.644
  (234 shorter events, 84.7 us)
Async XLA Ops:
  0.6 35.9 %copy-start.1 = (f32[3,1,128,128]{3,2,1,0:T(8,128)S(1)}, f32[3,1,128,128]{3,2,1,0:T(8,128)}, u32[]{:S(2)}) copy-start(f32[3,1,128,128]{3,2,1,0:T(8,128)} %param.7) | copy-start | bytes 589828
  0.6 35.9 %copy-start = (f32[3,1,128,128]{3,2,1,0:T(8,128)S(1)}, f32[3,1,128,128]{3,2,1,0:T(8,128)}, u32[]{:S(2)}) copy-start(f32[3,1,128,128]{3,2,1,0:T(8,128)} %param.6) | copy-start | bytes 589828
  0.7 16.9 %copy-start.4 = (s32[1,1,1,2]{3,2,1,0:T(1,128)S(1)}, s32[1,1,1,2]{3,2,1,0:T(1,128)}, u32[]{:S(2)}) copy-start(s32[1,1,1,2]{3,2,1,0:T(1,128)} %param.10) | copy-start | bytes 28
  0.7 20.7 %copy-start.3 = (f32[2,2,128,128]{3,2,1,0:T(8,128)S(1)}, f32[2,2,128,128]{3,2,1,0:T(8,128)}, u32[]{:S(2)}) copy-start(f32[2,2,128,128]{3,2,1,0:T(8,128)} %param.8) | copy-start | bytes 786436
  1.8 12.7 %collective-permute-start = (f32[2,3,128,128]{3,2,1,0:T(8,128)S(1)}, f32[2,3,128,128]{3,2,1,0:T(8,128)S(1)}, u32[]{:S(2)}, u32[]{:S(2)}) collective-permute-start(f32[2,3,128,128]{3,2,1,0:T(8,128)S(1)} %pad_maximum_fusion.8), channel_id=1, source_target_pairs={{0,504},{8,0},{16,8},{24,16},{32,24},{40,32},{48,40},{56,48},{64,5... | collective-permute-start | bytes 1179656 | tf_op jit(solution)/shard_map/ppermute | solution.py:18
  15.6 20.9 %collective-permute-start.1 = (f32[2,3,128,256]{3,2,1,0:T(8,128)S(1)}, f32[2,3,128,256]{3,2,1,0:T(8,128)S(1)}, u32[]{:S(2)}, u32[]{:S(2)}) collective-permute-start(f32[2,3,128,256]{3,2,1,0:T(8,128)S(1)} %pad_maximum_fusion.2), channel_id=1, source_target_pairs={{0,448},{8,456},{16,464},{24,472},{32,480},{40,488},{48,496},{56,5... | collective-permute-start | bytes 2359304 | tf_op jit(solution)/shard_map/ppermute | solution.py:18
  56.1 4.0 copy-start.2
  87.8 28.6 %collective-permute-start.2 = (f32[16,128,128]{2,1,0:T(8,128)S(1)}, f32[16,128,128]{2,1,0:T(8,128)S(1)}, u32[]{:S(2)}, u32[]{:S(2)}) collective-permute-start(f32[16,128,128]{2,1,0:T(8,128)S(1)} %pad_maximum_fusion), channel_id=1, source_target_pairs={{0,64},{8,72},{16,80},{24,88},{32,96},{40,104},{48,112},{56,120},{... | collective-permute-start | bytes 3145736 | tf_op jit(solution)/shard_map/ppermute | solution.py:18
  116.6 16.1 %collective-permute-start.3 = (f32[10,128,128]{2,1,0:T(8,128)S(1)}, f32[10,128,128]{2,1,0:T(8,128)S(1)}, u32[]{:S(2)}, u32[]{:S(2)}) collective-permute-start(f32[10,128,128]{2,1,0:T(8,128)S(1)} %pad_maximum_fusion.4), channel_id=1, source_target_pairs={{0,8},{8,16},{16,24},{24,32},{32,40},{40,48},{48,56},{56,64},{64,7... | collective-permute-start | bytes 1966088 | tf_op jit(solution)/shard_map/ppermute | solution.py:18
  132.8 4.0 collective-permute-start.4
  136.9 18.9 %collective-permute-start.5 = (f32[10,128,128]{2,1,0:T(8,128)S(1)}, f32[10,128,128]{2,1,0:T(8,128)S(1)}, u32[]{:S(2)}, u32[]{:S(2)}) collective-permute-start(f32[10,128,128]{2,1,0:T(8,128)S(1)} %fusion.1189), channel_id=1, source_target_pairs={{0,2},{1,3},{2,0},{3,1},{4,6},{5,7},{6,4},{7,5},{8,10},{9,11},{10,... | collective-permute-start | bytes 1966088 | tf_op jit(solution)/shard_map/ppermute | solution.py:82
  155.9 19.6 %collective-permute-start.6 = (f32[10,128,128]{2,1,0:T(8,128)S(1)}, f32[10,128,128]{2,1,0:T(8,128)S(1)}, u32[]{:S(2)}, u32[]{:S(2)}) collective-permute-start(f32[10,128,128]{2,1,0:T(8,128)S(1)} %add.814), channel_id=1, source_target_pairs={{0,4},{1,5},{2,6},{3,7},{4,0},{5,1},{6,2},{7,3},{8,12},{9,13},{10,... | collective-permute-start | bytes 1966088 | tf_op jit(solution)/shard_map/ppermute | solution.py:82
  175.6 27.0 %collective-permute-start.11 = (f32[2,3,128,128]{3,2,1,0:T(8,128)S(1)}, f32[2,3,128,128]{3,2,1,0:T(8,128)S(1)}, u32[]{:S(2)}, u32[]{:S(2)}) collective-permute-start(f32[2,3,128,128]{3,2,1,0:T(8,128)S(1)} %fusion.1187), channel_id=1, source_target_pairs={{0,504},{8,0},{16,8},{24,16},{32,24},{40,32},{48,40},{56,48},{64,5... | collective-permute-start | bytes 1179656 | tf_op jit(solution)/shard_map/ppermute | solution.py:18
  179.3 20.3 %collective-permute-start.7 = (f32[2,2,128,128]{2,3,0,1:T(8,128)S(1)}, f32[2,2,128,128]{2,3,0,1:T(8,128)S(1)}, u32[]{:S(2)}, u32[]{:S(2)}) collective-permute-start(f32[2,2,128,128]{2,3,0,1:T(8,128)S(1)} %copy.561), channel_id=1, source_target_pairs={{0,16},{8,24},{16,32},{24,40},{32,48},{40,56},{48,64},{56,72},{64,... | collective-permute-start | bytes 786440 | tf_op jit(solution)/shard_map/ppermute | solution.py:18
  199.6 15.1 %collective-permute-start.8 = (f32[2,2,128,128]{2,3,0,1:T(8,128)S(1)}, f32[2,2,128,128]{2,3,0,1:T(8,128)S(1)}, u32[]{:S(2)}, u32[]{:S(2)}) collective-permute-start(f32[2,2,128,128]{2,3,0,1:T(8,128)S(1)} %add.816), channel_id=1, source_target_pairs={{0,32},{8,40},{16,48},{24,56},{32,64},{40,72},{48,80},{56,88},{64,... | collective-permute-start | bytes 786440 | tf_op jit(solution)/shard_map/ppermute | solution.py:18
  202.7 38.7 %collective-permute-start.12 = (f32[2,3,128,256]{3,2,1,0:T(8,128)S(1)}, f32[2,3,128,256]{3,2,1,0:T(8,128)S(1)}, u32[]{:S(2)}, u32[]{:S(2)}) collective-permute-start(f32[2,3,128,256]{3,2,1,0:T(8,128)S(1)} %pad_maximum_fusion.3), channel_id=1, source_target_pairs={{0,448},{8,456},{16,464},{24,472},{32,480},{40,488},{48,496},{56,5... | collective-permute-start | bytes 2359304 | tf_op jit(solution)/shard_map/ppermute | solution.py:18
  214.8 10.5 %collective-permute-start.9 = (f32[2,2,128,128]{2,3,0,1:T(8,128)S(1)}, f32[2,2,128,128]{2,3,0,1:T(8,128)S(1)}, u32[]{:S(2)}, u32[]{:S(2)}) collective-permute-start(f32[2,2,128,128]{2,3,0,1:T(8,128)S(1)} %add.817), channel_id=1, source_target_pairs={{0,128},{8,136},{16,144},{24,152},{32,160},{40,168},{48,176},{56,1... | collective-permute-start | bytes 786440 | tf_op jit(solution)/shard_map/ppermute | solution.py:18
  225.4 16.0 %collective-permute-start.10 = (f32[2,2,128,128]{2,3,0,1:T(8,128)S(1)}, f32[2,2,128,128]{2,3,0,1:T(8,128)S(1)}, u32[]{:S(2)}, u32[]{:S(2)}) collective-permute-start(f32[2,2,128,128]{2,3,0,1:T(8,128)S(1)} %add.818), channel_id=1, source_target_pairs={{0,256},{8,264},{16,272},{24,280},{32,288},{40,296},{48,304},{56,3... | collective-permute-start | bytes 786440 | tf_op jit(solution)/shard_map/ppermute | solution.py:18
  292.6 22.0 %collective-permute-start.13 = (f32[16,128,128]{2,1,0:T(8,128)S(1)}, f32[16,128,128]{2,1,0:T(8,128)S(1)}, u32[]{:S(2)}, u32[]{:S(2)}) collective-permute-start(f32[16,128,128]{2,1,0:T(8,128)S(1)} %pad_maximum_fusion.1), channel_id=1, source_target_pairs={{0,64},{8,72},{16,80},{24,88},{32,96},{40,104},{48,112},{56,120},{... | collective-permute-start | bytes 3145736 | tf_op jit(solution)/shard_map/ppermute | solution.py:18
  314.8 29.0 %collective-permute-start.14 = (f32[10,128,128]{2,1,0:T(8,128)S(1)}, f32[10,128,128]{2,1,0:T(8,128)S(1)}, u32[]{:S(2)}, u32[]{:S(2)}) collective-permute-start(f32[10,128,128]{2,1,0:T(8,128)S(1)} %pad_maximum_fusion.6), channel_id=1, source_target_pairs={{0,8},{8,16},{16,24},{24,32},{32,40},{40,48},{48,56},{56,64},{64,7... | collective-permute-start | bytes 1966088 | tf_op jit(solution)/shard_map/ppermute | solution.py:18
  344.0 4.0 collective-permute-start.15
  348.0 21.3 %collective-permute-start.16 = (f32[10,128,128]{2,1,0:T(8,128)S(1)}, f32[10,128,128]{2,1,0:T(8,128)S(1)}, u32[]{:S(2)}, u32[]{:S(2)}) collective-permute-start(f32[10,128,128]{2,1,0:T(8,128)S(1)} %fusion.1188), channel_id=1, source_target_pairs={{0,2},{1,3},{2,0},{3,1},{4,6},{5,7},{6,4},{7,5},{8,10},{9,11},{10,... | collective-permute-start | bytes 1966088 | tf_op jit(solution)/shard_map/ppermute | solution.py:82
  369.4 19.7 %collective-permute-start.17 = (f32[10,128,128]{2,1,0:T(8,128)S(1)}, f32[10,128,128]{2,1,0:T(8,128)S(1)}, u32[]{:S(2)}, u32[]{:S(2)}) collective-permute-start(f32[10,128,128]{2,1,0:T(8,128)S(1)} %add.847), channel_id=1, source_target_pairs={{0,4},{1,5},{2,6},{3,7},{4,0},{5,1},{6,2},{7,3},{8,12},{9,13},{10,... | collective-permute-start | bytes 1966088 | tf_op jit(solution)/shard_map/ppermute | solution.py:82
  389.3 24.6 %collective-permute-start.18 = (f32[2,2,128,128]{2,3,0,1:T(8,128)S(1)}, f32[2,2,128,128]{2,3,0,1:T(8,128)S(1)}, u32[]{:S(2)}, u32[]{:S(2)}) collective-permute-start(f32[2,2,128,128]{2,3,0,1:T(8,128)S(1)} %copy.643), channel_id=1, source_target_pairs={{0,16},{8,24},{16,32},{24,40},{32,48},{40,56},{48,64},{56,72},{64,... | collective-permute-start | bytes 786440 | tf_op jit(solution)/shard_map/ppermute | solution.py:18
  413.9 20.6 %collective-permute-start.19 = (f32[2,2,128,128]{2,3,0,1:T(8,128)S(1)}, f32[2,2,128,128]{2,3,0,1:T(8,128)S(1)}, u32[]{:S(2)}, u32[]{:S(2)}) collective-permute-start(f32[2,2,128,128]{2,3,0,1:T(8,128)S(1)} %add.849), channel_id=1, source_target_pairs={{0,32},{8,40},{16,48},{24,56},{32,64},{40,72},{48,80},{56,88},{64,... | collective-permute-start | bytes 786440 | tf_op jit(solution)/shard_map/ppermute | solution.py:18
  434.5 11.3 %collective-permute-start.20 = (f32[2,2,128,128]{2,3,0,1:T(8,128)S(1)}, f32[2,2,128,128]{2,3,0,1:T(8,128)S(1)}, u32[]{:S(2)}, u32[]{:S(2)}) collective-permute-start(f32[2,2,128,128]{2,3,0,1:T(8,128)S(1)} %add.850), channel_id=1, source_target_pairs={{0,128},{8,136},{16,144},{24,152},{32,160},{40,168},{48,176},{56,1... | collective-permute-start | bytes 786440 | tf_op jit(solution)/shard_map/ppermute | solution.py:18
  445.9 26.6 %collective-permute-start.21 = (f32[2,2,128,128]{2,3,0,1:T(8,128)S(1)}, f32[2,2,128,128]{2,3,0,1:T(8,128)S(1)}, u32[]{:S(2)}, u32[]{:S(2)}) collective-permute-start(f32[2,2,128,128]{2,3,0,1:T(8,128)S(1)} %add.851), channel_id=1, source_target_pairs={{0,256},{8,264},{16,272},{24,280},{32,288},{40,296},{48,304},{56,3... | collective-permute-start | bytes 786440 | tf_op jit(solution)/shard_map/ppermute | solution.py:18

commit v2 on v1

--- a/solution.py
+++ b/solution.py
@@ -3,6 +3,8 @@
 import jax
 import jax.numpy as jnp
 from jax import lax
+from jax.experimental import pallas as pl
+from jax.experimental.pallas import tpu as pltpu
 from jax.sharding import PartitionSpec as P
 
 GRID = 8
@@ -73,6 +75,87 @@
     far_real, far_imag = transform(wave_real, wave_imag, tables, 1.0)
     intensity = jnp.sum(far_real**2 + far_imag**2, axis=0)
     return 0.5 * weight * jnp.sum((intensity - target) ** 2)
+
+
+def slot_kernel(cells_ref, probe_ref, target_ref, weight_ref, tab_ref, gcells_ref, gprobe_ref):
+    cosine, sine_table, kern_real, kern_imag = (tab_ref[0], tab_ref[1], tab_ref[2], tab_ref[3])
+
+    def dot(a, b):
+        return jnp.dot(a, b, precision=lax.Precision.HIGHEST, preferred_element_type=jnp.float32)
+
+    def forward(xr, xi):
+        lr = dot(cosine, xr) + dot(sine_table, xi)
+        li = dot(cosine, xi) - dot(sine_table, xr)
+        return (dot(lr, cosine) + dot(li, sine_table), dot(li, cosine) - dot(lr, sine_table))
+
+    def inverse(xr, xi):
+        lr = dot(cosine, xr) - dot(sine_table, xi)
+        li = dot(cosine, xi) + dot(sine_table, xr)
+        return (dot(lr, cosine) - dot(li, sine_table), dot(li, cosine) + dot(lr, sine_table))
+
+    def mul(a, b):
+        return (a[0] * b[0] - a[1] * b[1], a[0] * b[1] + a[1] * b[0])
+
+    def mul_conj(a, b):
+        return (a[0] * b[0] + a[1] * b[1], a[1] * b[0] - a[0] * b[1])
+
+    kern = (kern_real, kern_imag)
+    propagate = lambda x: inverse(*mul(forward(*x), kern))
+    propagate_adjoint = lambda x: inverse(*mul_conj(forward(*x), kern))
+    depth_count = cells_ref.shape[1]
+    mode_count = probe_ref.shape[0]
+    layers = [(cells_ref[0, d], cells_ref[1, d]) for d in range(depth_count)]
+    saved = []
+    intensity = None
+    for m in range(mode_count):
+        wave = (probe_ref[m, 0], probe_ref[m, 1])
+        inputs = []
+        for d in range(depth_count):
+            inputs.append(wave)
+            wave = mul(wave, layers[d])
+            if d < depth_count - 1:
+                wave = propagate(wave)
+        far = forward(*wave)
+        saved.append((inputs, far))
+        power = far[0] * far[0] + far[1] * far[1]
+        intensity = power if intensity is None else intensity + power
+    residual = weight_ref[...] * (intensity - target_ref[...])
+    layer_grads = [None] * depth_count
+    for m in range(mode_count):
+        inputs, far = saved[m]
+        grad = inverse(2.0 * residual * far[0], 2.0 * residual * far[1])
+        for d in reversed(range(depth_count)):
+            term = mul_conj(grad, inputs[d])
+            if layer_grads[d] is None:
+                layer_grads[d] = term
+            else:
+                layer_grads[d] = (layer_grads[d][0] + term[0], layer_grads[d][1] + term[1])
+            grad = mul_conj(grad, layers[d])
+            if d > 0:
+                grad = propagate_adjoint(grad)
+        gprobe_ref[m, 0] = grad[0]
+        gprobe_ref[m, 1] = grad[1]
+    for d in range(depth_count):
+        gcells_ref[0, d] = layer_grads[d][0]
+        gcells_ref[1, d] = layer_grads[d][1]
+
+
+def slot_grad(patch_cells, mode_values, target, weight, tables):
+    tab = jnp.stack(tables)
+    side = target.shape[-1]
+    dots = 2 * mode_values.shape[0] * 10 * 8
+    return pl.pallas_call(
+        slot_kernel,
+        out_shape=(
+            jax.ShapeDtypeStruct(patch_cells.shape, jnp.float32),
+            jax.ShapeDtypeStruct(mode_values.shape, jnp.float32),
+        ),
+        in_specs=[pl.BlockSpec(memory_space=pltpu.VMEM)] * 5,
+        out_specs=(pl.BlockSpec(memory_space=pltpu.VMEM), pl.BlockSpec(memory_space=pltpu.VMEM)),
+        cost_estimate=pl.CostEstimate(
+            flops=dots * 2 * side**3, bytes_accessed=4 * side * side * 22, transcendentals=0
+        ),
+    )(patch_cells, mode_values, target, weight.reshape(1, 1), tab)
 
 
 def xor_sum(values, axis):
@@ -122,14 +205,7 @@
             patch_cells = lax.dynamic_slice(canvas, starts, (2, slices, pattern_side, pattern_side))
             target = measured[0, 0, slot_index]
             weight = live[0, 0, slot_index].astype(jnp.float32)
-            _, pullback = jax.vjp(
-                lambda cell_values, mode_values: slot_loss(
-                    cell_values, mode_values, target, weight, tables
-                ),
-                patch_cells,
-                current_probe,
-            )
-            grad_patch, grad_modes = pullback(jnp.ones((), jnp.float32))
+            grad_patch, grad_modes = slot_grad(patch_cells, current_probe, target, weight, tables)
             current = lax.dynamic_slice(
                 grad_canvas, starts, (2, slices, pattern_side, pattern_side)
             )

time: 483 us -> 422 us (0.87)
  the two profiles are of different devices: /device:TPU:80 before, /device:TPU:1 now
where the time goes in v2:
time: 422 us; the launch traced here: 415 us
  waiting for transfers between devices  242 us (57%)
  starting transfers between devices  112 us (27%)
  Pallas kernels  32.7 us (8%)
  local copies, waits for them, and re-layouts  13.6 us (3%)
  other arithmetic  8.92 us (2%)
  between operations  5.65 us (1%)
    ppermute x16, waiting for transfers between devices, shifted(): lax.ppermute(shard, axis, [(i, (i + by) % size) for i in range(size)])  179 us
    ppermute x16, starting transfers between devices, shifted(): lax.ppermute(shard, axis, [(i, (i + by) % size) for i in range(size)])  83.4 us
    ppermute x6, waiting for transfers between devices, xor_sum(): lax.ppermute(values, axis, [(i, i ^ step) for i in range(size)])  63.3 us
    pallas_call x2, Pallas kernels, slot_grad(): pl.pallas_call(slot_kernel, out_shape=(jax.ShapeDtypeStruct(patch_cells.s...  32.7 us
    ppermute x6, starting transfers between devices, xor_sum(): lax.ppermute(values, axis, [(i, i ^ step) for i in range(size)])  28.6 us
  transfers between devices with their start and end apart: 22, of which 20 were waited for; matrix products, arithmetic and copies ran while one was open for 1% of the time, Pallas kernels for 0%

profile of v2, /device:TPU:1, one launch (start us, length us, event | category | flops | bytes accessed | tf_op | source)
XLA Modules:
  0.0 414.8 jit_solution(6813894121416851900)
XLA Ops:
  0.7 1.1 pad_maximum_fusion.8
  1.8 14.4 %collective-permute-start = (f32[2,3,128,128]{3,2,1,0:T(8,128)S(1)}, f32[2,3,128,128]{3,2,1,0:T(8,128)S(1)}, u32[]{:S(2)}, u32[]{:S(2)}) collective-permute-start(f32[2,3,128,128]{3,2,1,0:T(8,128)S(1)} %pad_maximum_fusion.8), channel_id=1, source_target_pairs={{0,504},{8,0},{16,8},{24,16},{32,24},{40,32},{48,40},{56,48},{64,5... | collective-permute-start | bytes 1179656 | tf_op jit(solution)/shard_map/ppermute | solution.py:20
  16.2 7.8 %collective-permute-done = f32[2,3,128,128]{3,2,1,0:T(8,128)S(1)} collective-permute-done((f32[2,3,128,128]{3,2,1,0:T(8,128)S(1)}, f32[2,3,128,128]{3,2,1,0:T(8,128)S(1)}, u32[]{:S(2)}, u32[]{:S(2)}) %collective-permute-start) | collective-permute-done | bytes 393248 | tf_op jit(solution)/shard_map/ppermute | solution.py:20
  23.9 1.1 pad_maximum_fusion.2
  25.0 2.2 collective-permute-start.1
  27.2 0.6 fusion.20
  32.3 0.3 sine_multiply_fusion
  32.6 0.3 fusion.9
  32.9 0.7 pad_maximum_fusion.9.tab_ref
  33.7 10.7 %collective-permute-done.1 = f32[2,3,128,256]{3,2,1,0:T(8,128)S(1)} collective-permute-done((f32[2,3,128,256]{3,2,1,0:T(8,128)S(1)}, f32[2,3,128,256]{3,2,1,0:T(8,128)S(1)}, u32[]{:S(2)}, u32[]{:S(2)}) %collective-permute-start.1) | collective-permute-done | bytes 786464 | tf_op jit(solution)/shard_map/ppermute | solution.py:20
  44.4 1.1 fusion.4.cells_ref
  45.5 16.3 %shard_map.85 = (f32[2,3,128,128]{3,2,1,0:T(8,128)}, f32[2,2,128,128]{3,2,1,0:T(8,128)}) custom-call(f32[2,3,128,128]{3,2,1,0:T(8,128)} %fusion.4.cells_ref, f32[2,2,128,128]{3,2,1,0:T(8,128)} %probe_ref.1, f32[128,128]{1,0:T(8,128)} %bitcast.57, f32[1,1]{1,0:T(1,128)} %bitcast.5.weight_ref, f32[4,128,128]{2,1,0:T(8,128)} %pad_maximum_fusion.9.tab_ref), custom_call_target="tpu_custom_call" | custom-call | flops 1342177280 | bytes 1441792 | tf_op jit(solution)/shard_map/pallas_call | solution.py:147
  61.9 0.1 broadcast.209.clone
  62.0 0.9 copy-done.6
  62.9 4.2 %dynamic_update_slice.6 = f32[2,3,256,256]{3,2,1,0:T(8,128)S(1)} dynamic-update-slice(f32[2,3,256,256]{3,2,1,0:T(8,128)S(1)} %broadcast.209.clone, f32[2,3,128,128]{3,2,1,0:T(8,128)S(1)} %copy-done.6, s32[]{:T(128)} %constant.13.clone.1, s32[]{:T(128)} %constant.13.clone.1, s32[]{:T(128)S(6)} %select_n.46, s32[]{:T(128)S(6)} %select_n.47) | dynamic-update-slice | bytes 786436 | tf_op jit(solution)/shard_map/dynamic_update_slice | solution.py:212
  67.1 0.2 fusion.19
  67.3 0.8 copy-done.4
  68.1 1.9 collective-permute-start.2
  70.1 23.2 %collective-permute-done.2 = f32[16,128,128]{2,1,0:T(8,128)S(1)} collective-permute-done((f32[16,128,128]{2,1,0:T(8,128)S(1)}, f32[16,128,128]{2,1,0:T(8,128)S(1)}, u32[]{:S(2)}, u32[]{:S(2)}) %collective-permute-start.2) | collective-permute-done | bytes 1048608 | tf_op jit(solution)/shard_map/ppermute | solution.py:20
  93.4 1.9 collective-permute-start.3
  95.3 17.9 %collective-permute-done.3 = f32[10,128,128]{2,1,0:T(8,128)S(1)} collective-permute-done((f32[10,128,128]{2,1,0:T(8,128)S(1)}, f32[10,128,128]{2,1,0:T(8,128)S(1)}, u32[]{:S(2)}, u32[]{:S(2)}) %collective-permute-start.3) | collective-permute-done | bytes 655392 | tf_op jit(solution)/shard_map/ppermute | solution.py:20
  113.3 5.8 %collective-permute-start.4 = (f32[10,128,128]{2,1,0:T(8,128)S(1)}, f32[10,128,128]{2,1,0:T(8,128)S(1)}, u32[]{:S(2)}, u32[]{:S(2)}) collective-permute-start(f32[10,128,128]{2,1,0:T(8,128)S(1)} %pad_maximum_fusion.5), channel_id=1, source_target_pairs={{0,1},{1,0},{2,3},{3,2},{4,5},{5,4},{6,7},{7,6},{8,9},{9,8},{10,11... | collective-permute-start | bytes 1966088 | tf_op jit(solution)/shard_map/ppermute | solution.py:165
  119.1 1.7 collective-permute-done.4
  120.9 3.3 collective-permute-start.5
  124.2 14.5 %collective-permute-done.5 = f32[10,128,128]{2,1,0:T(8,128)S(1)} collective-permute-done((f32[10,128,128]{2,1,0:T(8,128)S(1)}, f32[10,128,128]{2,1,0:T(8,128)S(1)}, u32[]{:S(2)}, u32[]{:S(2)}) %collective-permute-start.5) | collective-permute-done | bytes 655392 | tf_op jit(solution)/shard_map/ppermute | solution.py:165
  138.8 4.7 %collective-permute-start.6 = (f32[10,128,128]{2,1,0:T(8,128)S(1)}, f32[10,128,128]{2,1,0:T(8,128)S(1)}, u32[]{:S(2)}, u32[]{:S(2)}) collective-permute-start(f32[10,128,128]{2,1,0:T(8,128)S(1)} %add.154), channel_id=1, source_target_pairs={{0,4},{1,5},{2,6},{3,7},{4,0},{5,1},{6,2},{7,3},{8,12},{9,13},{10,... | collective-permute-start | bytes 1966088 | tf_op jit(solution)/shard_map/ppermute | solution.py:165
  143.5 13.7 %collective-permute-done.6 = f32[10,128,128]{2,1,0:T(8,128)S(1)} collective-permute-done((f32[10,128,128]{2,1,0:T(8,128)S(1)}, f32[10,128,128]{2,1,0:T(8,128)S(1)}, u32[]{:S(2)}, u32[]{:S(2)}) %collective-permute-start.6) | collective-permute-done | bytes 655392 | tf_op jit(solution)/shard_map/ppermute | solution.py:165
  157.4 3.4 collective-permute-start.7
  160.8 1.9 collective-permute-start.9
  162.7 9.5 %collective-permute-done.9 = f32[2,2,128,128]{3,2,1,0:T(8,128)S(1)} collective-permute-done((f32[2,2,128,128]{3,2,1,0:T(8,128)S(1)}, f32[2,2,128,128]{3,2,1,0:T(8,128)S(1)}, u32[]{:S(2)}, u32[]{:S(2)}) %collective-permute-start.9) | collective-permute-done | bytes 262176 | tf_op jit(solution)/shard_map/ppermute | solution.py:20
  172.3 5.2 %collective-permute-start.10 = (f32[2,2,128,128]{3,2,1,0:T(8,128)S(1)}, f32[2,2,128,128]{3,2,1,0:T(8,128)S(1)}, u32[]{:S(2)}, u32[]{:S(2)}) collective-permute-start(f32[2,2,128,128]{3,2,1,0:T(8,128)S(1)} %add.156), channel_id=1, source_target_pairs={{0,32},{8,40},{16,48},{24,56},{32,64},{40,72},{48,80},{56,88},{64,... | collective-permute-start | bytes 786440 | tf_op jit(solution)/shard_map/ppermute | solution.py:20
  177.5 1.9 collective-permute-start.8
  179.5 7.2 %collective-permute-done.10 = f32[2,2,128,128]{3,2,1,0:T(8,128)S(1)} collective-permute-done((f32[2,2,128,128]{3,2,1,0:T(8,128)S(1)}, f32[2,2,128,128]{3,2,1,0:T(8,128)S(1)}, u32[]{:S(2)}, u32[]{:S(2)}) %collective-permute-start.10) | collective-permute-done | bytes 262176 | tf_op jit(solution)/shard_map/ppermute | solution.py:20
  186.8 9.7 %collective-permute-start.11 = (f32[2,2,128,128]{3,2,1,0:T(8,128)S(1)}, f32[2,2,128,128]{3,2,1,0:T(8,128)S(1)}, u32[]{:S(2)}, u32[]{:S(2)}) collective-permute-start(f32[2,2,128,128]{3,2,1,0:T(8,128)S(1)} %add.157), channel_id=1, source_target_pairs={{0,128},{8,136},{16,144},{24,152},{32,160},{40,168},{48,176},{56,1... | collective-permute-start | bytes 786440 | tf_op jit(solution)/shard_map/ppermute | solution.py:20
  196.4 4.5 %collective-permute-done.11 = f32[2,2,128,128]{3,2,1,0:T(8,128)S(1)} collective-permute-done((f32[2,2,128,128]{3,2,1,0:T(8,128)S(1)}, f32[2,2,128,128]{3,2,1,0:T(8,128)S(1)}, u32[]{:S(2)}, u32[]{:S(2)}) %collective-permute-start.11) | collective-permute-done | bytes 262176 | tf_op jit(solution)/shard_map/ppermute | solution.py:20
  201.0 9.3 %collective-permute-start.12 = (f32[2,2,128,128]{3,2,1,0:T(8,128)S(1)}, f32[2,2,128,128]{3,2,1,0:T(8,128)S(1)}, u32[]{:S(2)}, u32[]{:S(2)}) collective-permute-start(f32[2,2,128,128]{3,2,1,0:T(8,128)S(1)} %add.158), channel_id=1, source_target_pairs={{0,256},{8,264},{16,272},{24,280},{32,288},{40,296},{48,304},{56,3... | collective-permute-start | bytes 786440 | tf_op jit(solution)/shard_map/ppermute | solution.py:20
  210.3 4.0 collective-permute-done.12
  214.3 0.8 multiply_subtract_fusion.1.probe_ref
  215.1 1.2 fusion.1.cells_ref
  216.2 16.3 %shard_map.86 = (f32[2,3,128,128]{3,2,1,0:T(8,128)}, f32[2,2,128,128]{3,2,1,0:T(8,128)}) custom-call(f32[2,3,128,128]{3,2,1,0:T(8,128)} %fusion.1.cells_ref, f32[2,2,128,128]{3,2,1,0:T(8,128)} %multiply_subtract_fusion.1.probe_ref, f32[128,128]{1,0:T(8,128)} %bitcast.58, f32[1,1]{1,0:T(1,128)} %bitcast.5.weight_ref, f32[4,128,128]{2,1,0:T(8,128)} %pad_maximum_fusion.9.tab_ref), custom_call_target="tpu_custom_call" | custom-call | flops 1342177280 | bytes 1441792 | tf_op jit(solution)/shard_map/pallas_call | solution.py:147
  232.7 0.9 copy-done.5
  233.5 4.2 %dynamic_update_slice.7 = f32[2,3,256,256]{3,2,1,0:T(8,128)S(1)} dynamic-update-slice(f32[2,3,256,256]{3,2,1,0:T(8,128)S(1)} %broadcast.209, f32[2,3,128,128]{3,2,1,0:T(8,128)S(1)} %copy-done.5, s32[]{:T(128)} %constant.13.clone.1, s32[]{:T(128)} %constant.13.clone.1, s32[]{:T(128)S(6)} %select_n.46, s32[]{:T(128)S(6)} %select_n.47) | dynamic-update-slice | bytes 786436 | tf_op jit(solution)/shard_map/dynamic_update_slice | solution.py:212
  237.7 0.2 fusion.18
  237.9 0.8 copy-done.3
  238.8 20.9 %collective-permute-start.13 = (f32[16,128,128]{2,1,0:T(8,128)S(1)}, f32[16,128,128]{2,1,0:T(8,128)S(1)}, u32[]{:S(2)}, u32[]{:S(2)}) collective-permute-start(f32[16,128,128]{2,1,0:T(8,128)S(1)} %pad_maximum_fusion.1), channel_id=1, source_target_pairs={{0,64},{8,72},{16,80},{24,88},{32,96},{40,104},{48,112},{56,120},{... | collective-permute-start | bytes 3145736 | tf_op jit(solution)/shard_map/ppermute | solution.py:20
  259.7 20.7 %collective-permute-done.13 = f32[16,128,128]{2,1,0:T(8,128)S(1)} collective-permute-done((f32[16,128,128]{2,1,0:T(8,128)S(1)}, f32[16,128,128]{2,1,0:T(8,128)S(1)}, u32[]{:S(2)}, u32[]{:S(2)}) %collective-permute-start.13) | collective-permute-done | bytes 1048608 | tf_op jit(solution)/shard_map/ppermute | solution.py:20
  280.5 1.9 collective-permute-start.14
  282.4 16.8 %collective-permute-done.14 = f32[10,128,128]{2,1,0:T(8,128)S(1)} collective-permute-done((f32[10,128,128]{2,1,0:T(8,128)S(1)}, f32[10,128,128]{2,1,0:T(8,128)S(1)}, u32[]{:S(2)}, u32[]{:S(2)}) %collective-permute-start.14) | collective-permute-done | bytes 655392 | tf_op jit(solution)/shard_map/ppermute | solution.py:20
  299.4 5.5 %collective-permute-start.15 = (f32[10,128,128]{2,1,0:T(8,128)S(1)}, f32[10,128,128]{2,1,0:T(8,128)S(1)}, u32[]{:S(2)}, u32[]{:S(2)}) collective-permute-start(f32[10,128,128]{2,1,0:T(8,128)S(1)} %pad_maximum_fusion.7), channel_id=1, source_target_pairs={{0,1},{1,0},{2,3},{3,2},{4,5},{5,4},{6,7},{7,6},{8,9},{9,8},{10,11... | collective-permute-start | bytes 1966088 | tf_op jit(solution)/shard_map/ppermute | solution.py:165
  304.9 1.7 collective-permute-done.15
  306.7 7.3 %collective-permute-start.16 = (f32[10,128,128]{2,1,0:T(8,128)S(1)}, f32[10,128,128]{2,1,0:T(8,128)S(1)}, u32[]{:S(2)}, u32[]{:S(2)}) collective-permute-start(f32[10,128,128]{2,1,0:T(8,128)S(1)} %fusion.16), channel_id=1, source_target_pairs={{0,2},{1,3},{2,0},{3,1},{4,6},{5,7},{6,4},{7,5},{8,10},{9,11},{10,... | collective-permute-start | bytes 1966088 | tf_op jit(solution)/shard_map/ppermute | solution.py:165
  314.1 14.8 %collective-permute-done.16 = f32[10,128,128]{2,1,0:T(8,128)S(1)} collective-permute-done((f32[10,128,128]{2,1,0:T(8,128)S(1)}, f32[10,128,128]{2,1,0:T(8,128)S(1)}, u32[]{:S(2)}, u32[]{:S(2)}) %collective-permute-start.16) | collective-permute-done | bytes 655392 | tf_op jit(solution)/shard_map/ppermute | solution.py:165
  328.9 1.9 collective-permute-start.17
  330.9 16.8 %collective-permute-done.17 = f32[10,128,128]{2,1,0:T(8,128)S(1)} collective-permute-done((f32[10,128,128]{2,1,0:T(8,128)S(1)}, f32[10,128,128]{2,1,0:T(8,128)S(1)}, u32[]{:S(2)}, u32[]{:S(2)}) %collective-permute-start.17) | collective-permute-done | bytes 655392 | tf_op jit(solution)/shard_map/ppermute | solution.py:165
  347.8 1.9 collective-permute-start.18
  349.7 17.6 %collective-permute-done.18 = f32[2,2,128,128]{3,2,1,0:T(8,128)S(1)} collective-permute-done((f32[2,2,128,128]{3,2,1,0:T(8,128)S(1)}, f32[2,2,128,128]{3,2,1,0:T(8,128)S(1)}, u32[]{:S(2)}, u32[]{:S(2)}) %collective-permute-start.18) | collective-permute-done | bytes 262176 | tf_op jit(solution)/shard_map/ppermute | solution.py:20
  367.3 1.9 collective-permute-start.19
  369.3 16.7 %collective-permute-done.19 = f32[2,2,128,128]{3,2,1,0:T(8,128)S(1)} collective-permute-done((f32[2,2,128,128]{3,2,1,0:T(8,128)S(1)}, f32[2,2,128,128]{3,2,1,0:T(8,128)S(1)}, u32[]{:S(2)}, u32[]{:S(2)}) %collective-permute-start.19) | collective-permute-done | bytes 262176 | tf_op jit(solution)/shard_map/ppermute | solution.py:20
  386.0 1.9 collective-permute-start.20
  388.0 12.2 %collective-permute-done.20 = f32[2,2,128,128]{3,2,1,0:T(8,128)S(1)} collective-permute-done((f32[2,2,128,128]{3,2,1,0:T(8,128)S(1)}, f32[2,2,128,128]{3,2,1,0:T(8,128)S(1)}, u32[]{:S(2)}, u32[]{:S(2)}) %collective-permute-start.20) | collective-permute-done | bytes 262176 | tf_op jit(solution)/shard_map/ppermute | solution.py:20
  400.2 3.0 collective-permute-start.21
  403.3 0.8 slice_bitcast_fusion
  404.1 10.0 %collective-permute-done.21 = f32[2,2,128,128]{3,2,1,0:T(8,128)S(1)} collective-permute-done((f32[2,2,128,128]{3,2,1,0:T(8,128)S(1)}, f32[2,2,128,128]{3,2,1,0:T(8,128)S(1)}, u32[]{:S(2)}, u32[]{:S(2)}) %collective-permute-start.21) | collective-permute-done | bytes 262176 | tf_op jit(solution)/shard_map/ppermute | solution.py:20
  414.1 0.7 multiply_subtract_fusion
  (51 shorter events, 1.8 us)
Async XLA Ops:
  0.6 26.6 %copy-start.8 = (s32[1,1,1,2]{3,2,1,0:T(1,128)S(1)}, s32[1,1,1,2]{3,2,1,0:T(1,128)}, u32[]{:S(2)}) copy-start(s32[1,1,1,2]{3,2,1,0:T(1,128)} %param.10) | copy-start | bytes 28
  0.6 43.8 %copy-start = (f32[3,1,128,128]{3,2,1,0:T(8,128)S(1)}, f32[3,1,128,128]{3,2,1,0:T(8,128)}, u32[]{:S(2)}) copy-start(f32[3,1,128,128]{3,2,1,0:T(8,128)} %param.6) | copy-start | bytes 589828
  0.7 43.7 %copy-start.1 = (f32[3,1,128,128]{3,2,1,0:T(8,128)S(1)}, f32[3,1,128,128]{3,2,1,0:T(8,128)}, u32[]{:S(2)}) copy-start(f32[3,1,128,128]{3,2,1,0:T(8,128)} %param.7) | copy-start | bytes 589828
  1.8 22.2 %collective-permute-start = (f32[2,3,128,128]{3,2,1,0:T(8,128)S(1)}, f32[2,3,128,128]{3,2,1,0:T(8,128)S(1)}, u32[]{:S(2)}, u32[]{:S(2)}) collective-permute-start(f32[2,3,128,128]{3,2,1,0:T(8,128)S(1)} %pad_maximum_fusion.8), channel_id=1, source_target_pairs={{0,504},{8,0},{16,8},{24,16},{32,24},{40,32},{48,40},{56,48},{64,5... | collective-permute-start | bytes 1179656 | tf_op jit(solution)/shard_map/ppermute | solution.py:20
  25.0 19.4 %collective-permute-start.1 = (f32[2,3,128,256]{3,2,1,0:T(8,128)S(1)}, f32[2,3,128,256]{3,2,1,0:T(8,128)S(1)}, u32[]{:S(2)}, u32[]{:S(2)}) collective-permute-start(f32[2,3,128,256]{3,2,1,0:T(8,128)S(1)} %pad_maximum_fusion.2), channel_id=1, source_target_pairs={{0,448},{8,456},{16,464},{24,472},{32,480},{40,488},{48,496},{56,5... | collective-permute-start | bytes 2359304 | tf_op jit(solution)/shard_map/ppermute | solution.py:20
  61.9 1.0 copy-start.6
  67.1 1.0 copy-start.4
  68.1 25.1 %collective-permute-start.2 = (f32[16,128,128]{2,1,0:T(8,128)S(1)}, f32[16,128,128]{2,1,0:T(8,128)S(1)}, u32[]{:S(2)}, u32[]{:S(2)}) collective-permute-start(f32[16,128,128]{2,1,0:T(8,128)S(1)} %pad_maximum_fusion), channel_id=1, source_target_pairs={{0,64},{8,72},{16,80},{24,88},{32,96},{40,104},{48,112},{56,120},{... | collective-permute-start | bytes 3145736 | tf_op jit(solution)/shard_map/ppermute | solution.py:20
  93.4 19.8 %collective-permute-start.3 = (f32[10,128,128]{2,1,0:T(8,128)S(1)}, f32[10,128,128]{2,1,0:T(8,128)S(1)}, u32[]{:S(2)}, u32[]{:S(2)}) collective-permute-start(f32[10,128,128]{2,1,0:T(8,128)S(1)} %pad_maximum_fusion.4), channel_id=1, source_target_pairs={{0,8},{8,16},{16,24},{24,32},{32,40},{40,48},{48,56},{56,64},{64,7... | collective-permute-start | bytes 1966088 | tf_op jit(solution)/shard_map/ppermute | solution.py:20
  113.3 7.5 %collective-permute-start.4 = (f32[10,128,128]{2,1,0:T(8,128)S(1)}, f32[10,128,128]{2,1,0:T(8,128)S(1)}, u32[]{:S(2)}, u32[]{:S(2)}) collective-permute-start(f32[10,128,128]{2,1,0:T(8,128)S(1)} %pad_maximum_fusion.5), channel_id=1, source_target_pairs={{0,1},{1,0},{2,3},{3,2},{4,5},{5,4},{6,7},{7,6},{8,9},{9,8},{10,11... | collective-permute-start | bytes 1966088 | tf_op jit(solution)/shard_map/ppermute | solution.py:165
  120.9 17.8 %collective-permute-start.5 = (f32[10,128,128]{2,1,0:T(8,128)S(1)}, f32[10,128,128]{2,1,0:T(8,128)S(1)}, u32[]{:S(2)}, u32[]{:S(2)}) collective-permute-start(f32[10,128,128]{2,1,0:T(8,128)S(1)} %fusion.17), channel_id=1, source_target_pairs={{0,2},{1,3},{2,0},{3,1},{4,6},{5,7},{6,4},{7,5},{8,10},{9,11},{10,... | collective-permute-start | bytes 1966088 | tf_op jit(solution)/shard_map/ppermute | solution.py:165
  138.8 18.4 %collective-permute-start.6 = (f32[10,128,128]{2,1,0:T(8,128)S(1)}, f32[10,128,128]{2,1,0:T(8,128)S(1)}, u32[]{:S(2)}, u32[]{:S(2)}) collective-permute-start(f32[10,128,128]{2,1,0:T(8,128)S(1)} %add.154), channel_id=1, source_target_pairs={{0,4},{1,5},{2,6},{3,7},{4,0},{5,1},{6,2},{7,3},{8,12},{9,13},{10,... | collective-permute-start | bytes 1966088 | tf_op jit(solution)/shard_map/ppermute | solution.py:165
  157.4 20.1 %collective-permute-start.7 = (f32[2,3,128,128]{3,2,1,0:T(8,128)S(1)}, f32[2,3,128,128]{3,2,1,0:T(8,128)S(1)}, u32[]{:S(2)}, u32[]{:S(2)}) collective-permute-start(f32[2,3,128,128]{3,2,1,0:T(8,128)S(1)} %fusion.15), channel_id=1, source_target_pairs={{0,504},{8,0},{16,8},{24,16},{32,24},{40,32},{48,40},{56,48},{64,5... | collective-permute-start | bytes 1179656 | tf_op jit(solution)/shard_map/ppermute | solution.py:20
  160.8 11.4 %collective-permute-start.9 = (f32[2,2,128,128]{3,2,1,0:T(8,128)S(1)}, f32[2,2,128,128]{3,2,1,0:T(8,128)S(1)}, u32[]{:S(2)}, u32[]{:S(2)}) collective-permute-start(f32[2,2,128,128]{3,2,1,0:T(8,128)S(1)} %bitcast.51), channel_id=1, source_target_pairs={{0,16},{8,24},{16,32},{24,40},{32,48},{40,56},{48,64},{56,72},{64,... | collective-permute-start | bytes 786440 | tf_op jit(solution)/shard_map/ppermute | solution.py:20
  172.3 42.0 %copy-start.7 = (f32[2,2,128,128]{3,2,1,0:T(8,128)S(1)}, f32[2,2,128,128]{3,2,1,0:T(8,128)}, u32[]{:S(2)}) copy-start(f32[2,2,128,128]{3,2,1,0:T(8,128)} %probe_ref.1) | copy-start | bytes 786436
  172.3 14.4 %collective-permute-start.10 = (f32[2,2,128,128]{3,2,1,0:T(8,128)S(1)}, f32[2,2,128,128]{3,2,1,0:T(8,128)S(1)}, u32[]{:S(2)}, u32[]{:S(2)}) collective-permute-start(f32[2,2,128,128]{3,2,1,0:T(8,128)S(1)} %add.156), channel_id=1, source_target_pairs={{0,32},{8,40},{16,48},{24,56},{32,64},{40,72},{48,80},{56,88},{64,... | collective-permute-start | bytes 786440 | tf_op jit(solution)/shard_map/ppermute | solution.py:20
  177.5 37.5 %collective-permute-start.8 = (f32[2,3,128,256]{3,2,1,0:T(8,128)S(1)}, f32[2,3,128,256]{3,2,1,0:T(8,128)S(1)}, u32[]{:S(2)}, u32[]{:S(2)}) collective-permute-start(f32[2,3,128,256]{3,2,1,0:T(8,128)S(1)} %pad_maximum_fusion.3), channel_id=1, source_target_pairs={{0,448},{8,456},{16,464},{24,472},{32,480},{40,488},{48,496},{56,5... | collective-permute-start | bytes 2359304 | tf_op jit(solution)/shard_map/ppermute | solution.py:20
  186.8 14.2 %collective-permute-start.11 = (f32[2,2,128,128]{3,2,1,0:T(8,128)S(1)}, f32[2,2,128,128]{3,2,1,0:T(8,128)S(1)}, u32[]{:S(2)}, u32[]{:S(2)}) collective-permute-start(f32[2,2,128,128]{3,2,1,0:T(8,128)S(1)} %add.157), channel_id=1, source_target_pairs={{0,128},{8,136},{16,144},{24,152},{32,160},{40,168},{48,176},{56,1... | collective-permute-start | bytes 786440 | tf_op jit(solution)/shard_map/ppermute | solution.py:20
  201.0 13.3 %collective-permute-start.12 = (f32[2,2,128,128]{3,2,1,0:T(8,128)S(1)}, f32[2,2,128,128]{3,2,1,0:T(8,128)S(1)}, u32[]{:S(2)}, u32[]{:S(2)}) collective-permute-start(f32[2,2,128,128]{3,2,1,0:T(8,128)S(1)} %add.158), channel_id=1, source_target_pairs={{0,256},{8,264},{16,272},{24,280},{32,288},{40,296},{48,304},{56,3... | collective-permute-start | bytes 786440 | tf_op jit(solution)/shard_map/ppermute | solution.py:20
  232.5 1.0 copy-start.5
  237.7 1.0 copy-start.3
  238.8 41.6 %collective-permute-start.13 = (f32[16,128,128]{2,1,0:T(8,128)S(1)}, f32[16,128,128]{2,1,0:T(8,128)S(1)}, u32[]{:S(2)}, u32[]{:S(2)}) collective-permute-start(f32[16,128,128]{2,1,0:T(8,128)S(1)} %pad_maximum_fusion.1), channel_id=1, source_target_pairs={{0,64},{8,72},{16,80},{24,88},{32,96},{40,104},{48,112},{56,120},{... | collective-permute-start | bytes 3145736 | tf_op jit(solution)/shard_map/ppermute | solution.py:20
  280.5 18.7 %collective-permute-start.14 = (f32[10,128,128]{2,1,0:T(8,128)S(1)}, f32[10,128,128]{2,1,0:T(8,128)S(1)}, u32[]{:S(2)}, u32[]{:S(2)}) collective-permute-start(f32[10,128,128]{2,1,0:T(8,128)S(1)} %pad_maximum_fusion.6), channel_id=1, source_target_pairs={{0,8},{8,16},{16,24},{24,32},{32,40},{40,48},{48,56},{56,64},{64,7... | collective-permute-start | bytes 1966088 | tf_op jit(solution)/shard_map/ppermute | solution.py:20
  299.4 7.2 %collective-permute-start.15 = (f32[10,128,128]{2,1,0:T(8,128)S(1)}, f32[10,128,128]{2,1,0:T(8,128)S(1)}, u32[]{:S(2)}, u32[]{:S(2)}) collective-permute-start(f32[10,128,128]{2,1,0:T(8,128)S(1)} %pad_maximum_fusion.7), channel_id=1, source_target_pairs={{0,1},{1,0},{2,3},{3,2},{4,5},{5,4},{6,7},{7,6},{8,9},{9,8},{10,11... | collective-permute-start | bytes 1966088 | tf_op jit(solution)/shard_map/ppermute | solution.py:165
  306.7 22.1 %collective-permute-start.16 = (f32[10,128,128]{2,1,0:T(8,128)S(1)}, f32[10,128,128]{2,1,0:T(8,128)S(1)}, u32[]{:S(2)}, u32[]{:S(2)}) collective-permute-start(f32[10,128,128]{2,1,0:T(8,128)S(1)} %fusion.16), channel_id=1, source_target_pairs={{0,2},{1,3},{2,0},{3,1},{4,6},{5,7},{6,4},{7,5},{8,10},{9,11},{10,... | collective-permute-start | bytes 1966088 | tf_op jit(solution)/shard_map/ppermute | solution.py:165
  328.9 18.8 %collective-permute-start.17 = (f32[10,128,128]{2,1,0:T(8,128)S(1)}, f32[10,128,128]{2,1,0:T(8,128)S(1)}, u32[]{:S(2)}, u32[]{:S(2)}) collective-permute-start(f32[10,128,128]{2,1,0:T(8,128)S(1)} %add.166), channel_id=1, source_target_pairs={{0,4},{1,5},{2,6},{3,7},{4,0},{5,1},{6,2},{7,3},{8,12},{9,13},{10,... | collective-permute-start | bytes 1966088 | tf_op jit(solution)/shard_map/ppermute | solution.py:165
  347.8 19.5 %collective-permute-start.18 = (f32[2,2,128,128]{3,2,1,0:T(8,128)S(1)}, f32[2,2,128,128]{3,2,1,0:T(8,128)S(1)}, u32[]{:S(2)}, u32[]{:S(2)}) collective-permute-start(f32[2,2,128,128]{3,2,1,0:T(8,128)S(1)} %bitcast.53), channel_id=1, source_target_pairs={{0,16},{8,24},{16,32},{24,40},{32,48},{40,56},{48,64},{56,72},{64,... | collective-permute-start | bytes 786440 | tf_op jit(solution)/shard_map/ppermute | solution.py:20
  367.3 18.6 %collective-permute-start.19 = (f32[2,2,128,128]{3,2,1,0:T(8,128)S(1)}, f32[2,2,128,128]{3,2,1,0:T(8,128)S(1)}, u32[]{:S(2)}, u32[]{:S(2)}) collective-permute-start(f32[2,2,128,128]{3,2,1,0:T(8,128)S(1)} %add.168), channel_id=1, source_target_pairs={{0,32},{8,40},{16,48},{24,56},{32,64},{40,72},{48,80},{56,88},{64,... | collective-permute-start | bytes 786440 | tf_op jit(solution)/shard_map/ppermute | solution.py:20
  386.0 14.2 %collective-permute-start.20 = (f32[2,2,128,128]{3,2,1,0:T(8,128)S(1)}, f32[2,2,128,128]{3,2,1,0:T(8,128)S(1)}, u32[]{:S(2)}, u32[]{:S(2)}) collective-permute-start(f32[2,2,128,128]{3,2,1,0:T(8,128)S(1)} %add.169), channel_id=1, source_target_pairs={{0,128},{8,136},{16,144},{24,152},{32,160},{40,168},{48,176},{56,1... | collective-permute-start | bytes 786440 | tf_op jit(solution)/shard_map/ppermute | solution.py:20
  388.0 26.1 %copy-start.2 = (f32[2,2,128,128]{3,2,1,0:T(8,128)S(1)}, f32[2,2,128,128]{3,2,1,0:T(8,128)}, u32[]{:S(2)}) copy-start(f32[2,2,128,128]{3,2,1,0:T(8,128)} %multiply_subtract_fusion.1.probe_ref) | copy-start | bytes 786436
  400.2 13.8 %collective-permute-start.21 = (f32[2,2,128,128]{3,2,1,0:T(8,128)S(1)}, f32[2,2,128,128]{3,2,1,0:T(8,128)S(1)}, u32[]{:S(2)}, u32[]{:S(2)}) collective-permute-start(f32[2,2,128,128]{3,2,1,0:T(8,128)S(1)} %add.170), channel_id=1, source_target_pairs={{0,256},{8,264},{16,272},{24,280},{32,288},{40,296},{48,304},{56,3... | collective-permute-start | bytes 786440 | tf_op jit(solution)/shard_map/ppermute | solution.py:20

commit v3 on v2

--- a/solution.py
+++ b/solution.py
@@ -158,12 +158,12 @@
     )(patch_cells, mode_values, target, weight.reshape(1, 1), tab)
 
 
-def xor_sum(values, axis):
+def xor_sum(values, axis, steps=None):
     size = lax.axis_size(axis)
-    step = 1
-    while step < size:
+    if steps is None:
+        steps = [1 << bit for bit in range(size.bit_length() - 1)]
+    for step in steps:
         values = values + lax.ppermute(values, axis, [(i, i ^ step) for i in range(size)])
-        step *= 2
     return values
 
 
@@ -178,20 +178,28 @@
     anchor = jnp.zeros((), jnp.int32)
     obj_state = jnp.stack([object_real[:, 0], object_imag[:, 0]])
     parts = 2 * slices
-    modes = probe_modes.shape[0]
+    tile_bits = [1 << bit for bit in range(tile_count.bit_length() - 1)]
+    first_bits = [b for b in tile_bits if b < GRID]
+    second_bits = [b for b in tile_bits if b >= GRID]
     pending = None
     for iteration in range(ITERS + 1):
-        if pending is not None:
-            probe_sum = pending
-            for step in (2, 4, 2 * GRID, 4 * GRID):
-                probe_sum = probe_sum + shifted(probe_sum, "tile", step)
+        if iteration == ITERS:
+            probe_sum = xor_sum(pending, "tile", second_bits)
             probe_modes = (
                 probe_modes - probe_rate / (slot_count * tile_count * group_count) * probe_sum
             )
-        if iteration == ITERS:
             break
+        probe_sum = pending
+        if pending is not None:
+            probe_sum = xor_sum(probe_sum, "tile", second_bits[:1])
         right_part = shifted(obj_state, "tile", -1)
         upper_half = jnp.concatenate([obj_state, right_part], axis=-1)
+        if pending is not None:
+            upper_half, probe_sum = lax.optimization_barrier((upper_half, probe_sum))
+            probe_sum = xor_sum(probe_sum, "tile", second_bits[1:])
+            probe_modes = (
+                probe_modes - probe_rate / (slot_count * tile_count * group_count) * probe_sum
+            )
         lower_half = shifted(upper_half, "tile", -GRID)
         canvas = jnp.concatenate([upper_half, lower_half], axis=-2)
         current_probe = probe_modes
@@ -212,25 +220,30 @@
             grad_canvas = lax.dynamic_update_slice(grad_canvas, current + grad_patch, starts)
             grad_probe = grad_probe + grad_modes
         planes = lambda a: a.reshape(-1, block_side, block_side)
-        probe_planes = planes(grad_probe)
         sent_down = jnp.concatenate(
             [
                 planes(grad_canvas[:, :, block_side:, :block_side]),
                 planes(grad_canvas[:, :, block_side:, block_side:]),
-                probe_planes,
             ]
         )
+        pair = lambda a, b: lax.optimization_barrier((a, b))
+        probe_partial = xor_sum(grad_probe, "scan", [1])
+        sent_down, probe_partial = pair(sent_down, probe_partial)
         came_down = shifted(sent_down, "tile", GRID)
+        probe_partial = xor_sum(probe_partial, "scan", [2])
         own_part = planes(grad_canvas[:, :, :block_side, :block_side]) + came_down[:parts]
-        right_side = planes(grad_canvas[:, :, :block_side, block_side:]) + came_down[parts : 2 * parts]
-        probe_partial = probe_planes + came_down[2 * parts :]
-        sent_left = jnp.concatenate([right_side, probe_partial])
-        came_left = shifted(sent_left, "tile", 1)
-        own_part = own_part + came_left[:parts]
-        probe_partial = probe_partial + came_left[parts:]
-        reduced = xor_sum(jnp.concatenate([own_part, probe_partial]), "scan")
-        grad_total = reduced[:parts].reshape(obj_state.shape)
-        pending = reduced[parts:].reshape(probe_modes.shape)
+        right_side = planes(grad_canvas[:, :, :block_side, block_side:]) + came_down[parts:]
+        right_side, probe_partial = pair(right_side, probe_partial)
+        came_left = shifted(right_side, "tile", 1)
+        probe_partial = xor_sum(probe_partial, "scan", [4])
+        own_part = own_part + came_left
+        for step in (1, 2, 4):
+            own_part, probe_partial = pair(own_part, probe_partial)
+            own_part = xor_sum(own_part, "scan", [step])
+            probe_partial = xor_sum(probe_partial, "tile", [step])
+        grad_total = own_part.reshape(obj_state.shape)
+        own_part, probe_partial = pair(own_part, probe_partial)
+        pending = probe_partial
         obj_state = obj_state - object_rate / (slot_count * group_count) * grad_total
     return (obj_state[0][:, None], obj_state[1][:, None], probe_modes)
 

time: 422 us -> 398 us (0.943); the launches traced: 415 us -> 397 us
  waiting for transfers between devices: 242 us -> 229 us
    ppermute x16 -> x8, waiting for transfers between devices: 179 us -> 45.7 us  [shifted(): lax.ppermute(shard, axis, [(i, (i + by) % size) for i in range(size)])]
    ppermute x6 -> x24, waiting for transfers between devices: 63.3 us -> 184 us  [xor_sum(): lax.ppermute(values, axis, [(i, i ^ step) for i in range(size)])]
    ppermute x16 -> x8, starting transfers between devices: 83.4 us -> 28.1 us  [shifted(): lax.ppermute(shard, axis, [(i, (i + by) % size) for i in range(size)])]
    ppermute x6 -> x24, starting transfers between devices: 28.6 us -> 80.7 us  [xor_sum(): lax.ppermute(values, axis, [(i, i ^ step) for i in range(size)])]
  transfers between devices with their start and end apart: 22 -> 32, of which waited for: 20 -> 23; matrix products, arithmetic and copies ran while one was open for 1% -> 3% of each run, Pallas kernels for 0% -> 0%
where the time goes in v3:
time: 398 us; the launch traced here: 397 us
  waiting for transfers between devices  229 us (58%)
  starting transfers between devices  109 us (27%)
  Pallas kernels  32.7 us (8%)
  local copies, waits for them, and re-layouts  12 us (3%)
  other arithmetic  8.45 us (2%)
  between operations  5.78 us (1%)
    ppermute x24, waiting for transfers between devices, xor_sum(): lax.ppermute(values, axis, [(i, i ^ step) for i in range(size)])  184 us
    ppermute x24, starting transfers between devices, xor_sum(): lax.ppermute(values, axis, [(i, i ^ step) for i in range(size)])  80.7 us
    ppermute x8, waiting for transfers between devices, shifted(): lax.ppermute(shard, axis, [(i, (i + by) % size) for i in range(size)])  45.7 us
    pallas_call x2, Pallas kernels, slot_grad(): pl.pallas_call(slot_kernel, out_shape=(jax.ShapeDtypeStruct(patch_cells.s...  32.7 us
    ppermute x8, starting transfers between devices, shifted(): lax.ppermute(shard, axis, [(i, (i + by) % size) for i in range(size)])  28.1 us
    dynamic_update_slice x2, local copies, waits for them, and re-layouts, local(): lax.dynamic_update_slice(grad_canvas, current + grad_patch, starts)  8.27 us
  transfers between devices with their start and end apart: 32, of which 23 were waited for; matrix products, arithmetic and copies ran while one was open for 3% of the time, Pallas kernels for 0%

profile of v3, /device:TPU:1, one launch (start us, length us, event | category | flops | bytes accessed | tf_op | source)
XLA Modules:
  0.0 397.0 jit_solution(12803563498353414123)
XLA Ops:
  0.7 1.1 pad_maximum_fusion.4
  1.8 14.4 %collective-permute-start = (f32[2,3,128,128]{3,2,1,0:T(8,128)S(1)}, f32[2,3,128,128]{3,2,1,0:T(8,128)S(1)}, u32[]{:S(2)}, u32[]{:S(2)}) collective-permute-start(f32[2,3,128,128]{3,2,1,0:T(8,128)S(1)} %pad_maximum_fusion.4), channel_id=1, source_target_pairs={{0,504},{8,0},{16,8},{24,16},{32,24},{40,32},{48,40},{56,48},{64,5... | collective-permute-start | bytes 1179656 | tf_op jit(solution)/shard_map/ppermute | solution.py:20
  16.2 7.8 %collective-permute-done = f32[2,3,128,128]{3,2,1,0:T(8,128)S(1)} collective-permute-done((f32[2,3,128,128]{3,2,1,0:T(8,128)S(1)}, f32[2,3,128,128]{3,2,1,0:T(8,128)S(1)}, u32[]{:S(2)}, u32[]{:S(2)}) %collective-permute-start) | collective-permute-done | bytes 393248 | tf_op jit(solution)/shard_map/ppermute | solution.py:20
  23.9 1.1 pad_maximum_fusion
  25.0 2.2 collective-permute-start.1
  33.7 10.7 %collective-permute-done.1 = f32[2,3,128,256]{3,2,1,0:T(8,128)S(1)} collective-permute-done((f32[2,3,128,256]{3,2,1,0:T(8,128)S(1)}, f32[2,3,128,256]{3,2,1,0:T(8,128)S(1)}, u32[]{:S(2)}, u32[]{:S(2)}) %collective-permute-start.1) | collective-permute-done | bytes 786464 | tf_op jit(solution)/shard_map/ppermute | solution.py:20
  44.4 1.1 fusion.3.cells_ref
  45.5 16.4 %shard_map.85 = (f32[2,3,128,128]{3,2,1,0:T(8,128)}, f32[2,2,128,128]{3,2,1,0:T(8,128)}) custom-call(f32[2,3,128,128]{3,2,1,0:T(8,128)} %fusion.3.cells_ref, f32[2,2,128,128]{3,2,1,0:T(8,128)} %probe_ref.1, f32[128,128]{1,0:T(8,128)} %bitcast.45, f32[1,1]{1,0:T(1,128)} %bitcast.5.weight_ref, f32[4,128,128]{2,1,0:T(8,128)} %pad_maximum_fusion.5.tab_ref), custom_call_target="tpu_custom_call" | custom-call | flops 1342177280 | bytes 1441792 | tf_op jit(solution)/shard_map/pallas_call | solution.py:147
  61.9 4.7 %collective-permute-start.2 = (f32[2,2,128,128]{3,2,1,0:T(8,128)}, f32[2,2,128,128]{3,2,1,0:T(8,128)S(1)}, u32[]{:S(2)}, u32[]{:S(2)}) collective-permute-start(f32[2,2,128,128]{3,2,1,0:T(8,128)} %get-tuple-element.32), channel_id=1, source_target_pairs={{0,1},{1,0},{2,3},{3,2},{4,5},{5,4},{6,7},{7,6},{8,9},{9,8},{10,11... | collective-permute-start | bytes 786440 | tf_op jit(solution)/shard_map/ppermute | solution.py:166
  66.7 4.1 %dynamic_update_slice.6 = f32[2,3,256,256]{3,2,1,0:T(8,128)S(1)} dynamic-update-slice(f32[2,3,256,256]{3,2,1,0:T(8,128)S(1)} %broadcast.209.clone, f32[2,3,128,128]{3,2,1,0:T(8,128)S(1)} %copy-done.4, s32[]{:T(128)} %constant.13.clone.1, s32[]{:T(128)} %constant.13.clone.1, s32[]{:T(128)S(6)} %select_n.46, s32[]{:T(128)S(6)} %select_n.47) | dynamic-update-slice | bytes 786436 | tf_op jit(solution)/shard_map/dynamic_update_slice | solution.py:220
  71.1 0.9 copy-done.6
  72.0 1.9 collective-permute-start.3
  74.0 3.3 collective-permute-start.4
  77.3 6.1 %collective-permute-done.4 = f32[2,2,128,128]{3,2,1,0:T(8,128)S(1)} collective-permute-done((f32[2,2,128,128]{3,2,1,0:T(8,128)S(1)}, f32[2,2,128,128]{3,2,1,0:T(8,128)S(1)}, u32[]{:S(2)}, u32[]{:S(2)}) %collective-permute-start.4) | collective-permute-done | bytes 262176 | tf_op jit(solution)/shard_map/ppermute | solution.py:166
  83.5 10.5 %collective-permute-done.3 = f32[12,128,128]{2,1,0:T(8,128)S(1)} collective-permute-done((f32[12,128,128]{2,1,0:T(8,128)S(1)}, f32[12,128,128]{2,1,0:T(8,128)S(1)}, u32[]{:S(2)}, u32[]{:S(2)}) %collective-permute-start.3) | collective-permute-done | bytes 786464 | tf_op jit(solution)/shard_map/ppermute | solution.py:20
  94.0 1.9 collective-permute-start.5
  95.9 5.6 %collective-permute-start.6 = (f32[2,2,128,128]{3,2,1,0:T(8,128)S(1)}, f32[2,2,128,128]{3,2,1,0:T(8,128)S(1)}, u32[]{:S(2)}, u32[]{:S(2)}) collective-permute-start(f32[2,2,128,128]{3,2,1,0:T(8,128)S(1)} %add.169), channel_id=1, source_target_pairs={{0,4},{1,5},{2,6},{3,7},{4,0},{5,1},{6,2},{7,3},{8,12},{9,13},{10,... | collective-permute-start | bytes 786440 | tf_op jit(solution)/shard_map/ppermute | solution.py:166
  101.6 6.0 %collective-permute-done.6 = f32[2,2,128,128]{3,2,1,0:T(8,128)S(1)} collective-permute-done((f32[2,2,128,128]{3,2,1,0:T(8,128)S(1)}, f32[2,2,128,128]{3,2,1,0:T(8,128)S(1)}, u32[]{:S(2)}, u32[]{:S(2)}) %collective-permute-start.6) | collective-permute-done | bytes 262176 | tf_op jit(solution)/shard_map/ppermute | solution.py:166
  107.6 3.6 collective-permute-done.5
  111.3 3.0 collective-permute-start.7
  114.4 1.9 collective-permute-start.8
  116.3 7.9 %collective-permute-done.8 = f32[2,2,128,128]{3,2,1,0:T(8,128)S(1)} collective-permute-done((f32[2,2,128,128]{3,2,1,0:T(8,128)S(1)}, f32[2,2,128,128]{3,2,1,0:T(8,128)S(1)}, u32[]{:S(2)}, u32[]{:S(2)}) %collective-permute-start.8) | collective-permute-done | bytes 262176 | tf_op jit(solution)/shard_map/ppermute | solution.py:166
  124.3 2.6 collective-permute-start.9
  126.9 1.9 collective-permute-start.10
  128.8 14.6 %collective-permute-done.10 = f32[2,2,128,128]{3,2,1,0:T(8,128)S(1)} collective-permute-done((f32[2,2,128,128]{3,2,1,0:T(8,128)S(1)}, f32[2,2,128,128]{3,2,1,0:T(8,128)S(1)}, u32[]{:S(2)}, u32[]{:S(2)}) %collective-permute-start.10) | collective-permute-done | bytes 262176 | tf_op jit(solution)/shard_map/ppermute | solution.py:166
  143.5 4.7 %collective-permute-start.11 = (f32[6,128,128]{2,1,0:T(8,128)S(1)}, f32[6,128,128]{2,1,0:T(8,128)S(1)}, u32[]{:S(2)}, u32[]{:S(2)}) collective-permute-start(f32[6,128,128]{2,1,0:T(8,128)S(1)} %add.174), channel_id=1, source_target_pairs={{0,4},{1,5},{2,6},{3,7},{4,0},{5,1},{6,2},{7,3},{8,12},{9,13},{10,... | collective-permute-start | bytes 1179656 | tf_op jit(solution)/shard_map/ppermute | solution.py:166
  148.3 3.8 collective-permute-start.13
  152.1 5.0 %collective-permute-done.11 = f32[6,128,128]{2,1,0:T(8,128)S(1)} collective-permute-done((f32[6,128,128]{2,1,0:T(8,128)S(1)}, f32[6,128,128]{2,1,0:T(8,128)S(1)}, u32[]{:S(2)}, u32[]{:S(2)}) %collective-permute-start.11) | collective-permute-done | bytes 393248 | tf_op jit(solution)/shard_map/ppermute | solution.py:166
  157.2 1.9 collective-permute-start.12
  159.2 7.6 %collective-permute-done.13 = f32[2,2,128,128]{3,2,1,0:T(8,128)S(1)} collective-permute-done((f32[2,2,128,128]{3,2,1,0:T(8,128)S(1)}, f32[2,2,128,128]{3,2,1,0:T(8,128)S(1)}, u32[]{:S(2)}, u32[]{:S(2)}) %collective-permute-start.13) | collective-permute-done | bytes 262176 | tf_op jit(solution)/shard_map/ppermute | solution.py:166
  166.8 2.1 collective-permute-start.14
  168.9 7.3 %collective-permute-done.14 = f32[2,2,128,128]{3,2,1,0:T(8,128)S(1)} collective-permute-done((f32[2,2,128,128]{3,2,1,0:T(8,128)S(1)}, f32[2,2,128,128]{3,2,1,0:T(8,128)S(1)}, u32[]{:S(2)}, u32[]{:S(2)}) %collective-permute-start.14) | collective-permute-done | bytes 262176 | tf_op jit(solution)/shard_map/ppermute | solution.py:166
  176.3 1.9 collective-permute-start.15
  178.2 3.4 collective-permute-start.16
  181.7 32.2 %collective-permute-done.16 = f32[2,2,128,128]{3,2,1,0:T(8,128)S(1)} collective-permute-done((f32[2,2,128,128]{3,2,1,0:T(8,128)S(1)}, f32[2,2,128,128]{3,2,1,0:T(8,128)S(1)}, u32[]{:S(2)}, u32[]{:S(2)}) %collective-permute-start.16) | collective-permute-done | bytes 262176 | tf_op jit(solution)/shard_map/ppermute | solution.py:166
  213.9 1.9 collective-permute-start.17
  215.8 9.1 %collective-permute-done.17 = f32[2,2,128,128]{3,2,1,0:T(8,128)S(1)} collective-permute-done((f32[2,2,128,128]{3,2,1,0:T(8,128)S(1)}, f32[2,2,128,128]{3,2,1,0:T(8,128)S(1)}, u32[]{:S(2)}, u32[]{:S(2)}) %collective-permute-start.17) | collective-permute-done | bytes 262176 | tf_op jit(solution)/shard_map/ppermute | solution.py:166
  225.7 1.0 fusion.cells_ref
  226.7 16.4 %shard_map.86 = (f32[2,3,128,128]{3,2,1,0:T(8,128)}, f32[2,2,128,128]{3,2,1,0:T(8,128)}) custom-call(f32[2,3,128,128]{3,2,1,0:T(8,128)} %fusion.cells_ref, f32[2,2,128,128]{3,2,1,0:T(8,128)} %multiply_subtract_fusion.1.probe_ref, f32[128,128]{1,0:T(8,128)} %bitcast.46, f32[1,1]{1,0:T(1,128)} %bitcast.5.weight_ref, f32[4,128,128]{2,1,0:T(8,128)} %pad_maximum_fusion.5.tab_ref), custom_call_target="tpu_custom_call" | custom-call | flops 1342177280 | bytes 1441792 | tf_op jit(solution)/shard_map/pallas_call | solution.py:147
  243.1 10.5 %collective-permute-start.18 = (f32[2,2,128,128]{3,2,1,0:T(8,128)}, f32[2,2,128,128]{3,2,1,0:T(8,128)S(1)}, u32[]{:S(2)}, u32[]{:S(2)}) collective-permute-start(f32[2,2,128,128]{3,2,1,0:T(8,128)} %get-tuple-element.47), channel_id=1, source_target_pairs={{0,1},{1,0},{2,3},{3,2},{4,5},{5,4},{6,7},{7,6},{8,9},{9,8},{10,11... | collective-permute-start | bytes 786440 | tf_op jit(solution)/shard_map/ppermute | solution.py:166
  253.8 4.1 %dynamic_update_slice.7 = f32[2,3,256,256]{3,2,1,0:T(8,128)S(1)} dynamic-update-slice(f32[2,3,256,256]{3,2,1,0:T(8,128)S(1)} %broadcast.209, f32[2,3,128,128]{3,2,1,0:T(8,128)S(1)} %copy-done.3, s32[]{:T(128)} %constant.13.clone.1, s32[]{:T(128)} %constant.13.clone.1, s32[]{:T(128)S(6)} %select_n.46, s32[]{:T(128)S(6)} %select_n.47) | dynamic-update-slice | bytes 786436 | tf_op jit(solution)/shard_map/dynamic_update_slice | solution.py:220
  259.1 1.9 collective-permute-start.19
  261.0 1.9 collective-permute-start.20
  262.9 7.5 %collective-permute-done.20 = f32[2,2,128,128]{3,2,1,0:T(8,128)S(1)} collective-permute-done((f32[2,2,128,128]{3,2,1,0:T(8,128)S(1)}, f32[2,2,128,128]{3,2,1,0:T(8,128)S(1)}, u32[]{:S(2)}, u32[]{:S(2)}) %collective-permute-start.20) | collective-permute-done | bytes 262176 | tf_op jit(solution)/shard_map/ppermute | solution.py:166
  270.5 10.5 %collective-permute-done.19 = f32[12,128,128]{2,1,0:T(8,128)S(1)} collective-permute-done((f32[12,128,128]{2,1,0:T(8,128)S(1)}, f32[12,128,128]{2,1,0:T(8,128)S(1)}, u32[]{:S(2)}, u32[]{:S(2)}) %collective-permute-start.19) | collective-permute-done | bytes 786464 | tf_op jit(solution)/shard_map/ppermute | solution.py:20
  281.0 1.9 collective-permute-start.21
  283.0 3.0 collective-permute-start.22
  285.9 7.1 %collective-permute-done.22 = f32[2,2,128,128]{3,2,1,0:T(8,128)S(1)} collective-permute-done((f32[2,2,128,128]{3,2,1,0:T(8,128)S(1)}, f32[2,2,128,128]{3,2,1,0:T(8,128)S(1)}, u32[]{:S(2)}, u32[]{:S(2)}) %collective-permute-start.22) | collective-permute-done | bytes 262176 | tf_op jit(solution)/shard_map/ppermute | solution.py:166
  293.0 2.7 collective-permute-done.21
  295.8 4.0 %collective-permute-start.23 = (f32[6,128,128]{2,1,0:T(8,128)S(1)}, f32[6,128,128]{2,1,0:T(8,128)S(1)}, u32[]{:S(2)}, u32[]{:S(2)}) collective-permute-start(f32[6,128,128]{2,1,0:T(8,128)S(1)} %fusion.4), channel_id=1, source_target_pairs={{0,1},{1,0},{2,3},{3,2},{4,5},{5,4},{6,7},{7,6},{8,9},{9,8},{10,11... | collective-permute-start | bytes 1179656 | tf_op jit(solution)/shard_map/ppermute | solution.py:166
  299.8 1.9 collective-permute-start.24
  301.7 7.9 %collective-permute-done.24 = f32[2,2,128,128]{3,2,1,0:T(8,128)S(1)} collective-permute-done((f32[2,2,128,128]{3,2,1,0:T(8,128)S(1)}, f32[2,2,128,128]{3,2,1,0:T(8,128)S(1)}, u32[]{:S(2)}, u32[]{:S(2)}) %collective-permute-start.24) | collective-permute-done | bytes 262176 | tf_op jit(solution)/shard_map/ppermute | solution.py:166
  309.7 2.1 collective-permute-start.25
  311.8 1.9 collective-permute-start.26
  313.8 14.6 %collective-permute-done.26 = f32[2,2,128,128]{3,2,1,0:T(8,128)S(1)} collective-permute-done((f32[2,2,128,128]{3,2,1,0:T(8,128)S(1)}, f32[2,2,128,128]{3,2,1,0:T(8,128)S(1)}, u32[]{:S(2)}, u32[]{:S(2)}) %collective-permute-start.26) | collective-permute-done | bytes 262176 | tf_op jit(solution)/shard_map/ppermute | solution.py:166
  328.5 3.4 collective-permute-start.27
  331.9 3.9 collective-permute-start.28
  335.8 14.6 %collective-permute-done.28 = f32[2,2,128,128]{3,2,1,0:T(8,128)S(1)} collective-permute-done((f32[2,2,128,128]{3,2,1,0:T(8,128)S(1)}, f32[2,2,128,128]{3,2,1,0:T(8,128)S(1)}, u32[]{:S(2)}, u32[]{:S(2)}) %collective-permute-start.28) | collective-permute-done | bytes 262176 | tf_op jit(solution)/shard_map/ppermute | solution.py:166
  350.6 1.9 collective-permute-start.29
  352.5 7.3 %collective-permute-done.29 = f32[2,2,128,128]{3,2,1,0:T(8,128)S(1)} collective-permute-done((f32[2,2,128,128]{3,2,1,0:T(8,128)S(1)}, f32[2,2,128,128]{3,2,1,0:T(8,128)S(1)}, u32[]{:S(2)}, u32[]{:S(2)}) %collective-permute-start.29) | collective-permute-done | bytes 262176 | tf_op jit(solution)/shard_map/ppermute | solution.py:166
  359.9 2.1 collective-permute-start.30
  361.9 14.7 %collective-permute-done.30 = f32[2,2,128,128]{3,2,1,0:T(8,128)S(1)} collective-permute-done((f32[2,2,128,128]{3,2,1,0:T(8,128)S(1)}, f32[2,2,128,128]{3,2,1,0:T(8,128)S(1)}, u32[]{:S(2)}, u32[]{:S(2)}) %collective-permute-start.30) | collective-permute-done | bytes 262176 | tf_op jit(solution)/shard_map/ppermute | solution.py:166
  376.6 5.0 %collective-permute-start.31 = (f32[2,2,128,128]{3,2,1,0:T(8,128)S(1)}, f32[2,2,128,128]{3,2,1,0:T(8,128)S(1)}, u32[]{:S(2)}, u32[]{:S(2)}) collective-permute-start(f32[2,2,128,128]{3,2,1,0:T(8,128)S(1)} %add.194), channel_id=1, source_target_pairs={{0,256},{8,264},{16,272},{24,280},{32,288},{40,296},{48,304},{56,3... | collective-permute-start | bytes 786440 | tf_op jit(solution)/shard_map/ppermute | solution.py:166
  382.5 13.8 %collective-permute-done.31 = f32[2,2,128,128]{3,2,1,0:T(8,128)S(1)} collective-permute-done((f32[2,2,128,128]{3,2,1,0:T(8,128)S(1)}, f32[2,2,128,128]{3,2,1,0:T(8,128)S(1)}, u32[]{:S(2)}, u32[]{:S(2)}) %collective-permute-start.31) | collective-permute-done | bytes 262176 | tf_op jit(solution)/shard_map/ppermute | solution.py:166
  (69 shorter events, 7.0 us)
Async XLA Ops:
  0.6 26.6 %copy-start.8 = (s32[1,1,1,2]{3,2,1,0:T(1,128)S(1)}, s32[1,1,1,2]{3,2,1,0:T(1,128)}, u32[]{:S(2)}) copy-start(s32[1,1,1,2]{3,2,1,0:T(1,128)} %param.10) | copy-start | bytes 28
  0.6 43.8 %copy-start = (f32[3,1,128,128]{3,2,1,0:T(8,128)S(1)}, f32[3,1,128,128]{3,2,1,0:T(8,128)}, u32[]{:S(2)}) copy-start(f32[3,1,128,128]{3,2,1,0:T(8,128)} %param.6) | copy-start | bytes 589828
  0.7 43.7 %copy-start.1 = (f32[3,1,128,128]{3,2,1,0:T(8,128)S(1)}, f32[3,1,128,128]{3,2,1,0:T(8,128)}, u32[]{:S(2)}) copy-start(f32[3,1,128,128]{3,2,1,0:T(8,128)} %param.7) | copy-start | bytes 589828
  1.8 22.2 %collective-permute-start = (f32[2,3,128,128]{3,2,1,0:T(8,128)S(1)}, f32[2,3,128,128]{3,2,1,0:T(8,128)S(1)}, u32[]{:S(2)}, u32[]{:S(2)}) collective-permute-start(f32[2,3,128,128]{3,2,1,0:T(8,128)S(1)} %pad_maximum_fusion.4), channel_id=1, source_target_pairs={{0,504},{8,0},{16,8},{24,16},{32,24},{40,32},{48,40},{56,48},{64,5... | collective-permute-start | bytes 1179656 | tf_op jit(solution)/shard_map/ppermute | solution.py:20
  25.0 19.4 %collective-permute-start.1 = (f32[2,3,128,256]{3,2,1,0:T(8,128)S(1)}, f32[2,3,128,256]{3,2,1,0:T(8,128)S(1)}, u32[]{:S(2)}, u32[]{:S(2)}) collective-permute-start(f32[2,3,128,256]{3,2,1,0:T(8,128)S(1)} %pad_maximum_fusion), channel_id=1, source_target_pairs={{0,448},{8,456},{16,464},{24,472},{32,480},{40,488},{48,496},{56,5... | collective-permute-start | bytes 2359304 | tf_op jit(solution)/shard_map/ppermute | solution.py:20
  61.9 4.8 %copy-start.4 = (f32[2,3,128,128]{3,2,1,0:T(8,128)S(1)}, f32[2,3,128,128]{3,2,1,0:T(8,128)}, u32[]{:S(2)}) copy-start(f32[2,3,128,128]{3,2,1,0:T(8,128)} %get-tuple-element.31) | copy-start | bytes 1179652
  61.9 9.2 %collective-permute-start.2 = (f32[2,2,128,128]{3,2,1,0:T(8,128)}, f32[2,2,128,128]{3,2,1,0:T(8,128)S(1)}, u32[]{:S(2)}, u32[]{:S(2)}) collective-permute-start(f32[2,2,128,128]{3,2,1,0:T(8,128)} %get-tuple-element.32), channel_id=1, source_target_pairs={{0,1},{1,0},{2,3},{3,2},{4,5},{5,4},{6,7},{7,6},{8,9},{9,8},{10,11... | collective-permute-start | bytes 786440 | tf_op jit(solution)/shard_map/ppermute | solution.py:166
  71.0 1.0 copy-start.6
  72.0 21.9 %collective-permute-start.3 = (f32[12,128,128]{2,1,0:T(8,128)S(1)}, f32[12,128,128]{2,1,0:T(8,128)S(1)}, u32[]{:S(2)}, u32[]{:S(2)}) collective-permute-start(f32[12,128,128]{2,1,0:T(8,128)S(1)} %pad_maximum_fusion.1), channel_id=1, source_target_pairs={{0,64},{8,72},{16,80},{24,88},{32,96},{40,104},{48,112},{56,120},{... | collective-permute-start | bytes 2359304 | tf_op jit(solution)/shard_map/ppermute | solution.py:20
  74.0 9.5 %collective-permute-start.4 = (f32[2,2,128,128]{3,2,1,0:T(8,128)S(1)}, f32[2,2,128,128]{3,2,1,0:T(8,128)S(1)}, u32[]{:S(2)}, u32[]{:S(2)}) collective-permute-start(f32[2,2,128,128]{3,2,1,0:T(8,128)S(1)} %add.166), channel_id=1, source_target_pairs={{0,2},{1,3},{2,0},{3,1},{4,6},{5,7},{6,4},{7,5},{8,10},{9,11},{10,... | collective-permute-start | bytes 786440 | tf_op jit(solution)/shard_map/ppermute | solution.py:166
  94.0 17.3 %collective-permute-start.5 = (f32[6,128,128]{2,1,0:T(8,128)S(1)}, f32[6,128,128]{2,1,0:T(8,128)S(1)}, u32[]{:S(2)}, u32[]{:S(2)}) collective-permute-start(f32[6,128,128]{2,1,0:T(8,128)S(1)} %slice_add_fusion.2), channel_id=1, source_target_pairs={{0,8},{8,16},{16,24},{24,32},{32,40},{40,48},{48,56},{56,64},{64,7... | collective-permute-start | bytes 1179656 | tf_op jit(solution)/shard_map/ppermute | solution.py:20
  95.9 11.7 %collective-permute-start.6 = (f32[2,2,128,128]{3,2,1,0:T(8,128)S(1)}, f32[2,2,128,128]{3,2,1,0:T(8,128)S(1)}, u32[]{:S(2)}, u32[]{:S(2)}) collective-permute-start(f32[2,2,128,128]{3,2,1,0:T(8,128)S(1)} %add.169), channel_id=1, source_target_pairs={{0,4},{1,5},{2,6},{3,7},{4,0},{5,1},{6,2},{7,3},{8,12},{9,13},{10,... | collective-permute-start | bytes 786440 | tf_op jit(solution)/shard_map/ppermute | solution.py:166
  111.3 12.9 %collective-permute-start.7 = (f32[6,128,128]{2,1,0:T(8,128)S(1)}, f32[6,128,128]{2,1,0:T(8,128)S(1)}, u32[]{:S(2)}, u32[]{:S(2)}) collective-permute-start(f32[6,128,128]{2,1,0:T(8,128)S(1)} %fusion.5), channel_id=1, source_target_pairs={{0,1},{1,0},{2,3},{3,2},{4,5},{5,4},{6,7},{7,6},{8,9},{9,8},{10,11... | collective-permute-start | bytes 1179656 | tf_op jit(solution)/shard_map/ppermute | solution.py:166
  114.4 9.8 %collective-permute-start.8 = (f32[2,2,128,128]{3,2,1,0:T(8,128)S(1)}, f32[2,2,128,128]{3,2,1,0:T(8,128)S(1)}, u32[]{:S(2)}, u32[]{:S(2)}) collective-permute-start(f32[2,2,128,128]{3,2,1,0:T(8,128)S(1)} %add.171), channel_id=1, source_target_pairs={{0,8},{8,0},{16,24},{24,16},{32,40},{40,32},{48,56},{56,48},{64,72... | collective-permute-start | bytes 786440 | tf_op jit(solution)/shard_map/ppermute | solution.py:166
  124.3 19.2 %collective-permute-start.9 = (f32[6,128,128]{2,1,0:T(8,128)S(1)}, f32[6,128,128]{2,1,0:T(8,128)S(1)}, u32[]{:S(2)}, u32[]{:S(2)}) collective-permute-start(f32[6,128,128]{2,1,0:T(8,128)S(1)} %add.172), channel_id=1, source_target_pairs={{0,2},{1,3},{2,0},{3,1},{4,6},{5,7},{6,4},{7,5},{8,10},{9,11},{10,... | collective-permute-start | bytes 1179656 | tf_op jit(solution)/shard_map/ppermute | solution.py:166
  126.9 16.6 %collective-permute-start.10 = (f32[2,2,128,128]{3,2,1,0:T(8,128)S(1)}, f32[2,2,128,128]{3,2,1,0:T(8,128)S(1)}, u32[]{:S(2)}, u32[]{:S(2)}) collective-permute-start(f32[2,2,128,128]{3,2,1,0:T(8,128)S(1)} %add.173), channel_id=1, source_target_pairs={{0,16},{8,24},{16,0},{24,8},{32,48},{40,56},{48,32},{56,40},{64,80... | collective-permute-start | bytes 786440 | tf_op jit(solution)/shard_map/ppermute | solution.py:166
  143.5 13.6 %collective-permute-start.11 = (f32[6,128,128]{2,1,0:T(8,128)S(1)}, f32[6,128,128]{2,1,0:T(8,128)S(1)}, u32[]{:S(2)}, u32[]{:S(2)}) collective-permute-start(f32[6,128,128]{2,1,0:T(8,128)S(1)} %add.174), channel_id=1, source_target_pairs={{0,4},{1,5},{2,6},{3,7},{4,0},{5,1},{6,2},{7,3},{8,12},{9,13},{10,... | collective-permute-start | bytes 1179656 | tf_op jit(solution)/shard_map/ppermute | solution.py:166
  148.3 18.4 %collective-permute-start.13 = (f32[2,2,128,128]{3,2,1,0:T(8,128)S(1)}, f32[2,2,128,128]{3,2,1,0:T(8,128)S(1)}, u32[]{:S(2)}, u32[]{:S(2)}) collective-permute-start(f32[2,2,128,128]{3,2,1,0:T(8,128)S(1)} %add.175), channel_id=1, source_target_pairs={{0,32},{8,40},{16,48},{24,56},{32,0},{40,8},{48,16},{56,24},{64,96... | collective-permute-start | bytes 786440 | tf_op jit(solution)/shard_map/ppermute | solution.py:166
  157.2 19.0 %collective-permute-start.12 = (f32[2,3,128,128]{3,2,1,0:T(8,128)S(1)}, f32[2,3,128,128]{3,2,1,0:T(8,128)S(1)}, u32[]{:S(2)}, u32[]{:S(2)}) collective-permute-start(f32[2,3,128,128]{3,2,1,0:T(8,128)S(1)} %fusion.16), channel_id=1, source_target_pairs={{0,504},{8,0},{16,8},{24,16},{32,24},{40,32},{48,40},{56,48},{64,5... | collective-permute-start | bytes 1179656 | tf_op jit(solution)/shard_map/ppermute | solution.py:20
  166.8 58.2 %copy-start.7 = (f32[2,2,128,128]{3,2,1,0:T(8,128)S(1)}, f32[2,2,128,128]{3,2,1,0:T(8,128)}, u32[]{:S(2)}) copy-start(f32[2,2,128,128]{3,2,1,0:T(8,128)} %probe_ref.1) | copy-start | bytes 786436
  166.8 9.4 %collective-permute-start.14 = (f32[2,2,128,128]{3,2,1,0:T(8,128)S(1)}, f32[2,2,128,128]{3,2,1,0:T(8,128)S(1)}, u32[]{:S(2)}, u32[]{:S(2)}) collective-permute-start(f32[2,2,128,128]{3,2,1,0:T(8,128)S(1)} %add.177), channel_id=1, source_target_pairs={{0,64},{8,72},{16,80},{24,88},{32,96},{40,104},{48,112},{56,120},{... | collective-permute-start | bytes 786440 | tf_op jit(solution)/shard_map/ppermute | solution.py:166
  176.3 49.4 %collective-permute-start.15 = (f32[2,3,128,256]{3,2,1,0:T(8,128)S(1)}, f32[2,3,128,256]{3,2,1,0:T(8,128)S(1)}, u32[]{:S(2)}, u32[]{:S(2)}) collective-permute-start(f32[2,3,128,256]{3,2,1,0:T(8,128)S(1)} %pad_maximum_fusion.2), channel_id=1, source_target_pairs={{0,448},{8,456},{16,464},{24,472},{32,480},{40,488},{48,496},{56,5... | collective-permute-start | bytes 2359304 | tf_op jit(solution)/shard_map/ppermute | solution.py:20
  178.2 35.6 %collective-permute-start.16 = (f32[2,2,128,128]{3,2,1,0:T(8,128)S(1)}, f32[2,2,128,128]{3,2,1,0:T(8,128)S(1)}, u32[]{:S(2)}, u32[]{:S(2)}) collective-permute-start(f32[2,2,128,128]{3,2,1,0:T(8,128)S(1)} %add.178), channel_id=1, source_target_pairs={{0,128},{8,136},{16,144},{24,152},{32,160},{40,168},{48,176},{56,1... | collective-permute-start | bytes 786440 | tf_op jit(solution)/shard_map/ppermute | solution.py:166
  213.9 11.1 %collective-permute-start.17 = (f32[2,2,128,128]{3,2,1,0:T(8,128)S(1)}, f32[2,2,128,128]{3,2,1,0:T(8,128)S(1)}, u32[]{:S(2)}, u32[]{:S(2)}) collective-permute-start(f32[2,2,128,128]{3,2,1,0:T(8,128)S(1)} %add.179), channel_id=1, source_target_pairs={{0,256},{8,264},{16,272},{24,280},{32,288},{40,296},{48,304},{56,3... | collective-permute-start | bytes 786440 | tf_op jit(solution)/shard_map/ppermute | solution.py:166
  243.1 10.7 %copy-start.3 = (f32[2,3,128,128]{3,2,1,0:T(8,128)S(1)}, f32[2,3,128,128]{3,2,1,0:T(8,128)}, u32[]{:S(2)}) copy-start(f32[2,3,128,128]{3,2,1,0:T(8,128)} %get-tuple-element.46) | copy-start | bytes 1179652
  243.1 15.1 %collective-permute-start.18 = (f32[2,2,128,128]{3,2,1,0:T(8,128)}, f32[2,2,128,128]{3,2,1,0:T(8,128)S(1)}, u32[]{:S(2)}, u32[]{:S(2)}) collective-permute-start(f32[2,2,128,128]{3,2,1,0:T(8,128)} %get-tuple-element.47), channel_id=1, source_target_pairs={{0,1},{1,0},{2,3},{3,2},{4,5},{5,4},{6,7},{7,6},{8,9},{9,8},{10,11... | collective-permute-start | bytes 786440 | tf_op jit(solution)/shard_map/ppermute | solution.py:166
  258.1 1.0 copy-start.5
  259.1 21.9 %collective-permute-start.19 = (f32[12,128,128]{2,1,0:T(8,128)S(1)}, f32[12,128,128]{2,1,0:T(8,128)S(1)}, u32[]{:S(2)}, u32[]{:S(2)}) collective-permute-start(f32[12,128,128]{2,1,0:T(8,128)S(1)} %pad_maximum_fusion.3), channel_id=1, source_target_pairs={{0,64},{8,72},{16,80},{24,88},{32,96},{40,104},{48,112},{56,120},{... | collective-permute-start | bytes 2359304 | tf_op jit(solution)/shard_map/ppermute | solution.py:20
  261.0 9.5 %collective-permute-start.20 = (f32[2,2,128,128]{3,2,1,0:T(8,128)S(1)}, f32[2,2,128,128]{3,2,1,0:T(8,128)S(1)}, u32[]{:S(2)}, u32[]{:S(2)}) collective-permute-start(f32[2,2,128,128]{3,2,1,0:T(8,128)S(1)} %add.181), channel_id=1, source_target_pairs={{0,2},{1,3},{2,0},{3,1},{4,6},{5,7},{6,4},{7,5},{8,10},{9,11},{10,... | collective-permute-start | bytes 786440 | tf_op jit(solution)/shard_map/ppermute | solution.py:166
  281.0 14.7 %collective-permute-start.21 = (f32[6,128,128]{2,1,0:T(8,128)S(1)}, f32[6,128,128]{2,1,0:T(8,128)S(1)}, u32[]{:S(2)}, u32[]{:S(2)}) collective-permute-start(f32[6,128,128]{2,1,0:T(8,128)S(1)} %slice_add_fusion), channel_id=1, source_target_pairs={{0,8},{8,16},{16,24},{24,32},{32,40},{40,48},{48,56},{56,64},{64,7... | collective-permute-start | bytes 1179656 | tf_op jit(solution)/shard_map/ppermute | solution.py:20
  283.0 10.0 %collective-permute-start.22 = (f32[2,2,128,128]{3,2,1,0:T(8,128)S(1)}, f32[2,2,128,128]{3,2,1,0:T(8,128)S(1)}, u32[]{:S(2)}, u32[]{:S(2)}) collective-permute-start(f32[2,2,128,128]{3,2,1,0:T(8,128)S(1)} %add.184), channel_id=1, source_target_pairs={{0,4},{1,5},{2,6},{3,7},{4,0},{5,1},{6,2},{7,3},{8,12},{9,13},{10,... | collective-permute-start | bytes 786440 | tf_op jit(solution)/shard_map/ppermute | solution.py:166
  295.8 13.9 %collective-permute-start.23 = (f32[6,128,128]{2,1,0:T(8,128)S(1)}, f32[6,128,128]{2,1,0:T(8,128)S(1)}, u32[]{:S(2)}, u32[]{:S(2)}) collective-permute-start(f32[6,128,128]{2,1,0:T(8,128)S(1)} %fusion.4), channel_id=1, source_target_pairs={{0,1},{1,0},{2,3},{3,2},{4,5},{5,4},{6,7},{7,6},{8,9},{9,8},{10,11... | collective-permute-start | bytes 1179656 | tf_op jit(solution)/shard_map/ppermute | solution.py:166
  299.8 9.8 %collective-permute-start.24 = (f32[2,2,128,128]{3,2,1,0:T(8,128)S(1)}, f32[2,2,128,128]{3,2,1,0:T(8,128)S(1)}, u32[]{:S(2)}, u32[]{:S(2)}) collective-permute-start(f32[2,2,128,128]{3,2,1,0:T(8,128)S(1)} %add.186), channel_id=1, source_target_pairs={{0,8},{8,0},{16,24},{24,16},{32,40},{40,32},{48,56},{56,48},{64,72... | collective-permute-start | bytes 786440 | tf_op jit(solution)/shard_map/ppermute | solution.py:166
  309.7 18.7 %collective-permute-start.25 = (f32[6,128,128]{2,1,0:T(8,128)S(1)}, f32[6,128,128]{2,1,0:T(8,128)S(1)}, u32[]{:S(2)}, u32[]{:S(2)}) collective-permute-start(f32[6,128,128]{2,1,0:T(8,128)S(1)} %add.187), channel_id=1, source_target_pairs={{0,2},{1,3},{2,0},{3,1},{4,6},{5,7},{6,4},{7,5},{8,10},{9,11},{10,... | collective-permute-start | bytes 1179656 | tf_op jit(solution)/shard_map/ppermute | solution.py:166
  311.8 16.6 %collective-permute-start.26 = (f32[2,2,128,128]{3,2,1,0:T(8,128)S(1)}, f32[2,2,128,128]{3,2,1,0:T(8,128)S(1)}, u32[]{:S(2)}, u32[]{:S(2)}) collective-permute-start(f32[2,2,128,128]{3,2,1,0:T(8,128)S(1)} %add.188), channel_id=1, source_target_pairs={{0,16},{8,24},{16,0},{24,8},{32,48},{40,56},{48,32},{56,40},{64,80... | collective-permute-start | bytes 786440 | tf_op jit(solution)/shard_map/ppermute | solution.py:166
  328.5 22.0 %collective-permute-start.27 = (f32[6,128,128]{2,1,0:T(8,128)S(1)}, f32[6,128,128]{2,1,0:T(8,128)S(1)}, u32[]{:S(2)}, u32[]{:S(2)}) collective-permute-start(f32[6,128,128]{2,1,0:T(8,128)S(1)} %add.189), channel_id=1, source_target_pairs={{0,4},{1,5},{2,6},{3,7},{4,0},{5,1},{6,2},{7,3},{8,12},{9,13},{10,... | collective-permute-start | bytes 1179656 | tf_op jit(solution)/shard_map/ppermute | solution.py:166
  331.9 18.5 %collective-permute-start.28 = (f32[2,2,128,128]{3,2,1,0:T(8,128)S(1)}, f32[2,2,128,128]{3,2,1,0:T(8,128)S(1)}, u32[]{:S(2)}, u32[]{:S(2)}) collective-permute-start(f32[2,2,128,128]{3,2,1,0:T(8,128)S(1)} %add.190), channel_id=1, source_target_pairs={{0,32},{8,40},{16,48},{24,56},{32,0},{40,8},{48,16},{56,24},{64,96... | collective-permute-start | bytes 786440 | tf_op jit(solution)/shard_map/ppermute | solution.py:166
  350.6 9.3 %collective-permute-start.29 = (f32[2,2,128,128]{3,2,1,0:T(8,128)S(1)}, f32[2,2,128,128]{3,2,1,0:T(8,128)S(1)}, u32[]{:S(2)}, u32[]{:S(2)}) collective-permute-start(f32[2,2,128,128]{3,2,1,0:T(8,128)S(1)} %add.192), channel_id=1, source_target_pairs={{0,64},{8,72},{16,80},{24,88},{32,96},{40,104},{48,112},{56,120},{... | collective-permute-start | bytes 786440 | tf_op jit(solution)/shard_map/ppermute | solution.py:166
  359.9 36.4 %copy-start.2 = (f32[2,2,128,128]{3,2,1,0:T(8,128)S(1)}, f32[2,2,128,128]{3,2,1,0:T(8,128)}, u32[]{:S(2)}) copy-start(f32[2,2,128,128]{3,2,1,0:T(8,128)} %multiply_subtract_fusion.1.probe_ref) | copy-start | bytes 786436
  359.9 16.7 %collective-permute-start.30 = (f32[2,2,128,128]{3,2,1,0:T(8,128)S(1)}, f32[2,2,128,128]{3,2,1,0:T(8,128)S(1)}, u32[]{:S(2)}, u32[]{:S(2)}) collective-permute-start(f32[2,2,128,128]{3,2,1,0:T(8,128)S(1)} %add.193), channel_id=1, source_target_pairs={{0,128},{8,136},{16,144},{24,152},{32,160},{40,168},{48,176},{56,1... | collective-permute-start | bytes 786440 | tf_op jit(solution)/shard_map/ppermute | solution.py:166
  376.6 19.6 %collective-permute-start.31 = (f32[2,2,128,128]{3,2,1,0:T(8,128)S(1)}, f32[2,2,128,128]{3,2,1,0:T(8,128)S(1)}, u32[]{:S(2)}, u32[]{:S(2)}) collective-permute-start(f32[2,2,128,128]{3,2,1,0:T(8,128)S(1)} %add.194), channel_id=1, source_target_pairs={{0,256},{8,264},{16,272},{24,280},{32,288},{40,296},{48,304},{56,3... | collective-permute-start | bytes 786440 | tf_op jit(solution)/shard_map/ppermute | solution.py:166

commit v4 on v2

--- a/solution.py
+++ b/solution.py
@@ -158,13 +158,36 @@
     )(patch_cells, mode_values, target, weight.reshape(1, 1), tab)
 
 
-def xor_sum(values, axis):
-    size = lax.axis_size(axis)
-    step = 1
-    while step < size:
+def xor_sum(values, axis, steps=None):
+    size = lax.axis_size(axis)
+    if steps is None:
+        steps = [1 << bit for bit in range(size.bit_length() - 1)]
+    for step in steps:
         values = values + lax.ppermute(values, axis, [(i, i ^ step) for i in range(size)])
-        step *= 2
     return values
+
+
+def a2a_sum(values, axis):
+    size = lax.axis_size(axis)
+    flat = values.reshape(size, -1)
+    part = jnp.sum(lax.all_to_all(flat, axis, 0, 0, tiled=True), axis=0, keepdims=True)
+    spread = lax.all_to_all(jnp.broadcast_to(part, flat.shape), axis, 0, 0, tiled=True)
+    return spread.reshape(values.shape)
+
+
+def scatter_sum(values, axis):
+    size = lax.axis_size(axis)
+    lead, rows, cols = values.shape
+    chunks = jnp.moveaxis(values.reshape(lead, size, rows // size, cols), 1, 0)
+    return jnp.sum(lax.all_to_all(chunks, axis, 0, 0, tiled=True), axis=0)
+
+
+def gather_rows(chunk, axis):
+    size = lax.axis_size(axis)
+    lead, rows, cols = chunk.shape
+    spread = jnp.broadcast_to(chunk[None], (size, lead, rows, cols))
+    got = lax.all_to_all(spread, axis, 0, 0, tiled=True)
+    return jnp.moveaxis(got, 0, 1).reshape(lead, size * rows, cols)
 
 
 def local(object_real, object_imag, probe_modes, measured, offsets, live):
@@ -178,24 +201,33 @@
     anchor = jnp.zeros((), jnp.int32)
     obj_state = jnp.stack([object_real[:, 0], object_imag[:, 0]])
     parts = 2 * slices
-    modes = probe_modes.shape[0]
-    pending = None
-    for iteration in range(ITERS + 1):
-        if pending is not None:
-            probe_sum = pending
-            for step in (2, 4, 2 * GRID, 4 * GRID):
-                probe_sum = probe_sum + shifted(probe_sum, "tile", step)
-            probe_modes = (
-                probe_modes - probe_rate / (slot_count * tile_count * group_count) * probe_sum
-            )
-        if iteration == ITERS:
-            break
-        right_part = shifted(obj_state, "tile", -1)
-        upper_half = jnp.concatenate([obj_state, right_part], axis=-1)
-        lower_half = shifted(upper_half, "tile", -GRID)
-        canvas = jnp.concatenate([upper_half, lower_half], axis=-2)
-        current_probe = probe_modes
-
+    probe_parts = probe_modes.shape[0] * probe_modes.shape[1]
+    chunk_rows = block_side // group_count
+    chunk_start = lax.axis_index("scan") * chunk_rows
+    object_step = object_rate / (slot_count * group_count)
+    probe_step = probe_rate / (slot_count * tile_count * group_count)
+    planes = lambda a: a.reshape(-1, block_side, block_side)
+
+    right_part = shifted(obj_state, "tile", -1)
+    upper_half = jnp.concatenate([obj_state, right_part], axis=-1)
+    lower_half = shifted(upper_half, "tile", -GRID)
+    quarters = jnp.stack(
+        [
+            planes(obj_state),
+            planes(right_part),
+            planes(lower_half[..., :block_side]),
+            planes(lower_half[..., block_side:]),
+        ]
+    )
+    for iteration in range(ITERS):
+        last = iteration == ITERS - 1
+        canvas = jnp.concatenate(
+            [
+                jnp.concatenate([quarters[0], quarters[1]], axis=-1),
+                jnp.concatenate([quarters[2], quarters[3]], axis=-1),
+            ],
+            axis=-2,
+        ).reshape(2, slices, 2 * block_side, 2 * block_side)
         grad_canvas = jnp.zeros_like(canvas)
         grad_probe = jnp.zeros_like(probe_modes)
         for slot_index in range(slot_count):
@@ -205,33 +237,61 @@
             patch_cells = lax.dynamic_slice(canvas, starts, (2, slices, pattern_side, pattern_side))
             target = measured[0, 0, slot_index]
             weight = live[0, 0, slot_index].astype(jnp.float32)
-            grad_patch, grad_modes = slot_grad(patch_cells, current_probe, target, weight, tables)
+            grad_patch, grad_modes = slot_grad(patch_cells, probe_modes, target, weight, tables)
             current = lax.dynamic_slice(
                 grad_canvas, starts, (2, slices, pattern_side, pattern_side)
             )
             grad_canvas = lax.dynamic_update_slice(grad_canvas, current + grad_patch, starts)
             grad_probe = grad_probe + grad_modes
-        planes = lambda a: a.reshape(-1, block_side, block_side)
-        probe_planes = planes(grad_probe)
-        sent_down = jnp.concatenate(
-            [
-                planes(grad_canvas[:, :, block_side:, :block_side]),
-                planes(grad_canvas[:, :, block_side:, block_side:]),
-                probe_planes,
-            ]
+        grad_quarters = [
+            planes(grad_canvas[:, :, :block_side, :block_side]),
+            planes(grad_canvas[:, :, :block_side, block_side:]),
+            planes(grad_canvas[:, :, block_side:, :block_side]),
+            planes(grad_canvas[:, :, block_side:, block_side:]),
+        ]
+        band = scatter_sum(jnp.concatenate(grad_quarters + [planes(grad_probe)]), "scan")
+        g_ul, g_ur, g_ll, g_lr = (band[q * parts : (q + 1) * parts] for q in range(4))
+        probe_band = band[4 * parts :]
+        flat = probe_band.reshape(tile_count, -1)
+        probe_part = jnp.sum(lax.all_to_all(flat, "tile", 0, 0, tiled=True), axis=0, keepdims=True)
+        probe_total = lax.all_to_all(
+            jnp.broadcast_to(probe_part, flat.shape), "tile", 0, 0, tiled=True
+        ).reshape(probe_band.shape)
+        from_left = shifted(jnp.concatenate([g_ur, g_lr]), "tile", 1)
+        from_right = shifted(jnp.concatenate([g_ul, g_ll]), "tile", -1)
+        row_own = g_ul + from_left[:parts]
+        row_right = g_ur + from_right[:parts]
+        row_below = g_ll + from_left[parts:]
+        row_corner = g_lr + from_right[parts:]
+        from_above = shifted(jnp.concatenate([row_below, row_corner]), "tile", GRID)
+        total_own = row_own + from_above[:parts]
+        old_bands = lax.dynamic_slice_in_dim(quarters, chunk_start, chunk_rows, axis=2)
+        probe_band_old = lax.dynamic_slice_in_dim(
+            probe_modes.reshape(probe_parts, pattern_side, pattern_side), chunk_start, chunk_rows, axis=1
         )
-        came_down = shifted(sent_down, "tile", GRID)
-        own_part = planes(grad_canvas[:, :, :block_side, :block_side]) + came_down[:parts]
-        right_side = planes(grad_canvas[:, :, :block_side, block_side:]) + came_down[parts : 2 * parts]
-        probe_partial = probe_planes + came_down[2 * parts :]
-        sent_left = jnp.concatenate([right_side, probe_partial])
-        came_left = shifted(sent_left, "tile", 1)
-        own_part = own_part + came_left[:parts]
-        probe_partial = probe_partial + came_left[parts:]
-        reduced = xor_sum(jnp.concatenate([own_part, probe_partial]), "scan")
-        grad_total = reduced[:parts].reshape(obj_state.shape)
-        pending = reduced[parts:].reshape(probe_modes.shape)
-        obj_state = obj_state - object_rate / (slot_count * group_count) * grad_total
+        new_probe_band = probe_band_old - probe_step * probe_total
+        if last:
+            new_own = old_bands[0] - object_step * total_own
+            full = gather_rows(jnp.concatenate([new_own, new_probe_band]), "scan")
+            obj_state = full[:parts].reshape(obj_state.shape)
+            probe_modes = full[parts:].reshape(probe_modes.shape)
+        else:
+            from_below = shifted(jnp.concatenate([row_own, row_right]), "tile", -GRID)
+            totals = jnp.stack(
+                [
+                    total_own,
+                    row_right + from_above[parts:],
+                    row_below + from_below[:parts],
+                    row_corner + from_below[parts:],
+                ]
+            )
+            new_bands = old_bands - object_step * totals
+            full = gather_rows(
+                jnp.concatenate([new_bands.reshape(4 * parts, chunk_rows, block_side), new_probe_band]),
+                "scan",
+            )
+            quarters = full[: 4 * parts].reshape(quarters.shape)
+            probe_modes = full[4 * parts :].reshape(probe_modes.shape)
     return (obj_state[0][:, None], obj_state[1][:, None], probe_modes)
 
 

time: 422 us -> 303 us (0.72); the launches traced: 415 us -> 302 us
  waiting for transfers between devices: 242 us -> 56.2 us
  blocking collectives: 0 us -> 107 us
  starting transfers between devices: 112 us -> 65.9 us
  local copies, waits for them, and re-layouts: 13.6 us -> 22.3 us
    ppermute x16 -> x9, waiting for transfers between devices: 179 us -> 20.8 us  [shifted(): lax.ppermute(shard, axis, [(i, (i + by) % size) for i in range(size)])]
    all_to_all x0 -> x4, blocking collectives: none -> 107 us  [the longest x2 58 us: scatter_sum(): return jnp.sum(lax.all_to_all(chunks, axis, 0, 0, tiled=True), axis=0)]
    ppermute x6 -> x0, waiting for transfers between devices: 63.3 us -> none  [xor_sum(): lax.ppermute(values, axis, [(i, i ^ step) for i in range(size)])]
    ppermute x16 -> x9, starting transfers between devices: 83.4 us -> 40.6 us  [shifted(): lax.ppermute(shard, axis, [(i, (i + by) % size) for i in range(size)])]
    all_to_all x0 -> x4, waiting for transfers between devices: none -> 35.4 us  [the longest x2 21.4 us: local(): lax.all_to_all(flat, 'tile', 0, 0, tiled=True)]
    ppermute x6 -> x0, starting transfers between devices: 28.6 us -> none  [xor_sum(): lax.ppermute(values, axis, [(i, i ^ step) for i in range(size)])]
    all_to_all x0 -> x4, starting transfers between devices: none -> 25.2 us  [the longest x2 16 us: local(): lax.all_to_all(flat, 'tile', 0, 0, tiled=True)]
    slice x4 -> x12, local copies, waits for them, and re-layouts: 0.4 us -> 5.77 us  [the longest x2 1.99 us: local(): probe_band = band[4 * parts:]]
  transfers between devices with their start and end apart: 22 -> 13, of which waited for: 20 -> 7; matrix products, arithmetic and copies ran while one was open for 1% -> 3% of each run, Pallas kernels for 0% -> 0%
where the time goes in v4:
time: 303 us; the launch traced here: 302 us
  blocking collectives  107 us (35%)
  starting transfers between devices  65.9 us (22%)
  waiting for transfers between devices  56.2 us (19%)
  Pallas kernels  32.7 us (11%)
  local copies, waits for them, and re-layouts  22.3 us (7%)
  other arithmetic  12.3 us (4%)
  between operations  5.68 us (2%)
    all_to_all x2, blocking collectives, scatter_sum(): return jnp.sum(lax.all_to_all(chunks, axis, 0, 0, tiled=True), axis=0)  58 us
    all_to_all x2, blocking collectives, gather_rows(): got = lax.all_to_all(spread, axis, 0, 0, tiled=True)  48.9 us
    ppermute x9, starting transfers between devices, shifted(): lax.ppermute(shard, axis, [(i, (i + by) % size) for i in range(size)])  40.6 us
    pallas_call x2, Pallas kernels, slot_grad(): pl.pallas_call(slot_kernel, out_shape=(jax.ShapeDtypeStruct(patch_cells.s...  32.7 us
    all_to_all x2, waiting for transfers between devices, local(): lax.all_to_all(flat, 'tile', 0, 0, tiled=True)  21.4 us
    ppermute x9, waiting for transfers between devices, shifted(): lax.ppermute(shard, axis, [(i, (i + by) % size) for i in range(size)])  20.8 us
    all_to_all x2, starting transfers between devices, local(): lax.all_to_all(flat, 'tile', 0, 0, tiled=True)  16 us
    all_to_all x2, waiting for transfers between devices, local(): lax.all_to_all(jnp.broadcast_to(probe_part, flat.shape), 'tile', 0, 0, ti...  14 us
  transfers between devices with their start and end apart: 13, of which 7 were waited for; matrix products, arithmetic and copies ran while one was open for 3% of the time, Pallas kernels for 0%

profile of v4, /device:TPU:1, one launch (start us, length us, event | category | flops | bytes accessed | tf_op | source)
XLA Modules:
  0.0 301.7 jit_solution(5236965776829657843)
XLA Ops:
  0.6 1.1 pad_maximum_fusion.1
  1.7 14.4 %collective-permute-start = (f32[2,3,128,128]{3,2,1,0:T(8,128)S(1)}, f32[2,3,128,128]{3,2,1,0:T(8,128)S(1)}, u32[]{:S(2)}, u32[]{:S(2)}) collective-permute-start(f32[2,3,128,128]{3,2,1,0:T(8,128)S(1)} %pad_maximum_fusion.1), channel_id=1, source_target_pairs={{0,504},{8,0},{16,8},{24,16},{32,24},{40,32},{48,40},{56,48},{64,5... | collective-permute-start | bytes 1179656 | tf_op jit(solution)/shard_map/ppermute | solution.py:20
  16.1 7.8 %collective-permute-done = f32[2,3,128,128]{3,2,1,0:T(8,128)S(1)} collective-permute-done((f32[2,3,128,128]{3,2,1,0:T(8,128)S(1)}, f32[2,3,128,128]{3,2,1,0:T(8,128)S(1)}, u32[]{:S(2)}, u32[]{:S(2)}) %collective-permute-start) | collective-permute-done | bytes 393248 | tf_op jit(solution)/shard_map/ppermute | solution.py:20
  23.9 1.1 pad_maximum_fusion
  24.9 2.2 collective-permute-start.1
  27.1 0.6 fusion.27
  32.3 0.3 cosine_multiply_fusion
  32.5 0.5 fusion.8
  33.1 0.7 pad_maximum_fusion.2.tab_ref
  33.8 10.5 %collective-permute-done.1 = f32[2,3,128,256]{3,2,1,0:T(8,128)S(1)} collective-permute-done((f32[2,3,128,256]{3,2,1,0:T(8,128)S(1)}, f32[2,3,128,256]{3,2,1,0:T(8,128)S(1)}, u32[]{:S(2)}, u32[]{:S(2)}) %collective-permute-start.1) | collective-permute-done | bytes 786464 | tf_op jit(solution)/shard_map/ppermute | solution.py:20
  44.5 0.9 constant_dynamic-slice_fusion.1.cells_ref
  45.4 16.3 %shard_map.85 = (f32[2,3,128,128]{3,2,1,0:T(8,128)}, f32[2,2,128,128]{3,2,1,0:T(8,128)}) custom-call(f32[2,3,128,128]{3,2,1,0:T(8,128)} %constant_dynamic-slice_fusion.1.cells_ref, f32[2,2,128,128]{3,2,1,0:T(8,128)} %probe_ref.1, f32[128,128]{1,0:T(8,128)} %bitcast.117, f32[1,1]{1,0:T(1,128)} %bitcast.14.weight_ref, f32[4,128,128]{2,1,0:T(8,128)} %pad_maximum_fusion.2.tab_ref), custom_call_target="tpu_custom_call" | custom-call | flops 1342177280 | bytes 1441792 | tf_op jit(solution)/shard_map/pallas_call | solution.py:147
  61.8 0.1 broadcast.214.clone
  61.9 4.9 %dynamic_update_slice.6 = f32[2,3,256,256]{3,2,1,0:T(8,128)S(1)} dynamic-update-slice(f32[2,3,256,256]{3,2,1,0:T(8,128)S(1)} %broadcast.214.clone, f32[2,3,128,128]{3,2,1,0:T(8,128)} %get-tuple-element.7, s32[]{:T(128)} %constant.14.clone.1, s32[]{:T(128)} %constant.14.clone.1, s32[]{:T(128)S(6)} %select_n.53, s32[]{:T(128)S(6)} %select_n.54) | dynamic-update-slice | bytes 786436 | tf_op jit(solution)/shard_map/dynamic_update_slice | solution.py:244
  66.8 0.2 fusion.22
  67.2 0.8 copy-done.2
  68.0 0.2 copy.12
  68.2 30.3 %all_to_all.52 = f32[8,28,16,128]{3,2,1,0:T(8,128)S(1)} all-to-all(f32[8,28,16,128]{3,2,1,0:T(8,128)S(1)} %copy.12), channel_id=1, replica_groups=mesh['tile'=64,'scan'=8] {'scan'}, dimensions={0} | all-to-all | bytes 3670016 | tf_op jit(solution)/shard_map/all_to_all | solution.py:182
  98.4 0.8 reduce_sum.36
  99.2 0.9 fusion.26
  100.1 8.6 %collective-permute-start.3 = (f32[12,16,128]{2,1,0:T(8,128)S(1)}, f32[12,16,128]{2,1,0:T(8,128)S(1)}, u32[]{:S(2)}, u32[]{:S(2)}) collective-permute-start(f32[12,16,128]{2,1,0:T(8,128)S(1)} %pad_maximum_fusion.5), channel_id=1, source_target_pairs={{0,504},{8,0},{16,8},{24,16},{32,24},{40,32},{48,40},{56,48},{64,5... | collective-permute-start | bytes 294920 | tf_op jit(solution)/shard_map/ppermute | solution.py:20
  108.8 1.9 collective-permute-start.2
  110.7 1.4 slice.216
  112.1 7.1 %all-to-all-start.1 = ((f32[64,1,128]{2,1,0:T(1,128)}), f32[64,1,128]{2,1,0:T(1,128)S(1)}, u32[]{:S(2)}, u32[]{:S(2)}) async-start(f32[64,1,128]{2,1,0:T(1,128)} %bitcast.27), calls=%async_computation.1 | async-start | bytes 65536 | tf_op jit(solution)/shard_map/all_to_all | solution.py:256
  119.2 10.8 %all-to-all-done.1 = f32[64,1,128]{2,1,0:T(1,128)S(1)} async-done(((f32[64,1,128]{2,1,0:T(1,128)}), f32[64,1,128]{2,1,0:T(1,128)S(1)}, u32[]{:S(2)}, u32[]{:S(2)}) %all-to-all-start.1) | async-done | bytes 32800 | tf_op jit(solution)/shard_map/all_to_all | solution.py:256
  130.0 0.6 broadcast_in_dim.8
  130.7 4.6 %all-to-all-start.2 = ((f32[64,1,128]{2,1,0:T(1,128)}), f32[64,1,128]{2,1,0:T(1,128)S(1)}, u32[]{:S(2)}, u32[]{:S(2)}) async-start(f32[64,1,128]{2,1,0:T(1,128)} %broadcast_in_dim.8), calls=%async_computation.2 | async-start | bytes 65536 | tf_op jit(solution)/shard_map/all_to_all | solution.py:257
  135.3 0.8 slice_add_fusion.10
  136.1 2.9 collective-permute-start.4
  139.0 7.0 %all-to-all-done.2 = f32[64,1,128]{2,1,0:T(1,128)S(1)} async-done(((f32[64,1,128]{2,1,0:T(1,128)}), f32[64,1,128]{2,1,0:T(1,128)S(1)}, u32[]{:S(2)}, u32[]{:S(2)}) %all-to-all-start.2) | async-done | bytes 32800 | tf_op jit(solution)/shard_map/all_to_all | solution.py:257
  146.1 0.8 fusion.17
  146.9 2.1 collective-permute-start.5
  149.1 0.8 bitcast_subtract_fusion.1
  149.9 2.4 collective-permute-done.5
  152.4 0.2 broadcast_in_dim.9
  152.5 31.4 %all_to_all.50 = f32[8,28,16,128]{3,2,1,0:T(8,128)S(1)} all-to-all(f32[8,28,16,128]{3,2,1,0:T(8,128)S(1)} %broadcast_in_dim.9), channel_id=1, replica_groups=mesh['tile'=64,'scan'=8] {'scan'}, dimensions={0} | all-to-all | bytes 3670016 | tf_op jit(solution)/shard_map/all_to_all | solution.py:189
  183.9 0.2 copy.21
  184.2 0.7 slice.222
  185.1 0.9 constant_dynamic-slice_fusion.cells_ref
  186.0 16.3 %shard_map.86 = (f32[2,3,128,128]{3,2,1,0:T(8,128)}, f32[2,2,128,128]{3,2,1,0:T(8,128)}) custom-call(f32[2,3,128,128]{3,2,1,0:T(8,128)} %constant_dynamic-slice_fusion.cells_ref, f32[2,2,128,128]{3,2,1,0:T(8,128)} %bitcast.107, f32[128,128]{1,0:T(8,128)} %bitcast.118, f32[1,1]{1,0:T(1,128)} %bitcast.14.weight_ref, f32[4,128,128]{2,1,0:T(8,128)} %pad_maximum_fusion.2.tab_ref), custom_call_target="tpu_custom_call" | custom-call | flops 1342177280 | bytes 1441792 | tf_op jit(solution)/shard_map/pallas_call | solution.py:147
  202.3 0.1 broadcast.214
  202.5 4.9 %dynamic_update_slice.7 = f32[2,3,256,256]{3,2,1,0:T(8,128)S(1)} dynamic-update-slice(f32[2,3,256,256]{3,2,1,0:T(8,128)S(1)} %broadcast.214, f32[2,3,128,128]{3,2,1,0:T(8,128)} %get-tuple-element.9, s32[]{:T(128)} %constant.14.clone.1, s32[]{:T(128)} %constant.14.clone.1, s32[]{:T(128)S(6)} %select_n.53, s32[]{:T(128)S(6)} %select_n.54) | dynamic-update-slice | bytes 786436 | tf_op jit(solution)/shard_map/dynamic_update_slice | solution.py:244
  207.4 0.2 fusion.21
  207.8 0.8 copy-done.1
  208.6 0.2 copy.14
  208.8 27.7 %all_to_all.53 = f32[8,28,16,128]{3,2,1,0:T(8,128)} all-to-all(f32[8,28,16,128]{3,2,1,0:T(8,128)S(1)} %copy.14), channel_id=1, replica_groups=mesh['tile'=64,'scan'=8] {'scan'}, dimensions={0} | all-to-all | bytes 3670016 | tf_op jit(solution)/shard_map/all_to_all | solution.py:182
  236.5 1.6 reduce_sum.38
  238.2 3.7 %collective-permute-start.7 = (f32[12,16,128]{2,1,0:T(8,128)S(1)}, f32[12,16,128]{2,1,0:T(8,128)}, u32[]{:S(2)}, u32[]{:S(2)}) collective-permute-start(f32[12,16,128]{2,1,0:T(8,128)S(1)} %pad_maximum_fusion.9), channel_id=1, source_target_pairs={{0,504},{8,0},{16,8},{24,16},{32,24},{40,32},{48,40},{56,48},{64,5... | collective-permute-start | bytes 294920 | tf_op jit(solution)/shard_map/ppermute | solution.py:20
  241.9 0.6 pad_maximum_fusion.8
  242.6 1.9 collective-permute-start.6
  244.5 0.6 slice.235
  245.1 9.0 %all-to-all-start.5 = ((f32[64,1,128]{2,1,0:T(1,128)}), f32[64,1,128]{2,1,0:T(1,128)S(1)}, u32[]{:S(2)}, u32[]{:S(2)}) async-start(f32[64,1,128]{2,1,0:T(1,128)} %bitcast.46), calls=%async_computation.5 | async-start | bytes 65536 | tf_op jit(solution)/shard_map/all_to_all | solution.py:256
  254.1 0.1 slice.217
  254.2 10.6 %all-to-all-done.5 = f32[64,1,128]{2,1,0:T(1,128)S(1)} async-done(((f32[64,1,128]{2,1,0:T(1,128)}), f32[64,1,128]{2,1,0:T(1,128)S(1)}, u32[]{:S(2)}, u32[]{:S(2)}) %all-to-all-start.5) | async-done | bytes 32800 | tf_op jit(solution)/shard_map/all_to_all | solution.py:256
  264.9 0.6 broadcast_in_dim.10
  265.6 4.6 %all-to-all-start.6 = ((f32[64,1,128]{2,1,0:T(1,128)}), f32[64,1,128]{2,1,0:T(1,128)S(1)}, u32[]{:S(2)}, u32[]{:S(2)}) async-start(f32[64,1,128]{2,1,0:T(1,128)} %broadcast_in_dim.10), calls=%async_computation.6 | async-start | bytes 65536 | tf_op jit(solution)/shard_map/all_to_all | solution.py:257
  270.2 0.9 slice_add_fusion.2
  271.1 2.9 collective-permute-start.8
  274.0 7.0 %all-to-all-done.6 = f32[64,1,128]{2,1,0:T(1,128)S(1)} async-done(((f32[64,1,128]{2,1,0:T(1,128)}), f32[64,1,128]{2,1,0:T(1,128)S(1)}, u32[]{:S(2)}, u32[]{:S(2)}) %all-to-all-start.6) | async-done | bytes 32800 | tf_op jit(solution)/shard_map/all_to_all | solution.py:257
  281.0 0.8 bitcast_subtract_fusion
  281.8 0.8 fusion.13
  282.7 17.5 %all_to_all.51 = f32[8,10,16,128]{3,2,1,0:T(8,128)S(1)} all-to-all(f32[8,10,16,128]{3,2,1,0:T(8,128)S(1)} %broadcast_in_dim.11), channel_id=1, replica_groups=mesh['tile'=64,'scan'=8] {'scan'}, dimensions={0} | all-to-all | bytes 1310720 | tf_op jit(solution)/shard_map/all_to_all | solution.py:189
  300.2 0.8 fusion.24
  301.0 0.7 slice.238
  (44 shorter events, 1.2 us)
Async XLA Ops:
  0.6 26.5 %copy-start.3 = (s32[1,1,1,2]{3,2,1,0:T(1,128)S(1)}, s32[1,1,1,2]{3,2,1,0:T(1,128)}, u32[]{:S(2)}) copy-start(s32[1,1,1,2]{3,2,1,0:T(1,128)} %param.10) | copy-start | bytes 28
  1.7 22.2 %collective-permute-start = (f32[2,3,128,128]{3,2,1,0:T(8,128)S(1)}, f32[2,3,128,128]{3,2,1,0:T(8,128)S(1)}, u32[]{:S(2)}, u32[]{:S(2)}) collective-permute-start(f32[2,3,128,128]{3,2,1,0:T(8,128)S(1)} %pad_maximum_fusion.1), channel_id=1, source_target_pairs={{0,504},{8,0},{16,8},{24,16},{32,24},{40,32},{48,40},{56,48},{64,5... | collective-permute-start | bytes 1179656 | tf_op jit(solution)/shard_map/ppermute | solution.py:20
  24.9 19.4 %collective-permute-start.1 = (f32[2,3,128,256]{3,2,1,0:T(8,128)S(1)}, f32[2,3,128,256]{3,2,1,0:T(8,128)S(1)}, u32[]{:S(2)}, u32[]{:S(2)}) collective-permute-start(f32[2,3,128,256]{3,2,1,0:T(8,128)S(1)} %pad_maximum_fusion), channel_id=1, source_target_pairs={{0,448},{8,456},{16,464},{24,472},{32,480},{40,488},{48,496},{56,5... | collective-permute-start | bytes 2359304 | tf_op jit(solution)/shard_map/ppermute | solution.py:20
  67.0 1.0 copy-start.2
  100.1 35.1 %collective-permute-start.3 = (f32[12,16,128]{2,1,0:T(8,128)S(1)}, f32[12,16,128]{2,1,0:T(8,128)S(1)}, u32[]{:S(2)}, u32[]{:S(2)}) collective-permute-start(f32[12,16,128]{2,1,0:T(8,128)S(1)} %pad_maximum_fusion.5), channel_id=1, source_target_pairs={{0,504},{8,0},{16,8},{24,16},{32,24},{40,32},{48,40},{56,48},{64,5... | collective-permute-start | bytes 294920 | tf_op jit(solution)/shard_map/ppermute | solution.py:20
  108.8 26.5 %collective-permute-start.2 = (f32[12,16,128]{2,1,0:T(8,128)S(1)}, f32[12,16,128]{2,1,0:T(8,128)S(1)}, u32[]{:S(2)}, u32[]{:S(2)}) collective-permute-start(f32[12,16,128]{2,1,0:T(8,128)S(1)} %pad_maximum_fusion.4), channel_id=1, source_target_pairs={{0,8},{8,16},{16,24},{24,32},{32,40},{40,48},{48,56},{56,64},{64,7... | collective-permute-start | bytes 294920 | tf_op jit(solution)/shard_map/ppermute | solution.py:20
  112.1 17.8 %all-to-all-start.1 = ((f32[64,1,128]{2,1,0:T(1,128)}), f32[64,1,128]{2,1,0:T(1,128)S(1)}, u32[]{:S(2)}, u32[]{:S(2)}) async-start(f32[64,1,128]{2,1,0:T(1,128)} %bitcast.27), calls=%async_computation.1 | async-start | bytes 65536 | tf_op jit(solution)/shard_map/all_to_all | solution.py:256
  130.7 15.4 %all-to-all-start.2 = ((f32[64,1,128]{2,1,0:T(1,128)}), f32[64,1,128]{2,1,0:T(1,128)S(1)}, u32[]{:S(2)}, u32[]{:S(2)}) async-start(f32[64,1,128]{2,1,0:T(1,128)} %broadcast_in_dim.8), calls=%async_computation.2 | async-start | bytes 65536 | tf_op jit(solution)/shard_map/all_to_all | solution.py:257
  136.1 9.9 %collective-permute-start.4 = (f32[12,16,128]{2,1,0:T(8,128)S(1)}, f32[12,16,128]{2,1,0:T(8,128)S(1)}, u32[]{:S(2)}, u32[]{:S(2)}) collective-permute-start(f32[12,16,128]{2,1,0:T(8,128)S(1)} %pad_maximum_fusion.6), channel_id=1, source_target_pairs={{0,64},{8,72},{16,80},{24,88},{32,96},{40,104},{48,112},{56,120},{... | collective-permute-start | bytes 294920 | tf_op jit(solution)/shard_map/ppermute | solution.py:20
  146.9 5.4 %collective-permute-start.5 = (f32[12,16,128]{2,1,0:T(8,128)S(1)}, f32[12,16,128]{2,1,0:T(8,128)S(1)}, u32[]{:S(2)}, u32[]{:S(2)}) collective-permute-start(f32[12,16,128]{2,1,0:T(8,128)S(1)} %pad_maximum_fusion.7), channel_id=1, source_target_pairs={{0,448},{8,456},{16,464},{24,472},{32,480},{40,488},{48,496},{56,5... | collective-permute-start | bytes 294920 | tf_op jit(solution)/shard_map/ppermute | solution.py:20
  207.6 1.0 copy-start.1
  238.1 7.0 %copy-start = (f32[28,16,128]{2,1,0:T(8,128)}, f32[28,16,128]{2,1,0:T(8,128)S(1)}, u32[]{:S(2)}) copy-start(f32[28,16,128]{2,1,0:T(8,128)S(1)} %reduce_sum.38) | copy-start | bytes 688132
  238.2 32.0 %collective-permute-start.7 = (f32[12,16,128]{2,1,0:T(8,128)S(1)}, f32[12,16,128]{2,1,0:T(8,128)}, u32[]{:S(2)}, u32[]{:S(2)}) collective-permute-start(f32[12,16,128]{2,1,0:T(8,128)S(1)} %pad_maximum_fusion.9), channel_id=1, source_target_pairs={{0,504},{8,0},{16,8},{24,16},{32,24},{40,32},{48,40},{56,48},{64,5... | collective-permute-start | bytes 294920 | tf_op jit(solution)/shard_map/ppermute | solution.py:20
  242.6 27.6 %collective-permute-start.6 = (f32[12,16,128]{2,1,0:T(8,128)}, f32[12,16,128]{2,1,0:T(8,128)}, u32[]{:S(2)}, u32[]{:S(2)}) collective-permute-start(f32[12,16,128]{2,1,0:T(8,128)} %pad_maximum_fusion.8), channel_id=1, source_target_pairs={{0,8},{8,16},{16,24},{24,32},{32,40},{40,48},{48,56},{56,64},{64,7... | collective-permute-start | bytes 294920 | tf_op jit(solution)/shard_map/ppermute | solution.py:20
  245.1 19.8 %all-to-all-start.5 = ((f32[64,1,128]{2,1,0:T(1,128)}), f32[64,1,128]{2,1,0:T(1,128)S(1)}, u32[]{:S(2)}, u32[]{:S(2)}) async-start(f32[64,1,128]{2,1,0:T(1,128)} %bitcast.46), calls=%async_computation.5 | async-start | bytes 65536 | tf_op jit(solution)/shard_map/all_to_all | solution.py:256
  265.6 15.4 %all-to-all-start.6 = ((f32[64,1,128]{2,1,0:T(1,128)}), f32[64,1,128]{2,1,0:T(1,128)S(1)}, u32[]{:S(2)}, u32[]{:S(2)}) async-start(f32[64,1,128]{2,1,0:T(1,128)} %broadcast_in_dim.10), calls=%async_computation.6 | async-start | bytes 65536 | tf_op jit(solution)/shard_map/all_to_all | solution.py:257
  271.1 10.7 %collective-permute-start.8 = (f32[12,16,128]{2,1,0:T(8,128)S(1)}, f32[12,16,128]{2,1,0:T(8,128)S(1)}, u32[]{:S(2)}, u32[]{:S(2)}) collective-permute-start(f32[12,16,128]{2,1,0:T(8,128)S(1)} %pad_maximum_fusion.10), channel_id=1, source_target_pairs={{0,64},{8,72},{16,80},{24,88},{32,96},{40,104},{48,112},{56,120},{... | collective-permute-start | bytes 294920 | tf_op jit(solution)/shard_map/ppermute | solution.py:20

commit v5 on v3

--- a/solution.py
+++ b/solution.py
@@ -167,6 +167,14 @@
     return values
 
 
+def a2a_sum(values, axis):
+    size = lax.axis_size(axis)
+    flat = values.reshape(size, -1)
+    part = jnp.sum(lax.all_to_all(flat, axis, 0, 0, tiled=True), axis=0, keepdims=True)
+    spread = lax.all_to_all(jnp.broadcast_to(part, flat.shape), axis, 0, 0, tiled=True)
+    return spread.reshape(values.shape)
+
+
 def local(object_real, object_imag, probe_modes, measured, offsets, live):
     slices = object_real.shape[0]
     block_side = object_real.shape[2]
@@ -183,23 +191,15 @@
     second_bits = [b for b in tile_bits if b >= GRID]
     pending = None
     for iteration in range(ITERS + 1):
-        if iteration == ITERS:
-            probe_sum = xor_sum(pending, "tile", second_bits)
+        if pending is not None:
+            probe_sum = pending
             probe_modes = (
                 probe_modes - probe_rate / (slot_count * tile_count * group_count) * probe_sum
             )
+        if iteration == ITERS:
             break
-        probe_sum = pending
-        if pending is not None:
-            probe_sum = xor_sum(probe_sum, "tile", second_bits[:1])
         right_part = shifted(obj_state, "tile", -1)
         upper_half = jnp.concatenate([obj_state, right_part], axis=-1)
-        if pending is not None:
-            upper_half, probe_sum = lax.optimization_barrier((upper_half, probe_sum))
-            probe_sum = xor_sum(probe_sum, "tile", second_bits[1:])
-            probe_modes = (
-                probe_modes - probe_rate / (slot_count * tile_count * group_count) * probe_sum
-            )
         lower_half = shifted(upper_half, "tile", -GRID)
         canvas = jnp.concatenate([upper_half, lower_half], axis=-2)
         current_probe = probe_modes
@@ -237,12 +237,11 @@
         came_left = shifted(right_side, "tile", 1)
         probe_partial = xor_sum(probe_partial, "scan", [4])
         own_part = own_part + came_left
-        for step in (1, 2, 4):
-            own_part, probe_partial = pair(own_part, probe_partial)
-            own_part = xor_sum(own_part, "scan", [step])
-            probe_partial = xor_sum(probe_partial, "tile", [step])
-        grad_total = own_part.reshape(obj_state.shape)
         own_part, probe_partial = pair(own_part, probe_partial)
+        probe_partial = a2a_sum(probe_partial, "tile")
+        own_part = xor_sum(own_part, "scan", [1, 2])
+        own_part, probe_partial = pair(own_part, probe_partial)
+        grad_total = xor_sum(own_part, "scan", [4]).reshape(obj_state.shape)
         pending = probe_partial
         obj_state = obj_state - object_rate / (slot_count * group_count) * grad_total
     return (obj_state[0][:, None], obj_state[1][:, None], probe_modes)

time: 398 us -> 307 us (0.77); the launches traced: 397 us -> 302 us
  waiting for transfers between devices: 229 us -> 133 us
    ppermute x24 -> x12, waiting for transfers between devices: 184 us -> 50.8 us  [xor_sum(): lax.ppermute(values, axis, [(i, i ^ step) for i in range(size)])]
    ppermute x24 -> x12, starting transfers between devices: 80.7 us -> 51.1 us  [xor_sum(): lax.ppermute(values, axis, [(i, i ^ step) for i in range(size)])]
    all_to_all x0 -> x4, starting transfers between devices: none -> 23.3 us  [the longest x2 14.1 us: a2a_sum(): lax.all_to_all(flat, axis, 0, 0, tiled=True)]
    all_to_all x0 -> x4, waiting for transfers between devices: none -> 22.3 us  [the longest x2 16.6 us: a2a_sum(): lax.all_to_all(flat, axis, 0, 0, tiled=True)]
    ppermute x8, waiting for transfers between devices: 45.7 us -> 60 us  [shifted(): lax.ppermute(shard, axis, [(i, (i + by) % size) for i in range(size)])]
  transfers between devices with their start and end apart: 32 -> 24, of which waited for: 23 -> 20; matrix products, arithmetic and copies ran while one was open for 3% -> 6% of each run, Pallas kernels for 0% -> 0%
where the time goes in v5:
time: 307 us; the launch traced here: 302 us
  waiting for transfers between devices  133 us (43%)
  starting transfers between devices  106 us (35%)
  Pallas kernels  32.7 us (11%)
  local copies, waits for them, and re-layouts  14.4 us (5%)
  other arithmetic  9.96 us (3%)
  between operations  5.64 us (2%)
    ppermute x8, waiting for transfers between devices, shifted(): lax.ppermute(shard, axis, [(i, (i + by) % size) for i in range(size)])  60 us
    ppermute x12, starting transfers between devices, xor_sum(): lax.ppermute(values, axis, [(i, i ^ step) for i in range(size)])  51.1 us
    ppermute x12, waiting for transfers between devices, xor_sum(): lax.ppermute(values, axis, [(i, i ^ step) for i in range(size)])  50.8 us
    pallas_call x2, Pallas kernels, slot_grad(): pl.pallas_call(slot_kernel, out_shape=(jax.ShapeDtypeStruct(patch_cells.s...  32.7 us
    ppermute x8, starting transfers between devices, shifted(): lax.ppermute(shard, axis, [(i, (i + by) % size) for i in range(size)])  31.6 us
    all_to_all x2, waiting for transfers between devices, a2a_sum(): lax.all_to_all(flat, axis, 0, 0, tiled=True)  16.6 us
    all_to_all x2, starting transfers between devices, a2a_sum(): lax.all_to_all(flat, axis, 0, 0, tiled=True)  14.1 us
    all_to_all x2, starting transfers between devices, a2a_sum(): lax.all_to_all(jnp.broadcast_to(part, flat.shape), axis, 0, 0, tiled=True)  9.22 us
  transfers between devices with their start and end apart: 24, of which 20 were waited for; matrix products, arithmetic and copies ran while one was open for 6% of the time, Pallas kernels for 0%

profile of v5, /device:TPU:1, one launch (start us, length us, event | category | flops | bytes accessed | tf_op | source)
XLA Modules:
  0.0 301.7 jit_solution(6112388350124540267)
XLA Ops:
  0.7 1.1 pad_maximum_fusion.4
  1.8 14.4 %collective-permute-start = (f32[2,3,128,128]{3,2,1,0:T(8,128)S(1)}, f32[2,3,128,128]{3,2,1,0:T(8,128)S(1)}, u32[]{:S(2)}, u32[]{:S(2)}) collective-permute-start(f32[2,3,128,128]{3,2,1,0:T(8,128)S(1)} %pad_maximum_fusion.4), channel_id=1, source_target_pairs={{0,504},{8,0},{16,8},{24,16},{32,24},{40,32},{48,40},{56,48},{64,5... | collective-permute-start | bytes 1179656 | tf_op jit(solution)/shard_map/ppermute | solution.py:20
  16.2 7.8 %collective-permute-done = f32[2,3,128,128]{3,2,1,0:T(8,128)S(1)} collective-permute-done((f32[2,3,128,128]{3,2,1,0:T(8,128)S(1)}, f32[2,3,128,128]{3,2,1,0:T(8,128)S(1)}, u32[]{:S(2)}, u32[]{:S(2)}) %collective-permute-start) | collective-permute-done | bytes 393248 | tf_op jit(solution)/shard_map/ppermute | solution.py:20
  23.9 1.1 pad_maximum_fusion
  25.0 2.2 collective-permute-start.1
  27.2 0.6 fusion.20
  32.6 0.3 fusion.11
  32.9 0.7 pad_maximum_fusion.5.tab_ref
  33.7 10.7 %collective-permute-done.1 = f32[2,3,128,256]{3,2,1,0:T(8,128)S(1)} collective-permute-done((f32[2,3,128,256]{3,2,1,0:T(8,128)S(1)}, f32[2,3,128,256]{3,2,1,0:T(8,128)S(1)}, u32[]{:S(2)}, u32[]{:S(2)}) %collective-permute-start.1) | collective-permute-done | bytes 786464 | tf_op jit(solution)/shard_map/ppermute | solution.py:20
  44.4 1.1 fusion.4.cells_ref
  45.5 16.3 %shard_map.85 = (f32[2,3,128,128]{3,2,1,0:T(8,128)}, f32[2,2,128,128]{3,2,1,0:T(8,128)}) custom-call(f32[2,3,128,128]{3,2,1,0:T(8,128)} %fusion.4.cells_ref, f32[2,2,128,128]{3,2,1,0:T(8,128)} %probe_ref.1, f32[128,128]{1,0:T(8,128)} %bitcast.51, f32[1,1]{1,0:T(1,128)} %bitcast.5.weight_ref, f32[4,128,128]{2,1,0:T(8,128)} %pad_maximum_fusion.5.tab_ref), custom_call_target="tpu_custom_call" | custom-call | flops 1342177280 | bytes 1441792 | tf_op jit(solution)/shard_map/pallas_call | solution.py:147
  61.9 4.7 %collective-permute-start.2 = (f32[2,2,128,128]{3,2,1,0:T(8,128)}, f32[2,2,128,128]{3,2,1,0:T(8,128)S(1)}, u32[]{:S(2)}, u32[]{:S(2)}) collective-permute-start(f32[2,2,128,128]{3,2,1,0:T(8,128)} %get-tuple-element.24), channel_id=1, source_target_pairs={{0,1},{1,0},{2,3},{3,2},{4,5},{5,4},{6,7},{7,6},{8,9},{9,8},{10,11... | collective-permute-start | bytes 786440 | tf_op jit(solution)/shard_map/ppermute | solution.py:166
  66.7 4.5 %dynamic_update_slice.6 = f32[2,3,256,256]{3,2,1,0:T(8,128)S(1)} dynamic-update-slice(f32[2,3,256,256]{3,2,1,0:T(8,128)S(1)} %broadcast.215.clone, f32[2,3,128,128]{3,2,1,0:T(8,128)S(1)} %copy-done.4, s32[]{:T(128)} %constant.13.clone.1, s32[]{:T(128)} %constant.13.clone.1, s32[]{:T(128)S(6)} %select_n.46, s32[]{:T(128)S(6)} %select_n.47) | dynamic-update-slice | bytes 786436 | tf_op jit(solution)/shard_map/dynamic_update_slice | solution.py:220
  71.4 0.9 copy-done.7
  72.3 1.9 collective-permute-start.3
  74.3 2.9 collective-permute-start.4
  77.2 7.1 %collective-permute-done.4 = f32[2,2,128,128]{3,2,1,0:T(8,128)S(1)} collective-permute-done((f32[2,2,128,128]{3,2,1,0:T(8,128)S(1)}, f32[2,2,128,128]{3,2,1,0:T(8,128)S(1)}, u32[]{:S(2)}, u32[]{:S(2)}) %collective-permute-start.4) | collective-permute-done | bytes 262176 | tf_op jit(solution)/shard_map/ppermute | solution.py:166
  84.3 10.5 %collective-permute-done.3 = f32[12,128,128]{2,1,0:T(8,128)S(1)} collective-permute-done((f32[12,128,128]{2,1,0:T(8,128)S(1)}, f32[12,128,128]{2,1,0:T(8,128)S(1)}, u32[]{:S(2)}, u32[]{:S(2)}) %collective-permute-start.3) | collective-permute-done | bytes 786464 | tf_op jit(solution)/shard_map/ppermute | solution.py:20
  94.9 1.9 collective-permute-start.5
  96.8 3.8 %collective-permute-start.6 = (f32[2,2,128,128]{3,2,1,0:T(8,128)S(1)}, f32[2,2,128,128]{3,2,1,0:T(8,128)S(1)}, u32[]{:S(2)}, u32[]{:S(2)}) collective-permute-start(f32[2,2,128,128]{3,2,1,0:T(8,128)S(1)} %add.133), channel_id=1, source_target_pairs={{0,4},{1,5},{2,6},{3,7},{4,0},{5,1},{6,2},{7,3},{8,12},{9,13},{10,... | collective-permute-start | bytes 786440 | tf_op jit(solution)/shard_map/ppermute | solution.py:166
  100.6 6.9 %collective-permute-done.6 = f32[2,2,128,128]{3,2,1,0:T(8,128)S(1)} collective-permute-done((f32[2,2,128,128]{3,2,1,0:T(8,128)S(1)}, f32[2,2,128,128]{3,2,1,0:T(8,128)S(1)}, u32[]{:S(2)}, u32[]{:S(2)}) %collective-permute-start.6) | collective-permute-done | bytes 262176 | tf_op jit(solution)/shard_map/ppermute | solution.py:166
  107.5 0.7 add.135
  108.2 2.4 collective-permute-done.5
  110.6 5.7 %all-to-all-start = ((f32[64,1,1024]{2,1,0:T(1,128)}), f32[64,1,1024]{2,1,0:T(1,128)S(1)}, u32[]{:S(2)}, u32[]{:S(2)}) async-start(f32[64,1,1024]{2,1,0:T(1,128)} %bitcast.10), calls=%async_computation | async-start | bytes 524288 | tf_op jit(solution)/shard_map/all_to_all | solution.py:173
  116.3 4.3 %collective-permute-start.7 = (f32[6,128,128]{2,1,0:T(8,128)S(1)}, f32[6,128,128]{2,1,0:T(8,128)S(1)}, u32[]{:S(2)}, u32[]{:S(2)}) collective-permute-start(f32[6,128,128]{2,1,0:T(8,128)S(1)} %fusion.6), channel_id=1, source_target_pairs={{0,1},{1,0},{2,3},{3,2},{4,5},{5,4},{6,7},{7,6},{8,9},{9,8},{10,11... | collective-permute-start | bytes 1179656 | tf_op jit(solution)/shard_map/ppermute | solution.py:166
  120.6 8.2 %all-to-all-done = f32[64,1,1024]{2,1,0:T(1,128)S(1)} async-done(((f32[64,1,1024]{2,1,0:T(1,128)}), f32[64,1,1024]{2,1,0:T(1,128)S(1)}, u32[]{:S(2)}, u32[]{:S(2)}) %all-to-all-start) | async-done | bytes 262176 | tf_op jit(solution)/shard_map/all_to_all | solution.py:173
  129.0 0.8 broadcast_in_dim.4
  129.8 4.6 %all-to-all-start.1 = ((f32[64,1,1024]{2,1,0:T(1,128)}), f32[64,1,1024]{2,1,0:T(1,128)S(1)}, u32[]{:S(2)}, u32[]{:S(2)}) async-start(f32[64,1,1024]{2,1,0:T(1,128)} %broadcast_in_dim.4), calls=%async_computation.1 | async-start | bytes 524288 | tf_op jit(solution)/shard_map/all_to_all | solution.py:174
  134.5 4.1 %collective-permute-start.8 = (f32[6,128,128]{2,1,0:T(8,128)S(1)}, f32[6,128,128]{2,1,0:T(8,128)S(1)}, u32[]{:S(2)}, u32[]{:S(2)}) collective-permute-start(f32[6,128,128]{2,1,0:T(8,128)S(1)} %add.136), channel_id=1, source_target_pairs={{0,2},{1,3},{2,0},{3,1},{4,6},{5,7},{6,4},{7,5},{8,10},{9,11},{10,... | collective-permute-start | bytes 1179656 | tf_op jit(solution)/shard_map/ppermute | solution.py:166
  138.5 6.2 %collective-permute-done.8 = f32[6,128,128]{2,1,0:T(8,128)S(1)} collective-permute-done((f32[6,128,128]{2,1,0:T(8,128)S(1)}, f32[6,128,128]{2,1,0:T(8,128)S(1)}, u32[]{:S(2)}, u32[]{:S(2)}) %collective-permute-start.8) | collective-permute-done | bytes 393248 | tf_op jit(solution)/shard_map/ppermute | solution.py:166
  144.8 2.2 all-to-all-done.1
  147.0 3.9 %collective-permute-start.9 = (f32[6,128,128]{2,1,0:T(8,128)S(1)}, f32[6,128,128]{2,1,0:T(8,128)S(1)}, u32[]{:S(2)}, u32[]{:S(2)}) collective-permute-start(f32[6,128,128]{2,1,0:T(8,128)S(1)} %add.137), channel_id=1, source_target_pairs={{0,4},{1,5},{2,6},{3,7},{4,0},{5,1},{6,2},{7,3},{8,12},{9,13},{10,... | collective-permute-start | bytes 1179656 | tf_op jit(solution)/shard_map/ppermute | solution.py:166
  150.9 6.1 %collective-permute-done.9 = f32[6,128,128]{2,1,0:T(8,128)S(1)} collective-permute-done((f32[6,128,128]{2,1,0:T(8,128)S(1)}, f32[6,128,128]{2,1,0:T(8,128)S(1)}, u32[]{:S(2)}, u32[]{:S(2)}) %collective-permute-start.9) | collective-permute-done | bytes 393248 | tf_op jit(solution)/shard_map/ppermute | solution.py:166
  157.2 4.2 %collective-permute-start.10 = (f32[2,3,128,128]{3,2,1,0:T(8,128)S(1)}, f32[2,3,128,128]{3,2,1,0:T(8,128)S(1)}, u32[]{:S(2)}, u32[]{:S(2)}) collective-permute-start(f32[2,3,128,128]{3,2,1,0:T(8,128)S(1)} %fusion.17), channel_id=1, source_target_pairs={{0,504},{8,0},{16,8},{24,16},{32,24},{40,32},{48,40},{56,48},{64,5... | collective-permute-start | bytes 1179656 | tf_op jit(solution)/shard_map/ppermute | solution.py:20
  161.4 4.7 %collective-permute-done.10 = f32[2,3,128,128]{3,2,1,0:T(8,128)S(1)} collective-permute-done((f32[2,3,128,128]{3,2,1,0:T(8,128)S(1)}, f32[2,3,128,128]{3,2,1,0:T(8,128)S(1)}, u32[]{:S(2)}, u32[]{:S(2)}) %collective-permute-start.10) | collective-permute-done | bytes 393248 | tf_op jit(solution)/shard_map/ppermute | solution.py:20
  166.1 3.0 %collective-permute-start.11 = (f32[2,3,128,256]{3,2,1,0:T(8,128)S(1)}, f32[2,3,128,256]{3,2,1,0:T(8,128)S(1)}, u32[]{:S(2)}, u32[]{:S(2)}) collective-permute-start(f32[2,3,128,256]{3,2,1,0:T(8,128)S(1)} %pad_maximum_fusion.2), channel_id=1, source_target_pairs={{0,448},{8,456},{16,464},{24,472},{32,480},{40,488},{48,496},{56,5... | collective-permute-start | bytes 2359304 | tf_op jit(solution)/shard_map/ppermute | solution.py:20
  169.2 0.7 multiply_subtract_fusion.1.probe_ref
  169.9 10.6 %collective-permute-done.11 = f32[2,3,128,256]{3,2,1,0:T(8,128)S(1)} collective-permute-done((f32[2,3,128,256]{3,2,1,0:T(8,128)S(1)}, f32[2,3,128,256]{3,2,1,0:T(8,128)S(1)}, u32[]{:S(2)}, u32[]{:S(2)}) %collective-permute-start.11) | collective-permute-done | bytes 786464 | tf_op jit(solution)/shard_map/ppermute | solution.py:20
  180.5 1.1 fusion.1.cells_ref
  181.7 16.3 %shard_map.86 = (f32[2,3,128,128]{3,2,1,0:T(8,128)}, f32[2,2,128,128]{3,2,1,0:T(8,128)}) custom-call(f32[2,3,128,128]{3,2,1,0:T(8,128)} %fusion.1.cells_ref, f32[2,2,128,128]{3,2,1,0:T(8,128)} %multiply_subtract_fusion.1.probe_ref, f32[128,128]{1,0:T(8,128)} %bitcast.52, f32[1,1]{1,0:T(1,128)} %bitcast.5.weight_ref, f32[4,128,128]{2,1,0:T(8,128)} %pad_maximum_fusion.5.tab_ref), custom_call_target="tpu_custom_call" | custom-call | flops 1342177280 | bytes 1441792 | tf_op jit(solution)/shard_map/pallas_call | solution.py:147
  198.0 9.7 %collective-permute-start.12 = (f32[2,2,128,128]{3,2,1,0:T(8,128)}, f32[2,2,128,128]{3,2,1,0:T(8,128)S(1)}, u32[]{:S(2)}, u32[]{:S(2)}) collective-permute-start(f32[2,2,128,128]{3,2,1,0:T(8,128)} %get-tuple-element.34), channel_id=1, source_target_pairs={{0,1},{1,0},{2,3},{3,2},{4,5},{5,4},{6,7},{7,6},{8,9},{9,8},{10,11... | collective-permute-start | bytes 786440 | tf_op jit(solution)/shard_map/ppermute | solution.py:166
  207.9 4.5 %dynamic_update_slice.7 = f32[2,3,256,256]{3,2,1,0:T(8,128)S(1)} dynamic-update-slice(f32[2,3,256,256]{3,2,1,0:T(8,128)S(1)} %broadcast.215, f32[2,3,128,128]{3,2,1,0:T(8,128)S(1)} %copy-done.3, s32[]{:T(128)} %constant.13.clone.1, s32[]{:T(128)} %constant.13.clone.1, s32[]{:T(128)S(6)} %select_n.46, s32[]{:T(128)S(6)} %select_n.47) | dynamic-update-slice | bytes 786436 | tf_op jit(solution)/shard_map/dynamic_update_slice | solution.py:220
  212.6 0.9 copy-done.6
  213.5 1.9 collective-permute-start.13
  215.5 3.6 %collective-permute-start.14 = (f32[2,2,128,128]{3,2,1,0:T(8,128)S(1)}, f32[2,2,128,128]{3,2,1,0:T(8,128)S(1)}, u32[]{:S(2)}, u32[]{:S(2)}) collective-permute-start(f32[2,2,128,128]{3,2,1,0:T(8,128)S(1)} %add.139), channel_id=1, source_target_pairs={{0,2},{1,3},{2,0},{3,1},{4,6},{5,7},{6,4},{7,5},{8,10},{9,11},{10,... | collective-permute-start | bytes 786440 | tf_op jit(solution)/shard_map/ppermute | solution.py:166
  219.1 6.1 %collective-permute-done.14 = f32[2,2,128,128]{3,2,1,0:T(8,128)S(1)} collective-permute-done((f32[2,2,128,128]{3,2,1,0:T(8,128)S(1)}, f32[2,2,128,128]{3,2,1,0:T(8,128)S(1)}, u32[]{:S(2)}, u32[]{:S(2)}) %collective-permute-start.14) | collective-permute-done | bytes 262176 | tf_op jit(solution)/shard_map/ppermute | solution.py:166
  225.3 10.7 %collective-permute-done.13 = f32[12,128,128]{2,1,0:T(8,128)S(1)} collective-permute-done((f32[12,128,128]{2,1,0:T(8,128)S(1)}, f32[12,128,128]{2,1,0:T(8,128)S(1)}, u32[]{:S(2)}, u32[]{:S(2)}) %collective-permute-start.13) | collective-permute-done | bytes 786464 | tf_op jit(solution)/shard_map/ppermute | solution.py:20
  236.0 2.0 collective-permute-start.15
  238.1 3.7 %collective-permute-start.16 = (f32[2,2,128,128]{3,2,1,0:T(8,128)S(1)}, f32[2,2,128,128]{3,2,1,0:T(8,128)S(1)}, u32[]{:S(2)}, u32[]{:S(2)}) collective-permute-start(f32[2,2,128,128]{3,2,1,0:T(8,128)S(1)} %add.142), channel_id=1, source_target_pairs={{0,4},{1,5},{2,6},{3,7},{4,0},{5,1},{6,2},{7,3},{8,12},{9,13},{10,... | collective-permute-start | bytes 786440 | tf_op jit(solution)/shard_map/ppermute | solution.py:166
  241.7 6.5 %collective-permute-done.16 = f32[2,2,128,128]{3,2,1,0:T(8,128)S(1)} collective-permute-done((f32[2,2,128,128]{3,2,1,0:T(8,128)S(1)}, f32[2,2,128,128]{3,2,1,0:T(8,128)S(1)}, u32[]{:S(2)}, u32[]{:S(2)}) %collective-permute-start.16) | collective-permute-done | bytes 262176 | tf_op jit(solution)/shard_map/ppermute | solution.py:166
  248.2 0.7 add.144
  249.0 2.6 collective-permute-done.15
  251.6 8.5 %all-to-all-start.2 = ((f32[64,1,1024]{2,1,0:T(1,128)}), f32[64,1,1024]{2,1,0:T(1,128)S(1)}, u32[]{:S(2)}, u32[]{:S(2)}) async-start(f32[64,1,1024]{2,1,0:T(1,128)} %bitcast.17), calls=%async_computation.2 | async-start | bytes 524288 | tf_op jit(solution)/shard_map/all_to_all | solution.py:173
  260.1 4.1 %collective-permute-start.17 = (f32[6,128,128]{2,1,0:T(8,128)S(1)}, f32[6,128,128]{2,1,0:T(8,128)S(1)}, u32[]{:S(2)}, u32[]{:S(2)}) collective-permute-start(f32[6,128,128]{2,1,0:T(8,128)S(1)} %fusion.5), channel_id=1, source_target_pairs={{0,1},{1,0},{2,3},{3,2},{4,5},{5,4},{6,7},{7,6},{8,9},{9,8},{10,11... | collective-permute-start | bytes 1179656 | tf_op jit(solution)/shard_map/ppermute | solution.py:166
  264.2 8.4 %all-to-all-done.2 = f32[64,1,1024]{2,1,0:T(1,128)S(1)} async-done(((f32[64,1,1024]{2,1,0:T(1,128)}), f32[64,1,1024]{2,1,0:T(1,128)S(1)}, u32[]{:S(2)}, u32[]{:S(2)}) %all-to-all-start.2) | async-done | bytes 262176 | tf_op jit(solution)/shard_map/all_to_all | solution.py:173
  272.8 0.8 broadcast_in_dim.5
  273.6 4.6 %all-to-all-start.3 = ((f32[64,1,1024]{2,1,0:T(1,128)}), f32[64,1,1024]{2,1,0:T(1,128)S(1)}, u32[]{:S(2)}, u32[]{:S(2)}) async-start(f32[64,1,1024]{2,1,0:T(1,128)} %broadcast_in_dim.5), calls=%async_computation.3 | async-start | bytes 524288 | tf_op jit(solution)/shard_map/all_to_all | solution.py:174
  278.3 3.1 %collective-permute-start.18 = (f32[6,128,128]{2,1,0:T(8,128)S(1)}, f32[6,128,128]{2,1,0:T(8,128)S(1)}, u32[]{:S(2)}, u32[]{:S(2)}) collective-permute-start(f32[6,128,128]{2,1,0:T(8,128)S(1)} %add.145), channel_id=1, source_target_pairs={{0,2},{1,3},{2,0},{3,1},{4,6},{5,7},{6,4},{7,5},{8,10},{9,11},{10,... | collective-permute-start | bytes 1179656 | tf_op jit(solution)/shard_map/ppermute | solution.py:166
  281.5 5.8 %collective-permute-done.18 = f32[6,128,128]{2,1,0:T(8,128)S(1)} collective-permute-done((f32[6,128,128]{2,1,0:T(8,128)S(1)}, f32[6,128,128]{2,1,0:T(8,128)S(1)}, u32[]{:S(2)}, u32[]{:S(2)}) %collective-permute-start.18) | collective-permute-done | bytes 393248 | tf_op jit(solution)/shard_map/ppermute | solution.py:166
  287.3 3.5 %all-to-all-done.3 = f32[64,1,1024]{2,1,0:T(1,128)S(1)} async-done(((f32[64,1,1024]{2,1,0:T(1,128)}), f32[64,1,1024]{2,1,0:T(1,128)S(1)}, u32[]{:S(2)}, u32[]{:S(2)}) %all-to-all-start.3) | async-done | bytes 262176 | tf_op jit(solution)/shard_map/all_to_all | solution.py:174
  290.8 3.2 %collective-permute-start.19 = (f32[6,128,128]{2,1,0:T(8,128)S(1)}, f32[6,128,128]{2,1,0:T(8,128)S(1)}, u32[]{:S(2)}, u32[]{:S(2)}) collective-permute-start(f32[6,128,128]{2,1,0:T(8,128)S(1)} %add.146), channel_id=1, source_target_pairs={{0,4},{1,5},{2,6},{3,7},{4,0},{5,1},{6,2},{7,3},{8,12},{9,13},{10,... | collective-permute-start | bytes 1179656 | tf_op jit(solution)/shard_map/ppermute | solution.py:166
  294.0 0.7 multiply_subtract_fusion
  294.8 6.0 %collective-permute-done.19 = f32[6,128,128]{2,1,0:T(8,128)S(1)} collective-permute-done((f32[6,128,128]{2,1,0:T(8,128)S(1)}, f32[6,128,128]{2,1,0:T(8,128)S(1)}, u32[]{:S(2)}, u32[]{:S(2)}) %collective-permute-start.19) | collective-permute-done | bytes 393248 | tf_op jit(solution)/shard_map/ppermute | solution.py:166
  301.0 0.8 slice_bitcast_fusion
  (47 shorter events, 2.2 us)
Async XLA Ops:
  0.6 26.6 %copy-start.8 = (s32[1,1,1,2]{3,2,1,0:T(1,128)S(1)}, s32[1,1,1,2]{3,2,1,0:T(1,128)}, u32[]{:S(2)}) copy-start(s32[1,1,1,2]{3,2,1,0:T(1,128)} %param.10) | copy-start | bytes 28
  0.6 43.8 %copy-start = (f32[3,1,128,128]{3,2,1,0:T(8,128)S(1)}, f32[3,1,128,128]{3,2,1,0:T(8,128)}, u32[]{:S(2)}) copy-start(f32[3,1,128,128]{3,2,1,0:T(8,128)} %param.6) | copy-start | bytes 589828
  0.7 43.7 %copy-start.1 = (f32[3,1,128,128]{3,2,1,0:T(8,128)S(1)}, f32[3,1,128,128]{3,2,1,0:T(8,128)}, u32[]{:S(2)}) copy-start(f32[3,1,128,128]{3,2,1,0:T(8,128)} %param.7) | copy-start | bytes 589828
  1.8 22.2 %collective-permute-start = (f32[2,3,128,128]{3,2,1,0:T(8,128)S(1)}, f32[2,3,128,128]{3,2,1,0:T(8,128)S(1)}, u32[]{:S(2)}, u32[]{:S(2)}) collective-permute-start(f32[2,3,128,128]{3,2,1,0:T(8,128)S(1)} %pad_maximum_fusion.4), channel_id=1, source_target_pairs={{0,504},{8,0},{16,8},{24,16},{32,24},{40,32},{48,40},{56,48},{64,5... | collective-permute-start | bytes 1179656 | tf_op jit(solution)/shard_map/ppermute | solution.py:20
  25.0 19.4 %collective-permute-start.1 = (f32[2,3,128,256]{3,2,1,0:T(8,128)S(1)}, f32[2,3,128,256]{3,2,1,0:T(8,128)S(1)}, u32[]{:S(2)}, u32[]{:S(2)}) collective-permute-start(f32[2,3,128,256]{3,2,1,0:T(8,128)S(1)} %pad_maximum_fusion), channel_id=1, source_target_pairs={{0,448},{8,456},{16,464},{24,472},{32,480},{40,488},{48,496},{56,5... | collective-permute-start | bytes 2359304 | tf_op jit(solution)/shard_map/ppermute | solution.py:20
  61.9 4.8 %copy-start.4 = (f32[2,3,128,128]{3,2,1,0:T(8,128)S(1)}, f32[2,3,128,128]{3,2,1,0:T(8,128)}, u32[]{:S(2)}) copy-start(f32[2,3,128,128]{3,2,1,0:T(8,128)} %get-tuple-element.23) | copy-start | bytes 1179652
  61.9 9.5 %collective-permute-start.2 = (f32[2,2,128,128]{3,2,1,0:T(8,128)}, f32[2,2,128,128]{3,2,1,0:T(8,128)S(1)}, u32[]{:S(2)}, u32[]{:S(2)}) collective-permute-start(f32[2,2,128,128]{3,2,1,0:T(8,128)} %get-tuple-element.24), channel_id=1, source_target_pairs={{0,1},{1,0},{2,3},{3,2},{4,5},{5,4},{6,7},{7,6},{8,9},{9,8},{10,11... | collective-permute-start | bytes 786440 | tf_op jit(solution)/shard_map/ppermute | solution.py:166
  71.4 1.0 copy-start.7
  72.3 22.5 %collective-permute-start.3 = (f32[12,128,128]{2,1,0:T(8,128)S(1)}, f32[12,128,128]{2,1,0:T(8,128)S(1)}, u32[]{:S(2)}, u32[]{:S(2)}) collective-permute-start(f32[12,128,128]{2,1,0:T(8,128)S(1)} %pad_maximum_fusion.1), channel_id=1, source_target_pairs={{0,64},{8,72},{16,80},{24,88},{32,96},{40,104},{48,112},{56,120},{... | collective-permute-start | bytes 2359304 | tf_op jit(solution)/shard_map/ppermute | solution.py:20
  74.3 10.0 %collective-permute-start.4 = (f32[2,2,128,128]{3,2,1,0:T(8,128)S(1)}, f32[2,2,128,128]{3,2,1,0:T(8,128)S(1)}, u32[]{:S(2)}, u32[]{:S(2)}) collective-permute-start(f32[2,2,128,128]{3,2,1,0:T(8,128)S(1)} %add.130), channel_id=1, source_target_pairs={{0,2},{1,3},{2,0},{3,1},{4,6},{5,7},{6,4},{7,5},{8,10},{9,11},{10,... | collective-permute-start | bytes 786440 | tf_op jit(solution)/shard_map/ppermute | solution.py:166
  94.9 15.7 %collective-permute-start.5 = (f32[6,128,128]{2,1,0:T(8,128)S(1)}, f32[6,128,128]{2,1,0:T(8,128)S(1)}, u32[]{:S(2)}, u32[]{:S(2)}) collective-permute-start(f32[6,128,128]{2,1,0:T(8,128)S(1)} %slice_add_fusion.2), channel_id=1, source_target_pairs={{0,8},{8,16},{16,24},{24,32},{32,40},{40,48},{48,56},{56,64},{64,7... | collective-permute-start | bytes 1179656 | tf_op jit(solution)/shard_map/ppermute | solution.py:20
  96.8 10.7 %collective-permute-start.6 = (f32[2,2,128,128]{3,2,1,0:T(8,128)S(1)}, f32[2,2,128,128]{3,2,1,0:T(8,128)S(1)}, u32[]{:S(2)}, u32[]{:S(2)}) collective-permute-start(f32[2,2,128,128]{3,2,1,0:T(8,128)S(1)} %add.133), channel_id=1, source_target_pairs={{0,4},{1,5},{2,6},{3,7},{4,0},{5,1},{6,2},{7,3},{8,12},{9,13},{10,... | collective-permute-start | bytes 786440 | tf_op jit(solution)/shard_map/ppermute | solution.py:166
  110.6 18.2 %all-to-all-start = ((f32[64,1,1024]{2,1,0:T(1,128)}), f32[64,1,1024]{2,1,0:T(1,128)S(1)}, u32[]{:S(2)}, u32[]{:S(2)}) async-start(f32[64,1,1024]{2,1,0:T(1,128)} %bitcast.10), calls=%async_computation | async-start | bytes 524288 | tf_op jit(solution)/shard_map/all_to_all | solution.py:173
  116.3 18.1 %collective-permute-start.7 = (f32[6,128,128]{2,1,0:T(8,128)S(1)}, f32[6,128,128]{2,1,0:T(8,128)S(1)}, u32[]{:S(2)}, u32[]{:S(2)}) collective-permute-start(f32[6,128,128]{2,1,0:T(8,128)S(1)} %fusion.6), channel_id=1, source_target_pairs={{0,1},{1,0},{2,3},{3,2},{4,5},{5,4},{6,7},{7,6},{8,9},{9,8},{10,11... | collective-permute-start | bytes 1179656 | tf_op jit(solution)/shard_map/ppermute | solution.py:166
  129.8 17.2 %all-to-all-start.1 = ((f32[64,1,1024]{2,1,0:T(1,128)}), f32[64,1,1024]{2,1,0:T(1,128)S(1)}, u32[]{:S(2)}, u32[]{:S(2)}) async-start(f32[64,1,1024]{2,1,0:T(1,128)} %broadcast_in_dim.4), calls=%async_computation.1 | async-start | bytes 524288 | tf_op jit(solution)/shard_map/all_to_all | solution.py:174
  134.5 10.3 %collective-permute-start.8 = (f32[6,128,128]{2,1,0:T(8,128)S(1)}, f32[6,128,128]{2,1,0:T(8,128)S(1)}, u32[]{:S(2)}, u32[]{:S(2)}) collective-permute-start(f32[6,128,128]{2,1,0:T(8,128)S(1)} %add.136), channel_id=1, source_target_pairs={{0,2},{1,3},{2,0},{3,1},{4,6},{5,7},{6,4},{7,5},{8,10},{9,11},{10,... | collective-permute-start | bytes 1179656 | tf_op jit(solution)/shard_map/ppermute | solution.py:166
  147.0 10.0 %collective-permute-start.9 = (f32[6,128,128]{2,1,0:T(8,128)S(1)}, f32[6,128,128]{2,1,0:T(8,128)S(1)}, u32[]{:S(2)}, u32[]{:S(2)}) collective-permute-start(f32[6,128,128]{2,1,0:T(8,128)S(1)} %add.137), channel_id=1, source_target_pairs={{0,4},{1,5},{2,6},{3,7},{4,0},{5,1},{6,2},{7,3},{8,12},{9,13},{10,... | collective-permute-start | bytes 1179656 | tf_op jit(solution)/shard_map/ppermute | solution.py:166
  157.1 12.1 %copy-start.5 = (f32[2,2,128,128]{3,2,1,0:T(8,128)S(1)}, f32[2,2,128,128]{3,2,1,0:T(8,128)}, u32[]{:S(2)}) copy-start(f32[2,2,128,128]{3,2,1,0:T(8,128)} %probe_ref.1) | copy-start | bytes 786436
  157.2 8.9 %collective-permute-start.10 = (f32[2,3,128,128]{3,2,1,0:T(8,128)S(1)}, f32[2,3,128,128]{3,2,1,0:T(8,128)S(1)}, u32[]{:S(2)}, u32[]{:S(2)}) collective-permute-start(f32[2,3,128,128]{3,2,1,0:T(8,128)S(1)} %fusion.17), channel_id=1, source_target_pairs={{0,504},{8,0},{16,8},{24,16},{32,24},{40,32},{48,40},{56,48},{64,5... | collective-permute-start | bytes 1179656 | tf_op jit(solution)/shard_map/ppermute | solution.py:20
  166.1 14.4 %collective-permute-start.11 = (f32[2,3,128,256]{3,2,1,0:T(8,128)S(1)}, f32[2,3,128,256]{3,2,1,0:T(8,128)S(1)}, u32[]{:S(2)}, u32[]{:S(2)}) collective-permute-start(f32[2,3,128,256]{3,2,1,0:T(8,128)S(1)} %pad_maximum_fusion.2), channel_id=1, source_target_pairs={{0,448},{8,456},{16,464},{24,472},{32,480},{40,488},{48,496},{56,5... | collective-permute-start | bytes 2359304 | tf_op jit(solution)/shard_map/ppermute | solution.py:20
  198.0 9.9 %copy-start.3 = (f32[2,3,128,128]{3,2,1,0:T(8,128)S(1)}, f32[2,3,128,128]{3,2,1,0:T(8,128)}, u32[]{:S(2)}) copy-start(f32[2,3,128,128]{3,2,1,0:T(8,128)} %get-tuple-element.33) | copy-start | bytes 1179652
  198.0 14.6 %collective-permute-start.12 = (f32[2,2,128,128]{3,2,1,0:T(8,128)}, f32[2,2,128,128]{3,2,1,0:T(8,128)S(1)}, u32[]{:S(2)}, u32[]{:S(2)}) collective-permute-start(f32[2,2,128,128]{3,2,1,0:T(8,128)} %get-tuple-element.34), channel_id=1, source_target_pairs={{0,1},{1,0},{2,3},{3,2},{4,5},{5,4},{6,7},{7,6},{8,9},{9,8},{10,11... | collective-permute-start | bytes 786440 | tf_op jit(solution)/shard_map/ppermute | solution.py:166
  212.5 1.0 copy-start.6
  213.5 22.5 %collective-permute-start.13 = (f32[12,128,128]{2,1,0:T(8,128)S(1)}, f32[12,128,128]{2,1,0:T(8,128)S(1)}, u32[]{:S(2)}, u32[]{:S(2)}) collective-permute-start(f32[12,128,128]{2,1,0:T(8,128)S(1)} %pad_maximum_fusion.3), channel_id=1, source_target_pairs={{0,64},{8,72},{16,80},{24,88},{32,96},{40,104},{48,112},{56,120},{... | collective-permute-start | bytes 2359304 | tf_op jit(solution)/shard_map/ppermute | solution.py:20
  215.5 9.8 %collective-permute-start.14 = (f32[2,2,128,128]{3,2,1,0:T(8,128)S(1)}, f32[2,2,128,128]{3,2,1,0:T(8,128)S(1)}, u32[]{:S(2)}, u32[]{:S(2)}) collective-permute-start(f32[2,2,128,128]{3,2,1,0:T(8,128)S(1)} %add.139), channel_id=1, source_target_pairs={{0,2},{1,3},{2,0},{3,1},{4,6},{5,7},{6,4},{7,5},{8,10},{9,11},{10,... | collective-permute-start | bytes 786440 | tf_op jit(solution)/shard_map/ppermute | solution.py:166
  236.0 15.5 %collective-permute-start.15 = (f32[6,128,128]{2,1,0:T(8,128)S(1)}, f32[6,128,128]{2,1,0:T(8,128)S(1)}, u32[]{:S(2)}, u32[]{:S(2)}) collective-permute-start(f32[6,128,128]{2,1,0:T(8,128)S(1)} %slice_add_fusion), channel_id=1, source_target_pairs={{0,8},{8,16},{16,24},{24,32},{32,40},{40,48},{48,56},{56,64},{64,7... | collective-permute-start | bytes 1179656 | tf_op jit(solution)/shard_map/ppermute | solution.py:20
  238.1 10.2 %collective-permute-start.16 = (f32[2,2,128,128]{3,2,1,0:T(8,128)S(1)}, f32[2,2,128,128]{3,2,1,0:T(8,128)S(1)}, u32[]{:S(2)}, u32[]{:S(2)}) collective-permute-start(f32[2,2,128,128]{3,2,1,0:T(8,128)S(1)} %add.142), channel_id=1, source_target_pairs={{0,4},{1,5},{2,6},{3,7},{4,0},{5,1},{6,2},{7,3},{8,12},{9,13},{10,... | collective-permute-start | bytes 786440 | tf_op jit(solution)/shard_map/ppermute | solution.py:166
  251.6 20.9 %all-to-all-start.2 = ((f32[64,1,1024]{2,1,0:T(1,128)}), f32[64,1,1024]{2,1,0:T(1,128)S(1)}, u32[]{:S(2)}, u32[]{:S(2)}) async-start(f32[64,1,1024]{2,1,0:T(1,128)} %bitcast.17), calls=%async_computation.2 | async-start | bytes 524288 | tf_op jit(solution)/shard_map/all_to_all | solution.py:173
  260.1 18.1 %collective-permute-start.17 = (f32[6,128,128]{2,1,0:T(8,128)S(1)}, f32[6,128,128]{2,1,0:T(8,128)S(1)}, u32[]{:S(2)}, u32[]{:S(2)}) collective-permute-start(f32[6,128,128]{2,1,0:T(8,128)S(1)} %fusion.5), channel_id=1, source_target_pairs={{0,1},{1,0},{2,3},{3,2},{4,5},{5,4},{6,7},{7,6},{8,9},{9,8},{10,11... | collective-permute-start | bytes 1179656 | tf_op jit(solution)/shard_map/ppermute | solution.py:166
  272.8 21.3 %copy-start.2 = (f32[2,2,128,128]{3,2,1,0:T(8,128)S(1)}, f32[2,2,128,128]{3,2,1,0:T(8,128)}, u32[]{:S(2)}) copy-start(f32[2,2,128,128]{3,2,1,0:T(8,128)} %multiply_subtract_fusion.1.probe_ref) | copy-start | bytes 786436
  273.6 17.2 %all-to-all-start.3 = ((f32[64,1,1024]{2,1,0:T(1,128)}), f32[64,1,1024]{2,1,0:T(1,128)S(1)}, u32[]{:S(2)}, u32[]{:S(2)}) async-start(f32[64,1,1024]{2,1,0:T(1,128)} %broadcast_in_dim.5), calls=%async_computation.3 | async-start | bytes 524288 | tf_op jit(solution)/shard_map/all_to_all | solution.py:174
  278.3 8.9 %collective-permute-start.18 = (f32[6,128,128]{2,1,0:T(8,128)S(1)}, f32[6,128,128]{2,1,0:T(8,128)S(1)}, u32[]{:S(2)}, u32[]{:S(2)}) collective-permute-start(f32[6,128,128]{2,1,0:T(8,128)S(1)} %add.145), channel_id=1, source_target_pairs={{0,2},{1,3},{2,0},{3,1},{4,6},{5,7},{6,4},{7,5},{8,10},{9,11},{10,... | collective-permute-start | bytes 1179656 | tf_op jit(solution)/shard_map/ppermute | solution.py:166
  290.8 10.0 %collective-permute-start.19 = (f32[6,128,128]{2,1,0:T(8,128)S(1)}, f32[6,128,128]{2,1,0:T(8,128)S(1)}, u32[]{:S(2)}, u32[]{:S(2)}) collective-permute-start(f32[6,128,128]{2,1,0:T(8,128)S(1)} %add.146), channel_id=1, source_target_pairs={{0,4},{1,5},{2,6},{3,7},{4,0},{5,1},{6,2},{7,3},{8,12},{9,13},{10,... | collective-permute-start | bytes 1179656 | tf_op jit(solution)/shard_map/ppermute | solution.py:166

commit v6 on v5

--- a/solution.py
+++ b/solution.py
@@ -78,7 +78,22 @@
 
 
 def slot_kernel(cells_ref, probe_ref, target_ref, weight_ref, tab_ref, gcells_ref, gprobe_ref):
-    cosine, sine_table, kern_real, kern_imag = (tab_ref[0], tab_ref[1], tab_ref[2], tab_ref[3])
+    side = target_ref.shape[0]
+    mode_count = probe_ref.shape[0]
+    depth_count = cells_ref.shape[1]
+    wide = lambda a: jnp.concatenate([a] * mode_count, axis=1)
+    cosine, sine_table = (tab_ref[0], tab_ref[1])
+    kern = (wide(tab_ref[2]), wide(tab_ref[3]))
+    zero = jnp.zeros_like(cosine)
+
+    def block(a):
+        rows = [
+            jnp.concatenate([a if j == i else zero for j in range(mode_count)], axis=1)
+            for i in range(mode_count)
+        ]
+        return jnp.concatenate(rows, axis=0)
+
+    cos_block, sin_block = (block(cosine), block(sine_table))
 
     def dot(a, b):
         return jnp.dot(a, b, precision=lax.Precision.HIGHEST, preferred_element_type=jnp.float32)
@@ -86,12 +101,12 @@
     def forward(xr, xi):
         lr = dot(cosine, xr) + dot(sine_table, xi)
         li = dot(cosine, xi) - dot(sine_table, xr)
-        return (dot(lr, cosine) + dot(li, sine_table), dot(li, cosine) - dot(lr, sine_table))
+        return (dot(lr, cos_block) + dot(li, sin_block), dot(li, cos_block) - dot(lr, sin_block))
 
     def inverse(xr, xi):
         lr = dot(cosine, xr) - dot(sine_table, xi)
         li = dot(cosine, xi) + dot(sine_table, xr)
-        return (dot(lr, cosine) - dot(li, sine_table), dot(li, cosine) + dot(lr, sine_table))
+        return (dot(lr, cos_block) - dot(li, sin_block), dot(li, cos_block) + dot(lr, sin_block))
 
     def mul(a, b):
         return (a[0] * b[0] - a[1] * b[1], a[0] * b[1] + a[1] * b[0])
@@ -99,45 +114,39 @@
     def mul_conj(a, b):
         return (a[0] * b[0] + a[1] * b[1], a[1] * b[0] - a[0] * b[1])
 
-    kern = (kern_real, kern_imag)
+    def fold(a):
+        total = a[:, :side]
+        for m in range(1, mode_count):
+            total = total + a[:, m * side : (m + 1) * side]
+        return total
+
     propagate = lambda x: inverse(*mul(forward(*x), kern))
     propagate_adjoint = lambda x: inverse(*mul_conj(forward(*x), kern))
-    depth_count = cells_ref.shape[1]
-    mode_count = probe_ref.shape[0]
-    layers = [(cells_ref[0, d], cells_ref[1, d]) for d in range(depth_count)]
-    saved = []
-    intensity = None
+    layers = [(wide(cells_ref[0, d]), wide(cells_ref[1, d])) for d in range(depth_count)]
+    wave = (
+        jnp.concatenate([probe_ref[m, 0] for m in range(mode_count)], axis=1),
+        jnp.concatenate([probe_ref[m, 1] for m in range(mode_count)], axis=1),
+    )
+    inputs = []
+    for d in range(depth_count):
+        inputs.append(wave)
+        wave = mul(wave, layers[d])
+        if d < depth_count - 1:
+            wave = propagate(wave)
+    far = forward(*wave)
+    intensity = fold(far[0] * far[0] + far[1] * far[1])
+    residual = wide(weight_ref[...] * (intensity - target_ref[...]))
+    grad = inverse(2.0 * residual * far[0], 2.0 * residual * far[1])
+    for d in reversed(range(depth_count)):
+        term = mul_conj(grad, inputs[d])
+        gcells_ref[0, d] = fold(term[0])
+        gcells_ref[1, d] = fold(term[1])
+        grad = mul_conj(grad, layers[d])
+        if d > 0:
+            grad = propagate_adjoint(grad)
     for m in range(mode_count):
-        wave = (probe_ref[m, 0], probe_ref[m, 1])
-        inputs = []
-        for d in range(depth_count):
-            inputs.append(wave)
-            wave = mul(wave, layers[d])
-            if d < depth_count - 1:
-                wave = propagate(wave)
-        far = forward(*wave)
-        saved.append((inputs, far))
-        power = far[0] * far[0] + far[1] * far[1]
-        intensity = power if intensity is None else intensity + power
-    residual = weight_ref[...] * (intensity - target_ref[...])
-    layer_grads = [None] * depth_count
-    for m in range(mode_count):
-        inputs, far = saved[m]
-        grad = inverse(2.0 * residual * far[0], 2.0 * residual * far[1])
-        for d in reversed(range(depth_count)):
-            term = mul_conj(grad, inputs[d])
-            if layer_grads[d] is None:
-                layer_grads[d] = term
-            else:
-                layer_grads[d] = (layer_grads[d][0] + term[0], layer_grads[d][1] + term[1])
-            grad = mul_conj(grad, layers[d])
-            if d > 0:
-                grad = propagate_adjoint(grad)
-        gprobe_ref[m, 0] = grad[0]
-        gprobe_ref[m, 1] = grad[1]
-    for d in range(depth_count):
-        gcells_ref[0, d] = layer_grads[d][0]
-        gcells_ref[1, d] = layer_grads[d][1]
+        gprobe_ref[m, 0] = grad[0][:, m * side : (m + 1) * side]
+        gprobe_ref[m, 1] = grad[1][:, m * side : (m + 1) * side]
 
 
 def slot_grad(patch_cells, mode_values, target, weight, tables):
@@ -220,28 +229,18 @@
             grad_canvas = lax.dynamic_update_slice(grad_canvas, current + grad_patch, starts)
             grad_probe = grad_probe + grad_modes
         planes = lambda a: a.reshape(-1, block_side, block_side)
+        probe_partial = a2a_sum(xor_sum(grad_probe, "scan"), "tile")
         sent_down = jnp.concatenate(
             [
                 planes(grad_canvas[:, :, block_side:, :block_side]),
                 planes(grad_canvas[:, :, block_side:, block_side:]),
             ]
         )
-        pair = lambda a, b: lax.optimization_barrier((a, b))
-        probe_partial = xor_sum(grad_probe, "scan", [1])
-        sent_down, probe_partial = pair(sent_down, probe_partial)
         came_down = shifted(sent_down, "tile", GRID)
-        probe_partial = xor_sum(probe_partial, "scan", [2])
         own_part = planes(grad_canvas[:, :, :block_side, :block_side]) + came_down[:parts]
         right_side = planes(grad_canvas[:, :, :block_side, block_side:]) + came_down[parts:]
-        right_side, probe_partial = pair(right_side, probe_partial)
-        came_left = shifted(right_side, "tile", 1)
-        probe_partial = xor_sum(probe_partial, "scan", [4])
-        own_part = own_part + came_left
-        own_part, probe_partial = pair(own_part, probe_partial)
-        probe_partial = a2a_sum(probe_partial, "tile")
-        own_part = xor_sum(own_part, "scan", [1, 2])
-        own_part, probe_partial = pair(own_part, probe_partial)
-        grad_total = xor_sum(own_part, "scan", [4]).reshape(obj_state.shape)
+        own_part = own_part + shifted(right_side, "tile", 1)
+        grad_total = xor_sum(own_part, "scan").reshape(obj_state.shape)
         pending = probe_partial
         obj_state = obj_state - object_rate / (slot_count * group_count) * grad_total
     return (obj_state[0][:, None], obj_state[1][:, None], probe_modes)

time: 307 us -> 288 us (0.938)
  waiting for transfers between devices: 133 us -> 101 us
  blocking collectives: 0 us -> 19.5 us
  Pallas kernels: 32.7 us -> 28.9 us
    ppermute x12, waiting for transfers between devices: 50.8 us -> 28.4 us  [xor_sum(): lax.ppermute(values, axis, [(i, i ^ step) for i in range(size)])]
    all_to_all x0 -> x1, blocking collectives: none -> 19.5 us  [a2a_sum(): lax.all_to_all(jnp.broadcast_to(part, flat.shape), axis, 0, 0, tiled=True)]
    all_to_all x2, waiting for transfers between devices: 16.6 us -> 9.27 us  [a2a_sum(): lax.all_to_all(flat, axis, 0, 0, tiled=True)]
    ppermute x8, waiting for transfers between devices: 60 us -> 54.9 us  [shifted(): lax.ppermute(shard, axis, [(i, (i + by) % size) for i in range(size)])]
    ppermute x12, starting transfers between devices: 51.1 us -> 47 us  [xor_sum(): lax.ppermute(values, axis, [(i, i ^ step) for i in range(size)])]
    ppermute x8, starting transfers between devices: 31.6 us -> 35.7 us  [shifted(): lax.ppermute(shard, axis, [(i, (i + by) % size) for i in range(size)])]
    pallas_call x2, Pallas kernels: 32.7 us -> 28.9 us  [slot_grad(): pl.pallas_call(slot_kernel, out_shape=(jax.ShapeDtypeStruct(patch_cells.s...]
    all_to_all x2 -> x1, waiting for transfers between devices: 5.73 us -> 8.62 us  [a2a_sum(): lax.all_to_all(jnp.broadcast_to(part, flat.shape), axis, 0, 0, tiled=True)]
  transfers between devices with their start and end apart: 24 -> 23, of which waited for: 20 -> 15; matrix products, arithmetic and copies ran while one was open for 6% -> 3% of each run, Pallas kernels for 0% -> 0%
where the time goes in v6:
time: 288 us; the launch traced here: 285 us
  starting transfers between devices  106 us (37%)
  waiting for transfers between devices  101 us (35%)
  Pallas kernels  28.9 us (10%)
  blocking collectives  19.5 us (7%)
  local copies, waits for them, and re-layouts  12.7 us (4%)
  other arithmetic  11.4 us (4%)
  between operations  5.66 us (2%)
    ppermute x8, waiting for transfers between devices, shifted(): lax.ppermute(shard, axis, [(i, (i + by) % size) for i in range(size)])  54.9 us
    ppermute x12, starting transfers between devices, xor_sum(): lax.ppermute(values, axis, [(i, i ^ step) for i in range(size)])  47 us
    ppermute x8, starting transfers between devices, shifted(): lax.ppermute(shard, axis, [(i, (i + by) % size) for i in range(size)])  35.7 us
    pallas_call x2, Pallas kernels, slot_grad(): pl.pallas_call(slot_kernel, out_shape=(jax.ShapeDtypeStruct(patch_cells.s...  28.9 us
    ppermute x12, waiting for transfers between devices, xor_sum(): lax.ppermute(values, axis, [(i, i ^ step) for i in range(size)])  28.4 us
    all_to_all x1, blocking collectives, a2a_sum(): lax.all_to_all(jnp.broadcast_to(part, flat.shape), axis, 0, 0, tiled=True)  19.5 us
    all_to_all x2, starting transfers between devices, a2a_sum(): lax.all_to_all(flat, axis, 0, 0, tiled=True)  12.8 us
    all_to_all x1, starting transfers between devices, a2a_sum(): lax.all_to_all(jnp.broadcast_to(part, flat.shape), axis, 0, 0, tiled=True)  10.3 us
  transfers between devices with their start and end apart: 23, of which 15 were waited for; matrix products, arithmetic and copies ran while one was open for 3% of the time, Pallas kernels for 0%

profile of v6, /device:TPU:1, one launch (start us, length us, event | category | flops | bytes accessed | tf_op | source)
XLA Modules:
  0.0 285.2 jit_solution(4457894853028803201)
XLA Ops:
  0.7 1.1 pad_maximum_fusion.4
  1.8 14.4 %collective-permute-start = (f32[2,3,128,128]{3,2,1,0:T(8,128)S(1)}, f32[2,3,128,128]{3,2,1,0:T(8,128)S(1)}, u32[]{:S(2)}, u32[]{:S(2)}) collective-permute-start(f32[2,3,128,128]{3,2,1,0:T(8,128)S(1)} %pad_maximum_fusion.4), channel_id=1, source_target_pairs={{0,504},{8,0},{16,8},{24,16},{32,24},{40,32},{48,40},{56,48},{64,5... | collective-permute-start | bytes 1179656 | tf_op jit(solution)/shard_map/ppermute | solution.py:20
  16.2 7.8 %collective-permute-done = f32[2,3,128,128]{3,2,1,0:T(8,128)S(1)} collective-permute-done((f32[2,3,128,128]{3,2,1,0:T(8,128)S(1)}, f32[2,3,128,128]{3,2,1,0:T(8,128)S(1)}, u32[]{:S(2)}, u32[]{:S(2)}) %collective-permute-start) | collective-permute-done | bytes 393248 | tf_op jit(solution)/shard_map/ppermute | solution.py:20
  23.9 1.1 pad_maximum_fusion
  25.0 2.2 collective-permute-start.1
  27.2 0.6 fusion.20
  32.3 0.3 sine_multiply_fusion
  32.6 0.3 fusion.11
  32.9 0.7 pad_maximum_fusion.5.tab_ref
  33.7 10.7 %collective-permute-done.1 = f32[2,3,128,256]{3,2,1,0:T(8,128)S(1)} collective-permute-done((f32[2,3,128,256]{3,2,1,0:T(8,128)S(1)}, f32[2,3,128,256]{3,2,1,0:T(8,128)S(1)}, u32[]{:S(2)}, u32[]{:S(2)}) %collective-permute-start.1) | collective-permute-done | bytes 786464 | tf_op jit(solution)/shard_map/ppermute | solution.py:20
  44.4 1.1 fusion.4.cells_ref
  45.5 14.4 %shard_map.85 = (f32[2,3,128,128]{3,2,1,0:T(8,128)}, f32[2,2,128,128]{3,2,1,0:T(8,128)}) custom-call(f32[2,3,128,128]{3,2,1,0:T(8,128)} %fusion.4.cells_ref, f32[2,2,128,128]{3,2,1,0:T(8,128)} %probe_ref.1, f32[128,128]{1,0:T(8,128)} %bitcast.51, f32[1,1]{1,0:T(1,128)} %bitcast.5.weight_ref, f32[4,128,128]{2,1,0:T(8,128)} %pad_maximum_fusion.5.tab_ref), custom_call_target="tpu_custom_call" | custom-call | flops 1342177280 | bytes 1441792 | tf_op jit(solution)/shard_map/pallas_call | solution.py:156
  60.1 0.9 copy-done.4
  61.0 4.0 %dynamic_update_slice.6 = f32[2,3,256,256]{3,2,1,0:T(8,128)S(1)} dynamic-update-slice(f32[2,3,256,256]{3,2,1,0:T(8,128)S(1)} %broadcast.218.clone, f32[2,3,128,128]{3,2,1,0:T(8,128)S(1)} %copy-done.4, s32[]{:T(128)} %constant.13.clone.1, s32[]{:T(128)} %constant.13.clone.1, s32[]{:T(128)S(6)} %select_n.46, s32[]{:T(128)S(6)} %select_n.47) | dynamic-update-slice | bytes 786436 | tf_op jit(solution)/shard_map/dynamic_update_slice | solution.py:229
  65.2 1.9 collective-permute-start.2
  67.2 17.6 %collective-permute-done.2 = f32[12,128,128]{2,1,0:T(8,128)S(1)} collective-permute-done((f32[12,128,128]{2,1,0:T(8,128)S(1)}, f32[12,128,128]{2,1,0:T(8,128)S(1)}, u32[]{:S(2)}, u32[]{:S(2)}) %collective-permute-start.2) | collective-permute-done | bytes 786464 | tf_op jit(solution)/shard_map/ppermute | solution.py:20
  84.8 2.1 collective-permute-start.3
  86.9 11.3 %collective-permute-done.3 = f32[6,128,128]{2,1,0:T(8,128)S(1)} collective-permute-done((f32[6,128,128]{2,1,0:T(8,128)S(1)}, f32[6,128,128]{2,1,0:T(8,128)S(1)}, u32[]{:S(2)}, u32[]{:S(2)}) %collective-permute-start.3) | collective-permute-done | bytes 393248 | tf_op jit(solution)/shard_map/ppermute | solution.py:20
  98.2 6.2 %collective-permute-start.4 = (f32[6,128,128]{2,1,0:T(8,128)S(1)}, f32[6,128,128]{2,1,0:T(8,128)S(1)}, u32[]{:S(2)}, u32[]{:S(2)}) collective-permute-start(f32[6,128,128]{2,1,0:T(8,128)S(1)} %fusion.6), channel_id=1, source_target_pairs={{0,1},{1,0},{2,3},{3,2},{4,5},{5,4},{6,7},{7,6},{8,9},{9,8},{10,11... | collective-permute-start | bytes 1179656 | tf_op jit(solution)/shard_map/ppermute | solution.py:175
  104.4 1.3 collective-permute-done.4
  105.8 3.8 %collective-permute-start.5 = (f32[6,128,128]{2,1,0:T(8,128)S(1)}, f32[6,128,128]{2,1,0:T(8,128)S(1)}, u32[]{:S(2)}, u32[]{:S(2)}) collective-permute-start(f32[6,128,128]{2,1,0:T(8,128)S(1)} %add.133), channel_id=1, source_target_pairs={{0,2},{1,3},{2,0},{3,1},{4,6},{5,7},{6,4},{7,5},{8,10},{9,11},{10,... | collective-permute-start | bytes 1179656 | tf_op jit(solution)/shard_map/ppermute | solution.py:175
  109.6 2.6 collective-permute-start.9
  112.2 6.6 %collective-permute-done.5 = f32[6,128,128]{2,1,0:T(8,128)S(1)} collective-permute-done((f32[6,128,128]{2,1,0:T(8,128)S(1)}, f32[6,128,128]{2,1,0:T(8,128)S(1)}, u32[]{:S(2)}, u32[]{:S(2)}) %collective-permute-start.5) | collective-permute-done | bytes 393248 | tf_op jit(solution)/shard_map/ppermute | solution.py:175
  118.8 4.1 %collective-permute-start.6 = (f32[6,128,128]{2,1,0:T(8,128)S(1)}, f32[6,128,128]{2,1,0:T(8,128)S(1)}, u32[]{:S(2)}, u32[]{:S(2)}) collective-permute-start(f32[6,128,128]{2,1,0:T(8,128)S(1)} %add.134), channel_id=1, source_target_pairs={{0,4},{1,5},{2,6},{3,7},{4,0},{5,1},{6,2},{7,3},{8,12},{9,13},{10,... | collective-permute-start | bytes 1179656 | tf_op jit(solution)/shard_map/ppermute | solution.py:175
  123.0 2.5 collective-permute-start.10
  125.5 11.6 %collective-permute-done.10 = f32[2,2,128,128]{3,2,1,0:T(8,128)S(1)} collective-permute-done((f32[2,2,128,128]{3,2,1,0:T(8,128)S(1)}, f32[2,2,128,128]{3,2,1,0:T(8,128)S(1)}, u32[]{:S(2)}, u32[]{:S(2)}) %collective-permute-start.10) | collective-permute-done | bytes 262176 | tf_op jit(solution)/shard_map/ppermute | solution.py:175
  137.1 3.8 %collective-permute-start.11 = (f32[2,2,128,128]{3,2,1,0:T(8,128)S(1)}, f32[2,2,128,128]{3,2,1,0:T(8,128)S(1)}, u32[]{:S(2)}, u32[]{:S(2)}) collective-permute-start(f32[2,2,128,128]{3,2,1,0:T(8,128)S(1)} %add.137), channel_id=1, source_target_pairs={{0,4},{1,5},{2,6},{3,7},{4,0},{5,1},{6,2},{7,3},{8,12},{9,13},{10,... | collective-permute-start | bytes 786440 | tf_op jit(solution)/shard_map/ppermute | solution.py:175
  141.1 3.4 %collective-permute-start.7 = (f32[2,3,128,128]{3,2,1,0:T(8,128)S(1)}, f32[2,3,128,128]{3,2,1,0:T(8,128)S(1)}, u32[]{:S(2)}, u32[]{:S(2)}) collective-permute-start(f32[2,3,128,128]{3,2,1,0:T(8,128)S(1)} %fusion.17), channel_id=1, source_target_pairs={{0,504},{8,0},{16,8},{24,16},{32,24},{40,32},{48,40},{56,48},{64,5... | collective-permute-start | bytes 1179656 | tf_op jit(solution)/shard_map/ppermute | solution.py:20
  144.4 1.8 collective-permute-done.11
  146.2 0.7 add.138
  147.0 4.6 %all-to-all-start = ((f32[64,1,1024]{2,1,0:T(1,128)}), f32[64,1,1024]{2,1,0:T(1,128)S(1)}, u32[]{:S(2)}, u32[]{:S(2)}) async-start(f32[64,1,1024]{2,1,0:T(1,128)} %bitcast.11), calls=%async_computation | async-start | bytes 524288 | tf_op jit(solution)/shard_map/all_to_all | solution.py:182
  151.6 0.9 pad_maximum_fusion.2
  152.5 4.4 %collective-permute-start.8 = (f32[2,3,128,256]{3,2,1,0:T(8,128)}, f32[2,3,128,256]{3,2,1,0:T(8,128)S(1)}, u32[]{:S(2)}, u32[]{:S(2)}) collective-permute-start(f32[2,3,128,256]{3,2,1,0:T(8,128)} %pad_maximum_fusion.2), channel_id=1, source_target_pairs={{0,448},{8,456},{16,464},{24,472},{32,480},{40,488},{48,496},{56,5... | collective-permute-start | bytes 2359304 | tf_op jit(solution)/shard_map/ppermute | solution.py:20
  156.9 7.2 %all-to-all-done = f32[64,1,1024]{2,1,0:T(1,128)S(1)} async-done(((f32[64,1,1024]{2,1,0:T(1,128)}), f32[64,1,1024]{2,1,0:T(1,128)S(1)}, u32[]{:S(2)}, u32[]{:S(2)}) %all-to-all-start) | async-done | bytes 262176 | tf_op jit(solution)/shard_map/all_to_all | solution.py:182
  164.1 0.2 reduce_sum.18
  164.4 19.5 %all_to_all.30 = f32[64,1,1024]{2,1,0:T(1,128)S(1)} all-to-all(f32[64,1,1024]{2,1,0:T(1,128)S(1)} %broadcast_in_dim.4), channel_id=1, replica_groups=mesh['tile'=64,'scan'=8] {'tile'}, dimensions={0} | all-to-all | bytes 524288 | tf_op jit(solution)/shard_map/all_to_all | solution.py:183
  183.9 0.3 broadcast_multiply_fusion.1
  184.2 0.7 sub.20.probe_ref
  185.0 1.1 fusion.1.cells_ref
  186.1 14.4 %shard_map.86 = (f32[2,3,128,128]{3,2,1,0:T(8,128)}, f32[2,2,128,128]{3,2,1,0:T(8,128)}) custom-call(f32[2,3,128,128]{3,2,1,0:T(8,128)} %fusion.1.cells_ref, f32[2,2,128,128]{3,2,1,0:T(8,128)} %sub.20.probe_ref, f32[128,128]{1,0:T(8,128)} %bitcast.52, f32[1,1]{1,0:T(1,128)} %bitcast.5.weight_ref, f32[4,128,128]{2,1,0:T(8,128)} %pad_maximum_fusion.5.tab_ref), custom_call_target="tpu_custom_call" | custom-call | flops 1342177280 | bytes 1441792 | tf_op jit(solution)/shard_map/pallas_call | solution.py:156
  200.7 0.9 copy-done.3
  201.5 4.0 %dynamic_update_slice.7 = f32[2,3,256,256]{3,2,1,0:T(8,128)S(1)} dynamic-update-slice(f32[2,3,256,256]{3,2,1,0:T(8,128)S(1)} %broadcast.218, f32[2,3,128,128]{3,2,1,0:T(8,128)S(1)} %copy-done.3, s32[]{:T(128)} %constant.13.clone.1, s32[]{:T(128)} %constant.13.clone.1, s32[]{:T(128)S(6)} %select_n.46, s32[]{:T(128)S(6)} %select_n.47) | dynamic-update-slice | bytes 786436 | tf_op jit(solution)/shard_map/dynamic_update_slice | solution.py:229
  205.8 4.4 %collective-permute-start.12 = (f32[12,128,128]{2,1,0:T(8,128)S(1)}, f32[12,128,128]{2,1,0:T(8,128)S(1)}, u32[]{:S(2)}, u32[]{:S(2)}) collective-permute-start(f32[12,128,128]{2,1,0:T(8,128)S(1)} %pad_maximum_fusion.3), channel_id=1, source_target_pairs={{0,64},{8,72},{16,80},{24,88},{32,96},{40,104},{48,112},{56,120},{... | collective-permute-start | bytes 2359304 | tf_op jit(solution)/shard_map/ppermute | solution.py:20
  210.3 4.0 %collective-permute-start.17 = (f32[2,2,128,128]{3,2,1,0:T(8,128)S(1)}, f32[2,2,128,128]{3,2,1,0:T(8,128)S(1)}, u32[]{:S(2)}, u32[]{:S(2)}) collective-permute-start(f32[2,2,128,128]{3,2,1,0:T(8,128)S(1)} %copy-done.7), channel_id=1, source_target_pairs={{0,1},{1,0},{2,3},{3,2},{4,5},{5,4},{6,7},{7,6},{8,9},{9,8},{10,11... | collective-permute-start | bytes 786440 | tf_op jit(solution)/shard_map/ppermute | solution.py:175
  214.3 1.1 collective-permute-done.17
  215.5 2.8 collective-permute-start.18
  218.3 7.6 %collective-permute-done.12 = f32[12,128,128]{2,1,0:T(8,128)S(1)} collective-permute-done((f32[12,128,128]{2,1,0:T(8,128)S(1)}, f32[12,128,128]{2,1,0:T(8,128)S(1)}, u32[]{:S(2)}, u32[]{:S(2)}) %collective-permute-start.12) | collective-permute-done | bytes 786464 | tf_op jit(solution)/shard_map/ppermute | solution.py:20
  225.9 2.9 %collective-permute-start.13 = (f32[6,128,128]{2,1,0:T(8,128)S(1)}, f32[6,128,128]{2,1,0:T(8,128)S(1)}, u32[]{:S(2)}, u32[]{:S(2)}) collective-permute-start(f32[6,128,128]{2,1,0:T(8,128)S(1)} %slice_add_fusion), channel_id=1, source_target_pairs={{0,8},{8,16},{16,24},{24,32},{32,40},{40,48},{48,56},{56,64},{64,7... | collective-permute-start | bytes 1179656 | tf_op jit(solution)/shard_map/ppermute | solution.py:20
  228.9 4.3 %collective-permute-start.19 = (f32[2,2,128,128]{3,2,1,0:T(8,128)S(1)}, f32[2,2,128,128]{3,2,1,0:T(8,128)S(1)}, u32[]{:S(2)}, u32[]{:S(2)}) collective-permute-start(f32[2,2,128,128]{3,2,1,0:T(8,128)S(1)} %add.146), channel_id=1, source_target_pairs={{0,4},{1,5},{2,6},{3,7},{4,0},{5,1},{6,2},{7,3},{8,12},{9,13},{10,... | collective-permute-start | bytes 786440 | tf_op jit(solution)/shard_map/ppermute | solution.py:175
  233.2 4.6 %collective-permute-done.19 = f32[2,2,128,128]{3,2,1,0:T(8,128)S(1)} collective-permute-done((f32[2,2,128,128]{3,2,1,0:T(8,128)S(1)}, f32[2,2,128,128]{3,2,1,0:T(8,128)S(1)}, u32[]{:S(2)}, u32[]{:S(2)}) %collective-permute-start.19) | collective-permute-done | bytes 262176 | tf_op jit(solution)/shard_map/ppermute | solution.py:175
  237.8 0.7 add.147
  238.5 8.2 %all-to-all-start.2 = ((f32[64,1,1024]{2,1,0:T(1,128)}), f32[64,1,1024]{2,1,0:T(1,128)S(1)}, u32[]{:S(2)}, u32[]{:S(2)}) async-start(f32[64,1,1024]{2,1,0:T(1,128)} %bitcast.22), calls=%async_computation.2 | async-start | bytes 524288 | tf_op jit(solution)/shard_map/all_to_all | solution.py:182
  246.8 6.3 %collective-permute-start.14 = (f32[6,128,128]{2,1,0:T(8,128)S(1)}, f32[6,128,128]{2,1,0:T(8,128)S(1)}, u32[]{:S(2)}, u32[]{:S(2)}) collective-permute-start(f32[6,128,128]{2,1,0:T(8,128)S(1)} %fusion.5), channel_id=1, source_target_pairs={{0,1},{1,0},{2,3},{3,2},{4,5},{5,4},{6,7},{7,6},{8,9},{9,8},{10,11... | collective-permute-start | bytes 1179656 | tf_op jit(solution)/shard_map/ppermute | solution.py:175
  253.1 1.3 collective-permute-done.14
  254.5 2.7 collective-permute-start.15
  257.2 2.1 all-to-all-done.2
  259.3 0.2 reduce_sum.19
  259.4 0.8 broadcast_in_dim.5
  260.3 10.3 %all-to-all-start.3 = ((f32[64,1,1024]{2,1,0:T(1,128)}), f32[64,1,1024]{2,1,0:T(1,128)S(1)}, u32[]{:S(2)}, u32[]{:S(2)}) async-start(f32[64,1,1024]{2,1,0:T(1,128)} %broadcast_in_dim.5), calls=%async_computation.3 | async-start | bytes 524288 | tf_op jit(solution)/shard_map/all_to_all | solution.py:183
  270.7 4.0 %collective-permute-start.16 = (f32[6,128,128]{2,1,0:T(8,128)S(1)}, f32[6,128,128]{2,1,0:T(8,128)S(1)}, u32[]{:S(2)}, u32[]{:S(2)}) collective-permute-start(f32[6,128,128]{2,1,0:T(8,128)S(1)} %add.143), channel_id=1, source_target_pairs={{0,4},{1,5},{2,6},{3,7},{4,0},{5,1},{6,2},{7,3},{8,12},{9,13},{10,... | collective-permute-start | bytes 1179656 | tf_op jit(solution)/shard_map/ppermute | solution.py:175
  274.7 8.6 %all-to-all-done.3 = f32[64,1,1024]{2,1,0:T(1,128)S(1)} async-done(((f32[64,1,1024]{2,1,0:T(1,128)}), f32[64,1,1024]{2,1,0:T(1,128)S(1)}, u32[]{:S(2)}, u32[]{:S(2)}) %all-to-all-start.3) | async-done | bytes 262176 | tf_op jit(solution)/shard_map/all_to_all | solution.py:183
  283.3 0.3 broadcast_multiply_fusion
  283.6 0.7 sub.22
  284.4 0.8 slice_bitcast_fusion
  (48 shorter events, 1.7 us)
Async XLA Ops:
  0.6 26.6 %copy-start.8 = (s32[1,1,1,2]{3,2,1,0:T(1,128)S(1)}, s32[1,1,1,2]{3,2,1,0:T(1,128)}, u32[]{:S(2)}) copy-start(s32[1,1,1,2]{3,2,1,0:T(1,128)} %param.10) | copy-start | bytes 28
  0.6 43.8 %copy-start = (f32[3,1,128,128]{3,2,1,0:T(8,128)S(1)}, f32[3,1,128,128]{3,2,1,0:T(8,128)}, u32[]{:S(2)}) copy-start(f32[3,1,128,128]{3,2,1,0:T(8,128)} %param.6) | copy-start | bytes 589828
  0.7 43.7 %copy-start.1 = (f32[3,1,128,128]{3,2,1,0:T(8,128)S(1)}, f32[3,1,128,128]{3,2,1,0:T(8,128)}, u32[]{:S(2)}) copy-start(f32[3,1,128,128]{3,2,1,0:T(8,128)} %param.7) | copy-start | bytes 589828
  1.8 22.2 %collective-permute-start = (f32[2,3,128,128]{3,2,1,0:T(8,128)S(1)}, f32[2,3,128,128]{3,2,1,0:T(8,128)S(1)}, u32[]{:S(2)}, u32[]{:S(2)}) collective-permute-start(f32[2,3,128,128]{3,2,1,0:T(8,128)S(1)} %pad_maximum_fusion.4), channel_id=1, source_target_pairs={{0,504},{8,0},{16,8},{24,16},{32,24},{40,32},{48,40},{56,48},{64,5... | collective-permute-start | bytes 1179656 | tf_op jit(solution)/shard_map/ppermute | solution.py:20
  25.0 19.4 %collective-permute-start.1 = (f32[2,3,128,256]{3,2,1,0:T(8,128)S(1)}, f32[2,3,128,256]{3,2,1,0:T(8,128)S(1)}, u32[]{:S(2)}, u32[]{:S(2)}) collective-permute-start(f32[2,3,128,256]{3,2,1,0:T(8,128)S(1)} %pad_maximum_fusion), channel_id=1, source_target_pairs={{0,448},{8,456},{16,464},{24,472},{32,480},{40,488},{48,496},{56,5... | collective-permute-start | bytes 2359304 | tf_op jit(solution)/shard_map/ppermute | solution.py:20
  60.0 1.0 copy-start.4
  65.2 19.5 %collective-permute-start.2 = (f32[12,128,128]{2,1,0:T(8,128)S(1)}, f32[12,128,128]{2,1,0:T(8,128)S(1)}, u32[]{:S(2)}, u32[]{:S(2)}) collective-permute-start(f32[12,128,128]{2,1,0:T(8,128)S(1)} %pad_maximum_fusion.1), channel_id=1, source_target_pairs={{0,64},{8,72},{16,80},{24,88},{32,96},{40,104},{48,112},{56,120},{... | collective-permute-start | bytes 2359304 | tf_op jit(solution)/shard_map/ppermute | solution.py:20
  84.8 24.8 %copy-start.6 = (f32[2,2,128,128]{3,2,1,0:T(8,128)S(1)}, f32[2,2,128,128]{3,2,1,0:T(8,128)}, u32[]{:S(2)}) copy-start(f32[2,2,128,128]{3,2,1,0:T(8,128)} %get-tuple-element.8) | copy-start | bytes 786436
  84.8 13.3 %collective-permute-start.3 = (f32[6,128,128]{2,1,0:T(8,128)S(1)}, f32[6,128,128]{2,1,0:T(8,128)S(1)}, u32[]{:S(2)}, u32[]{:S(2)}) collective-permute-start(f32[6,128,128]{2,1,0:T(8,128)S(1)} %slice_add_fusion.2), channel_id=1, source_target_pairs={{0,8},{8,16},{16,24},{24,32},{32,40},{40,48},{48,56},{56,64},{64,7... | collective-permute-start | bytes 1179656 | tf_op jit(solution)/shard_map/ppermute | solution.py:20
  98.2 7.5 %collective-permute-start.4 = (f32[6,128,128]{2,1,0:T(8,128)S(1)}, f32[6,128,128]{2,1,0:T(8,128)S(1)}, u32[]{:S(2)}, u32[]{:S(2)}) collective-permute-start(f32[6,128,128]{2,1,0:T(8,128)S(1)} %fusion.6), channel_id=1, source_target_pairs={{0,1},{1,0},{2,3},{3,2},{4,5},{5,4},{6,7},{7,6},{8,9},{9,8},{10,11... | collective-permute-start | bytes 1179656 | tf_op jit(solution)/shard_map/ppermute | solution.py:175
  105.8 13.0 %collective-permute-start.5 = (f32[6,128,128]{2,1,0:T(8,128)S(1)}, f32[6,128,128]{2,1,0:T(8,128)S(1)}, u32[]{:S(2)}, u32[]{:S(2)}) collective-permute-start(f32[6,128,128]{2,1,0:T(8,128)S(1)} %add.133), channel_id=1, source_target_pairs={{0,2},{1,3},{2,0},{3,1},{4,6},{5,7},{6,4},{7,5},{8,10},{9,11},{10,... | collective-permute-start | bytes 1179656 | tf_op jit(solution)/shard_map/ppermute | solution.py:175
  109.6 13.3 %collective-permute-start.9 = (f32[2,2,128,128]{3,2,1,0:T(8,128)S(1)}, f32[2,2,128,128]{3,2,1,0:T(8,128)S(1)}, u32[]{:S(2)}, u32[]{:S(2)}) collective-permute-start(f32[2,2,128,128]{3,2,1,0:T(8,128)S(1)} %copy-done.6), channel_id=1, source_target_pairs={{0,1},{1,0},{2,3},{3,2},{4,5},{5,4},{6,7},{7,6},{8,9},{9,8},{10,11... | collective-permute-start | bytes 786440 | tf_op jit(solution)/shard_map/ppermute | solution.py:175
  118.8 22.1 %collective-permute-start.6 = (f32[6,128,128]{2,1,0:T(8,128)S(1)}, f32[6,128,128]{2,1,0:T(8,128)S(1)}, u32[]{:S(2)}, u32[]{:S(2)}) collective-permute-start(f32[6,128,128]{2,1,0:T(8,128)S(1)} %add.134), channel_id=1, source_target_pairs={{0,4},{1,5},{2,6},{3,7},{4,0},{5,1},{6,2},{7,3},{8,12},{9,13},{10,... | collective-permute-start | bytes 1179656 | tf_op jit(solution)/shard_map/ppermute | solution.py:175
  123.0 14.1 %collective-permute-start.10 = (f32[2,2,128,128]{3,2,1,0:T(8,128)S(1)}, f32[2,2,128,128]{3,2,1,0:T(8,128)S(1)}, u32[]{:S(2)}, u32[]{:S(2)}) collective-permute-start(f32[2,2,128,128]{3,2,1,0:T(8,128)S(1)} %add.136), channel_id=1, source_target_pairs={{0,2},{1,3},{2,0},{3,1},{4,6},{5,7},{6,4},{7,5},{8,10},{9,11},{10,... | collective-permute-start | bytes 786440 | tf_op jit(solution)/shard_map/ppermute | solution.py:175
  137.1 9.1 %collective-permute-start.11 = (f32[2,2,128,128]{3,2,1,0:T(8,128)S(1)}, f32[2,2,128,128]{3,2,1,0:T(8,128)S(1)}, u32[]{:S(2)}, u32[]{:S(2)}) collective-permute-start(f32[2,2,128,128]{3,2,1,0:T(8,128)S(1)} %add.137), channel_id=1, source_target_pairs={{0,4},{1,5},{2,6},{3,7},{4,0},{5,1},{6,2},{7,3},{8,12},{9,13},{10,... | collective-permute-start | bytes 786440 | tf_op jit(solution)/shard_map/ppermute | solution.py:175
  141.1 10.5 %collective-permute-start.7 = (f32[2,3,128,128]{3,2,1,0:T(8,128)S(1)}, f32[2,3,128,128]{3,2,1,0:T(8,128)S(1)}, u32[]{:S(2)}, u32[]{:S(2)}) collective-permute-start(f32[2,3,128,128]{3,2,1,0:T(8,128)S(1)} %fusion.17), channel_id=1, source_target_pairs={{0,504},{8,0},{16,8},{24,16},{32,24},{40,32},{48,40},{56,48},{64,5... | collective-permute-start | bytes 1179656 | tf_op jit(solution)/shard_map/ppermute | solution.py:20
  147.0 17.1 %all-to-all-start = ((f32[64,1,1024]{2,1,0:T(1,128)}), f32[64,1,1024]{2,1,0:T(1,128)S(1)}, u32[]{:S(2)}, u32[]{:S(2)}) async-start(f32[64,1,1024]{2,1,0:T(1,128)} %bitcast.11), calls=%async_computation | async-start | bytes 524288 | tf_op jit(solution)/shard_map/all_to_all | solution.py:182
  151.6 32.6 %copy-start.5 = (f32[2,2,128,128]{3,2,1,0:T(8,128)S(1)}, f32[2,2,128,128]{3,2,1,0:T(8,128)}, u32[]{:S(2)}) copy-start(f32[2,2,128,128]{3,2,1,0:T(8,128)} %probe_ref.1) | copy-start | bytes 786436
  152.5 32.4 %collective-permute-start.8 = (f32[2,3,128,256]{3,2,1,0:T(8,128)}, f32[2,3,128,256]{3,2,1,0:T(8,128)S(1)}, u32[]{:S(2)}, u32[]{:S(2)}) collective-permute-start(f32[2,3,128,256]{3,2,1,0:T(8,128)} %pad_maximum_fusion.2), channel_id=1, source_target_pairs={{0,448},{8,456},{16,464},{24,472},{32,480},{40,488},{48,496},{56,5... | collective-permute-start | bytes 2359304 | tf_op jit(solution)/shard_map/ppermute | solution.py:20
  200.5 1.0 copy-start.3
  205.7 4.5 %copy-start.7 = (f32[2,2,128,128]{3,2,1,0:T(8,128)S(1)}, f32[2,2,128,128]{3,2,1,0:T(8,128)}, u32[]{:S(2)}) copy-start(f32[2,2,128,128]{3,2,1,0:T(8,128)} %get-tuple-element.10) | copy-start | bytes 786436
  205.8 20.0 %collective-permute-start.12 = (f32[12,128,128]{2,1,0:T(8,128)S(1)}, f32[12,128,128]{2,1,0:T(8,128)S(1)}, u32[]{:S(2)}, u32[]{:S(2)}) collective-permute-start(f32[12,128,128]{2,1,0:T(8,128)S(1)} %pad_maximum_fusion.3), channel_id=1, source_target_pairs={{0,64},{8,72},{16,80},{24,88},{32,96},{40,104},{48,112},{56,120},{... | collective-permute-start | bytes 2359304 | tf_op jit(solution)/shard_map/ppermute | solution.py:20
  210.3 5.2 %collective-permute-start.17 = (f32[2,2,128,128]{3,2,1,0:T(8,128)S(1)}, f32[2,2,128,128]{3,2,1,0:T(8,128)S(1)}, u32[]{:S(2)}, u32[]{:S(2)}) collective-permute-start(f32[2,2,128,128]{3,2,1,0:T(8,128)S(1)} %copy-done.7), channel_id=1, source_target_pairs={{0,1},{1,0},{2,3},{3,2},{4,5},{5,4},{6,7},{7,6},{8,9},{9,8},{10,11... | collective-permute-start | bytes 786440 | tf_op jit(solution)/shard_map/ppermute | solution.py:175
  215.5 13.4 %collective-permute-start.18 = (f32[2,2,128,128]{3,2,1,0:T(8,128)S(1)}, f32[2,2,128,128]{3,2,1,0:T(8,128)S(1)}, u32[]{:S(2)}, u32[]{:S(2)}) collective-permute-start(f32[2,2,128,128]{3,2,1,0:T(8,128)S(1)} %add.145), channel_id=1, source_target_pairs={{0,2},{1,3},{2,0},{3,1},{4,6},{5,7},{6,4},{7,5},{8,10},{9,11},{10,... | collective-permute-start | bytes 786440 | tf_op jit(solution)/shard_map/ppermute | solution.py:175
  225.9 20.8 %collective-permute-start.13 = (f32[6,128,128]{2,1,0:T(8,128)S(1)}, f32[6,128,128]{2,1,0:T(8,128)S(1)}, u32[]{:S(2)}, u32[]{:S(2)}) collective-permute-start(f32[6,128,128]{2,1,0:T(8,128)S(1)} %slice_add_fusion), channel_id=1, source_target_pairs={{0,8},{8,16},{16,24},{24,32},{32,40},{40,48},{48,56},{56,64},{64,7... | collective-permute-start | bytes 1179656 | tf_op jit(solution)/shard_map/ppermute | solution.py:20
  228.9 8.9 %collective-permute-start.19 = (f32[2,2,128,128]{3,2,1,0:T(8,128)S(1)}, f32[2,2,128,128]{3,2,1,0:T(8,128)S(1)}, u32[]{:S(2)}, u32[]{:S(2)}) collective-permute-start(f32[2,2,128,128]{3,2,1,0:T(8,128)S(1)} %add.146), channel_id=1, source_target_pairs={{0,4},{1,5},{2,6},{3,7},{4,0},{5,1},{6,2},{7,3},{8,12},{9,13},{10,... | collective-permute-start | bytes 786440 | tf_op jit(solution)/shard_map/ppermute | solution.py:175
  238.5 20.7 %all-to-all-start.2 = ((f32[64,1,1024]{2,1,0:T(1,128)}), f32[64,1,1024]{2,1,0:T(1,128)S(1)}, u32[]{:S(2)}, u32[]{:S(2)}) async-start(f32[64,1,1024]{2,1,0:T(1,128)} %bitcast.22), calls=%async_computation.2 | async-start | bytes 524288 | tf_op jit(solution)/shard_map/all_to_all | solution.py:182
  246.8 7.6 %collective-permute-start.14 = (f32[6,128,128]{2,1,0:T(8,128)S(1)}, f32[6,128,128]{2,1,0:T(8,128)S(1)}, u32[]{:S(2)}, u32[]{:S(2)}) collective-permute-start(f32[6,128,128]{2,1,0:T(8,128)S(1)} %fusion.5), channel_id=1, source_target_pairs={{0,1},{1,0},{2,3},{3,2},{4,5},{5,4},{6,7},{7,6},{8,9},{9,8},{10,11... | collective-permute-start | bytes 1179656 | tf_op jit(solution)/shard_map/ppermute | solution.py:175
  254.5 29.1 %copy-start.2 = (f32[2,2,128,128]{3,2,1,0:T(8,128)S(1)}, f32[2,2,128,128]{3,2,1,0:T(8,128)}, u32[]{:S(2)}) copy-start(f32[2,2,128,128]{3,2,1,0:T(8,128)} %sub.20.probe_ref) | copy-start | bytes 786436
  254.5 16.2 %collective-permute-start.15 = (f32[6,128,128]{2,1,0:T(8,128)S(1)}, f32[6,128,128]{2,1,0:T(8,128)S(1)}, u32[]{:S(2)}, u32[]{:S(2)}) collective-permute-start(f32[6,128,128]{2,1,0:T(8,128)S(1)} %add.142), channel_id=1, source_target_pairs={{0,2},{1,3},{2,0},{3,1},{4,6},{5,7},{6,4},{7,5},{8,10},{9,11},{10,... | collective-permute-start | bytes 1179656 | tf_op jit(solution)/shard_map/ppermute | solution.py:175
  260.3 23.0 %all-to-all-start.3 = ((f32[64,1,1024]{2,1,0:T(1,128)}), f32[64,1,1024]{2,1,0:T(1,128)S(1)}, u32[]{:S(2)}, u32[]{:S(2)}) async-start(f32[64,1,1024]{2,1,0:T(1,128)} %broadcast_in_dim.5), calls=%async_computation.3 | async-start | bytes 524288 | tf_op jit(solution)/shard_map/all_to_all | solution.py:183
  270.7 13.6 %collective-permute-start.16 = (f32[6,128,128]{2,1,0:T(8,128)S(1)}, f32[6,128,128]{2,1,0:T(8,128)S(1)}, u32[]{:S(2)}, u32[]{:S(2)}) collective-permute-start(f32[6,128,128]{2,1,0:T(8,128)S(1)} %add.143), channel_id=1, source_target_pairs={{0,4},{1,5},{2,6},{3,7},{4,0},{5,1},{6,2},{7,3},{8,12},{9,13},{10,... | collective-permute-start | bytes 1179656 | tf_op jit(solution)/shard_map/ppermute | solution.py:175

commit v7 on v6

--- a/solution.py
+++ b/solution.py
@@ -228,17 +228,34 @@
             )
             grad_canvas = lax.dynamic_update_slice(grad_canvas, current + grad_patch, starts)
             grad_probe = grad_probe + grad_modes
+        if slot_count == 1 and pattern_side == block_side:
+            spread = jnp.pad(
+                grad_patch, ((0, 0), (0, 0), (block_side, block_side), (block_side, block_side))
+            )
+            quarter = lambda y0, x0: lax.dynamic_slice(
+                spread,
+                (anchor, anchor, y0 - row_start, x0 - col_start),
+                (2, slices, block_side, block_side),
+            )
+            grad_ul, grad_ur = (quarter(block_side, block_side), quarter(block_side, 2 * block_side))
+            grad_ll = quarter(2 * block_side, block_side)
+            grad_lr = quarter(2 * block_side, 2 * block_side)
+        else:
+            grad_ul = grad_canvas[:, :, :block_side, :block_side]
+            grad_ur = grad_canvas[:, :, :block_side, block_side:]
+            grad_ll = grad_canvas[:, :, block_side:, :block_side]
+            grad_lr = grad_canvas[:, :, block_side:, block_side:]
         planes = lambda a: a.reshape(-1, block_side, block_side)
         probe_partial = a2a_sum(xor_sum(grad_probe, "scan"), "tile")
         sent_down = jnp.concatenate(
             [
-                planes(grad_canvas[:, :, block_side:, :block_side]),
-                planes(grad_canvas[:, :, block_side:, block_side:]),
+                planes(grad_ll),
+                planes(grad_lr),
             ]
         )
         came_down = shifted(sent_down, "tile", GRID)
-        own_part = planes(grad_canvas[:, :, :block_side, :block_side]) + came_down[:parts]
-        right_side = planes(grad_canvas[:, :, :block_side, block_side:]) + came_down[parts:]
+        own_part = planes(grad_ul) + came_down[:parts]
+        right_side = planes(grad_ur) + came_down[parts:]
         own_part = own_part + shifted(right_side, "tile", 1)
         grad_total = xor_sum(own_part, "scan").reshape(obj_state.shape)
         pending = probe_partial

time: 288 us -> 280 us (0.972)
  local copies, waits for them, and re-layouts: 12.7 us -> 5.85 us
  between operations: 5.66 us -> 10.8 us
  waiting for transfers between devices: 101 us -> 96.6 us
    dynamic_update_slice x2 -> x0, local copies, waits for them, and re-layouts: 8.06 us -> none  [local(): lax.dynamic_update_slice(grad_canvas, current + grad_patch, starts)]
    ppermute x8, waiting for transfers between devices: 54.9 us -> 48.7 us  [shifted(): lax.ppermute(shard, axis, [(i, (i + by) % size) for i in range(size)])]
    dynamic_slice x0 -> x2, local copies, waits for them, and re-layouts: none -> 3.49 us  [local(): lax.dynamic_slice(spread, (anchor, anchor, y0 - row_start, x0 - col_start...]
where the time goes in v7:
time: 280 us; the launch traced here: 277 us
  starting transfers between devices  107 us (38%)
  waiting for transfers between devices  96.6 us (34%)
  Pallas kernels  28.9 us (10%)
  blocking collectives  18.5 us (7%)
  between operations  10.8 us (4%)
  other arithmetic  9.6 us (3%)
  local copies, waits for them, and re-layouts  5.85 us (2%)
    ppermute x8, waiting for transfers between devices, shifted(): lax.ppermute(shard, axis, [(i, (i + by) % size) for i in range(size)])  48.7 us
    ppermute x12, starting transfers between devices, xor_sum(): lax.ppermute(values, axis, [(i, i ^ step) for i in range(size)])  46 us
    ppermute x8, starting transfers between devices, shifted(): lax.ppermute(shard, axis, [(i, (i + by) % size) for i in range(size)])  36.5 us
    pallas_call x2, Pallas kernels, slot_grad(): pl.pallas_call(slot_kernel, out_shape=(jax.ShapeDtypeStruct(patch_cells.s...  28.9 us
    ppermute x12, waiting for transfers between devices, xor_sum(): lax.ppermute(values, axis, [(i, i ^ step) for i in range(size)])  28.6 us
    all_to_all x1, blocking collectives, a2a_sum(): lax.all_to_all(jnp.broadcast_to(part, flat.shape), axis, 0, 0, tiled=True)  18.5 us
    all_to_all x2, starting transfers between devices, a2a_sum(): lax.all_to_all(flat, axis, 0, 0, tiled=True)  14 us
    all_to_all x1, starting transfers between devices, a2a_sum(): lax.all_to_all(jnp.broadcast_to(part, flat.shape), axis, 0, 0, tiled=True)  10.7 us
  transfers between devices with their start and end apart: 23, of which 15 were waited for; matrix products, arithmetic and copies ran while one was open for 3% of the time, Pallas kernels for 0%

profile of v7, /device:TPU:1, one launch (start us, length us, event | category | flops | bytes accessed | tf_op | source)
XLA Modules:
  0.0 277.5 jit_solution(18439477825315025630)
XLA Ops:
  0.7 1.1 pad_maximum_fusion.4
  1.8 14.4 %collective-permute-start = (f32[2,3,128,128]{3,2,1,0:T(8,128)S(1)}, f32[2,3,128,128]{3,2,1,0:T(8,128)S(1)}, u32[]{:S(2)}, u32[]{:S(2)}) collective-permute-start(f32[2,3,128,128]{3,2,1,0:T(8,128)S(1)} %pad_maximum_fusion.4), channel_id=1, source_target_pairs={{0,504},{8,0},{16,8},{24,16},{32,24},{40,32},{48,40},{56,48},{64,5... | collective-permute-start | bytes 1179656 | tf_op jit(solution)/shard_map/ppermute | solution.py:20
  16.2 7.8 %collective-permute-done = f32[2,3,128,128]{3,2,1,0:T(8,128)S(1)} collective-permute-done((f32[2,3,128,128]{3,2,1,0:T(8,128)S(1)}, f32[2,3,128,128]{3,2,1,0:T(8,128)S(1)}, u32[]{:S(2)}, u32[]{:S(2)}) %collective-permute-start) | collective-permute-done | bytes 393248 | tf_op jit(solution)/shard_map/ppermute | solution.py:20
  24.0 2.2 collective-permute-start.1
  26.2 0.6 fusion.18
  36.5 0.3 sine_multiply_fusion
  36.8 0.3 fusion.11
  37.1 0.7 pad_maximum_fusion.5.tab_ref
  37.8 5.6 %collective-permute-done.1 = f32[2,3,128,256]{3,2,1,0:T(8,128)S(1)} collective-permute-done((f32[2,3,128,256]{3,2,1,0:T(8,128)S(1)}, f32[2,3,128,256]{3,2,1,0:T(8,128)S(1)}, u32[]{:S(2)}, u32[]{:S(2)}) %collective-permute-start.1) | collective-permute-done | bytes 786464 | tf_op jit(solution)/shard_map/ppermute | solution.py:20
  43.4 1.1 fusion.4.cells_ref
  44.5 14.4 %shard_map.85 = (f32[2,3,128,128]{3,2,1,0:T(8,128)}, f32[2,2,128,128]{3,2,1,0:T(8,128)}) custom-call(f32[2,3,128,128]{3,2,1,0:T(8,128)} %fusion.4.cells_ref, f32[2,2,128,128]{3,2,1,0:T(8,128)} %probe_ref.1, f32[128,128]{1,0:T(8,128)} %bitcast.51, f32[1,1]{1,0:T(1,128)} %bitcast.5.weight_ref, f32[4,128,128]{2,1,0:T(8,128)} %pad_maximum_fusion.5.tab_ref), custom_call_target="tpu_custom_call" | custom-call | flops 1342177280 | bytes 1441792 | tf_op jit(solution)/shard_map/pallas_call | solution.py:156
  58.9 1.7 pad_dynamic-slice_fusion.7
  60.8 2.1 collective-permute-start.2
  62.9 17.6 %collective-permute-done.2 = f32[12,128,128]{2,1,0:T(8,128)S(1)} collective-permute-done((f32[12,128,128]{2,1,0:T(8,128)S(1)}, f32[12,128,128]{2,1,0:T(8,128)S(1)}, u32[]{:S(2)}, u32[]{:S(2)}) %collective-permute-start.2) | collective-permute-done | bytes 786464 | tf_op jit(solution)/shard_map/ppermute | solution.py:20
  80.4 0.1 slice_add_fusion.2
  80.5 1.9 collective-permute-start.3
  82.4 11.4 %collective-permute-done.3 = f32[6,128,128]{2,1,0:T(8,128)S(1)} collective-permute-done((f32[6,128,128]{2,1,0:T(8,128)S(1)}, f32[6,128,128]{2,1,0:T(8,128)S(1)}, u32[]{:S(2)}, u32[]{:S(2)}) %collective-permute-start.3) | collective-permute-done | bytes 393248 | tf_op jit(solution)/shard_map/ppermute | solution.py:20
  93.8 0.1 fusion.6
  93.9 6.1 %collective-permute-start.4 = (f32[6,128,128]{2,1,0:T(8,128)S(1)}, f32[6,128,128]{2,1,0:T(8,128)S(1)}, u32[]{:S(2)}, u32[]{:S(2)}) collective-permute-start(f32[6,128,128]{2,1,0:T(8,128)S(1)} %fusion.6), channel_id=1, source_target_pairs={{0,1},{1,0},{2,3},{3,2},{4,5},{5,4},{6,7},{7,6},{8,9},{9,8},{10,11... | collective-permute-start | bytes 1179656 | tf_op jit(solution)/shard_map/ppermute | solution.py:175
  100.0 1.3 collective-permute-done.4
  101.4 3.2 %collective-permute-start.5 = (f32[6,128,128]{2,1,0:T(8,128)S(1)}, f32[6,128,128]{2,1,0:T(8,128)S(1)}, u32[]{:S(2)}, u32[]{:S(2)}) collective-permute-start(f32[6,128,128]{2,1,0:T(8,128)S(1)} %add.165), channel_id=1, source_target_pairs={{0,2},{1,3},{2,0},{3,1},{4,6},{5,7},{6,4},{7,5},{8,10},{9,11},{10,... | collective-permute-start | bytes 1179656 | tf_op jit(solution)/shard_map/ppermute | solution.py:175
  104.6 2.6 collective-permute-start.9
  107.2 6.4 %collective-permute-done.5 = f32[6,128,128]{2,1,0:T(8,128)S(1)} collective-permute-done((f32[6,128,128]{2,1,0:T(8,128)S(1)}, f32[6,128,128]{2,1,0:T(8,128)S(1)}, u32[]{:S(2)}, u32[]{:S(2)}) %collective-permute-start.5) | collective-permute-done | bytes 393248 | tf_op jit(solution)/shard_map/ppermute | solution.py:175
  113.7 4.7 %collective-permute-start.6 = (f32[6,128,128]{2,1,0:T(8,128)S(1)}, f32[6,128,128]{2,1,0:T(8,128)S(1)}, u32[]{:S(2)}, u32[]{:S(2)}) collective-permute-start(f32[6,128,128]{2,1,0:T(8,128)S(1)} %add.166), channel_id=1, source_target_pairs={{0,4},{1,5},{2,6},{3,7},{4,0},{5,1},{6,2},{7,3},{8,12},{9,13},{10,... | collective-permute-start | bytes 1179656 | tf_op jit(solution)/shard_map/ppermute | solution.py:175
  118.4 2.2 collective-permute-start.10
  120.6 11.6 %collective-permute-done.10 = f32[2,2,128,128]{3,2,1,0:T(8,128)S(1)} collective-permute-done((f32[2,2,128,128]{3,2,1,0:T(8,128)S(1)}, f32[2,2,128,128]{3,2,1,0:T(8,128)S(1)}, u32[]{:S(2)}, u32[]{:S(2)}) %collective-permute-start.10) | collective-permute-done | bytes 262176 | tf_op jit(solution)/shard_map/ppermute | solution.py:175
  132.3 3.7 %collective-permute-start.11 = (f32[2,2,128,128]{3,2,1,0:T(8,128)S(1)}, f32[2,2,128,128]{3,2,1,0:T(8,128)S(1)}, u32[]{:S(2)}, u32[]{:S(2)}) collective-permute-start(f32[2,2,128,128]{3,2,1,0:T(8,128)S(1)} %add.169), channel_id=1, source_target_pairs={{0,4},{1,5},{2,6},{3,7},{4,0},{5,1},{6,2},{7,3},{8,12},{9,13},{10,... | collective-permute-start | bytes 786440 | tf_op jit(solution)/shard_map/ppermute | solution.py:175
  136.1 3.4 %collective-permute-start.7 = (f32[2,3,128,128]{3,2,1,0:T(8,128)S(1)}, f32[2,3,128,128]{3,2,1,0:T(8,128)S(1)}, u32[]{:S(2)}, u32[]{:S(2)}) collective-permute-start(f32[2,3,128,128]{3,2,1,0:T(8,128)S(1)} %fusion.17), channel_id=1, source_target_pairs={{0,504},{8,0},{16,8},{24,16},{32,24},{40,32},{48,40},{56,48},{64,5... | collective-permute-start | bytes 1179656 | tf_op jit(solution)/shard_map/ppermute | solution.py:20
  139.5 1.9 collective-permute-done.11
  141.3 0.7 add.170
  142.0 4.6 %all-to-all-start = ((f32[64,1,1024]{2,1,0:T(1,128)}), f32[64,1,1024]{2,1,0:T(1,128)S(1)}, u32[]{:S(2)}, u32[]{:S(2)}) async-start(f32[64,1,1024]{2,1,0:T(1,128)} %bitcast.11), calls=%async_computation | async-start | bytes 524288 | tf_op jit(solution)/shard_map/all_to_all | solution.py:182
  146.7 4.4 %collective-permute-start.8 = (f32[2,3,128,256]{3,2,1,0:T(8,128)S(1)}, f32[2,3,128,256]{3,2,1,0:T(8,128)S(1)}, u32[]{:S(2)}, u32[]{:S(2)}) collective-permute-start(f32[2,3,128,256]{3,2,1,0:T(8,128)S(1)} %pad_maximum_fusion.2), channel_id=1, source_target_pairs={{0,448},{8,456},{16,464},{24,472},{32,480},{40,488},{48,496},{56,5... | collective-permute-start | bytes 2359304 | tf_op jit(solution)/shard_map/ppermute | solution.py:20
  151.1 8.1 %all-to-all-done = f32[64,1,1024]{2,1,0:T(1,128)S(1)} async-done(((f32[64,1,1024]{2,1,0:T(1,128)}), f32[64,1,1024]{2,1,0:T(1,128)S(1)}, u32[]{:S(2)}, u32[]{:S(2)}) %all-to-all-start) | async-done | bytes 262176 | tf_op jit(solution)/shard_map/all_to_all | solution.py:182
  159.2 0.2 reduce_sum.18
  159.4 0.1 broadcast_in_dim.4
  159.5 18.5 %all_to_all.30 = f32[64,1,1024]{2,1,0:T(1,128)S(1)} all-to-all(f32[64,1,1024]{2,1,0:T(1,128)S(1)} %broadcast_in_dim.4), channel_id=1, replica_groups=mesh['tile'=64,'scan'=8] {'tile'}, dimensions={0} | all-to-all | bytes 524288 | tf_op jit(solution)/shard_map/all_to_all | solution.py:183
  178.0 0.3 broadcast_multiply_fusion.1
  178.3 0.8 sub.48.probe_ref
  179.1 1.1 fusion.1.cells_ref
  180.2 14.5 %shard_map.86 = (f32[2,3,128,128]{3,2,1,0:T(8,128)}, f32[2,2,128,128]{3,2,1,0:T(8,128)}) custom-call(f32[2,3,128,128]{3,2,1,0:T(8,128)} %fusion.1.cells_ref, f32[2,2,128,128]{3,2,1,0:T(8,128)} %sub.48.probe_ref, f32[128,128]{1,0:T(8,128)} %bitcast.52, f32[1,1]{1,0:T(1,128)} %bitcast.5.weight_ref, f32[4,128,128]{2,1,0:T(8,128)} %pad_maximum_fusion.5.tab_ref), custom_call_target="tpu_custom_call" | custom-call | flops 1342177280 | bytes 1441792 | tf_op jit(solution)/shard_map/pallas_call | solution.py:156
  194.7 1.7 pad_dynamic-slice_fusion.3
  196.5 5.2 %collective-permute-start.12 = (f32[12,128,128]{2,1,0:T(8,128)S(1)}, f32[12,128,128]{2,1,0:T(8,128)S(1)}, u32[]{:S(2)}, u32[]{:S(2)}) collective-permute-start(f32[12,128,128]{2,1,0:T(8,128)S(1)} %pad_maximum_fusion.3), channel_id=1, source_target_pairs={{0,64},{8,72},{16,80},{24,88},{32,96},{40,104},{48,112},{56,120},{... | collective-permute-start | bytes 2359304 | tf_op jit(solution)/shard_map/ppermute | solution.py:20
  201.7 4.1 %collective-permute-start.17 = (f32[2,2,128,128]{3,2,1,0:T(8,128)S(1)}, f32[2,2,128,128]{3,2,1,0:T(8,128)S(1)}, u32[]{:S(2)}, u32[]{:S(2)}) collective-permute-start(f32[2,2,128,128]{3,2,1,0:T(8,128)S(1)} %copy-done.5), channel_id=1, source_target_pairs={{0,1},{1,0},{2,3},{3,2},{4,5},{5,4},{6,7},{7,6},{8,9},{9,8},{10,11... | collective-permute-start | bytes 786440 | tf_op jit(solution)/shard_map/ppermute | solution.py:175
  205.8 1.1 collective-permute-done.17
  207.0 3.1 %collective-permute-start.18 = (f32[2,2,128,128]{3,2,1,0:T(8,128)S(1)}, f32[2,2,128,128]{3,2,1,0:T(8,128)S(1)}, u32[]{:S(2)}, u32[]{:S(2)}) collective-permute-start(f32[2,2,128,128]{3,2,1,0:T(8,128)S(1)} %add.177), channel_id=1, source_target_pairs={{0,2},{1,3},{2,0},{3,1},{4,6},{5,7},{6,4},{7,5},{8,10},{9,11},{10,... | collective-permute-start | bytes 786440 | tf_op jit(solution)/shard_map/ppermute | solution.py:175
  210.1 6.5 %collective-permute-done.12 = f32[12,128,128]{2,1,0:T(8,128)S(1)} collective-permute-done((f32[12,128,128]{2,1,0:T(8,128)S(1)}, f32[12,128,128]{2,1,0:T(8,128)S(1)}, u32[]{:S(2)}, u32[]{:S(2)}) %collective-permute-start.12) | collective-permute-done | bytes 786464 | tf_op jit(solution)/shard_map/ppermute | solution.py:20
  216.6 3.0 %collective-permute-start.13 = (f32[6,128,128]{2,1,0:T(8,128)S(1)}, f32[6,128,128]{2,1,0:T(8,128)S(1)}, u32[]{:S(2)}, u32[]{:S(2)}) collective-permute-start(f32[6,128,128]{2,1,0:T(8,128)S(1)} %slice_add_fusion), channel_id=1, source_target_pairs={{0,8},{8,16},{16,24},{24,32},{32,40},{40,48},{48,56},{56,64},{64,7... | collective-permute-start | bytes 1179656 | tf_op jit(solution)/shard_map/ppermute | solution.py:20
  219.6 4.0 %collective-permute-start.19 = (f32[2,2,128,128]{3,2,1,0:T(8,128)S(1)}, f32[2,2,128,128]{3,2,1,0:T(8,128)S(1)}, u32[]{:S(2)}, u32[]{:S(2)}) collective-permute-start(f32[2,2,128,128]{3,2,1,0:T(8,128)S(1)} %add.178), channel_id=1, source_target_pairs={{0,4},{1,5},{2,6},{3,7},{4,0},{5,1},{6,2},{7,3},{8,12},{9,13},{10,... | collective-permute-start | bytes 786440 | tf_op jit(solution)/shard_map/ppermute | solution.py:175
  223.6 4.9 %collective-permute-done.19 = f32[2,2,128,128]{3,2,1,0:T(8,128)S(1)} collective-permute-done((f32[2,2,128,128]{3,2,1,0:T(8,128)S(1)}, f32[2,2,128,128]{3,2,1,0:T(8,128)S(1)}, u32[]{:S(2)}, u32[]{:S(2)}) %collective-permute-start.19) | collective-permute-done | bytes 262176 | tf_op jit(solution)/shard_map/ppermute | solution.py:175
  228.6 0.7 add.179
  229.3 9.4 %all-to-all-start.2 = ((f32[64,1,1024]{2,1,0:T(1,128)}), f32[64,1,1024]{2,1,0:T(1,128)S(1)}, u32[]{:S(2)}, u32[]{:S(2)}) async-start(f32[64,1,1024]{2,1,0:T(1,128)} %bitcast.22), calls=%async_computation.2 | async-start | bytes 524288 | tf_op jit(solution)/shard_map/all_to_all | solution.py:182
  238.8 6.1 %collective-permute-start.14 = (f32[6,128,128]{2,1,0:T(8,128)S(1)}, f32[6,128,128]{2,1,0:T(8,128)S(1)}, u32[]{:S(2)}, u32[]{:S(2)}) collective-permute-start(f32[6,128,128]{2,1,0:T(8,128)S(1)} %fusion.5), channel_id=1, source_target_pairs={{0,1},{1,0},{2,3},{3,2},{4,5},{5,4},{6,7},{7,6},{8,9},{9,8},{10,11... | collective-permute-start | bytes 1179656 | tf_op jit(solution)/shard_map/ppermute | solution.py:175
  244.9 1.3 collective-permute-done.14
  246.3 3.1 %collective-permute-start.15 = (f32[6,128,128]{2,1,0:T(8,128)S(1)}, f32[6,128,128]{2,1,0:T(8,128)S(1)}, u32[]{:S(2)}, u32[]{:S(2)}) collective-permute-start(f32[6,128,128]{2,1,0:T(8,128)S(1)} %add.174), channel_id=1, source_target_pairs={{0,2},{1,3},{2,0},{3,1},{4,6},{5,7},{6,4},{7,5},{8,10},{9,11},{10,... | collective-permute-start | bytes 1179656 | tf_op jit(solution)/shard_map/ppermute | solution.py:175
  249.4 1.8 all-to-all-done.2
  251.2 0.2 reduce_sum.19
  251.3 0.8 broadcast_in_dim.5
  252.2 10.7 %all-to-all-start.3 = ((f32[64,1,1024]{2,1,0:T(1,128)}), f32[64,1,1024]{2,1,0:T(1,128)S(1)}, u32[]{:S(2)}, u32[]{:S(2)}) async-start(f32[64,1,1024]{2,1,0:T(1,128)} %broadcast_in_dim.5), calls=%async_computation.3 | async-start | bytes 524288 | tf_op jit(solution)/shard_map/all_to_all | solution.py:183
  262.9 3.1 %collective-permute-start.16 = (f32[6,128,128]{2,1,0:T(8,128)S(1)}, f32[6,128,128]{2,1,0:T(8,128)S(1)}, u32[]{:S(2)}, u32[]{:S(2)}) collective-permute-start(f32[6,128,128]{2,1,0:T(8,128)S(1)} %add.175), channel_id=1, source_target_pairs={{0,4},{1,5},{2,6},{3,7},{4,0},{5,1},{6,2},{7,3},{8,12},{9,13},{10,... | collective-permute-start | bytes 1179656 | tf_op jit(solution)/shard_map/ppermute | solution.py:175
  266.1 9.5 %all-to-all-done.3 = f32[64,1,1024]{2,1,0:T(1,128)S(1)} async-done(((f32[64,1,1024]{2,1,0:T(1,128)}), f32[64,1,1024]{2,1,0:T(1,128)S(1)}, u32[]{:S(2)}, u32[]{:S(2)}) %all-to-all-start.3) | async-done | bytes 262176 | tf_op jit(solution)/shard_map/all_to_all | solution.py:183
  275.5 0.3 broadcast_multiply_fusion
  275.8 0.7 sub.50
  276.6 0.1 fusion.19
  276.7 0.8 slice_bitcast_fusion
  (40 shorter events, 0.9 us)
Async XLA Ops:
  0.6 23.3 %copy-start.1 = (f32[3,1,128,128]{3,2,1,0:T(8,128)S(1)}, f32[3,1,128,128]{3,2,1,0:T(8,128)}, u32[]{:S(2)}) copy-start(f32[3,1,128,128]{3,2,1,0:T(8,128)} %param.7) | copy-start | bytes 589828
  0.6 23.3 %copy-start = (f32[3,1,128,128]{3,2,1,0:T(8,128)S(1)}, f32[3,1,128,128]{3,2,1,0:T(8,128)}, u32[]{:S(2)}) copy-start(f32[3,1,128,128]{3,2,1,0:T(8,128)} %param.6) | copy-start | bytes 589828
  1.8 24.4 %copy-start.6 = (s32[1,1,1,2]{3,2,1,0:T(1,128)S(1)}, s32[1,1,1,2]{3,2,1,0:T(1,128)}, u32[]{:S(2)}) copy-start(s32[1,1,1,2]{3,2,1,0:T(1,128)} %param.10) | copy-start | bytes 28
  1.8 22.2 %collective-permute-start = (f32[2,3,128,128]{3,2,1,0:T(8,128)S(1)}, f32[2,3,128,128]{3,2,1,0:T(8,128)S(1)}, u32[]{:S(2)}, u32[]{:S(2)}) collective-permute-start(f32[2,3,128,128]{3,2,1,0:T(8,128)S(1)} %pad_maximum_fusion.4), channel_id=1, source_target_pairs={{0,504},{8,0},{16,8},{24,16},{32,24},{40,32},{48,40},{56,48},{64,5... | collective-permute-start | bytes 1179656 | tf_op jit(solution)/shard_map/ppermute | solution.py:20
  24.0 19.4 %collective-permute-start.1 = (f32[2,3,128,256]{3,2,1,0:T(8,128)S(1)}, f32[2,3,128,256]{3,2,1,0:T(8,128)S(1)}, u32[]{:S(2)}, u32[]{:S(2)}) collective-permute-start(f32[2,3,128,256]{3,2,1,0:T(8,128)S(1)} %pad_maximum_fusion), channel_id=1, source_target_pairs={{0,448},{8,456},{16,464},{24,472},{32,480},{40,488},{48,496},{56,5... | collective-permute-start | bytes 2359304 | tf_op jit(solution)/shard_map/ppermute | solution.py:20
  60.8 19.7 %collective-permute-start.2 = (f32[12,128,128]{2,1,0:T(8,128)S(1)}, f32[12,128,128]{2,1,0:T(8,128)S(1)}, u32[]{:S(2)}, u32[]{:S(2)}) collective-permute-start(f32[12,128,128]{2,1,0:T(8,128)S(1)} %pad_maximum_fusion.1), channel_id=1, source_target_pairs={{0,64},{8,72},{16,80},{24,88},{32,96},{40,104},{48,112},{56,120},{... | collective-permute-start | bytes 2359304 | tf_op jit(solution)/shard_map/ppermute | solution.py:20
  80.5 13.3 %collective-permute-start.3 = (f32[6,128,128]{2,1,0:T(8,128)S(1)}, f32[6,128,128]{2,1,0:T(8,128)S(1)}, u32[]{:S(2)}, u32[]{:S(2)}) collective-permute-start(f32[6,128,128]{2,1,0:T(8,128)S(1)} %slice_add_fusion.2), channel_id=1, source_target_pairs={{0,8},{8,16},{16,24},{24,32},{32,40},{40,48},{48,56},{56,64},{64,7... | collective-permute-start | bytes 1179656 | tf_op jit(solution)/shard_map/ppermute | solution.py:20
  93.9 10.7 %copy-start.4 = (f32[2,2,128,128]{3,2,1,0:T(8,128)S(1)}, f32[2,2,128,128]{3,2,1,0:T(8,128)}, u32[]{:S(2)}) copy-start(f32[2,2,128,128]{3,2,1,0:T(8,128)} %get-tuple-element.8) | copy-start | bytes 786436
  93.9 7.5 %collective-permute-start.4 = (f32[6,128,128]{2,1,0:T(8,128)S(1)}, f32[6,128,128]{2,1,0:T(8,128)S(1)}, u32[]{:S(2)}, u32[]{:S(2)}) collective-permute-start(f32[6,128,128]{2,1,0:T(8,128)S(1)} %fusion.6), channel_id=1, source_target_pairs={{0,1},{1,0},{2,3},{3,2},{4,5},{5,4},{6,7},{7,6},{8,9},{9,8},{10,11... | collective-permute-start | bytes 1179656 | tf_op jit(solution)/shard_map/ppermute | solution.py:175
  101.4 12.2 %collective-permute-start.5 = (f32[6,128,128]{2,1,0:T(8,128)S(1)}, f32[6,128,128]{2,1,0:T(8,128)S(1)}, u32[]{:S(2)}, u32[]{:S(2)}) collective-permute-start(f32[6,128,128]{2,1,0:T(8,128)S(1)} %add.165), channel_id=1, source_target_pairs={{0,2},{1,3},{2,0},{3,1},{4,6},{5,7},{6,4},{7,5},{8,10},{9,11},{10,... | collective-permute-start | bytes 1179656 | tf_op jit(solution)/shard_map/ppermute | solution.py:175
  104.6 13.8 %collective-permute-start.9 = (f32[2,2,128,128]{3,2,1,0:T(8,128)S(1)}, f32[2,2,128,128]{3,2,1,0:T(8,128)S(1)}, u32[]{:S(2)}, u32[]{:S(2)}) collective-permute-start(f32[2,2,128,128]{3,2,1,0:T(8,128)S(1)} %copy-done.4), channel_id=1, source_target_pairs={{0,1},{1,0},{2,3},{3,2},{4,5},{5,4},{6,7},{7,6},{8,9},{9,8},{10,11... | collective-permute-start | bytes 786440 | tf_op jit(solution)/shard_map/ppermute | solution.py:175
  113.7 22.3 %collective-permute-start.6 = (f32[6,128,128]{2,1,0:T(8,128)S(1)}, f32[6,128,128]{2,1,0:T(8,128)S(1)}, u32[]{:S(2)}, u32[]{:S(2)}) collective-permute-start(f32[6,128,128]{2,1,0:T(8,128)S(1)} %add.166), channel_id=1, source_target_pairs={{0,4},{1,5},{2,6},{3,7},{4,0},{5,1},{6,2},{7,3},{8,12},{9,13},{10,... | collective-permute-start | bytes 1179656 | tf_op jit(solution)/shard_map/ppermute | solution.py:175
  118.4 13.8 %collective-permute-start.10 = (f32[2,2,128,128]{3,2,1,0:T(8,128)S(1)}, f32[2,2,128,128]{3,2,1,0:T(8,128)S(1)}, u32[]{:S(2)}, u32[]{:S(2)}) collective-permute-start(f32[2,2,128,128]{3,2,1,0:T(8,128)S(1)} %add.168), channel_id=1, source_target_pairs={{0,2},{1,3},{2,0},{3,1},{4,6},{5,7},{6,4},{7,5},{8,10},{9,11},{10,... | collective-permute-start | bytes 786440 | tf_op jit(solution)/shard_map/ppermute | solution.py:175
  132.3 9.1 %collective-permute-start.11 = (f32[2,2,128,128]{3,2,1,0:T(8,128)S(1)}, f32[2,2,128,128]{3,2,1,0:T(8,128)S(1)}, u32[]{:S(2)}, u32[]{:S(2)}) collective-permute-start(f32[2,2,128,128]{3,2,1,0:T(8,128)S(1)} %add.169), channel_id=1, source_target_pairs={{0,4},{1,5},{2,6},{3,7},{4,0},{5,1},{6,2},{7,3},{8,12},{9,13},{10,... | collective-permute-start | bytes 786440 | tf_op jit(solution)/shard_map/ppermute | solution.py:175
  136.1 10.6 %collective-permute-start.7 = (f32[2,3,128,128]{3,2,1,0:T(8,128)S(1)}, f32[2,3,128,128]{3,2,1,0:T(8,128)S(1)}, u32[]{:S(2)}, u32[]{:S(2)}) collective-permute-start(f32[2,3,128,128]{3,2,1,0:T(8,128)S(1)} %fusion.17), channel_id=1, source_target_pairs={{0,504},{8,0},{16,8},{24,16},{32,24},{40,32},{48,40},{56,48},{64,5... | collective-permute-start | bytes 1179656 | tf_op jit(solution)/shard_map/ppermute | solution.py:20
  142.0 17.2 %all-to-all-start = ((f32[64,1,1024]{2,1,0:T(1,128)}), f32[64,1,1024]{2,1,0:T(1,128)S(1)}, u32[]{:S(2)}, u32[]{:S(2)}) async-start(f32[64,1,1024]{2,1,0:T(1,128)} %bitcast.11), calls=%async_computation | async-start | bytes 524288 | tf_op jit(solution)/shard_map/all_to_all | solution.py:182
  146.7 32.3 %collective-permute-start.8 = (f32[2,3,128,256]{3,2,1,0:T(8,128)S(1)}, f32[2,3,128,256]{3,2,1,0:T(8,128)S(1)}, u32[]{:S(2)}, u32[]{:S(2)}) collective-permute-start(f32[2,3,128,256]{3,2,1,0:T(8,128)S(1)} %pad_maximum_fusion.2), channel_id=1, source_target_pairs={{0,448},{8,456},{16,464},{24,472},{32,480},{40,488},{48,496},{56,5... | collective-permute-start | bytes 2359304 | tf_op jit(solution)/shard_map/ppermute | solution.py:20
  159.4 18.9 %copy-start.3 = (f32[2,2,128,128]{3,2,1,0:T(8,128)S(1)}, f32[2,2,128,128]{3,2,1,0:T(8,128)}, u32[]{:S(2)}) copy-start(f32[2,2,128,128]{3,2,1,0:T(8,128)} %probe_ref.1) | copy-start | bytes 786436
  196.4 5.2 %copy-start.5 = (f32[2,2,128,128]{3,2,1,0:T(8,128)S(1)}, f32[2,2,128,128]{3,2,1,0:T(8,128)}, u32[]{:S(2)}) copy-start(f32[2,2,128,128]{3,2,1,0:T(8,128)} %get-tuple-element.10) | copy-start | bytes 786436
  196.5 20.0 %collective-permute-start.12 = (f32[12,128,128]{2,1,0:T(8,128)S(1)}, f32[12,128,128]{2,1,0:T(8,128)S(1)}, u32[]{:S(2)}, u32[]{:S(2)}) collective-permute-start(f32[12,128,128]{2,1,0:T(8,128)S(1)} %pad_maximum_fusion.3), channel_id=1, source_target_pairs={{0,64},{8,72},{16,80},{24,88},{32,96},{40,104},{48,112},{56,120},{... | collective-permute-start | bytes 2359304 | tf_op jit(solution)/shard_map/ppermute | solution.py:20
  201.7 5.3 %collective-permute-start.17 = (f32[2,2,128,128]{3,2,1,0:T(8,128)S(1)}, f32[2,2,128,128]{3,2,1,0:T(8,128)S(1)}, u32[]{:S(2)}, u32[]{:S(2)}) collective-permute-start(f32[2,2,128,128]{3,2,1,0:T(8,128)S(1)} %copy-done.5), channel_id=1, source_target_pairs={{0,1},{1,0},{2,3},{3,2},{4,5},{5,4},{6,7},{7,6},{8,9},{9,8},{10,11... | collective-permute-start | bytes 786440 | tf_op jit(solution)/shard_map/ppermute | solution.py:175
  207.0 12.6 %collective-permute-start.18 = (f32[2,2,128,128]{3,2,1,0:T(8,128)S(1)}, f32[2,2,128,128]{3,2,1,0:T(8,128)S(1)}, u32[]{:S(2)}, u32[]{:S(2)}) collective-permute-start(f32[2,2,128,128]{3,2,1,0:T(8,128)S(1)} %add.177), channel_id=1, source_target_pairs={{0,2},{1,3},{2,0},{3,1},{4,6},{5,7},{6,4},{7,5},{8,10},{9,11},{10,... | collective-permute-start | bytes 786440 | tf_op jit(solution)/shard_map/ppermute | solution.py:175
  216.6 22.1 %collective-permute-start.13 = (f32[6,128,128]{2,1,0:T(8,128)S(1)}, f32[6,128,128]{2,1,0:T(8,128)S(1)}, u32[]{:S(2)}, u32[]{:S(2)}) collective-permute-start(f32[6,128,128]{2,1,0:T(8,128)S(1)} %slice_add_fusion), channel_id=1, source_target_pairs={{0,8},{8,16},{16,24},{24,32},{32,40},{40,48},{48,56},{56,64},{64,7... | collective-permute-start | bytes 1179656 | tf_op jit(solution)/shard_map/ppermute | solution.py:20
  219.6 8.9 %collective-permute-start.19 = (f32[2,2,128,128]{3,2,1,0:T(8,128)S(1)}, f32[2,2,128,128]{3,2,1,0:T(8,128)S(1)}, u32[]{:S(2)}, u32[]{:S(2)}) collective-permute-start(f32[2,2,128,128]{3,2,1,0:T(8,128)S(1)} %add.178), channel_id=1, source_target_pairs={{0,4},{1,5},{2,6},{3,7},{4,0},{5,1},{6,2},{7,3},{8,12},{9,13},{10,... | collective-permute-start | bytes 786440 | tf_op jit(solution)/shard_map/ppermute | solution.py:175
  229.3 21.9 %all-to-all-start.2 = ((f32[64,1,1024]{2,1,0:T(1,128)}), f32[64,1,1024]{2,1,0:T(1,128)S(1)}, u32[]{:S(2)}, u32[]{:S(2)}) async-start(f32[64,1,1024]{2,1,0:T(1,128)} %bitcast.22), calls=%async_computation.2 | async-start | bytes 524288 | tf_op jit(solution)/shard_map/all_to_all | solution.py:182
  238.8 7.4 %collective-permute-start.14 = (f32[6,128,128]{2,1,0:T(8,128)S(1)}, f32[6,128,128]{2,1,0:T(8,128)S(1)}, u32[]{:S(2)}, u32[]{:S(2)}) collective-permute-start(f32[6,128,128]{2,1,0:T(8,128)S(1)} %fusion.5), channel_id=1, source_target_pairs={{0,1},{1,0},{2,3},{3,2},{4,5},{5,4},{6,7},{7,6},{8,9},{9,8},{10,11... | collective-permute-start | bytes 1179656 | tf_op jit(solution)/shard_map/ppermute | solution.py:175
  246.3 16.6 %collective-permute-start.15 = (f32[6,128,128]{2,1,0:T(8,128)S(1)}, f32[6,128,128]{2,1,0:T(8,128)S(1)}, u32[]{:S(2)}, u32[]{:S(2)}) collective-permute-start(f32[6,128,128]{2,1,0:T(8,128)S(1)} %add.174), channel_id=1, source_target_pairs={{0,2},{1,3},{2,0},{3,1},{4,6},{5,7},{6,4},{7,5},{8,10},{9,11},{10,... | collective-permute-start | bytes 1179656 | tf_op jit(solution)/shard_map/ppermute | solution.py:175
  252.2 23.3 %all-to-all-start.3 = ((f32[64,1,1024]{2,1,0:T(1,128)}), f32[64,1,1024]{2,1,0:T(1,128)S(1)}, u32[]{:S(2)}, u32[]{:S(2)}) async-start(f32[64,1,1024]{2,1,0:T(1,128)} %broadcast_in_dim.5), calls=%async_computation.3 | async-start | bytes 524288 | tf_op jit(solution)/shard_map/all_to_all | solution.py:183
  262.9 12.9 %copy-start.2 = (f32[2,2,128,128]{3,2,1,0:T(8,128)S(1)}, f32[2,2,128,128]{3,2,1,0:T(8,128)}, u32[]{:S(2)}) copy-start(f32[2,2,128,128]{3,2,1,0:T(8,128)} %sub.48.probe_ref) | copy-start | bytes 786436
  262.9 13.6 %collective-permute-start.16 = (f32[6,128,128]{2,1,0:T(8,128)S(1)}, f32[6,128,128]{2,1,0:T(8,128)S(1)}, u32[]{:S(2)}, u32[]{:S(2)}) collective-permute-start(f32[6,128,128]{2,1,0:T(8,128)S(1)} %add.175), channel_id=1, source_target_pairs={{0,4},{1,5},{2,6},{3,7},{4,0},{5,1},{6,2},{7,3},{8,12},{9,13},{10,... | collective-permute-start | bytes 1179656 | tf_op jit(solution)/shard_map/ppermute | solution.py:175

commit v8 on v7

--- a/solution.py
+++ b/solution.py
@@ -208,8 +208,10 @@
         if iteration == ITERS:
             break
         right_part = shifted(obj_state, "tile", -1)
+        below_part = shifted(obj_state, "tile", -GRID)
+        corner_part = shifted(below_part, "tile", -1)
         upper_half = jnp.concatenate([obj_state, right_part], axis=-1)
-        lower_half = shifted(upper_half, "tile", -GRID)
+        lower_half = jnp.concatenate([below_part, corner_part], axis=-1)
         canvas = jnp.concatenate([upper_half, lower_half], axis=-2)
         current_probe = probe_modes
 

time: 280 us -> 291 us (1.039)
  starting transfers between devices: 107 us -> 129 us
  blocking collectives: 18.5 us -> 0 us
  waiting for transfers between devices: 96.6 us -> 103 us
    ppermute x8 -> x10, starting transfers between devices: 36.5 us -> 58.4 us  [shifted(): lax.ppermute(shard, axis, [(i, (i + by) % size) for i in range(size)])]
    all_to_all x1 -> x0, blocking collectives: 18.5 us -> none  [a2a_sum(): lax.all_to_all(jnp.broadcast_to(part, flat.shape), axis, 0, 0, tiled=True)]
    ppermute x12, starting transfers between devices: 46 us -> 40.2 us  [xor_sum(): lax.ppermute(values, axis, [(i, i ^ step) for i in range(size)])]
    all_to_all x1 -> x2, waiting for transfers between devices: 9.45 us -> 13.8 us  [a2a_sum(): lax.all_to_all(jnp.broadcast_to(part, flat.shape), axis, 0, 0, tiled=True)]
    all_to_all x1 -> x2, starting transfers between devices: 10.7 us -> 14.9 us  [a2a_sum(): lax.all_to_all(jnp.broadcast_to(part, flat.shape), axis, 0, 0, tiled=True)]
    ppermute x8 -> x10, waiting for transfers between devices: 48.7 us -> 49.9 us  [shifted(): lax.ppermute(shard, axis, [(i, (i + by) % size) for i in range(size)])]
  transfers between devices with their start and end apart: 23 -> 26, of which waited for: 15 -> 16; matrix products, arithmetic and copies ran while one was open for 3% -> 3% of each run, Pallas kernels for 0% -> 0%
where the time goes in v8:
time: 291 us; the launch traced here: 288 us
  starting transfers between devices  129 us (44%)
  waiting for transfers between devices  103 us (35%)
  Pallas kernels  28.9 us (10%)
  between operations  10.8 us (4%)
  other arithmetic  9.69 us (3%)
  local copies, waits for them, and re-layouts  6.45 us (2%)
    ppermute x10, starting transfers between devices, shifted(): lax.ppermute(shard, axis, [(i, (i + by) % size) for i in range(size)])  58.4 us
    ppermute x10, waiting for transfers between devices, shifted(): lax.ppermute(shard, axis, [(i, (i + by) % size) for i in range(size)])  49.9 us
    ppermute x12, starting transfers between devices, xor_sum(): lax.ppermute(values, axis, [(i, i ^ step) for i in range(size)])  40.2 us
    pallas_call x2, Pallas kernels, slot_grad(): pl.pallas_call(slot_kernel, out_shape=(jax.ShapeDtypeStruct(patch_cells.s...  28.9 us
    ppermute x12, waiting for transfers between devices, xor_sum(): lax.ppermute(values, axis, [(i, i ^ step) for i in range(size)])  28.6 us
    all_to_all x2, starting transfers between devices, a2a_sum(): lax.all_to_all(flat, axis, 0, 0, tiled=True)  15.4 us
    all_to_all x2, starting transfers between devices, a2a_sum(): lax.all_to_all(jnp.broadcast_to(part, flat.shape), axis, 0, 0, tiled=True)  14.9 us
    all_to_all x2, waiting for transfers between devices, a2a_sum(): lax.all_to_all(jnp.broadcast_to(part, flat.shape), axis, 0, 0, tiled=True)  13.8 us
  transfers between devices with their start and end apart: 26, of which 16 were waited for; matrix products, arithmetic and copies ran while one was open for 3% of the time, Pallas kernels for 0%

profile of v8, /device:TPU:1, one launch (start us, length us, event | category | flops | bytes accessed | tf_op | source)
XLA Modules:
  0.0 288.1 jit_solution(1906633004947822933)
XLA Ops:
  0.7 1.1 pad_maximum_fusion.2
  1.8 11.5 %collective-permute-start.1 = (f32[2,3,128,128]{3,2,1,0:T(8,128)S(1)}, f32[2,3,128,128]{3,2,1,0:T(8,128)S(1)}, u32[]{:S(2)}, u32[]{:S(2)}) collective-permute-start(f32[2,3,128,128]{3,2,1,0:T(8,128)S(1)} %pad_maximum_fusion.2), channel_id=1, source_target_pairs={{0,448},{8,456},{16,464},{24,472},{32,480},{40,488},{48,496},{56,5... | collective-permute-start | bytes 1179656 | tf_op jit(solution)/shard_map/ppermute | solution.py:20
  13.3 5.1 %collective-permute-start = (f32[2,3,128,128]{3,2,1,0:T(8,128)S(1)}, f32[2,3,128,128]{3,2,1,0:T(8,128)S(1)}, u32[]{:S(2)}, u32[]{:S(2)}) collective-permute-start(f32[2,3,128,128]{3,2,1,0:T(8,128)S(1)} %pad_maximum_fusion.2), channel_id=1, source_target_pairs={{0,504},{8,0},{16,8},{24,16},{32,24},{40,32},{48,40},{56,48},{64,5... | collective-permute-start | bytes 1179656 | tf_op jit(solution)/shard_map/ppermute | solution.py:20
  18.4 0.6 fusion.20
  19.0 0.3 sine_multiply_fusion
  19.2 1.8 collective-permute-done.1
  21.0 16.6 %collective-permute-start.2 = (f32[2,3,128,128]{3,2,1,0:T(8,128)S(1)}, f32[2,3,128,128]{3,2,1,0:T(8,128)S(1)}, u32[]{:S(2)}, u32[]{:S(2)}) collective-permute-start(f32[2,3,128,128]{3,2,1,0:T(8,128)S(1)} %collective-permute-done.1), channel_id=1, source_target_pairs={{0,504},{8,0},{16,8},{24,16},{32,24},{40,32},{48,40},{56,48},{64,5... | collective-permute-start | bytes 1179656 | tf_op jit(solution)/shard_map/ppermute | solution.py:20
  47.4 0.3 fusion.13
  47.7 0.7 pad_maximum_fusion.3.tab_ref
  48.5 1.3 fusion.5.cells_ref
  49.7 14.4 %shard_map.85 = (f32[2,3,128,128]{3,2,1,0:T(8,128)}, f32[2,2,128,128]{3,2,1,0:T(8,128)}) custom-call(f32[2,3,128,128]{3,2,1,0:T(8,128)} %fusion.5.cells_ref, f32[2,2,128,128]{3,2,1,0:T(8,128)} %probe_ref.1, f32[128,128]{1,0:T(8,128)} %bitcast.49, f32[1,1]{1,0:T(1,128)} %bitcast.5.weight_ref, f32[4,128,128]{2,1,0:T(8,128)} %pad_maximum_fusion.3.tab_ref), custom_call_target="tpu_custom_call" | custom-call | flops 1342177280 | bytes 1441792 | tf_op jit(solution)/shard_map/pallas_call | solution.py:156
  64.2 1.7 pad_dynamic-slice_fusion.7
  65.9 1.9 collective-permute-start.3
  67.8 18.3 %collective-permute-done.3 = f32[12,128,128]{2,1,0:T(8,128)S(1)} collective-permute-done((f32[12,128,128]{2,1,0:T(8,128)S(1)}, f32[12,128,128]{2,1,0:T(8,128)S(1)}, u32[]{:S(2)}, u32[]{:S(2)}) %collective-permute-start.3) | collective-permute-done | bytes 786464 | tf_op jit(solution)/shard_map/ppermute | solution.py:20
  86.3 2.1 collective-permute-start.4
  88.4 10.9 %collective-permute-done.4 = f32[6,128,128]{2,1,0:T(8,128)S(1)} collective-permute-done((f32[6,128,128]{2,1,0:T(8,128)S(1)}, f32[6,128,128]{2,1,0:T(8,128)S(1)}, u32[]{:S(2)}, u32[]{:S(2)}) %collective-permute-start.4) | collective-permute-done | bytes 393248 | tf_op jit(solution)/shard_map/ppermute | solution.py:20
  99.4 5.6 %collective-permute-start.5 = (f32[6,128,128]{2,1,0:T(8,128)S(1)}, f32[6,128,128]{2,1,0:T(8,128)S(1)}, u32[]{:S(2)}, u32[]{:S(2)}) collective-permute-start(f32[6,128,128]{2,1,0:T(8,128)S(1)} %fusion.8), channel_id=1, source_target_pairs={{0,1},{1,0},{2,3},{3,2},{4,5},{5,4},{6,7},{7,6},{8,9},{9,8},{10,11... | collective-permute-start | bytes 1179656 | tf_op jit(solution)/shard_map/ppermute | solution.py:175
  105.0 1.9 collective-permute-start.11
  107.0 3.2 %collective-permute-start.6 = (f32[6,128,128]{2,1,0:T(8,128)S(1)}, f32[6,128,128]{2,1,0:T(8,128)S(1)}, u32[]{:S(2)}, u32[]{:S(2)}) collective-permute-start(f32[6,128,128]{2,1,0:T(8,128)S(1)} %add.165), channel_id=1, source_target_pairs={{0,2},{1,3},{2,0},{3,1},{4,6},{5,7},{6,4},{7,5},{8,10},{9,11},{10,... | collective-permute-start | bytes 1179656 | tf_op jit(solution)/shard_map/ppermute | solution.py:175
  110.3 2.1 collective-permute-start.12
  112.4 6.7 %collective-permute-done.6 = f32[6,128,128]{2,1,0:T(8,128)S(1)} collective-permute-done((f32[6,128,128]{2,1,0:T(8,128)S(1)}, f32[6,128,128]{2,1,0:T(8,128)S(1)}, u32[]{:S(2)}, u32[]{:S(2)}) %collective-permute-start.6) | collective-permute-done | bytes 393248 | tf_op jit(solution)/shard_map/ppermute | solution.py:175
  119.1 4.7 %collective-permute-start.7 = (f32[6,128,128]{2,1,0:T(8,128)S(1)}, f32[6,128,128]{2,1,0:T(8,128)S(1)}, u32[]{:S(2)}, u32[]{:S(2)}) collective-permute-start(f32[6,128,128]{2,1,0:T(8,128)S(1)} %add.166), channel_id=1, source_target_pairs={{0,4},{1,5},{2,6},{3,7},{4,0},{5,1},{6,2},{7,3},{8,12},{9,13},{10,... | collective-permute-start | bytes 1179656 | tf_op jit(solution)/shard_map/ppermute | solution.py:175
  123.8 0.9 collective-permute-done.12
  124.8 4.7 %collective-permute-start.13 = (f32[2,2,128,128]{3,2,1,0:T(8,128)S(1)}, f32[2,2,128,128]{3,2,1,0:T(8,128)S(1)}, u32[]{:S(2)}, u32[]{:S(2)}) collective-permute-start(f32[2,2,128,128]{3,2,1,0:T(8,128)S(1)} %add.169), channel_id=1, source_target_pairs={{0,4},{1,5},{2,6},{3,7},{4,0},{5,1},{6,2},{7,3},{8,12},{9,13},{10,... | collective-permute-start | bytes 786440 | tf_op jit(solution)/shard_map/ppermute | solution.py:175
  129.4 11.5 %collective-permute-done.13 = f32[2,2,128,128]{3,2,1,0:T(8,128)S(1)} collective-permute-done((f32[2,2,128,128]{3,2,1,0:T(8,128)S(1)}, f32[2,2,128,128]{3,2,1,0:T(8,128)S(1)}, u32[]{:S(2)}, u32[]{:S(2)}) %collective-permute-start.13) | collective-permute-done | bytes 262176 | tf_op jit(solution)/shard_map/ppermute | solution.py:175
  140.9 0.7 add.170
  141.6 4.6 %all-to-all-start = ((f32[64,1,1024]{2,1,0:T(1,128)}), f32[64,1,1024]{2,1,0:T(1,128)S(1)}, u32[]{:S(2)}, u32[]{:S(2)}) async-start(f32[64,1,1024]{2,1,0:T(1,128)} %bitcast.11), calls=%async_computation | async-start | bytes 524288 | tf_op jit(solution)/shard_map/all_to_all | solution.py:182
  146.4 4.5 %collective-permute-start.9 = (f32[2,3,128,128]{3,2,1,0:T(8,128)S(1)}, f32[2,3,128,128]{3,2,1,0:T(8,128)S(1)}, u32[]{:S(2)}, u32[]{:S(2)}) collective-permute-start(f32[2,3,128,128]{3,2,1,0:T(8,128)S(1)} %fusion.19), channel_id=1, source_target_pairs={{0,448},{8,456},{16,464},{24,472},{32,480},{40,488},{48,496},{56,5... | collective-permute-start | bytes 1179656 | tf_op jit(solution)/shard_map/ppermute | solution.py:20
  150.9 7.8 %all-to-all-done = f32[64,1,1024]{2,1,0:T(1,128)S(1)} async-done(((f32[64,1,1024]{2,1,0:T(1,128)}), f32[64,1,1024]{2,1,0:T(1,128)S(1)}, u32[]{:S(2)}, u32[]{:S(2)}) %all-to-all-start) | async-done | bytes 262176 | tf_op jit(solution)/shard_map/all_to_all | solution.py:182
  158.7 0.2 reduce_sum.18
  158.9 0.8 broadcast_in_dim.4
  159.7 5.8 %all-to-all-start.1 = ((f32[64,1,1024]{2,1,0:T(1,128)}), f32[64,1,1024]{2,1,0:T(1,128)S(1)}, u32[]{:S(2)}, u32[]{:S(2)}) async-start(f32[64,1,1024]{2,1,0:T(1,128)} %broadcast_in_dim.4), calls=%async_computation.1 | async-start | bytes 524288 | tf_op jit(solution)/shard_map/all_to_all | solution.py:183
  165.5 6.6 %collective-permute-start.8 = (f32[2,3,128,128]{3,2,1,0:T(8,128)S(1)}, f32[2,3,128,128]{3,2,1,0:T(8,128)S(1)}, u32[]{:S(2)}, u32[]{:S(2)}) collective-permute-start(f32[2,3,128,128]{3,2,1,0:T(8,128)S(1)} %fusion.19), channel_id=1, source_target_pairs={{0,504},{8,0},{16,8},{24,16},{32,24},{40,32},{48,40},{56,48},{64,5... | collective-permute-start | bytes 1179656 | tf_op jit(solution)/shard_map/ppermute | solution.py:20
  172.0 3.1 %collective-permute-start.10 = (f32[2,3,128,128]{3,2,1,0:T(8,128)S(1)}, f32[2,3,128,128]{3,2,1,0:T(8,128)S(1)}, u32[]{:S(2)}, u32[]{:S(2)}) collective-permute-start(f32[2,3,128,128]{3,2,1,0:T(8,128)S(1)} %collective-permute-done.9), channel_id=1, source_target_pairs={{0,504},{8,0},{16,8},{24,16},{32,24},{40,32},{48,40},{56,48},{64,5... | collective-permute-start | bytes 1179656 | tf_op jit(solution)/shard_map/ppermute | solution.py:20
  175.1 2.8 all-to-all-done.1
  178.0 0.3 broadcast_multiply_fusion.1
  178.2 0.7 sub.48.probe_ref
  179.0 1.2 collective-permute-done.8
  180.2 8.4 %collective-permute-done.10 = f32[2,3,128,128]{3,2,1,0:T(8,128)S(1)} collective-permute-done((f32[2,3,128,128]{3,2,1,0:T(8,128)S(1)}, f32[2,3,128,128]{3,2,1,0:T(8,128)S(1)}, u32[]{:S(2)}, u32[]{:S(2)}) %collective-permute-start.10) | collective-permute-done | bytes 393248 | tf_op jit(solution)/shard_map/ppermute | solution.py:20
  188.6 1.2 fusion.1.cells_ref
  189.8 14.4 %shard_map.86 = (f32[2,3,128,128]{3,2,1,0:T(8,128)}, f32[2,2,128,128]{3,2,1,0:T(8,128)}) custom-call(f32[2,3,128,128]{3,2,1,0:T(8,128)} %fusion.1.cells_ref, f32[2,2,128,128]{3,2,1,0:T(8,128)} %sub.48.probe_ref, f32[128,128]{1,0:T(8,128)} %bitcast.50, f32[1,1]{1,0:T(1,128)} %bitcast.5.weight_ref, f32[4,128,128]{2,1,0:T(8,128)} %pad_maximum_fusion.3.tab_ref), custom_call_target="tpu_custom_call" | custom-call | flops 1342177280 | bytes 1441792 | tf_op jit(solution)/shard_map/pallas_call | solution.py:156
  204.3 1.7 pad_dynamic-slice_fusion.3
  206.1 2.9 %collective-permute-start.14 = (f32[12,128,128]{2,1,0:T(8,128)S(1)}, f32[12,128,128]{2,1,0:T(8,128)S(1)}, u32[]{:S(2)}, u32[]{:S(2)}) collective-permute-start(f32[12,128,128]{2,1,0:T(8,128)S(1)} %pad_maximum_fusion.1), channel_id=1, source_target_pairs={{0,64},{8,72},{16,80},{24,88},{32,96},{40,104},{48,112},{56,120},{... | collective-permute-start | bytes 2359304 | tf_op jit(solution)/shard_map/ppermute | solution.py:20
  209.0 4.3 %collective-permute-start.19 = (f32[2,2,128,128]{3,2,1,0:T(8,128)S(1)}, f32[2,2,128,128]{3,2,1,0:T(8,128)S(1)}, u32[]{:S(2)}, u32[]{:S(2)}) collective-permute-start(f32[2,2,128,128]{3,2,1,0:T(8,128)S(1)} %copy-done.5), channel_id=1, source_target_pairs={{0,1},{1,0},{2,3},{3,2},{4,5},{5,4},{6,7},{7,6},{8,9},{9,8},{10,11... | collective-permute-start | bytes 786440 | tf_op jit(solution)/shard_map/ppermute | solution.py:175
  213.2 1.1 collective-permute-done.19
  214.4 2.1 collective-permute-start.20
  216.6 9.2 %collective-permute-done.14 = f32[12,128,128]{2,1,0:T(8,128)S(1)} collective-permute-done((f32[12,128,128]{2,1,0:T(8,128)S(1)}, f32[12,128,128]{2,1,0:T(8,128)S(1)}, u32[]{:S(2)}, u32[]{:S(2)}) %collective-permute-start.14) | collective-permute-done | bytes 786464 | tf_op jit(solution)/shard_map/ppermute | solution.py:20
  225.9 4.1 %collective-permute-start.15 = (f32[6,128,128]{2,1,0:T(8,128)S(1)}, f32[6,128,128]{2,1,0:T(8,128)S(1)}, u32[]{:S(2)}, u32[]{:S(2)}) collective-permute-start(f32[6,128,128]{2,1,0:T(8,128)S(1)} %slice_add_fusion), channel_id=1, source_target_pairs={{0,8},{8,16},{16,24},{24,32},{32,40},{40,48},{48,56},{56,64},{64,7... | collective-permute-start | bytes 1179656 | tf_op jit(solution)/shard_map/ppermute | solution.py:20
  230.0 1.9 collective-permute-start.21
  231.9 7.0 %collective-permute-done.21 = f32[2,2,128,128]{3,2,1,0:T(8,128)S(1)} collective-permute-done((f32[2,2,128,128]{3,2,1,0:T(8,128)S(1)}, f32[2,2,128,128]{3,2,1,0:T(8,128)S(1)}, u32[]{:S(2)}, u32[]{:S(2)}) %collective-permute-start.21) | collective-permute-done | bytes 262176 | tf_op jit(solution)/shard_map/ppermute | solution.py:175
  238.9 0.7 add.179
  239.6 10.8 %all-to-all-start.2 = ((f32[64,1,1024]{2,1,0:T(1,128)}), f32[64,1,1024]{2,1,0:T(1,128)S(1)}, u32[]{:S(2)}, u32[]{:S(2)}) async-start(f32[64,1,1024]{2,1,0:T(1,128)} %bitcast.22), calls=%async_computation.2 | async-start | bytes 524288 | tf_op jit(solution)/shard_map/all_to_all | solution.py:182
  250.6 5.9 %collective-permute-start.16 = (f32[6,128,128]{2,1,0:T(8,128)S(1)}, f32[6,128,128]{2,1,0:T(8,128)S(1)}, u32[]{:S(2)}, u32[]{:S(2)}) collective-permute-start(f32[6,128,128]{2,1,0:T(8,128)S(1)} %fusion.7), channel_id=1, source_target_pairs={{0,1},{1,0},{2,3},{3,2},{4,5},{5,4},{6,7},{7,6},{8,9},{9,8},{10,11... | collective-permute-start | bytes 1179656 | tf_op jit(solution)/shard_map/ppermute | solution.py:175
  256.4 1.3 collective-permute-done.16
  257.8 1.9 collective-permute-start.17
  259.7 3.3 %all-to-all-done.2 = f32[64,1,1024]{2,1,0:T(1,128)S(1)} async-done(((f32[64,1,1024]{2,1,0:T(1,128)}), f32[64,1,1024]{2,1,0:T(1,128)S(1)}, u32[]{:S(2)}, u32[]{:S(2)}) %all-to-all-start.2) | async-done | bytes 262176 | tf_op jit(solution)/shard_map/all_to_all | solution.py:182
  263.0 0.2 reduce_sum.19
  263.2 0.8 broadcast_in_dim.5
  264.1 9.1 %all-to-all-start.3 = ((f32[64,1,1024]{2,1,0:T(1,128)}), f32[64,1,1024]{2,1,0:T(1,128)S(1)}, u32[]{:S(2)}, u32[]{:S(2)}) async-start(f32[64,1,1024]{2,1,0:T(1,128)} %broadcast_in_dim.5), calls=%async_computation.3 | async-start | bytes 524288 | tf_op jit(solution)/shard_map/all_to_all | solution.py:183
  273.3 1.9 collective-permute-start.18
  275.2 11.0 %all-to-all-done.3 = f32[64,1,1024]{2,1,0:T(1,128)S(1)} async-done(((f32[64,1,1024]{2,1,0:T(1,128)}), f32[64,1,1024]{2,1,0:T(1,128)S(1)}, u32[]{:S(2)}, u32[]{:S(2)}) %all-to-all-start.3) | async-done | bytes 262176 | tf_op jit(solution)/shard_map/all_to_all | solution.py:183
  286.2 0.3 broadcast_multiply_fusion
  286.5 0.7 sub.50
  287.4 0.8 slice_bitcast_fusion
  (43 shorter events, 1.0 us)
Async XLA Ops:
  0.6 17.7 %copy-start.6 = (s32[1,1,1,2]{3,2,1,0:T(1,128)S(1)}, s32[1,1,1,2]{3,2,1,0:T(1,128)}, u32[]{:S(2)}) copy-start(s32[1,1,1,2]{3,2,1,0:T(1,128)} %param.10) | copy-start | bytes 28
  0.6 47.8 %copy-start = (f32[3,1,128,128]{3,2,1,0:T(8,128)S(1)}, f32[3,1,128,128]{3,2,1,0:T(8,128)}, u32[]{:S(2)}) copy-start(f32[3,1,128,128]{3,2,1,0:T(8,128)} %param.6) | copy-start | bytes 589828
  0.7 47.8 %copy-start.1 = (f32[3,1,128,128]{3,2,1,0:T(8,128)S(1)}, f32[3,1,128,128]{3,2,1,0:T(8,128)}, u32[]{:S(2)}) copy-start(f32[3,1,128,128]{3,2,1,0:T(8,128)} %param.7) | copy-start | bytes 589828
  1.8 19.3 %collective-permute-start.1 = (f32[2,3,128,128]{3,2,1,0:T(8,128)S(1)}, f32[2,3,128,128]{3,2,1,0:T(8,128)S(1)}, u32[]{:S(2)}, u32[]{:S(2)}) collective-permute-start(f32[2,3,128,128]{3,2,1,0:T(8,128)S(1)} %pad_maximum_fusion.2), channel_id=1, source_target_pairs={{0,448},{8,456},{16,464},{24,472},{32,480},{40,488},{48,496},{56,5... | collective-permute-start | bytes 1179656 | tf_op jit(solution)/shard_map/ppermute | solution.py:20
  13.3 35.2 %collective-permute-start = (f32[2,3,128,128]{3,2,1,0:T(8,128)S(1)}, f32[2,3,128,128]{3,2,1,0:T(8,128)S(1)}, u32[]{:S(2)}, u32[]{:S(2)}) collective-permute-start(f32[2,3,128,128]{3,2,1,0:T(8,128)S(1)} %pad_maximum_fusion.2), channel_id=1, source_target_pairs={{0,504},{8,0},{16,8},{24,16},{32,24},{40,32},{48,40},{56,48},{64,5... | collective-permute-start | bytes 1179656 | tf_op jit(solution)/shard_map/ppermute | solution.py:20
  21.0 27.4 %collective-permute-start.2 = (f32[2,3,128,128]{3,2,1,0:T(8,128)S(1)}, f32[2,3,128,128]{3,2,1,0:T(8,128)S(1)}, u32[]{:S(2)}, u32[]{:S(2)}) collective-permute-start(f32[2,3,128,128]{3,2,1,0:T(8,128)S(1)} %collective-permute-done.1), channel_id=1, source_target_pairs={{0,504},{8,0},{16,8},{24,16},{32,24},{40,32},{48,40},{56,48},{64,5... | collective-permute-start | bytes 1179656 | tf_op jit(solution)/shard_map/ppermute | solution.py:20
  65.9 20.3 %collective-permute-start.3 = (f32[12,128,128]{2,1,0:T(8,128)S(1)}, f32[12,128,128]{2,1,0:T(8,128)S(1)}, u32[]{:S(2)}, u32[]{:S(2)}) collective-permute-start(f32[12,128,128]{2,1,0:T(8,128)S(1)} %pad_maximum_fusion), channel_id=1, source_target_pairs={{0,64},{8,72},{16,80},{24,88},{32,96},{40,104},{48,112},{56,120},{... | collective-permute-start | bytes 2359304 | tf_op jit(solution)/shard_map/ppermute | solution.py:20
  86.3 13.0 %collective-permute-start.4 = (f32[6,128,128]{2,1,0:T(8,128)S(1)}, f32[6,128,128]{2,1,0:T(8,128)S(1)}, u32[]{:S(2)}, u32[]{:S(2)}) collective-permute-start(f32[6,128,128]{2,1,0:T(8,128)S(1)} %slice_add_fusion.2), channel_id=1, source_target_pairs={{0,8},{8,16},{16,24},{24,32},{32,40},{40,48},{48,56},{56,64},{64,7... | collective-permute-start | bytes 1179656 | tf_op jit(solution)/shard_map/ppermute | solution.py:20
  99.3 5.7 %copy-start.4 = (f32[2,2,128,128]{3,2,1,0:T(8,128)S(1)}, f32[2,2,128,128]{3,2,1,0:T(8,128)}, u32[]{:S(2)}) copy-start(f32[2,2,128,128]{3,2,1,0:T(8,128)} %get-tuple-element.8) | copy-start | bytes 786436
  99.4 7.6 %collective-permute-start.5 = (f32[6,128,128]{2,1,0:T(8,128)S(1)}, f32[6,128,128]{2,1,0:T(8,128)S(1)}, u32[]{:S(2)}, u32[]{:S(2)}) collective-permute-start(f32[6,128,128]{2,1,0:T(8,128)S(1)} %fusion.8), channel_id=1, source_target_pairs={{0,1},{1,0},{2,3},{3,2},{4,5},{5,4},{6,7},{7,6},{8,9},{9,8},{10,11... | collective-permute-start | bytes 1179656 | tf_op jit(solution)/shard_map/ppermute | solution.py:175
  105.0 5.2 %collective-permute-start.11 = (f32[2,2,128,128]{3,2,1,0:T(8,128)S(1)}, f32[2,2,128,128]{3,2,1,0:T(8,128)S(1)}, u32[]{:S(2)}, u32[]{:S(2)}) collective-permute-start(f32[2,2,128,128]{3,2,1,0:T(8,128)S(1)} %copy-done.4), channel_id=1, source_target_pairs={{0,1},{1,0},{2,3},{3,2},{4,5},{5,4},{6,7},{7,6},{8,9},{9,8},{10,11... | collective-permute-start | bytes 786440 | tf_op jit(solution)/shard_map/ppermute | solution.py:175
  107.0 12.1 %collective-permute-start.6 = (f32[6,128,128]{2,1,0:T(8,128)S(1)}, f32[6,128,128]{2,1,0:T(8,128)S(1)}, u32[]{:S(2)}, u32[]{:S(2)}) collective-permute-start(f32[6,128,128]{2,1,0:T(8,128)S(1)} %add.165), channel_id=1, source_target_pairs={{0,2},{1,3},{2,0},{3,1},{4,6},{5,7},{6,4},{7,5},{8,10},{9,11},{10,... | collective-permute-start | bytes 1179656 | tf_op jit(solution)/shard_map/ppermute | solution.py:175
  110.3 14.5 %collective-permute-start.12 = (f32[2,2,128,128]{3,2,1,0:T(8,128)S(1)}, f32[2,2,128,128]{3,2,1,0:T(8,128)S(1)}, u32[]{:S(2)}, u32[]{:S(2)}) collective-permute-start(f32[2,2,128,128]{3,2,1,0:T(8,128)S(1)} %add.168), channel_id=1, source_target_pairs={{0,2},{1,3},{2,0},{3,1},{4,6},{5,7},{6,4},{7,5},{8,10},{9,11},{10,... | collective-permute-start | bytes 786440 | tf_op jit(solution)/shard_map/ppermute | solution.py:175
  119.1 27.1 %collective-permute-start.7 = (f32[6,128,128]{2,1,0:T(8,128)S(1)}, f32[6,128,128]{2,1,0:T(8,128)S(1)}, u32[]{:S(2)}, u32[]{:S(2)}) collective-permute-start(f32[6,128,128]{2,1,0:T(8,128)S(1)} %add.166), channel_id=1, source_target_pairs={{0,4},{1,5},{2,6},{3,7},{4,0},{5,1},{6,2},{7,3},{8,12},{9,13},{10,... | collective-permute-start | bytes 1179656 | tf_op jit(solution)/shard_map/ppermute | solution.py:175
  124.8 16.1 %collective-permute-start.13 = (f32[2,2,128,128]{3,2,1,0:T(8,128)S(1)}, f32[2,2,128,128]{3,2,1,0:T(8,128)S(1)}, u32[]{:S(2)}, u32[]{:S(2)}) collective-permute-start(f32[2,2,128,128]{3,2,1,0:T(8,128)S(1)} %add.169), channel_id=1, source_target_pairs={{0,4},{1,5},{2,6},{3,7},{4,0},{5,1},{6,2},{7,3},{8,12},{9,13},{10,... | collective-permute-start | bytes 786440 | tf_op jit(solution)/shard_map/ppermute | solution.py:175
  141.6 17.1 %all-to-all-start = ((f32[64,1,1024]{2,1,0:T(1,128)}), f32[64,1,1024]{2,1,0:T(1,128)S(1)}, u32[]{:S(2)}, u32[]{:S(2)}) async-start(f32[64,1,1024]{2,1,0:T(1,128)} %bitcast.11), calls=%async_computation | async-start | bytes 524288 | tf_op jit(solution)/shard_map/all_to_all | solution.py:182
  146.3 31.9 %copy-start.3 = (f32[2,2,128,128]{3,2,1,0:T(8,128)S(1)}, f32[2,2,128,128]{3,2,1,0:T(8,128)}, u32[]{:S(2)}) copy-start(f32[2,2,128,128]{3,2,1,0:T(8,128)} %probe_ref.1) | copy-start | bytes 786436
  146.4 25.7 %collective-permute-start.9 = (f32[2,3,128,128]{3,2,1,0:T(8,128)S(1)}, f32[2,3,128,128]{3,2,1,0:T(8,128)S(1)}, u32[]{:S(2)}, u32[]{:S(2)}) collective-permute-start(f32[2,3,128,128]{3,2,1,0:T(8,128)S(1)} %fusion.19), channel_id=1, source_target_pairs={{0,448},{8,456},{16,464},{24,472},{32,480},{40,488},{48,496},{56,5... | collective-permute-start | bytes 1179656 | tf_op jit(solution)/shard_map/ppermute | solution.py:20
  159.7 18.3 %all-to-all-start.1 = ((f32[64,1,1024]{2,1,0:T(1,128)}), f32[64,1,1024]{2,1,0:T(1,128)S(1)}, u32[]{:S(2)}, u32[]{:S(2)}) async-start(f32[64,1,1024]{2,1,0:T(1,128)} %broadcast_in_dim.4), calls=%async_computation.1 | async-start | bytes 524288 | tf_op jit(solution)/shard_map/all_to_all | solution.py:183
  165.5 14.7 %collective-permute-start.8 = (f32[2,3,128,128]{3,2,1,0:T(8,128)S(1)}, f32[2,3,128,128]{3,2,1,0:T(8,128)S(1)}, u32[]{:S(2)}, u32[]{:S(2)}) collective-permute-start(f32[2,3,128,128]{3,2,1,0:T(8,128)S(1)} %fusion.19), channel_id=1, source_target_pairs={{0,504},{8,0},{16,8},{24,16},{32,24},{40,32},{48,40},{56,48},{64,5... | collective-permute-start | bytes 1179656 | tf_op jit(solution)/shard_map/ppermute | solution.py:20
  172.0 16.5 %collective-permute-start.10 = (f32[2,3,128,128]{3,2,1,0:T(8,128)S(1)}, f32[2,3,128,128]{3,2,1,0:T(8,128)S(1)}, u32[]{:S(2)}, u32[]{:S(2)}) collective-permute-start(f32[2,3,128,128]{3,2,1,0:T(8,128)S(1)} %collective-permute-done.9), channel_id=1, source_target_pairs={{0,504},{8,0},{16,8},{24,16},{32,24},{40,32},{48,40},{56,48},{64,5... | collective-permute-start | bytes 1179656 | tf_op jit(solution)/shard_map/ppermute | solution.py:20
  206.0 3.0 %copy-start.5 = (f32[2,2,128,128]{3,2,1,0:T(8,128)S(1)}, f32[2,2,128,128]{3,2,1,0:T(8,128)}, u32[]{:S(2)}) copy-start(f32[2,2,128,128]{3,2,1,0:T(8,128)} %get-tuple-element.10) | copy-start | bytes 786436
  206.1 19.8 %collective-permute-start.14 = (f32[12,128,128]{2,1,0:T(8,128)S(1)}, f32[12,128,128]{2,1,0:T(8,128)S(1)}, u32[]{:S(2)}, u32[]{:S(2)}) collective-permute-start(f32[12,128,128]{2,1,0:T(8,128)S(1)} %pad_maximum_fusion.1), channel_id=1, source_target_pairs={{0,64},{8,72},{16,80},{24,88},{32,96},{40,104},{48,112},{56,120},{... | collective-permute-start | bytes 2359304 | tf_op jit(solution)/shard_map/ppermute | solution.py:20
  209.0 5.4 %collective-permute-start.19 = (f32[2,2,128,128]{3,2,1,0:T(8,128)S(1)}, f32[2,2,128,128]{3,2,1,0:T(8,128)S(1)}, u32[]{:S(2)}, u32[]{:S(2)}) collective-permute-start(f32[2,2,128,128]{3,2,1,0:T(8,128)S(1)} %copy-done.5), channel_id=1, source_target_pairs={{0,1},{1,0},{2,3},{3,2},{4,5},{5,4},{6,7},{7,6},{8,9},{9,8},{10,11... | collective-permute-start | bytes 786440 | tf_op jit(solution)/shard_map/ppermute | solution.py:175
  214.4 15.5 %collective-permute-start.20 = (f32[2,2,128,128]{3,2,1,0:T(8,128)S(1)}, f32[2,2,128,128]{3,2,1,0:T(8,128)S(1)}, u32[]{:S(2)}, u32[]{:S(2)}) collective-permute-start(f32[2,2,128,128]{3,2,1,0:T(8,128)S(1)} %add.177), channel_id=1, source_target_pairs={{0,2},{1,3},{2,0},{3,1},{4,6},{5,7},{6,4},{7,5},{8,10},{9,11},{10,... | collective-permute-start | bytes 786440 | tf_op jit(solution)/shard_map/ppermute | solution.py:175
  225.9 24.6 %collective-permute-start.15 = (f32[6,128,128]{2,1,0:T(8,128)S(1)}, f32[6,128,128]{2,1,0:T(8,128)S(1)}, u32[]{:S(2)}, u32[]{:S(2)}) collective-permute-start(f32[6,128,128]{2,1,0:T(8,128)S(1)} %slice_add_fusion), channel_id=1, source_target_pairs={{0,8},{8,16},{16,24},{24,32},{32,40},{40,48},{48,56},{56,64},{64,7... | collective-permute-start | bytes 1179656 | tf_op jit(solution)/shard_map/ppermute | solution.py:20
  230.0 8.9 %collective-permute-start.21 = (f32[2,2,128,128]{3,2,1,0:T(8,128)S(1)}, f32[2,2,128,128]{3,2,1,0:T(8,128)S(1)}, u32[]{:S(2)}, u32[]{:S(2)}) collective-permute-start(f32[2,2,128,128]{3,2,1,0:T(8,128)S(1)} %add.178), channel_id=1, source_target_pairs={{0,4},{1,5},{2,6},{3,7},{4,0},{5,1},{6,2},{7,3},{8,12},{9,13},{10,... | collective-permute-start | bytes 786440 | tf_op jit(solution)/shard_map/ppermute | solution.py:175
  239.6 23.4 %all-to-all-start.2 = ((f32[64,1,1024]{2,1,0:T(1,128)}), f32[64,1,1024]{2,1,0:T(1,128)S(1)}, u32[]{:S(2)}, u32[]{:S(2)}) async-start(f32[64,1,1024]{2,1,0:T(1,128)} %bitcast.22), calls=%async_computation.2 | async-start | bytes 524288 | tf_op jit(solution)/shard_map/all_to_all | solution.py:182
  250.6 7.2 %collective-permute-start.16 = (f32[6,128,128]{2,1,0:T(8,128)S(1)}, f32[6,128,128]{2,1,0:T(8,128)S(1)}, u32[]{:S(2)}, u32[]{:S(2)}) collective-permute-start(f32[6,128,128]{2,1,0:T(8,128)S(1)} %fusion.7), channel_id=1, source_target_pairs={{0,1},{1,0},{2,3},{3,2},{4,5},{5,4},{6,7},{7,6},{8,9},{9,8},{10,11... | collective-permute-start | bytes 1179656 | tf_op jit(solution)/shard_map/ppermute | solution.py:175
  257.8 15.4 %collective-permute-start.17 = (f32[6,128,128]{2,1,0:T(8,128)S(1)}, f32[6,128,128]{2,1,0:T(8,128)S(1)}, u32[]{:S(2)}, u32[]{:S(2)}) collective-permute-start(f32[6,128,128]{2,1,0:T(8,128)S(1)} %add.174), channel_id=1, source_target_pairs={{0,2},{1,3},{2,0},{3,1},{4,6},{5,7},{6,4},{7,5},{8,10},{9,11},{10,... | collective-permute-start | bytes 1179656 | tf_op jit(solution)/shard_map/ppermute | solution.py:175
  264.1 22.2 %all-to-all-start.3 = ((f32[64,1,1024]{2,1,0:T(1,128)}), f32[64,1,1024]{2,1,0:T(1,128)S(1)}, u32[]{:S(2)}, u32[]{:S(2)}) async-start(f32[64,1,1024]{2,1,0:T(1,128)} %broadcast_in_dim.5), calls=%async_computation.3 | async-start | bytes 524288 | tf_op jit(solution)/shard_map/all_to_all | solution.py:183
  273.2 13.3 %copy-start.2 = (f32[2,2,128,128]{3,2,1,0:T(8,128)S(1)}, f32[2,2,128,128]{3,2,1,0:T(8,128)}, u32[]{:S(2)}) copy-start(f32[2,2,128,128]{3,2,1,0:T(8,128)} %sub.48.probe_ref) | copy-start | bytes 786436
  273.3 14.0 %collective-permute-start.18 = (f32[6,128,128]{2,1,0:T(8,128)S(1)}, f32[6,128,128]{2,1,0:T(8,128)S(1)}, u32[]{:S(2)}, u32[]{:S(2)}) collective-permute-start(f32[6,128,128]{2,1,0:T(8,128)S(1)} %add.175), channel_id=1, source_target_pairs={{0,4},{1,5},{2,6},{3,7},{4,0},{5,1},{6,2},{7,3},{8,12},{9,13},{10,... | collective-permute-start | bytes 1179656 | tf_op jit(solution)/shard_map/ppermute | solution.py:175

commit v9 on v7

--- a/solution.py
+++ b/solution.py
@@ -84,16 +84,13 @@
     wide = lambda a: jnp.concatenate([a] * mode_count, axis=1)
     cosine, sine_table = (tab_ref[0], tab_ref[1])
     kern = (wide(tab_ref[2]), wide(tab_ref[3]))
-    zero = jnp.zeros_like(cosine)
-
-    def block(a):
-        rows = [
-            jnp.concatenate([a if j == i else zero for j in range(mode_count)], axis=1)
-            for i in range(mode_count)
-        ]
-        return jnp.concatenate(rows, axis=0)
-
-    cos_block, sin_block = (block(cosine), block(sine_table))
+
+    stack = lambda a: jnp.concatenate(
+        [a[:, m * side : (m + 1) * side] for m in range(mode_count)], axis=0
+    )
+    unstack = lambda a: jnp.concatenate(
+        [a[m * side : (m + 1) * side] for m in range(mode_count)], axis=1
+    )
 
     def dot(a, b):
         return jnp.dot(a, b, precision=lax.Precision.HIGHEST, preferred_element_type=jnp.float32)
@@ -101,12 +98,20 @@
     def forward(xr, xi):
         lr = dot(cosine, xr) + dot(sine_table, xi)
         li = dot(cosine, xi) - dot(sine_table, xr)
-        return (dot(lr, cos_block) + dot(li, sin_block), dot(li, cos_block) - dot(lr, sin_block))
+        lr, li = (stack(lr), stack(li))
+        return (
+            unstack(dot(lr, cosine) + dot(li, sine_table)),
+            unstack(dot(li, cosine) - dot(lr, sine_table)),
+        )
 
     def inverse(xr, xi):
         lr = dot(cosine, xr) - dot(sine_table, xi)
         li = dot(cosine, xi) + dot(sine_table, xr)
-        return (dot(lr, cos_block) - dot(li, sin_block), dot(li, cos_block) + dot(lr, sin_block))
+        lr, li = (stack(lr), stack(li))
+        return (
+            unstack(dot(lr, cosine) - dot(li, sine_table)),
+            unstack(dot(li, cosine) + dot(lr, sine_table)),
+        )
 
     def mul(a, b):
         return (a[0] * b[0] - a[1] * b[1], a[0] * b[1] + a[1] * b[0])

time: 280 us -> 280 us (level)
  no operation moved by 1% of the time
where the time goes in v9:
time: 280 us; the launch traced here: 277 us
  starting transfers between devices  106 us (38%)
  waiting for transfers between devices  97.5 us (35%)
  Pallas kernels  28.8 us (10%)
  blocking collectives  18.5 us (7%)
  between operations  10.8 us (4%)
  other arithmetic  9.6 us (3%)
  local copies, waits for them, and re-layouts  5.67 us (2%)
    ppermute x8, waiting for transfers between devices, shifted(): lax.ppermute(shard, axis, [(i, (i + by) % size) for i in range(size)])  49.3 us
    ppermute x12, starting transfers between devices, xor_sum(): lax.ppermute(values, axis, [(i, i ^ step) for i in range(size)])  45.5 us
    ppermute x8, starting transfers between devices, shifted(): lax.ppermute(shard, axis, [(i, (i + by) % size) for i in range(size)])  36.3 us
    pallas_call x2, Pallas kernels, slot_grad(): pl.pallas_call(slot_kernel, out_shape=(jax.ShapeDtypeStruct(patch_cells.s...  28.8 us
    ppermute x12, waiting for transfers between devices, xor_sum(): lax.ppermute(values, axis, [(i, i ^ step) for i in range(size)])  28.8 us
    all_to_all x1, blocking collectives, a2a_sum(): lax.all_to_all(jnp.broadcast_to(part, flat.shape), axis, 0, 0, tiled=True)  18.5 us
    all_to_all x2, starting transfers between devices, a2a_sum(): lax.all_to_all(flat, axis, 0, 0, tiled=True)  14.1 us
    all_to_all x1, starting transfers between devices, a2a_sum(): lax.all_to_all(jnp.broadcast_to(part, flat.shape), axis, 0, 0, tiled=True)  10.6 us
  transfers between devices with their start and end apart: 23, of which 15 were waited for; matrix products, arithmetic and copies ran while one was open for 3% of the time, Pallas kernels for 0%

profile of v9, /device:TPU:1, one launch (start us, length us, event | category | flops | bytes accessed | tf_op | source)
XLA Modules:
  0.0 277.3 jit_solution(17713768223947731402)
XLA Ops:
  0.7 1.1 pad_maximum_fusion.4
  1.8 14.4 %collective-permute-start = (f32[2,3,128,128]{3,2,1,0:T(8,128)S(1)}, f32[2,3,128,128]{3,2,1,0:T(8,128)S(1)}, u32[]{:S(2)}, u32[]{:S(2)}) collective-permute-start(f32[2,3,128,128]{3,2,1,0:T(8,128)S(1)} %pad_maximum_fusion.4), channel_id=1, source_target_pairs={{0,504},{8,0},{16,8},{24,16},{32,24},{40,32},{48,40},{56,48},{64,5... | collective-permute-start | bytes 1179656 | tf_op jit(solution)/shard_map/ppermute | solution.py:20
  16.2 7.8 %collective-permute-done = f32[2,3,128,128]{3,2,1,0:T(8,128)S(1)} collective-permute-done((f32[2,3,128,128]{3,2,1,0:T(8,128)S(1)}, f32[2,3,128,128]{3,2,1,0:T(8,128)S(1)}, u32[]{:S(2)}, u32[]{:S(2)}) %collective-permute-start) | collective-permute-done | bytes 393248 | tf_op jit(solution)/shard_map/ppermute | solution.py:20
  24.0 2.2 collective-permute-start.1
  26.2 0.6 fusion.18
  36.5 0.3 sine_multiply_fusion
  36.8 0.3 fusion.11
  37.1 0.7 pad_maximum_fusion.5.tab_ref
  37.8 5.6 %collective-permute-done.1 = f32[2,3,128,256]{3,2,1,0:T(8,128)S(1)} collective-permute-done((f32[2,3,128,256]{3,2,1,0:T(8,128)S(1)}, f32[2,3,128,256]{3,2,1,0:T(8,128)S(1)}, u32[]{:S(2)}, u32[]{:S(2)}) %collective-permute-start.1) | collective-permute-done | bytes 786464 | tf_op jit(solution)/shard_map/ppermute | solution.py:20
  43.4 1.1 fusion.4.cells_ref
  44.5 14.4 %shard_map.85 = (f32[2,3,128,128]{3,2,1,0:T(8,128)}, f32[2,2,128,128]{3,2,1,0:T(8,128)}) custom-call(f32[2,3,128,128]{3,2,1,0:T(8,128)} %fusion.4.cells_ref, f32[2,2,128,128]{3,2,1,0:T(8,128)} %probe_ref.1, f32[128,128]{1,0:T(8,128)} %bitcast.51, f32[1,1]{1,0:T(1,128)} %bitcast.5.weight_ref, f32[4,128,128]{2,1,0:T(8,128)} %pad_maximum_fusion.5.tab_ref), custom_call_target="tpu_custom_call" | custom-call | flops 1342177280 | bytes 1441792 | tf_op jit(solution)/shard_map/pallas_call | solution.py:161
  58.9 1.7 pad_dynamic-slice_fusion.7
  60.6 1.9 collective-permute-start.2
  62.5 17.7 %collective-permute-done.2 = f32[12,128,128]{2,1,0:T(8,128)S(1)} collective-permute-done((f32[12,128,128]{2,1,0:T(8,128)S(1)}, f32[12,128,128]{2,1,0:T(8,128)S(1)}, u32[]{:S(2)}, u32[]{:S(2)}) %collective-permute-start.2) | collective-permute-done | bytes 786464 | tf_op jit(solution)/shard_map/ppermute | solution.py:20
  80.3 0.1 slice_add_fusion.2
  80.3 1.9 collective-permute-start.3
  82.3 11.6 %collective-permute-done.3 = f32[6,128,128]{2,1,0:T(8,128)S(1)} collective-permute-done((f32[6,128,128]{2,1,0:T(8,128)S(1)}, f32[6,128,128]{2,1,0:T(8,128)S(1)}, u32[]{:S(2)}, u32[]{:S(2)}) %collective-permute-start.3) | collective-permute-done | bytes 393248 | tf_op jit(solution)/shard_map/ppermute | solution.py:20
  93.9 0.1 fusion.6
  94.0 6.3 %collective-permute-start.4 = (f32[6,128,128]{2,1,0:T(8,128)S(1)}, f32[6,128,128]{2,1,0:T(8,128)S(1)}, u32[]{:S(2)}, u32[]{:S(2)}) collective-permute-start(f32[6,128,128]{2,1,0:T(8,128)S(1)} %fusion.6), channel_id=1, source_target_pairs={{0,1},{1,0},{2,3},{3,2},{4,5},{5,4},{6,7},{7,6},{8,9},{9,8},{10,11... | collective-permute-start | bytes 1179656 | tf_op jit(solution)/shard_map/ppermute | solution.py:180
  100.2 1.1 collective-permute-done.4
  101.4 3.1 %collective-permute-start.5 = (f32[6,128,128]{2,1,0:T(8,128)S(1)}, f32[6,128,128]{2,1,0:T(8,128)S(1)}, u32[]{:S(2)}, u32[]{:S(2)}) collective-permute-start(f32[6,128,128]{2,1,0:T(8,128)S(1)} %add.165), channel_id=1, source_target_pairs={{0,2},{1,3},{2,0},{3,1},{4,6},{5,7},{6,4},{7,5},{8,10},{9,11},{10,... | collective-permute-start | bytes 1179656 | tf_op jit(solution)/shard_map/ppermute | solution.py:180
  104.6 2.6 collective-permute-start.9
  107.2 6.5 %collective-permute-done.5 = f32[6,128,128]{2,1,0:T(8,128)S(1)} collective-permute-done((f32[6,128,128]{2,1,0:T(8,128)S(1)}, f32[6,128,128]{2,1,0:T(8,128)S(1)}, u32[]{:S(2)}, u32[]{:S(2)}) %collective-permute-start.5) | collective-permute-done | bytes 393248 | tf_op jit(solution)/shard_map/ppermute | solution.py:180
  113.7 4.6 %collective-permute-start.6 = (f32[6,128,128]{2,1,0:T(8,128)S(1)}, f32[6,128,128]{2,1,0:T(8,128)S(1)}, u32[]{:S(2)}, u32[]{:S(2)}) collective-permute-start(f32[6,128,128]{2,1,0:T(8,128)S(1)} %add.166), channel_id=1, source_target_pairs={{0,4},{1,5},{2,6},{3,7},{4,0},{5,1},{6,2},{7,3},{8,12},{9,13},{10,... | collective-permute-start | bytes 1179656 | tf_op jit(solution)/shard_map/ppermute | solution.py:180
  118.3 2.3 collective-permute-start.10
  120.6 11.6 %collective-permute-done.10 = f32[2,2,128,128]{3,2,1,0:T(8,128)S(1)} collective-permute-done((f32[2,2,128,128]{3,2,1,0:T(8,128)S(1)}, f32[2,2,128,128]{3,2,1,0:T(8,128)S(1)}, u32[]{:S(2)}, u32[]{:S(2)}) %collective-permute-start.10) | collective-permute-done | bytes 262176 | tf_op jit(solution)/shard_map/ppermute | solution.py:180
  132.2 3.7 %collective-permute-start.11 = (f32[2,2,128,128]{3,2,1,0:T(8,128)S(1)}, f32[2,2,128,128]{3,2,1,0:T(8,128)S(1)}, u32[]{:S(2)}, u32[]{:S(2)}) collective-permute-start(f32[2,2,128,128]{3,2,1,0:T(8,128)S(1)} %add.169), channel_id=1, source_target_pairs={{0,4},{1,5},{2,6},{3,7},{4,0},{5,1},{6,2},{7,3},{8,12},{9,13},{10,... | collective-permute-start | bytes 786440 | tf_op jit(solution)/shard_map/ppermute | solution.py:180
  136.0 3.4 %collective-permute-start.7 = (f32[2,3,128,128]{3,2,1,0:T(8,128)S(1)}, f32[2,3,128,128]{3,2,1,0:T(8,128)S(1)}, u32[]{:S(2)}, u32[]{:S(2)}) collective-permute-start(f32[2,3,128,128]{3,2,1,0:T(8,128)S(1)} %fusion.17), channel_id=1, source_target_pairs={{0,504},{8,0},{16,8},{24,16},{32,24},{40,32},{48,40},{56,48},{64,5... | collective-permute-start | bytes 1179656 | tf_op jit(solution)/shard_map/ppermute | solution.py:20
  139.4 1.9 collective-permute-done.11
  141.3 0.7 add.170
  142.0 4.6 %all-to-all-start = ((f32[64,1,1024]{2,1,0:T(1,128)}), f32[64,1,1024]{2,1,0:T(1,128)S(1)}, u32[]{:S(2)}, u32[]{:S(2)}) async-start(f32[64,1,1024]{2,1,0:T(1,128)} %bitcast.11), calls=%async_computation | async-start | bytes 524288 | tf_op jit(solution)/shard_map/all_to_all | solution.py:187
  146.7 4.4 %collective-permute-start.8 = (f32[2,3,128,256]{3,2,1,0:T(8,128)S(1)}, f32[2,3,128,256]{3,2,1,0:T(8,128)S(1)}, u32[]{:S(2)}, u32[]{:S(2)}) collective-permute-start(f32[2,3,128,256]{3,2,1,0:T(8,128)S(1)} %pad_maximum_fusion.2), channel_id=1, source_target_pairs={{0,448},{8,456},{16,464},{24,472},{32,480},{40,488},{48,496},{56,5... | collective-permute-start | bytes 2359304 | tf_op jit(solution)/shard_map/ppermute | solution.py:20
  151.1 8.1 %all-to-all-done = f32[64,1,1024]{2,1,0:T(1,128)S(1)} async-done(((f32[64,1,1024]{2,1,0:T(1,128)}), f32[64,1,1024]{2,1,0:T(1,128)S(1)}, u32[]{:S(2)}, u32[]{:S(2)}) %all-to-all-start) | async-done | bytes 262176 | tf_op jit(solution)/shard_map/all_to_all | solution.py:187
  159.2 0.2 reduce_sum.18
  159.4 0.1 broadcast_in_dim.4
  159.5 18.5 %all_to_all.30 = f32[64,1,1024]{2,1,0:T(1,128)S(1)} all-to-all(f32[64,1,1024]{2,1,0:T(1,128)S(1)} %broadcast_in_dim.4), channel_id=1, replica_groups=mesh['tile'=64,'scan'=8] {'tile'}, dimensions={0} | all-to-all | bytes 524288 | tf_op jit(solution)/shard_map/all_to_all | solution.py:188
  178.0 0.3 broadcast_multiply_fusion.1
  178.3 0.8 sub.48.probe_ref
  179.0 1.1 fusion.1.cells_ref
  180.2 14.4 %shard_map.86 = (f32[2,3,128,128]{3,2,1,0:T(8,128)}, f32[2,2,128,128]{3,2,1,0:T(8,128)}) custom-call(f32[2,3,128,128]{3,2,1,0:T(8,128)} %fusion.1.cells_ref, f32[2,2,128,128]{3,2,1,0:T(8,128)} %sub.48.probe_ref, f32[128,128]{1,0:T(8,128)} %bitcast.52, f32[1,1]{1,0:T(1,128)} %bitcast.5.weight_ref, f32[4,128,128]{2,1,0:T(8,128)} %pad_maximum_fusion.5.tab_ref), custom_call_target="tpu_custom_call" | custom-call | flops 1342177280 | bytes 1441792 | tf_op jit(solution)/shard_map/pallas_call | solution.py:161
  194.6 1.7 pad_dynamic-slice_fusion.3
  196.3 5.3 %collective-permute-start.12 = (f32[12,128,128]{2,1,0:T(8,128)S(1)}, f32[12,128,128]{2,1,0:T(8,128)S(1)}, u32[]{:S(2)}, u32[]{:S(2)}) collective-permute-start(f32[12,128,128]{2,1,0:T(8,128)S(1)} %pad_maximum_fusion.3), channel_id=1, source_target_pairs={{0,64},{8,72},{16,80},{24,88},{32,96},{40,104},{48,112},{56,120},{... | collective-permute-start | bytes 2359304 | tf_op jit(solution)/shard_map/ppermute | solution.py:20
  201.6 4.1 %collective-permute-start.17 = (f32[2,2,128,128]{3,2,1,0:T(8,128)S(1)}, f32[2,2,128,128]{3,2,1,0:T(8,128)S(1)}, u32[]{:S(2)}, u32[]{:S(2)}) collective-permute-start(f32[2,2,128,128]{3,2,1,0:T(8,128)S(1)} %copy-done.5), channel_id=1, source_target_pairs={{0,1},{1,0},{2,3},{3,2},{4,5},{5,4},{6,7},{7,6},{8,9},{9,8},{10,11... | collective-permute-start | bytes 786440 | tf_op jit(solution)/shard_map/ppermute | solution.py:180
  205.7 1.1 collective-permute-done.17
  206.9 3.0 %collective-permute-start.18 = (f32[2,2,128,128]{3,2,1,0:T(8,128)S(1)}, f32[2,2,128,128]{3,2,1,0:T(8,128)S(1)}, u32[]{:S(2)}, u32[]{:S(2)}) collective-permute-start(f32[2,2,128,128]{3,2,1,0:T(8,128)S(1)} %add.177), channel_id=1, source_target_pairs={{0,2},{1,3},{2,0},{3,1},{4,6},{5,7},{6,4},{7,5},{8,10},{9,11},{10,... | collective-permute-start | bytes 786440 | tf_op jit(solution)/shard_map/ppermute | solution.py:180
  209.8 6.7 %collective-permute-done.12 = f32[12,128,128]{2,1,0:T(8,128)S(1)} collective-permute-done((f32[12,128,128]{2,1,0:T(8,128)S(1)}, f32[12,128,128]{2,1,0:T(8,128)S(1)}, u32[]{:S(2)}, u32[]{:S(2)}) %collective-permute-start.12) | collective-permute-done | bytes 786464 | tf_op jit(solution)/shard_map/ppermute | solution.py:20
  216.6 2.8 %collective-permute-start.13 = (f32[6,128,128]{2,1,0:T(8,128)S(1)}, f32[6,128,128]{2,1,0:T(8,128)S(1)}, u32[]{:S(2)}, u32[]{:S(2)}) collective-permute-start(f32[6,128,128]{2,1,0:T(8,128)S(1)} %slice_add_fusion), channel_id=1, source_target_pairs={{0,8},{8,16},{16,24},{24,32},{32,40},{40,48},{48,56},{56,64},{64,7... | collective-permute-start | bytes 1179656 | tf_op jit(solution)/shard_map/ppermute | solution.py:20
  219.4 3.7 %collective-permute-start.19 = (f32[2,2,128,128]{3,2,1,0:T(8,128)S(1)}, f32[2,2,128,128]{3,2,1,0:T(8,128)S(1)}, u32[]{:S(2)}, u32[]{:S(2)}) collective-permute-start(f32[2,2,128,128]{3,2,1,0:T(8,128)S(1)} %add.178), channel_id=1, source_target_pairs={{0,4},{1,5},{2,6},{3,7},{4,0},{5,1},{6,2},{7,3},{8,12},{9,13},{10,... | collective-permute-start | bytes 786440 | tf_op jit(solution)/shard_map/ppermute | solution.py:180
  223.1 5.2 %collective-permute-done.19 = f32[2,2,128,128]{3,2,1,0:T(8,128)S(1)} collective-permute-done((f32[2,2,128,128]{3,2,1,0:T(8,128)S(1)}, f32[2,2,128,128]{3,2,1,0:T(8,128)S(1)}, u32[]{:S(2)}, u32[]{:S(2)}) %collective-permute-start.19) | collective-permute-done | bytes 262176 | tf_op jit(solution)/shard_map/ppermute | solution.py:180
  228.3 0.7 add.179
  229.1 9.5 %all-to-all-start.2 = ((f32[64,1,1024]{2,1,0:T(1,128)}), f32[64,1,1024]{2,1,0:T(1,128)S(1)}, u32[]{:S(2)}, u32[]{:S(2)}) async-start(f32[64,1,1024]{2,1,0:T(1,128)} %bitcast.22), calls=%async_computation.2 | async-start | bytes 524288 | tf_op jit(solution)/shard_map/all_to_all | solution.py:187
  238.7 6.1 %collective-permute-start.14 = (f32[6,128,128]{2,1,0:T(8,128)S(1)}, f32[6,128,128]{2,1,0:T(8,128)S(1)}, u32[]{:S(2)}, u32[]{:S(2)}) collective-permute-start(f32[6,128,128]{2,1,0:T(8,128)S(1)} %fusion.5), channel_id=1, source_target_pairs={{0,1},{1,0},{2,3},{3,2},{4,5},{5,4},{6,7},{7,6},{8,9},{9,8},{10,11... | collective-permute-start | bytes 1179656 | tf_op jit(solution)/shard_map/ppermute | solution.py:180
  244.8 1.3 collective-permute-done.14
  246.2 3.1 %collective-permute-start.15 = (f32[6,128,128]{2,1,0:T(8,128)S(1)}, f32[6,128,128]{2,1,0:T(8,128)S(1)}, u32[]{:S(2)}, u32[]{:S(2)}) collective-permute-start(f32[6,128,128]{2,1,0:T(8,128)S(1)} %add.174), channel_id=1, source_target_pairs={{0,2},{1,3},{2,0},{3,1},{4,6},{5,7},{6,4},{7,5},{8,10},{9,11},{10,... | collective-permute-start | bytes 1179656 | tf_op jit(solution)/shard_map/ppermute | solution.py:180
  249.2 1.8 all-to-all-done.2
  251.1 0.2 reduce_sum.19
  251.3 0.8 broadcast_in_dim.5
  252.1 10.6 %all-to-all-start.3 = ((f32[64,1,1024]{2,1,0:T(1,128)}), f32[64,1,1024]{2,1,0:T(1,128)S(1)}, u32[]{:S(2)}, u32[]{:S(2)}) async-start(f32[64,1,1024]{2,1,0:T(1,128)} %broadcast_in_dim.5), calls=%async_computation.3 | async-start | bytes 524288 | tf_op jit(solution)/shard_map/all_to_all | solution.py:188
  262.8 3.1 %collective-permute-start.16 = (f32[6,128,128]{2,1,0:T(8,128)S(1)}, f32[6,128,128]{2,1,0:T(8,128)S(1)}, u32[]{:S(2)}, u32[]{:S(2)}) collective-permute-start(f32[6,128,128]{2,1,0:T(8,128)S(1)} %add.175), channel_id=1, source_target_pairs={{0,4},{1,5},{2,6},{3,7},{4,0},{5,1},{6,2},{7,3},{8,12},{9,13},{10,... | collective-permute-start | bytes 1179656 | tf_op jit(solution)/shard_map/ppermute | solution.py:180
  265.9 9.5 %all-to-all-done.3 = f32[64,1,1024]{2,1,0:T(1,128)S(1)} async-done(((f32[64,1,1024]{2,1,0:T(1,128)}), f32[64,1,1024]{2,1,0:T(1,128)S(1)}, u32[]{:S(2)}, u32[]{:S(2)}) %all-to-all-start.3) | async-done | bytes 262176 | tf_op jit(solution)/shard_map/all_to_all | solution.py:188
  275.4 0.3 broadcast_multiply_fusion
  275.7 0.7 sub.50
  276.4 0.1 fusion.19
  276.5 0.8 slice_bitcast_fusion
  (40 shorter events, 0.9 us)
Async XLA Ops:
  0.6 23.3 %copy-start.1 = (f32[3,1,128,128]{3,2,1,0:T(8,128)S(1)}, f32[3,1,128,128]{3,2,1,0:T(8,128)}, u32[]{:S(2)}) copy-start(f32[3,1,128,128]{3,2,1,0:T(8,128)} %param.7) | copy-start | bytes 589828
  0.6 23.3 %copy-start = (f32[3,1,128,128]{3,2,1,0:T(8,128)S(1)}, f32[3,1,128,128]{3,2,1,0:T(8,128)}, u32[]{:S(2)}) copy-start(f32[3,1,128,128]{3,2,1,0:T(8,128)} %param.6) | copy-start | bytes 589828
  1.8 24.4 %copy-start.6 = (s32[1,1,1,2]{3,2,1,0:T(1,128)S(1)}, s32[1,1,1,2]{3,2,1,0:T(1,128)}, u32[]{:S(2)}) copy-start(s32[1,1,1,2]{3,2,1,0:T(1,128)} %param.10) | copy-start | bytes 28
  1.8 22.2 %collective-permute-start = (f32[2,3,128,128]{3,2,1,0:T(8,128)S(1)}, f32[2,3,128,128]{3,2,1,0:T(8,128)S(1)}, u32[]{:S(2)}, u32[]{:S(2)}) collective-permute-start(f32[2,3,128,128]{3,2,1,0:T(8,128)S(1)} %pad_maximum_fusion.4), channel_id=1, source_target_pairs={{0,504},{8,0},{16,8},{24,16},{32,24},{40,32},{48,40},{56,48},{64,5... | collective-permute-start | bytes 1179656 | tf_op jit(solution)/shard_map/ppermute | solution.py:20
  24.0 19.4 %collective-permute-start.1 = (f32[2,3,128,256]{3,2,1,0:T(8,128)S(1)}, f32[2,3,128,256]{3,2,1,0:T(8,128)S(1)}, u32[]{:S(2)}, u32[]{:S(2)}) collective-permute-start(f32[2,3,128,256]{3,2,1,0:T(8,128)S(1)} %pad_maximum_fusion), channel_id=1, source_target_pairs={{0,448},{8,456},{16,464},{24,472},{32,480},{40,488},{48,496},{56,5... | collective-permute-start | bytes 2359304 | tf_op jit(solution)/shard_map/ppermute | solution.py:20
  60.6 19.6 %collective-permute-start.2 = (f32[12,128,128]{2,1,0:T(8,128)S(1)}, f32[12,128,128]{2,1,0:T(8,128)S(1)}, u32[]{:S(2)}, u32[]{:S(2)}) collective-permute-start(f32[12,128,128]{2,1,0:T(8,128)S(1)} %pad_maximum_fusion.1), channel_id=1, source_target_pairs={{0,64},{8,72},{16,80},{24,88},{32,96},{40,104},{48,112},{56,120},{... | collective-permute-start | bytes 2359304 | tf_op jit(solution)/shard_map/ppermute | solution.py:20
  80.3 13.5 %collective-permute-start.3 = (f32[6,128,128]{2,1,0:T(8,128)S(1)}, f32[6,128,128]{2,1,0:T(8,128)S(1)}, u32[]{:S(2)}, u32[]{:S(2)}) collective-permute-start(f32[6,128,128]{2,1,0:T(8,128)S(1)} %slice_add_fusion.2), channel_id=1, source_target_pairs={{0,8},{8,16},{16,24},{24,32},{32,40},{40,48},{48,56},{56,64},{64,7... | collective-permute-start | bytes 1179656 | tf_op jit(solution)/shard_map/ppermute | solution.py:20
  94.0 10.6 %copy-start.4 = (f32[2,2,128,128]{3,2,1,0:T(8,128)S(1)}, f32[2,2,128,128]{3,2,1,0:T(8,128)}, u32[]{:S(2)}) copy-start(f32[2,2,128,128]{3,2,1,0:T(8,128)} %get-tuple-element.8) | copy-start | bytes 786436
  94.0 7.4 %collective-permute-start.4 = (f32[6,128,128]{2,1,0:T(8,128)S(1)}, f32[6,128,128]{2,1,0:T(8,128)S(1)}, u32[]{:S(2)}, u32[]{:S(2)}) collective-permute-start(f32[6,128,128]{2,1,0:T(8,128)S(1)} %fusion.6), channel_id=1, source_target_pairs={{0,1},{1,0},{2,3},{3,2},{4,5},{5,4},{6,7},{7,6},{8,9},{9,8},{10,11... | collective-permute-start | bytes 1179656 | tf_op jit(solution)/shard_map/ppermute | solution.py:180
  101.4 12.2 %collective-permute-start.5 = (f32[6,128,128]{2,1,0:T(8,128)S(1)}, f32[6,128,128]{2,1,0:T(8,128)S(1)}, u32[]{:S(2)}, u32[]{:S(2)}) collective-permute-start(f32[6,128,128]{2,1,0:T(8,128)S(1)} %add.165), channel_id=1, source_target_pairs={{0,2},{1,3},{2,0},{3,1},{4,6},{5,7},{6,4},{7,5},{8,10},{9,11},{10,... | collective-permute-start | bytes 1179656 | tf_op jit(solution)/shard_map/ppermute | solution.py:180
  104.6 13.7 %collective-permute-start.9 = (f32[2,2,128,128]{3,2,1,0:T(8,128)S(1)}, f32[2,2,128,128]{3,2,1,0:T(8,128)S(1)}, u32[]{:S(2)}, u32[]{:S(2)}) collective-permute-start(f32[2,2,128,128]{3,2,1,0:T(8,128)S(1)} %copy-done.4), channel_id=1, source_target_pairs={{0,1},{1,0},{2,3},{3,2},{4,5},{5,4},{6,7},{7,6},{8,9},{9,8},{10,11... | collective-permute-start | bytes 786440 | tf_op jit(solution)/shard_map/ppermute | solution.py:180
  113.7 22.2 %collective-permute-start.6 = (f32[6,128,128]{2,1,0:T(8,128)S(1)}, f32[6,128,128]{2,1,0:T(8,128)S(1)}, u32[]{:S(2)}, u32[]{:S(2)}) collective-permute-start(f32[6,128,128]{2,1,0:T(8,128)S(1)} %add.166), channel_id=1, source_target_pairs={{0,4},{1,5},{2,6},{3,7},{4,0},{5,1},{6,2},{7,3},{8,12},{9,13},{10,... | collective-permute-start | bytes 1179656 | tf_op jit(solution)/shard_map/ppermute | solution.py:180
  118.3 13.8 %collective-permute-start.10 = (f32[2,2,128,128]{3,2,1,0:T(8,128)S(1)}, f32[2,2,128,128]{3,2,1,0:T(8,128)S(1)}, u32[]{:S(2)}, u32[]{:S(2)}) collective-permute-start(f32[2,2,128,128]{3,2,1,0:T(8,128)S(1)} %add.168), channel_id=1, source_target_pairs={{0,2},{1,3},{2,0},{3,1},{4,6},{5,7},{6,4},{7,5},{8,10},{9,11},{10,... | collective-permute-start | bytes 786440 | tf_op jit(solution)/shard_map/ppermute | solution.py:180
  132.2 9.1 %collective-permute-start.11 = (f32[2,2,128,128]{3,2,1,0:T(8,128)S(1)}, f32[2,2,128,128]{3,2,1,0:T(8,128)S(1)}, u32[]{:S(2)}, u32[]{:S(2)}) collective-permute-start(f32[2,2,128,128]{3,2,1,0:T(8,128)S(1)} %add.169), channel_id=1, source_target_pairs={{0,4},{1,5},{2,6},{3,7},{4,0},{5,1},{6,2},{7,3},{8,12},{9,13},{10,... | collective-permute-start | bytes 786440 | tf_op jit(solution)/shard_map/ppermute | solution.py:180
  136.0 10.6 %collective-permute-start.7 = (f32[2,3,128,128]{3,2,1,0:T(8,128)S(1)}, f32[2,3,128,128]{3,2,1,0:T(8,128)S(1)}, u32[]{:S(2)}, u32[]{:S(2)}) collective-permute-start(f32[2,3,128,128]{3,2,1,0:T(8,128)S(1)} %fusion.17), channel_id=1, source_target_pairs={{0,504},{8,0},{16,8},{24,16},{32,24},{40,32},{48,40},{56,48},{64,5... | collective-permute-start | bytes 1179656 | tf_op jit(solution)/shard_map/ppermute | solution.py:20
  142.0 17.2 %all-to-all-start = ((f32[64,1,1024]{2,1,0:T(1,128)}), f32[64,1,1024]{2,1,0:T(1,128)S(1)}, u32[]{:S(2)}, u32[]{:S(2)}) async-start(f32[64,1,1024]{2,1,0:T(1,128)} %bitcast.11), calls=%async_computation | async-start | bytes 524288 | tf_op jit(solution)/shard_map/all_to_all | solution.py:187
  146.7 32.3 %collective-permute-start.8 = (f32[2,3,128,256]{3,2,1,0:T(8,128)S(1)}, f32[2,3,128,256]{3,2,1,0:T(8,128)S(1)}, u32[]{:S(2)}, u32[]{:S(2)}) collective-permute-start(f32[2,3,128,256]{3,2,1,0:T(8,128)S(1)} %pad_maximum_fusion.2), channel_id=1, source_target_pairs={{0,448},{8,456},{16,464},{24,472},{32,480},{40,488},{48,496},{56,5... | collective-permute-start | bytes 2359304 | tf_op jit(solution)/shard_map/ppermute | solution.py:20
  159.4 18.9 %copy-start.3 = (f32[2,2,128,128]{3,2,1,0:T(8,128)S(1)}, f32[2,2,128,128]{3,2,1,0:T(8,128)}, u32[]{:S(2)}) copy-start(f32[2,2,128,128]{3,2,1,0:T(8,128)} %probe_ref.1) | copy-start | bytes 786436
  196.2 5.4 %copy-start.5 = (f32[2,2,128,128]{3,2,1,0:T(8,128)S(1)}, f32[2,2,128,128]{3,2,1,0:T(8,128)}, u32[]{:S(2)}) copy-start(f32[2,2,128,128]{3,2,1,0:T(8,128)} %get-tuple-element.10) | copy-start | bytes 786436
  196.3 20.2 %collective-permute-start.12 = (f32[12,128,128]{2,1,0:T(8,128)S(1)}, f32[12,128,128]{2,1,0:T(8,128)S(1)}, u32[]{:S(2)}, u32[]{:S(2)}) collective-permute-start(f32[12,128,128]{2,1,0:T(8,128)S(1)} %pad_maximum_fusion.3), channel_id=1, source_target_pairs={{0,64},{8,72},{16,80},{24,88},{32,96},{40,104},{48,112},{56,120},{... | collective-permute-start | bytes 2359304 | tf_op jit(solution)/shard_map/ppermute | solution.py:20
  201.6 5.2 %collective-permute-start.17 = (f32[2,2,128,128]{3,2,1,0:T(8,128)S(1)}, f32[2,2,128,128]{3,2,1,0:T(8,128)S(1)}, u32[]{:S(2)}, u32[]{:S(2)}) collective-permute-start(f32[2,2,128,128]{3,2,1,0:T(8,128)S(1)} %copy-done.5), channel_id=1, source_target_pairs={{0,1},{1,0},{2,3},{3,2},{4,5},{5,4},{6,7},{7,6},{8,9},{9,8},{10,11... | collective-permute-start | bytes 786440 | tf_op jit(solution)/shard_map/ppermute | solution.py:180
  206.9 12.5 %collective-permute-start.18 = (f32[2,2,128,128]{3,2,1,0:T(8,128)S(1)}, f32[2,2,128,128]{3,2,1,0:T(8,128)S(1)}, u32[]{:S(2)}, u32[]{:S(2)}) collective-permute-start(f32[2,2,128,128]{3,2,1,0:T(8,128)S(1)} %add.177), channel_id=1, source_target_pairs={{0,2},{1,3},{2,0},{3,1},{4,6},{5,7},{6,4},{7,5},{8,10},{9,11},{10,... | collective-permute-start | bytes 786440 | tf_op jit(solution)/shard_map/ppermute | solution.py:180
  216.6 22.0 %collective-permute-start.13 = (f32[6,128,128]{2,1,0:T(8,128)S(1)}, f32[6,128,128]{2,1,0:T(8,128)S(1)}, u32[]{:S(2)}, u32[]{:S(2)}) collective-permute-start(f32[6,128,128]{2,1,0:T(8,128)S(1)} %slice_add_fusion), channel_id=1, source_target_pairs={{0,8},{8,16},{16,24},{24,32},{32,40},{40,48},{48,56},{56,64},{64,7... | collective-permute-start | bytes 1179656 | tf_op jit(solution)/shard_map/ppermute | solution.py:20
  219.4 8.9 %collective-permute-start.19 = (f32[2,2,128,128]{3,2,1,0:T(8,128)S(1)}, f32[2,2,128,128]{3,2,1,0:T(8,128)S(1)}, u32[]{:S(2)}, u32[]{:S(2)}) collective-permute-start(f32[2,2,128,128]{3,2,1,0:T(8,128)S(1)} %add.178), channel_id=1, source_target_pairs={{0,4},{1,5},{2,6},{3,7},{4,0},{5,1},{6,2},{7,3},{8,12},{9,13},{10,... | collective-permute-start | bytes 786440 | tf_op jit(solution)/shard_map/ppermute | solution.py:180
  229.1 22.0 %all-to-all-start.2 = ((f32[64,1,1024]{2,1,0:T(1,128)}), f32[64,1,1024]{2,1,0:T(1,128)S(1)}, u32[]{:S(2)}, u32[]{:S(2)}) async-start(f32[64,1,1024]{2,1,0:T(1,128)} %bitcast.22), calls=%async_computation.2 | async-start | bytes 524288 | tf_op jit(solution)/shard_map/all_to_all | solution.py:187
  238.7 7.4 %collective-permute-start.14 = (f32[6,128,128]{2,1,0:T(8,128)S(1)}, f32[6,128,128]{2,1,0:T(8,128)S(1)}, u32[]{:S(2)}, u32[]{:S(2)}) collective-permute-start(f32[6,128,128]{2,1,0:T(8,128)S(1)} %fusion.5), channel_id=1, source_target_pairs={{0,1},{1,0},{2,3},{3,2},{4,5},{5,4},{6,7},{7,6},{8,9},{9,8},{10,11... | collective-permute-start | bytes 1179656 | tf_op jit(solution)/shard_map/ppermute | solution.py:180
  246.2 16.6 %collective-permute-start.15 = (f32[6,128,128]{2,1,0:T(8,128)S(1)}, f32[6,128,128]{2,1,0:T(8,128)S(1)}, u32[]{:S(2)}, u32[]{:S(2)}) collective-permute-start(f32[6,128,128]{2,1,0:T(8,128)S(1)} %add.174), channel_id=1, source_target_pairs={{0,2},{1,3},{2,0},{3,1},{4,6},{5,7},{6,4},{7,5},{8,10},{9,11},{10,... | collective-permute-start | bytes 1179656 | tf_op jit(solution)/shard_map/ppermute | solution.py:180
  252.1 23.3 %all-to-all-start.3 = ((f32[64,1,1024]{2,1,0:T(1,128)}), f32[64,1,1024]{2,1,0:T(1,128)S(1)}, u32[]{:S(2)}, u32[]{:S(2)}) async-start(f32[64,1,1024]{2,1,0:T(1,128)} %broadcast_in_dim.5), calls=%async_computation.3 | async-start | bytes 524288 | tf_op jit(solution)/shard_map/all_to_all | solution.py:188
  262.7 12.9 %copy-start.2 = (f32[2,2,128,128]{3,2,1,0:T(8,128)S(1)}, f32[2,2,128,128]{3,2,1,0:T(8,128)}, u32[]{:S(2)}) copy-start(f32[2,2,128,128]{3,2,1,0:T(8,128)} %sub.48.probe_ref) | copy-start | bytes 786436
  262.8 13.6 %collective-permute-start.16 = (f32[6,128,128]{2,1,0:T(8,128)S(1)}, f32[6,128,128]{2,1,0:T(8,128)S(1)}, u32[]{:S(2)}, u32[]{:S(2)}) collective-permute-start(f32[6,128,128]{2,1,0:T(8,128)S(1)} %add.175), channel_id=1, source_target_pairs={{0,4},{1,5},{2,6},{3,7},{4,0},{5,1},{6,2},{7,3},{8,12},{9,13},{10,... | collective-permute-start | bytes 1179656 | tf_op jit(solution)/shard_map/ppermute | solution.py:180

commit v10 on v9

--- a/solution.py
+++ b/solution.py
@@ -251,17 +251,25 @@
             grad_ll = grad_canvas[:, :, block_side:, :block_side]
             grad_lr = grad_canvas[:, :, block_side:, block_side:]
         planes = lambda a: a.reshape(-1, block_side, block_side)
-        probe_partial = a2a_sum(xor_sum(grad_probe, "scan"), "tile")
         sent_down = jnp.concatenate(
             [
                 planes(grad_ll),
                 planes(grad_lr),
             ]
         )
+        pair = lambda a, b: lax.optimization_barrier((a, b))
+        probe_partial = xor_sum(grad_probe, "scan", [1])
+        sent_down, probe_partial = pair(sent_down, probe_partial)
         came_down = shifted(sent_down, "tile", GRID)
+        probe_partial = xor_sum(probe_partial, "scan", [2])
         own_part = planes(grad_ul) + came_down[:parts]
         right_side = planes(grad_ur) + came_down[parts:]
-        own_part = own_part + shifted(right_side, "tile", 1)
+        right_side, probe_partial = pair(right_side, probe_partial)
+        came_left = shifted(right_side, "tile", 1)
+        probe_partial = xor_sum(probe_partial, "scan", [4])
+        own_part = own_part + came_left
+        own_part, probe_partial = pair(own_part, probe_partial)
+        probe_partial = a2a_sum(probe_partial, "tile")
         grad_total = xor_sum(own_part, "scan").reshape(obj_state.shape)
         pending = probe_partial
         obj_state = obj_state - object_rate / (slot_count * group_count) * grad_total

time: 280 us -> 283 us (1.011)
  waiting for transfers between devices: 97.5 us -> 104 us
  starting transfers between devices: 106 us -> 102 us
    ppermute x12, waiting for transfers between devices: 28.8 us -> 43.7 us  [xor_sum(): lax.ppermute(values, axis, [(i, i ^ step) for i in range(size)])]
    ppermute x8, waiting for transfers between devices: 49.3 us -> 40.3 us  [shifted(): lax.ppermute(shard, axis, [(i, (i + by) % size) for i in range(size)])]
    ppermute x12, starting transfers between devices: 45.5 us -> 50.7 us  [xor_sum(): lax.ppermute(values, axis, [(i, i ^ step) for i in range(size)])]
    all_to_all x2, starting transfers between devices: 14.1 us -> 9.97 us  [a2a_sum(): lax.all_to_all(flat, axis, 0, 0, tiled=True)]
    ppermute x8, starting transfers between devices: 36.3 us -> 33.1 us  [shifted(): lax.ppermute(shard, axis, [(i, (i + by) % size) for i in range(size)])]
  transfers between devices with their start and end apart: 23 -> 23, of which waited for: 15 -> 18; matrix products, arithmetic and copies ran while one was open for 3% -> 4% of each run, Pallas kernels for 0% -> 0%
where the time goes in v10:
time: 283 us; the launch traced here: 280 us
  waiting for transfers between devices  104 us (37%)
  starting transfers between devices  102 us (36%)
  Pallas kernels  28.8 us (10%)
  blocking collectives  17.5 us (6%)
  between operations  10.7 us (4%)
  other arithmetic  9.64 us (3%)
  local copies, waits for them, and re-layouts  7.44 us (3%)
    ppermute x12, starting transfers between devices, xor_sum(): lax.ppermute(values, axis, [(i, i ^ step) for i in range(size)])  50.7 us
    ppermute x12, waiting for transfers between devices, xor_sum(): lax.ppermute(values, axis, [(i, i ^ step) for i in range(size)])  43.7 us
    ppermute x8, waiting for transfers between devices, shifted(): lax.ppermute(shard, axis, [(i, (i + by) % size) for i in range(size)])  40.3 us
    ppermute x8, starting transfers between devices, shifted(): lax.ppermute(shard, axis, [(i, (i + by) % size) for i in range(size)])  33.1 us
    pallas_call x2, Pallas kernels, slot_grad(): pl.pallas_call(slot_kernel, out_shape=(jax.ShapeDtypeStruct(patch_cells.s...  28.8 us
    all_to_all x1, blocking collectives, a2a_sum(): lax.all_to_all(jnp.broadcast_to(part, flat.shape), axis, 0, 0, tiled=True)  17.5 us
    all_to_all x2, waiting for transfers between devices, a2a_sum(): lax.all_to_all(flat, axis, 0, 0, tiled=True)  12 us
    all_to_all x2, starting transfers between devices, a2a_sum(): lax.all_to_all(flat, axis, 0, 0, tiled=True)  9.97 us
  transfers between devices with their start and end apart: 23, of which 18 were waited for; matrix products, arithmetic and copies ran while one was open for 4% of the time, Pallas kernels for 0%

profile of v10, /device:TPU:1, one launch (start us, length us, event | category | flops | bytes accessed | tf_op | source)
XLA Modules:
  0.0 280.4 jit_solution(4628884355637098328)
XLA Ops:
  0.7 1.1 pad_maximum_fusion.4
  1.8 14.4 %collective-permute-start = (f32[2,3,128,128]{3,2,1,0:T(8,128)S(1)}, f32[2,3,128,128]{3,2,1,0:T(8,128)S(1)}, u32[]{:S(2)}, u32[]{:S(2)}) collective-permute-start(f32[2,3,128,128]{3,2,1,0:T(8,128)S(1)} %pad_maximum_fusion.4), channel_id=1, source_target_pairs={{0,504},{8,0},{16,8},{24,16},{32,24},{40,32},{48,40},{56,48},{64,5... | collective-permute-start | bytes 1179656 | tf_op jit(solution)/shard_map/ppermute | solution.py:20
  16.2 7.8 %collective-permute-done = f32[2,3,128,128]{3,2,1,0:T(8,128)S(1)} collective-permute-done((f32[2,3,128,128]{3,2,1,0:T(8,128)S(1)}, f32[2,3,128,128]{3,2,1,0:T(8,128)S(1)}, u32[]{:S(2)}, u32[]{:S(2)}) %collective-permute-start) | collective-permute-done | bytes 393248 | tf_op jit(solution)/shard_map/ppermute | solution.py:20
  24.0 2.2 collective-permute-start.1
  26.2 0.6 fusion.18
  36.5 0.3 sine_multiply_fusion
  36.8 0.3 fusion.11
  37.1 0.7 pad_maximum_fusion.5.tab_ref
  37.8 5.6 %collective-permute-done.1 = f32[2,3,128,256]{3,2,1,0:T(8,128)S(1)} collective-permute-done((f32[2,3,128,256]{3,2,1,0:T(8,128)S(1)}, f32[2,3,128,256]{3,2,1,0:T(8,128)S(1)}, u32[]{:S(2)}, u32[]{:S(2)}) %collective-permute-start.1) | collective-permute-done | bytes 786464 | tf_op jit(solution)/shard_map/ppermute | solution.py:20
  43.4 1.1 fusion.4.cells_ref
  44.5 14.4 %shard_map.85 = (f32[2,3,128,128]{3,2,1,0:T(8,128)}, f32[2,2,128,128]{3,2,1,0:T(8,128)}) custom-call(f32[2,3,128,128]{3,2,1,0:T(8,128)} %fusion.4.cells_ref, f32[2,2,128,128]{3,2,1,0:T(8,128)} %probe_ref.1, f32[128,128]{1,0:T(8,128)} %bitcast.51, f32[1,1]{1,0:T(1,128)} %bitcast.5.weight_ref, f32[4,128,128]{2,1,0:T(8,128)} %pad_maximum_fusion.5.tab_ref), custom_call_target="tpu_custom_call" | custom-call | flops 1342177280 | bytes 1441792 | tf_op jit(solution)/shard_map/pallas_call | solution.py:161
  58.9 4.5 %collective-permute-start.2 = (f32[2,2,128,128]{3,2,1,0:T(8,128)}, f32[2,2,128,128]{3,2,1,0:T(8,128)S(1)}, u32[]{:S(2)}, u32[]{:S(2)}) collective-permute-start(f32[2,2,128,128]{3,2,1,0:T(8,128)} %get-tuple-element.20), channel_id=1, source_target_pairs={{0,1},{1,0},{2,3},{3,2},{4,5},{5,4},{6,7},{7,6},{8,9},{9,8},{10,11... | collective-permute-start | bytes 786440 | tf_op jit(solution)/shard_map/ppermute | solution.py:180
  63.4 1.7 pad_dynamic-slice_fusion.7
  65.2 0.9 copy-done.5
  66.1 1.9 collective-permute-start.3
  68.0 3.1 %collective-permute-start.4 = (f32[2,2,128,128]{3,2,1,0:T(8,128)S(1)}, f32[2,2,128,128]{3,2,1,0:T(8,128)S(1)}, u32[]{:S(2)}, u32[]{:S(2)}) collective-permute-start(f32[2,2,128,128]{3,2,1,0:T(8,128)S(1)} %add.162), channel_id=1, source_target_pairs={{0,2},{1,3},{2,0},{3,1},{4,6},{5,7},{6,4},{7,5},{8,10},{9,11},{10,... | collective-permute-start | bytes 786440 | tf_op jit(solution)/shard_map/ppermute | solution.py:180
  71.2 6.6 %collective-permute-done.4 = f32[2,2,128,128]{3,2,1,0:T(8,128)S(1)} collective-permute-done((f32[2,2,128,128]{3,2,1,0:T(8,128)S(1)}, f32[2,2,128,128]{3,2,1,0:T(8,128)S(1)}, u32[]{:S(2)}, u32[]{:S(2)}) %collective-permute-start.4) | collective-permute-done | bytes 262176 | tf_op jit(solution)/shard_map/ppermute | solution.py:180
  77.8 10.5 %collective-permute-done.3 = f32[12,128,128]{2,1,0:T(8,128)S(1)} collective-permute-done((f32[12,128,128]{2,1,0:T(8,128)S(1)}, f32[12,128,128]{2,1,0:T(8,128)S(1)}, u32[]{:S(2)}, u32[]{:S(2)}) %collective-permute-start.3) | collective-permute-done | bytes 786464 | tf_op jit(solution)/shard_map/ppermute | solution.py:20
  88.4 1.9 collective-permute-start.5
  90.3 4.7 %collective-permute-start.6 = (f32[2,2,128,128]{3,2,1,0:T(8,128)S(1)}, f32[2,2,128,128]{3,2,1,0:T(8,128)S(1)}, u32[]{:S(2)}, u32[]{:S(2)}) collective-permute-start(f32[2,2,128,128]{3,2,1,0:T(8,128)S(1)} %add.165), channel_id=1, source_target_pairs={{0,4},{1,5},{2,6},{3,7},{4,0},{5,1},{6,2},{7,3},{8,12},{9,13},{10,... | collective-permute-start | bytes 786440 | tf_op jit(solution)/shard_map/ppermute | solution.py:180
  95.0 5.6 %collective-permute-done.6 = f32[2,2,128,128]{3,2,1,0:T(8,128)S(1)} collective-permute-done((f32[2,2,128,128]{3,2,1,0:T(8,128)S(1)}, f32[2,2,128,128]{3,2,1,0:T(8,128)S(1)}, u32[]{:S(2)}, u32[]{:S(2)}) %collective-permute-start.6) | collective-permute-done | bytes 262176 | tf_op jit(solution)/shard_map/ppermute | solution.py:180
  100.7 0.7 add.167
  101.4 3.3 %collective-permute-done.5 = f32[6,128,128]{2,1,0:T(8,128)S(1)} collective-permute-done((f32[6,128,128]{2,1,0:T(8,128)S(1)}, f32[6,128,128]{2,1,0:T(8,128)S(1)}, u32[]{:S(2)}, u32[]{:S(2)}) %collective-permute-start.5) | collective-permute-done | bytes 393248 | tf_op jit(solution)/shard_map/ppermute | solution.py:20
  104.8 3.2 %collective-permute-start.7 = (f32[6,128,128]{2,1,0:T(8,128)S(1)}, f32[6,128,128]{2,1,0:T(8,128)S(1)}, u32[]{:S(2)}, u32[]{:S(2)}) collective-permute-start(f32[6,128,128]{2,1,0:T(8,128)S(1)} %fusion.6), channel_id=1, source_target_pairs={{0,1},{1,0},{2,3},{3,2},{4,5},{5,4},{6,7},{7,6},{8,9},{9,8},{10,11... | collective-permute-start | bytes 1179656 | tf_op jit(solution)/shard_map/ppermute | solution.py:180
  108.0 1.3 collective-permute-done.7
  109.4 3.1 %collective-permute-start.8 = (f32[6,128,128]{2,1,0:T(8,128)S(1)}, f32[6,128,128]{2,1,0:T(8,128)S(1)}, u32[]{:S(2)}, u32[]{:S(2)}) collective-permute-start(f32[6,128,128]{2,1,0:T(8,128)S(1)} %add.168), channel_id=1, source_target_pairs={{0,2},{1,3},{2,0},{3,1},{4,6},{5,7},{6,4},{7,5},{8,10},{9,11},{10,... | collective-permute-start | bytes 1179656 | tf_op jit(solution)/shard_map/ppermute | solution.py:180
  112.5 9.1 %collective-permute-done.8 = f32[6,128,128]{2,1,0:T(8,128)S(1)} collective-permute-done((f32[6,128,128]{2,1,0:T(8,128)S(1)}, f32[6,128,128]{2,1,0:T(8,128)S(1)}, u32[]{:S(2)}, u32[]{:S(2)}) %collective-permute-start.8) | collective-permute-done | bytes 393248 | tf_op jit(solution)/shard_map/ppermute | solution.py:180
  121.6 4.7 %collective-permute-start.9 = (f32[6,128,128]{2,1,0:T(8,128)S(1)}, f32[6,128,128]{2,1,0:T(8,128)S(1)}, u32[]{:S(2)}, u32[]{:S(2)}) collective-permute-start(f32[6,128,128]{2,1,0:T(8,128)S(1)} %add.169), channel_id=1, source_target_pairs={{0,4},{1,5},{2,6},{3,7},{4,0},{5,1},{6,2},{7,3},{8,12},{9,13},{10,... | collective-permute-start | bytes 1179656 | tf_op jit(solution)/shard_map/ppermute | solution.py:180
  126.4 8.1 %collective-permute-done.9 = f32[6,128,128]{2,1,0:T(8,128)S(1)} collective-permute-done((f32[6,128,128]{2,1,0:T(8,128)S(1)}, f32[6,128,128]{2,1,0:T(8,128)S(1)}, u32[]{:S(2)}, u32[]{:S(2)}) %collective-permute-start.9) | collective-permute-done | bytes 393248 | tf_op jit(solution)/shard_map/ppermute | solution.py:180
  134.6 4.7 %collective-permute-start.10 = (f32[2,3,128,128]{3,2,1,0:T(8,128)S(1)}, f32[2,3,128,128]{3,2,1,0:T(8,128)S(1)}, u32[]{:S(2)}, u32[]{:S(2)}) collective-permute-start(f32[2,3,128,128]{3,2,1,0:T(8,128)S(1)} %fusion.17), channel_id=1, source_target_pairs={{0,504},{8,0},{16,8},{24,16},{32,24},{40,32},{48,40},{56,48},{64,5... | collective-permute-start | bytes 1179656 | tf_op jit(solution)/shard_map/ppermute | solution.py:20
  139.3 4.6 %all-to-all-start = ((f32[64,1,1024]{2,1,0:T(1,128)}), f32[64,1,1024]{2,1,0:T(1,128)S(1)}, u32[]{:S(2)}, u32[]{:S(2)}) async-start(f32[64,1,1024]{2,1,0:T(1,128)} %bitcast.11), calls=%async_computation | async-start | bytes 524288 | tf_op jit(solution)/shard_map/all_to_all | solution.py:187
  143.9 1.6 collective-permute-done.10
  145.6 2.8 collective-permute-start.11
  148.4 8.0 %all-to-all-done = f32[64,1,1024]{2,1,0:T(1,128)S(1)} async-done(((f32[64,1,1024]{2,1,0:T(1,128)}), f32[64,1,1024]{2,1,0:T(1,128)S(1)}, u32[]{:S(2)}, u32[]{:S(2)}) %all-to-all-start) | async-done | bytes 262176 | tf_op jit(solution)/shard_map/all_to_all | solution.py:187
  156.4 0.2 reduce_sum.18
  156.8 17.5 %all_to_all.30 = f32[64,1,1024]{2,1,0:T(1,128)S(1)} all-to-all(f32[64,1,1024]{2,1,0:T(1,128)S(1)} %broadcast_in_dim.4), channel_id=1, replica_groups=mesh['tile'=64,'scan'=8] {'tile'}, dimensions={0} | all-to-all | bytes 524288 | tf_op jit(solution)/shard_map/all_to_all | solution.py:188
  174.3 0.3 broadcast_multiply_fusion.1
  174.6 0.8 sub.48.probe_ref
  175.4 1.1 fusion.1.cells_ref
  176.5 14.4 %shard_map.86 = (f32[2,3,128,128]{3,2,1,0:T(8,128)}, f32[2,2,128,128]{3,2,1,0:T(8,128)}) custom-call(f32[2,3,128,128]{3,2,1,0:T(8,128)} %fusion.1.cells_ref, f32[2,2,128,128]{3,2,1,0:T(8,128)} %sub.48.probe_ref, f32[128,128]{1,0:T(8,128)} %bitcast.52, f32[1,1]{1,0:T(1,128)} %bitcast.5.weight_ref, f32[4,128,128]{2,1,0:T(8,128)} %pad_maximum_fusion.5.tab_ref), custom_call_target="tpu_custom_call" | custom-call | flops 1342177280 | bytes 1441792 | tf_op jit(solution)/shard_map/pallas_call | solution.py:161
  190.9 7.5 %collective-permute-start.12 = (f32[2,2,128,128]{3,2,1,0:T(8,128)}, f32[2,2,128,128]{3,2,1,0:T(8,128)S(1)}, u32[]{:S(2)}, u32[]{:S(2)}) collective-permute-start(f32[2,2,128,128]{3,2,1,0:T(8,128)} %get-tuple-element.28), channel_id=1, source_target_pairs={{0,1},{1,0},{2,3},{3,2},{4,5},{5,4},{6,7},{7,6},{8,9},{9,8},{10,11... | collective-permute-start | bytes 786440 | tf_op jit(solution)/shard_map/ppermute | solution.py:180
  198.4 1.7 pad_dynamic-slice_fusion.3
  200.2 0.9 copy-done.4
  201.1 2.4 collective-permute-start.13
  203.5 3.1 %collective-permute-start.14 = (f32[2,2,128,128]{3,2,1,0:T(8,128)S(1)}, f32[2,2,128,128]{3,2,1,0:T(8,128)S(1)}, u32[]{:S(2)}, u32[]{:S(2)}) collective-permute-start(f32[2,2,128,128]{3,2,1,0:T(8,128)S(1)} %add.171), channel_id=1, source_target_pairs={{0,2},{1,3},{2,0},{3,1},{4,6},{5,7},{6,4},{7,5},{8,10},{9,11},{10,... | collective-permute-start | bytes 786440 | tf_op jit(solution)/shard_map/ppermute | solution.py:180
  206.7 6.3 %collective-permute-done.14 = f32[2,2,128,128]{3,2,1,0:T(8,128)S(1)} collective-permute-done((f32[2,2,128,128]{3,2,1,0:T(8,128)S(1)}, f32[2,2,128,128]{3,2,1,0:T(8,128)S(1)}, u32[]{:S(2)}, u32[]{:S(2)}) %collective-permute-start.14) | collective-permute-done | bytes 262176 | tf_op jit(solution)/shard_map/ppermute | solution.py:180
  213.0 10.3 %collective-permute-done.13 = f32[12,128,128]{2,1,0:T(8,128)S(1)} collective-permute-done((f32[12,128,128]{2,1,0:T(8,128)S(1)}, f32[12,128,128]{2,1,0:T(8,128)S(1)}, u32[]{:S(2)}, u32[]{:S(2)}) %collective-permute-start.13) | collective-permute-done | bytes 786464 | tf_op jit(solution)/shard_map/ppermute | solution.py:20
  223.3 2.7 collective-permute-start.15
  226.1 4.9 %collective-permute-start.16 = (f32[2,2,128,128]{3,2,1,0:T(8,128)S(1)}, f32[2,2,128,128]{3,2,1,0:T(8,128)S(1)}, u32[]{:S(2)}, u32[]{:S(2)}) collective-permute-start(f32[2,2,128,128]{3,2,1,0:T(8,128)S(1)} %add.174), channel_id=1, source_target_pairs={{0,4},{1,5},{2,6},{3,7},{4,0},{5,1},{6,2},{7,3},{8,12},{9,13},{10,... | collective-permute-start | bytes 786440 | tf_op jit(solution)/shard_map/ppermute | solution.py:180
  231.0 5.3 %collective-permute-done.16 = f32[2,2,128,128]{3,2,1,0:T(8,128)S(1)} collective-permute-done((f32[2,2,128,128]{3,2,1,0:T(8,128)S(1)}, f32[2,2,128,128]{3,2,1,0:T(8,128)S(1)}, u32[]{:S(2)}, u32[]{:S(2)}) %collective-permute-start.16) | collective-permute-done | bytes 262176 | tf_op jit(solution)/shard_map/ppermute | solution.py:180
  236.2 0.7 add.176
  237.0 1.4 collective-permute-done.15
  238.4 5.3 %all-to-all-start.2 = ((f32[64,1,1024]{2,1,0:T(1,128)}), f32[64,1,1024]{2,1,0:T(1,128)S(1)}, u32[]{:S(2)}, u32[]{:S(2)}) async-start(f32[64,1,1024]{2,1,0:T(1,128)} %bitcast.22), calls=%async_computation.2 | async-start | bytes 524288 | tf_op jit(solution)/shard_map/all_to_all | solution.py:187
  243.8 4.1 %collective-permute-start.17 = (f32[6,128,128]{2,1,0:T(8,128)S(1)}, f32[6,128,128]{2,1,0:T(8,128)S(1)}, u32[]{:S(2)}, u32[]{:S(2)}) collective-permute-start(f32[6,128,128]{2,1,0:T(8,128)S(1)} %fusion.5), channel_id=1, source_target_pairs={{0,1},{1,0},{2,3},{3,2},{4,5},{5,4},{6,7},{7,6},{8,9},{9,8},{10,11... | collective-permute-start | bytes 1179656 | tf_op jit(solution)/shard_map/ppermute | solution.py:180
  247.8 1.3 collective-permute-done.17
  249.2 3.1 %collective-permute-start.18 = (f32[6,128,128]{2,1,0:T(8,128)S(1)}, f32[6,128,128]{2,1,0:T(8,128)S(1)}, u32[]{:S(2)}, u32[]{:S(2)}) collective-permute-start(f32[6,128,128]{2,1,0:T(8,128)S(1)} %add.177), channel_id=1, source_target_pairs={{0,2},{1,3},{2,0},{3,1},{4,6},{5,7},{6,4},{7,5},{8,10},{9,11},{10,... | collective-permute-start | bytes 1179656 | tf_op jit(solution)/shard_map/ppermute | solution.py:180
  252.3 4.0 %all-to-all-done.2 = f32[64,1,1024]{2,1,0:T(1,128)S(1)} async-done(((f32[64,1,1024]{2,1,0:T(1,128)}), f32[64,1,1024]{2,1,0:T(1,128)S(1)}, u32[]{:S(2)}, u32[]{:S(2)}) %all-to-all-start.2) | async-done | bytes 262176 | tf_op jit(solution)/shard_map/all_to_all | solution.py:187
  256.4 0.8 broadcast_in_dim.5
  257.3 8.5 %all-to-all-start.3 = ((f32[64,1,1024]{2,1,0:T(1,128)}), f32[64,1,1024]{2,1,0:T(1,128)S(1)}, u32[]{:S(2)}, u32[]{:S(2)}) async-start(f32[64,1,1024]{2,1,0:T(1,128)} %broadcast_in_dim.5), calls=%async_computation.3 | async-start | bytes 524288 | tf_op jit(solution)/shard_map/all_to_all | solution.py:188
  265.8 4.6 %collective-permute-start.19 = (f32[6,128,128]{2,1,0:T(8,128)S(1)}, f32[6,128,128]{2,1,0:T(8,128)S(1)}, u32[]{:S(2)}, u32[]{:S(2)}) collective-permute-start(f32[6,128,128]{2,1,0:T(8,128)S(1)} %add.178), channel_id=1, source_target_pairs={{0,4},{1,5},{2,6},{3,7},{4,0},{5,1},{6,2},{7,3},{8,12},{9,13},{10,... | collective-permute-start | bytes 1179656 | tf_op jit(solution)/shard_map/ppermute | solution.py:180
  270.4 8.0 %all-to-all-done.3 = f32[64,1,1024]{2,1,0:T(1,128)S(1)} async-done(((f32[64,1,1024]{2,1,0:T(1,128)}), f32[64,1,1024]{2,1,0:T(1,128)S(1)}, u32[]{:S(2)}, u32[]{:S(2)}) %all-to-all-start.3) | async-done | bytes 262176 | tf_op jit(solution)/shard_map/all_to_all | solution.py:188
  278.4 0.3 broadcast_multiply_fusion
  278.7 0.7 sub.50
  279.6 0.8 slice_bitcast_fusion
  (40 shorter events, 1.5 us)
Async XLA Ops:
  0.6 23.3 %copy-start.1 = (f32[3,1,128,128]{3,2,1,0:T(8,128)S(1)}, f32[3,1,128,128]{3,2,1,0:T(8,128)}, u32[]{:S(2)}) copy-start(f32[3,1,128,128]{3,2,1,0:T(8,128)} %param.7) | copy-start | bytes 589828
  0.6 23.3 %copy-start = (f32[3,1,128,128]{3,2,1,0:T(8,128)S(1)}, f32[3,1,128,128]{3,2,1,0:T(8,128)}, u32[]{:S(2)}) copy-start(f32[3,1,128,128]{3,2,1,0:T(8,128)} %param.6) | copy-start | bytes 589828
  1.8 24.4 %copy-start.6 = (s32[1,1,1,2]{3,2,1,0:T(1,128)S(1)}, s32[1,1,1,2]{3,2,1,0:T(1,128)}, u32[]{:S(2)}) copy-start(s32[1,1,1,2]{3,2,1,0:T(1,128)} %param.10) | copy-start | bytes 28
  1.8 22.2 %collective-permute-start = (f32[2,3,128,128]{3,2,1,0:T(8,128)S(1)}, f32[2,3,128,128]{3,2,1,0:T(8,128)S(1)}, u32[]{:S(2)}, u32[]{:S(2)}) collective-permute-start(f32[2,3,128,128]{3,2,1,0:T(8,128)S(1)} %pad_maximum_fusion.4), channel_id=1, source_target_pairs={{0,504},{8,0},{16,8},{24,16},{32,24},{40,32},{48,40},{56,48},{64,5... | collective-permute-start | bytes 1179656 | tf_op jit(solution)/shard_map/ppermute | solution.py:20
  24.0 19.4 %collective-permute-start.1 = (f32[2,3,128,256]{3,2,1,0:T(8,128)S(1)}, f32[2,3,128,256]{3,2,1,0:T(8,128)S(1)}, u32[]{:S(2)}, u32[]{:S(2)}) collective-permute-start(f32[2,3,128,256]{3,2,1,0:T(8,128)S(1)} %pad_maximum_fusion), channel_id=1, source_target_pairs={{0,448},{8,456},{16,464},{24,472},{32,480},{40,488},{48,496},{56,5... | collective-permute-start | bytes 2359304 | tf_op jit(solution)/shard_map/ppermute | solution.py:20
  58.9 6.3 %collective-permute-start.2 = (f32[2,2,128,128]{3,2,1,0:T(8,128)}, f32[2,2,128,128]{3,2,1,0:T(8,128)S(1)}, u32[]{:S(2)}, u32[]{:S(2)}) collective-permute-start(f32[2,2,128,128]{3,2,1,0:T(8,128)} %get-tuple-element.20), channel_id=1, source_target_pairs={{0,1},{1,0},{2,3},{3,2},{4,5},{5,4},{6,7},{7,6},{8,9},{9,8},{10,11... | collective-permute-start | bytes 786440 | tf_op jit(solution)/shard_map/ppermute | solution.py:180
  65.1 0.9 copy-start.5
  66.1 22.2 %collective-permute-start.3 = (f32[12,128,128]{2,1,0:T(8,128)S(1)}, f32[12,128,128]{2,1,0:T(8,128)S(1)}, u32[]{:S(2)}, u32[]{:S(2)}) collective-permute-start(f32[12,128,128]{2,1,0:T(8,128)S(1)} %pad_maximum_fusion.1), channel_id=1, source_target_pairs={{0,64},{8,72},{16,80},{24,88},{32,96},{40,104},{48,112},{56,120},{... | collective-permute-start | bytes 2359304 | tf_op jit(solution)/shard_map/ppermute | solution.py:20
  68.0 9.8 %collective-permute-start.4 = (f32[2,2,128,128]{3,2,1,0:T(8,128)S(1)}, f32[2,2,128,128]{3,2,1,0:T(8,128)S(1)}, u32[]{:S(2)}, u32[]{:S(2)}) collective-permute-start(f32[2,2,128,128]{3,2,1,0:T(8,128)S(1)} %add.162), channel_id=1, source_target_pairs={{0,2},{1,3},{2,0},{3,1},{4,6},{5,7},{6,4},{7,5},{8,10},{9,11},{10,... | collective-permute-start | bytes 786440 | tf_op jit(solution)/shard_map/ppermute | solution.py:180
  88.4 16.3 %collective-permute-start.5 = (f32[6,128,128]{2,1,0:T(8,128)S(1)}, f32[6,128,128]{2,1,0:T(8,128)S(1)}, u32[]{:S(2)}, u32[]{:S(2)}) collective-permute-start(f32[6,128,128]{2,1,0:T(8,128)S(1)} %slice_add_fusion.2), channel_id=1, source_target_pairs={{0,8},{8,16},{16,24},{24,32},{32,40},{40,48},{48,56},{56,64},{64,7... | collective-permute-start | bytes 1179656 | tf_op jit(solution)/shard_map/ppermute | solution.py:20
  90.3 10.4 %collective-permute-start.6 = (f32[2,2,128,128]{3,2,1,0:T(8,128)S(1)}, f32[2,2,128,128]{3,2,1,0:T(8,128)S(1)}, u32[]{:S(2)}, u32[]{:S(2)}) collective-permute-start(f32[2,2,128,128]{3,2,1,0:T(8,128)S(1)} %add.165), channel_id=1, source_target_pairs={{0,4},{1,5},{2,6},{3,7},{4,0},{5,1},{6,2},{7,3},{8,12},{9,13},{10,... | collective-permute-start | bytes 786440 | tf_op jit(solution)/shard_map/ppermute | solution.py:180
  104.8 4.6 %collective-permute-start.7 = (f32[6,128,128]{2,1,0:T(8,128)S(1)}, f32[6,128,128]{2,1,0:T(8,128)S(1)}, u32[]{:S(2)}, u32[]{:S(2)}) collective-permute-start(f32[6,128,128]{2,1,0:T(8,128)S(1)} %fusion.6), channel_id=1, source_target_pairs={{0,1},{1,0},{2,3},{3,2},{4,5},{5,4},{6,7},{7,6},{8,9},{9,8},{10,11... | collective-permute-start | bytes 1179656 | tf_op jit(solution)/shard_map/ppermute | solution.py:180
  109.4 12.2 %collective-permute-start.8 = (f32[6,128,128]{2,1,0:T(8,128)S(1)}, f32[6,128,128]{2,1,0:T(8,128)S(1)}, u32[]{:S(2)}, u32[]{:S(2)}) collective-permute-start(f32[6,128,128]{2,1,0:T(8,128)S(1)} %add.168), channel_id=1, source_target_pairs={{0,2},{1,3},{2,0},{3,1},{4,6},{5,7},{6,4},{7,5},{8,10},{9,11},{10,... | collective-permute-start | bytes 1179656 | tf_op jit(solution)/shard_map/ppermute | solution.py:180
  121.6 12.8 %collective-permute-start.9 = (f32[6,128,128]{2,1,0:T(8,128)S(1)}, f32[6,128,128]{2,1,0:T(8,128)S(1)}, u32[]{:S(2)}, u32[]{:S(2)}) collective-permute-start(f32[6,128,128]{2,1,0:T(8,128)S(1)} %add.169), channel_id=1, source_target_pairs={{0,4},{1,5},{2,6},{3,7},{4,0},{5,1},{6,2},{7,3},{8,12},{9,13},{10,... | collective-permute-start | bytes 1179656 | tf_op jit(solution)/shard_map/ppermute | solution.py:180
  134.6 11.0 %collective-permute-start.10 = (f32[2,3,128,128]{3,2,1,0:T(8,128)S(1)}, f32[2,3,128,128]{3,2,1,0:T(8,128)S(1)}, u32[]{:S(2)}, u32[]{:S(2)}) collective-permute-start(f32[2,3,128,128]{3,2,1,0:T(8,128)S(1)} %fusion.17), channel_id=1, source_target_pairs={{0,504},{8,0},{16,8},{24,16},{32,24},{40,32},{48,40},{56,48},{64,5... | collective-permute-start | bytes 1179656 | tf_op jit(solution)/shard_map/ppermute | solution.py:20
  139.3 17.1 %all-to-all-start = ((f32[64,1,1024]{2,1,0:T(1,128)}), f32[64,1,1024]{2,1,0:T(1,128)S(1)}, u32[]{:S(2)}, u32[]{:S(2)}) async-start(f32[64,1,1024]{2,1,0:T(1,128)} %bitcast.11), calls=%async_computation | async-start | bytes 524288 | tf_op jit(solution)/shard_map/all_to_all | solution.py:187
  145.6 29.7 %collective-permute-start.11 = (f32[2,3,128,256]{3,2,1,0:T(8,128)S(1)}, f32[2,3,128,256]{3,2,1,0:T(8,128)S(1)}, u32[]{:S(2)}, u32[]{:S(2)}) collective-permute-start(f32[2,3,128,256]{3,2,1,0:T(8,128)S(1)} %pad_maximum_fusion.2), channel_id=1, source_target_pairs={{0,448},{8,456},{16,464},{24,472},{32,480},{40,488},{48,496},{56,5... | collective-permute-start | bytes 2359304 | tf_op jit(solution)/shard_map/ppermute | solution.py:20
  156.6 18.0 %copy-start.3 = (f32[2,2,128,128]{3,2,1,0:T(8,128)S(1)}, f32[2,2,128,128]{3,2,1,0:T(8,128)}, u32[]{:S(2)}) copy-start(f32[2,2,128,128]{3,2,1,0:T(8,128)} %probe_ref.1) | copy-start | bytes 786436
  190.9 9.2 %collective-permute-start.12 = (f32[2,2,128,128]{3,2,1,0:T(8,128)}, f32[2,2,128,128]{3,2,1,0:T(8,128)S(1)}, u32[]{:S(2)}, u32[]{:S(2)}) collective-permute-start(f32[2,2,128,128]{3,2,1,0:T(8,128)} %get-tuple-element.28), channel_id=1, source_target_pairs={{0,1},{1,0},{2,3},{3,2},{4,5},{5,4},{6,7},{7,6},{8,9},{9,8},{10,11... | collective-permute-start | bytes 786440 | tf_op jit(solution)/shard_map/ppermute | solution.py:180
  200.1 0.9 copy-start.4
  201.1 22.2 %collective-permute-start.13 = (f32[12,128,128]{2,1,0:T(8,128)S(1)}, f32[12,128,128]{2,1,0:T(8,128)S(1)}, u32[]{:S(2)}, u32[]{:S(2)}) collective-permute-start(f32[12,128,128]{2,1,0:T(8,128)S(1)} %pad_maximum_fusion.3), channel_id=1, source_target_pairs={{0,64},{8,72},{16,80},{24,88},{32,96},{40,104},{48,112},{56,120},{... | collective-permute-start | bytes 2359304 | tf_op jit(solution)/shard_map/ppermute | solution.py:20
  203.5 9.4 %collective-permute-start.14 = (f32[2,2,128,128]{3,2,1,0:T(8,128)S(1)}, f32[2,2,128,128]{3,2,1,0:T(8,128)S(1)}, u32[]{:S(2)}, u32[]{:S(2)}) collective-permute-start(f32[2,2,128,128]{3,2,1,0:T(8,128)S(1)} %add.171), channel_id=1, source_target_pairs={{0,2},{1,3},{2,0},{3,1},{4,6},{5,7},{6,4},{7,5},{8,10},{9,11},{10,... | collective-permute-start | bytes 786440 | tf_op jit(solution)/shard_map/ppermute | solution.py:180
  223.3 15.0 %collective-permute-start.15 = (f32[6,128,128]{2,1,0:T(8,128)S(1)}, f32[6,128,128]{2,1,0:T(8,128)S(1)}, u32[]{:S(2)}, u32[]{:S(2)}) collective-permute-start(f32[6,128,128]{2,1,0:T(8,128)S(1)} %slice_add_fusion), channel_id=1, source_target_pairs={{0,8},{8,16},{16,24},{24,32},{32,40},{40,48},{48,56},{56,64},{64,7... | collective-permute-start | bytes 1179656 | tf_op jit(solution)/shard_map/ppermute | solution.py:20
  226.1 10.2 %collective-permute-start.16 = (f32[2,2,128,128]{3,2,1,0:T(8,128)S(1)}, f32[2,2,128,128]{3,2,1,0:T(8,128)S(1)}, u32[]{:S(2)}, u32[]{:S(2)}) collective-permute-start(f32[2,2,128,128]{3,2,1,0:T(8,128)S(1)} %add.174), channel_id=1, source_target_pairs={{0,4},{1,5},{2,6},{3,7},{4,0},{5,1},{6,2},{7,3},{8,12},{9,13},{10,... | collective-permute-start | bytes 786440 | tf_op jit(solution)/shard_map/ppermute | solution.py:180
  238.4 17.8 %all-to-all-start.2 = ((f32[64,1,1024]{2,1,0:T(1,128)}), f32[64,1,1024]{2,1,0:T(1,128)S(1)}, u32[]{:S(2)}, u32[]{:S(2)}) async-start(f32[64,1,1024]{2,1,0:T(1,128)} %bitcast.22), calls=%async_computation.2 | async-start | bytes 524288 | tf_op jit(solution)/shard_map/all_to_all | solution.py:187
  243.8 5.4 %collective-permute-start.17 = (f32[6,128,128]{2,1,0:T(8,128)S(1)}, f32[6,128,128]{2,1,0:T(8,128)S(1)}, u32[]{:S(2)}, u32[]{:S(2)}) collective-permute-start(f32[6,128,128]{2,1,0:T(8,128)S(1)} %fusion.5), channel_id=1, source_target_pairs={{0,1},{1,0},{2,3},{3,2},{4,5},{5,4},{6,7},{7,6},{8,9},{9,8},{10,11... | collective-permute-start | bytes 1179656 | tf_op jit(solution)/shard_map/ppermute | solution.py:180
  249.2 16.6 %collective-permute-start.18 = (f32[6,128,128]{2,1,0:T(8,128)S(1)}, f32[6,128,128]{2,1,0:T(8,128)S(1)}, u32[]{:S(2)}, u32[]{:S(2)}) collective-permute-start(f32[6,128,128]{2,1,0:T(8,128)S(1)} %add.177), channel_id=1, source_target_pairs={{0,2},{1,3},{2,0},{3,1},{4,6},{5,7},{6,4},{7,5},{8,10},{9,11},{10,... | collective-permute-start | bytes 1179656 | tf_op jit(solution)/shard_map/ppermute | solution.py:180
  257.3 21.1 %all-to-all-start.3 = ((f32[64,1,1024]{2,1,0:T(1,128)}), f32[64,1,1024]{2,1,0:T(1,128)S(1)}, u32[]{:S(2)}, u32[]{:S(2)}) async-start(f32[64,1,1024]{2,1,0:T(1,128)} %broadcast_in_dim.5), calls=%async_computation.3 | async-start | bytes 524288 | tf_op jit(solution)/shard_map/all_to_all | solution.py:188
  265.8 12.9 %copy-start.2 = (f32[2,2,128,128]{3,2,1,0:T(8,128)S(1)}, f32[2,2,128,128]{3,2,1,0:T(8,128)}, u32[]{:S(2)}) copy-start(f32[2,2,128,128]{3,2,1,0:T(8,128)} %sub.48.probe_ref) | copy-start | bytes 786436
  265.8 13.6 %collective-permute-start.19 = (f32[6,128,128]{2,1,0:T(8,128)S(1)}, f32[6,128,128]{2,1,0:T(8,128)S(1)}, u32[]{:S(2)}, u32[]{:S(2)}) collective-permute-start(f32[6,128,128]{2,1,0:T(8,128)S(1)} %add.178), channel_id=1, source_target_pairs={{0,4},{1,5},{2,6},{3,7},{4,0},{5,1},{6,2},{7,3},{8,12},{9,13},{10,... | collective-permute-start | bytes 1179656 | tf_op jit(solution)/shard_map/ppermute | solution.py:180
